TPU v7x, 512 devices: a whole 4x4x16 slice. The times are simulated.
512 devices in a mesh: dp: 32 (over z, x_hi), mp: 16 (over x_lo, y, core).
Axes of the slice: x: 4 (x_hi: 2, x_lo: 2; x = x_hi * 2 + x_lo), y: 4, z: 16, core: 2. Of those that a mesh axis runs over, the one named last changes fastest.
Arguments:
- tokens: bfloat16 [32768, 2048], P('dp', 'mp'), may hold values from -6 to 6
- norm_gain: bfloat16 [2048], replicated, may hold values from 0.099609375 to 1.8984375
- wi_gate: bfloat16 [2048, 5120], P(None, 'mp'), may hold values from -0.125 to 0.125
- wi_linear: bfloat16 [2048, 5120], P(None, 'mp'), may hold values from -0.125 to 0.125
- wo_out: bfloat16 [5120, 2048], P('mp'), may hold values from -0.078125 to 0.078125
- task_table: float32 [8, 64], replicated, may hold values from -5 to 5
- layer_table: float32 [24, 64], replicated, may hold values from -5 to 5
- task_ids: int32 [256], P('dp'), may hold values from 0 to 7
- layer_index: int32 [1], replicated, may hold values from 0 to 23
- hyper_in: bfloat16 [128, 1024], P(None, 'mp'), may hold values from -0.5 to 0.5
- gen_down: bfloat16 [1024, 131072], P(None, ('mp', 'dp')), may hold values from -0.0078125 to 0.0078125
- gen_up: bfloat16 [1024, 131072], P(None, ('mp', 'dp')), may hold values from -0.046875 to 0.046875
Outputs:
- mixed: bfloat16 [32768, 2048], P('dp', 'mp')
All inputs are finite; a program needn't handle non-finite values.
Results may differ from a plain program's by a relative error of at most 0.019.
Values may be sent and summed in bfloat16 or wider, within the bound.
No kernel may reach another device: no remote copies, remote signals or barrier semaphores. Data moves between devices by JAX's collectives and lax.ppermute only.
A program may use at most 64 MiB of HBM per device.

v0:
```python
import jax
import jax.numpy as jnp
from jax import lax
from jax.sharding import PartitionSpec as P

R = 64


def laid_out(blocks, dim):
    lengths = list(blocks.shape[1:])
    lengths[dim] *= blocks.shape[0]
    return jnp.moveaxis(blocks, 0, dim).reshape(lengths)


def from_everyone(shard, axis):
    copies = jnp.broadcast_to(shard, (lax.axis_size(axis), *shard.shape))
    return lax.all_to_all(copies, axis, split_axis=0, concat_axis=0, tiled=True)


def gather_directly(shard, axis, dim):
    return laid_out(from_everyone(shard, axis), dim)


def of_everyone(shard, axis):
    everything = from_everyone(shard, axis)
    return jnp.sum(everything.astype(jnp.float32), axis=0)


def matmul(left, right):
    return jnp.dot(left, right, preferred_element_type=jnp.float32)


def per_device(
    tokens,
    norm_gain,
    wi_gate,
    wi_linear,
    wo_out,
    task_table,
    layer_table,
    task_ids,
    layer_index,
    hyper_in,
    gen_down,
    gen_up,
):
    task_count = task_table.shape[0]
    layer_row = jnp.take(layer_table, layer_index, axis=0)
    embed = jnp.concatenate(
        [task_table, jnp.broadcast_to(layer_row, (task_count, layer_row.shape[1]))], axis=1
    ).astype(jnp.bfloat16)
    hidden_part = jnp.maximum(matmul(embed, hyper_in), 0.0).astype(jnp.bfloat16)
    hidden = gather_directly(hidden_part, "mp", 1)
    every_id = gather_directly(task_ids, "dp", 0)
    wanted = jnp.take(hidden, every_id, axis=0)
    made = (
        matmul(wanted, gen_down).astype(jnp.bfloat16),
        matmul(wanted, gen_up).astype(jnp.bfloat16),
    )
    local_down, local_up = (
        lax.all_to_all(made[0], "dp", split_axis=0, concat_axis=1, tiled=True),
        lax.all_to_all(made[1], "dp", split_axis=0, concat_axis=1, tiled=True),
    )
    full_rows = lax.all_gather(tokens, "mp", axis=1, tiled=True)
    wide = full_rows.astype(jnp.float32)
    scale = lax.rsqrt(jnp.mean(wide * wide, axis=-1, keepdims=True) + 1e-06)
    normed = (wide * scale * norm_gain.astype(jnp.float32)).astype(jnp.bfloat16)
    gate = matmul(normed, wi_gate)
    linear = matmul(normed, wi_linear)
    act = (jax.nn.gelu(gate, approximate=True) * linear).astype(jnp.bfloat16)
    seqs_dev = task_ids.shape[0]
    tok_dev = tokens.shape[0]
    seq_len = tok_dev // seqs_dev
    partial_sums = matmul(act, wo_out)
    ffout = lax.psum_scatter(
        partial_sums.astype(jnp.bfloat16), "mp", scatter_dimension=1, tiled=True
    )
    down_block = local_down.reshape(seqs_dev, -1, R)
    up_block = local_up.reshape(seqs_dev, -1, R)
    blocks = ffout.reshape(seqs_dev, seq_len, -1)
    squeeze_part = jnp.einsum(
        "std,sdr->str", blocks, down_block, preferred_element_type=jnp.float32
    )
    squeeze_full = of_everyone(squeeze_part.astype(jnp.bfloat16), "mp").astype(jnp.float32)
    squeezed = jnp.maximum(squeeze_full, 0.0).astype(jnp.bfloat16)
    expand = jnp.einsum("str,sdr->std", squeezed, up_block, preferred_element_type=jnp.float32)
    total = tokens.astype(jnp.float32) + ffout.astype(jnp.float32) + expand.reshape(tok_dev, -1)
    return total.astype(jnp.bfloat16)


def solution(mesh):
    return jax.shard_map(
        per_device,
        mesh=mesh,
        in_specs=(
            P("dp", "mp"),
            P(),
            P(None, "mp"),
            P(None, "mp"),
            P("mp", None),
            P(),
            P(),
            P("dp"),
            P(),
            P(None, "mp"),
            P(None, ("mp", "dp")),
            P(None, ("mp", "dp")),
        ),
        out_specs=P("dp", "mp"),
        check_vma=False,
    )
```

profile of v0, /device:TPU:1, one launch (start us, length us, event | category | flops | bytes accessed | tf_op | source)
XLA Modules:
  0.0 218.8 jit_solution(13709303609028139173)
XLA Ops:
  6.5 0.7 all-gather.2.cloned.1.call-update
  7.3 0.0 reduce-scatter.4.cloned.1.call-start
  7.3 0.7 convert_element_type.45
  8.0 61.3 %all-gather.2.cloned.1.call-done = bf16[1024,2048]{1,0:T(8,128)(2,1)} async-done(((bf16[1024,128]{1,0:T(8,128)(2,1)}), bf16[1024,2048]{1,0:T(8,128)(2,1)}) %all-gather.2.cloned.1.call-update) | async-done | bytes 4194320 | tf_op jit(solution)/shard_map/all_gather | solution.py:64
  69.3 3.2 %fusion = f32[1024]{0:T(1024)S(1)} fusion(bf16[1024,2048]{1,0:T(8,128)(2,1)} %all-gather.2.cloned.1.call-done), kind=kLoop, calls=%fused_computation.3 | loop fusion | flops 6290432 | bytes 4198400 | tf_op jit(solution)/shard_map/reduce_sum | solution.py:66
  72.5 0.2 copy-done.1
  72.7 4.2 %fusion.12 = f32[1024,320]{0,1:T(8,128)} fusion(bf16[2048,320]{0,1:T(8,128)(2,1)} %param.14, bf16[1024,2048]{1,0:T(8,128)(2,1)S(1)} %copy-done.1, f32[2048]{0:T(1024)S(1)} %convert_element_type.45, f32[1024]{0:T(1024)S(1)} %add_rsqrt_fusion), kind=kOutput, calls=%fused_computation.18 | convolution fusion | flops 1350565888 | bytes 6828032 | tf_op jit(solution)/shard_map/dot_general | solution.py:30
  76.9 8.6 %convolution_convert_fusion = bf16[1024,2048]{1,0:T(8,128)(2,1)} fusion(bf16[320,2048]{1,0:T(8,128)(2,1)S(1)} %copy-done, bf16[2048,320]{0,1:T(8,128)(2,1)S(1)} %copy-done.10, f32[1024,320]{0,1:T(8,128)} %fusion.12, bf16[1024,2048]{1,0:T(8,128)(2,1)} %all-gather.2.cloned.1.call-done, f32[2048]{0:T(1024)S(1)} %convert_element_type.45, f32[1024]{0:T(1024)S(1)} %add_rsqrt_fusion), kind=kOutput, calls=%fused_computation.7 | convolution fusion | flops 2698117120 | bytes 12333056 | tf_op jit(solution)/shard_map/dot_general | solution.py:30
  85.6 6.4 %copy.23 = bf16[1024,2048]{0,1:T(8,128)(2,1)} copy(bf16[1024,2048]{1,0:T(8,128)(2,1)} %convolution_convert_fusion) | data formatting | bytes 8388608
  92.0 0.0 reduce-scatter.4.cloned.1.call-update
  92.0 0.6 copy-done.9
  92.6 0.6 broadcast_in_dim.38
  93.2 13.2 %all-to-all-start = ((s32[32,1,8]{2,1,0:T(1,128)}), s32[32,1,8]{2,1,0:T(1,128)S(1)}, u32[]{:S(2)}, u32[]{:S(2)}) async-start(s32[32,1,8]{2,1,0:T(1,128)} %broadcast_in_dim.38), calls=%async_computation | async-start | bytes 32768 | tf_op jit(solution)/shard_map/all_to_all | solution.py:17
  107.1 0.7 fusion.30
  107.8 0.1 pad.3.clone
  107.9 0.1 fusion.18
  108.0 0.7 reshape.145
  108.7 11.3 %all-to-all-done = s32[32,1,8]{2,1,0:T(1,128)S(1)} async-done(((s32[32,1,8]{2,1,0:T(1,128)}), s32[32,1,8]{2,1,0:T(1,128)S(1)}, u32[]{:S(2)}, u32[]{:S(2)}) %all-to-all-start) | async-done | bytes 1056 | tf_op jit(solution)/shard_map/all_to_all | solution.py:17
  120.0 5.0 %all-to-all-start.1 = ((bf16[16,2,256]{2,1,0:T(2,128)(2,1)}), bf16[16,2,256]{2,1,0:T(2,128)(2,1)S(1)}, u32[]{:S(2)}, u32[]{:S(2)}) async-start(bf16[16,2,256]{2,1,0:T(2,128)(2,1)} %reshape.145), calls=%async_computation.1 | async-start | bytes 32768 | tf_op jit(solution)/shard_map/all_to_all | solution.py:17
  125.0 0.1 reshape.91
  125.1 0.6 broadcast.82
  125.7 0.7 reduce.5
  126.4 0.1 reshape.89
  126.5 4.3 %all-to-all-done.1 = bf16[16,2,256]{2,1,0:T(2,128)(2,1)S(1)} async-done(((bf16[16,2,256]{2,1,0:T(2,128)(2,1)}), bf16[16,2,256]{2,1,0:T(2,128)(2,1)S(1)}, u32[]{:S(2)}, u32[]{:S(2)}) %all-to-all-start.1) | async-done | bytes 16416 | tf_op jit(solution)/shard_map/all_to_all | solution.py:17
  130.8 0.1 reshape.146
  130.9 0.1 reshape.90
  131.0 0.0 copy-start.11
  131.0 1.2 gather_fusion
  132.2 0.0 copy-start.12
  132.2 1.0 fusion.14
  133.2 3.8 %all-to-all-start.2 = ((bf16[32,8,256]{2,1,0:T(8,128)(2,1)}), bf16[32,8,256]{2,1,0:T(8,128)(2,1)S(1)}, u32[]{:S(2)}, u32[]{:S(2)}) async-start(bf16[32,8,256]{2,1,0:T(8,128)(2,1)} %fusion.14), calls=%async_computation.2 | async-start | bytes 262144 | tf_op jit(solution)/shard_map/all_to_all | solution.py:61
  137.1 1.0 fusion.15
  138.1 14.6 %all-to-all-done.2 = bf16[32,8,256]{2,1,0:T(8,128)(2,1)S(1)} async-done(((bf16[32,8,256]{2,1,0:T(8,128)(2,1)}), bf16[32,8,256]{2,1,0:T(8,128)(2,1)S(1)}, u32[]{:S(2)}, u32[]{:S(2)}) %all-to-all-start.2) | async-done | bytes 131104 | tf_op jit(solution)/shard_map/all_to_all | solution.py:61
  152.6 5.2 %all-to-all-start.4 = ((bf16[32,8,256]{2,1,0:T(8,128)(2,1)}), bf16[32,8,256]{2,1,0:T(8,128)(2,1)S(1)}, u32[]{:S(2)}, u32[]{:S(2)}) async-start(bf16[32,8,256]{2,1,0:T(8,128)(2,1)} %fusion.15), calls=%async_computation.4 | async-start | bytes 262144 | tf_op jit(solution)/shard_map/all_to_all | solution.py:62
  157.9 0.2 reshape.92
  158.1 5.4 %reduce-scatter.4.cloned.1.call-done = bf16[128,1024]{1,0:T(8,128)(2,1)} async-done(((bf16[2048,1024]{1,0:T(8,128)(2,1)}), bf16[128,1024]{1,0:T(8,128)(2,1)}) %reduce-scatter.4.cloned.1.call-update) | async-done | bytes 262160
  163.5 1.1 copy.24
  164.6 0.3 convolution_convert_fusion.2
  164.9 7.7 %all-to-all-done.4 = bf16[32,8,256]{2,1,0:T(8,128)(2,1)S(1)} async-done(((bf16[32,8,256]{2,1,0:T(8,128)(2,1)}), bf16[32,8,256]{2,1,0:T(8,128)(2,1)S(1)}, u32[]{:S(2)}, u32[]{:S(2)}) %all-to-all-start.4) | async-done | bytes 131104 | tf_op jit(solution)/shard_map/all_to_all | solution.py:62
  172.6 1.9 broadcast_in_dim.46
  174.5 7.2 %all-to-all-start.3 = ((bf16[16,8,128,64]{2,3,1,0:T(8,128)(2,1)}), bf16[16,8,128,64]{2,3,1,0:T(8,128)(2,1)S(1)}, u32[]{:S(2)}, u32[]{:S(2)}) async-start(bf16[16,8,128,64]{2,3,1,0:T(8,128)(2,1)} %broadcast_in_dim.46), calls=%async_computation.3 | async-start | bytes 4194304 | tf_op jit(solution)/shard_map/all_to_all | solution.py:17
  181.7 0.9 copy.19
  182.6 0.9 reshape.93
  183.5 26.3 %all-to-all-done.3 = bf16[16,8,128,64]{2,3,1,0:T(8,128)(2,1)S(1)} async-done(((bf16[16,8,128,64]{2,3,1,0:T(8,128)(2,1)}), bf16[16,8,128,64]{2,3,1,0:T(8,128)(2,1)S(1)}, u32[]{:S(2)}, u32[]{:S(2)}) %all-to-all-start.3) | async-done | bytes 2097184 | tf_op jit(solution)/shard_map/all_to_all | solution.py:17
  209.8 0.3 convert_reduce_fusion
  210.2 0.6 copy-done.5
  210.8 0.3 fusion.24
  211.1 0.8 fusion.23
  (30 shorter events, 0.1 us)
Async XLA Ops:
  6.5 70.4 %copy-start = (bf16[320,2048]{1,0:T(8,128)(2,1)S(1)}, bf16[320,2048]{1,0:T(8,128)(2,1)}, u32[]{:S(2)}) copy-start(bf16[320,2048]{1,0:T(8,128)(2,1)} %param.16) | copy-start | bytes 3932164
  6.5 62.7 %all-gather.2.cloned.1.call-start = ((), (), s32[]{:S(2)}) async-start(), calls=%async_computation.6 | async-start | bytes 4456448 | tf_op jit(solution)/shard_map/all_gather | solution.py:64
  7.3 156.2 %reduce-scatter.4.cloned.1.call-start = ((), (), s32[]{:S(2)}) async-start(), calls=%async_computation.7 | async-start | bytes 4456448
  69.3 3.4 %copy-start.1 = (bf16[1024,2048]{1,0:T(8,128)(2,1)S(1)}, bf16[1024,2048]{1,0:T(8,128)(2,1)}, u32[]{:S(2)}) copy-start(bf16[1024,2048]{1,0:T(8,128)(2,1)} %all-gather.2.cloned.1.call-done) | copy-start | bytes 12582916
  72.7 4.2 %copy-start.10 = (bf16[2048,320]{0,1:T(8,128)(2,1)S(1)}, bf16[2048,320]{0,1:T(8,128)(2,1)}, u32[]{:S(2)}) copy-start(bf16[2048,320]{0,1:T(8,128)(2,1)} %param.15) | copy-start | bytes 3932164
  92.0 0.7 copy-start.9
  92.0 15.1 %copy-start.8 = (f32[8,64]{1,0:T(8,128)S(1)}, f32[8,64]{1,0:T(8,128)}, u32[]{:S(2)}) copy-start(f32[8,64]{1,0:T(8,128)} %param.17) | copy-start | bytes 6148
  92.0 15.9 %copy-start.7 = (bf16[128,64]{0,1:T(8,128)(2,1)S(1)}, bf16[128,64]{0,1:T(8,128)(2,1)}, u32[]{:S(2)}) copy-start(bf16[128,64]{0,1:T(8,128)(2,1)} %param.21) | copy-start | bytes 49156
  93.2 26.7 %all-to-all-start = ((s32[32,1,8]{2,1,0:T(1,128)}), s32[32,1,8]{2,1,0:T(1,128)S(1)}, u32[]{:S(2)}, u32[]{:S(2)}) async-start(s32[32,1,8]{2,1,0:T(1,128)} %broadcast_in_dim.38), calls=%async_computation | async-start | bytes 32768 | tf_op jit(solution)/shard_map/all_to_all | solution.py:17
  120.0 10.8 %all-to-all-start.1 = ((bf16[16,2,256]{2,1,0:T(2,128)(2,1)}), bf16[16,2,256]{2,1,0:T(2,128)(2,1)S(1)}, u32[]{:S(2)}, u32[]{:S(2)}) async-start(bf16[16,2,256]{2,1,0:T(2,128)(2,1)} %reshape.145), calls=%async_computation.1 | async-start | bytes 32768 | tf_op jit(solution)/shard_map/all_to_all | solution.py:17
  131.0 1.2 copy-start.11
  132.2 4.9 %copy-start.12 = (bf16[1024,256]{1,0:T(8,128)(2,1)S(1)}, bf16[1024,256]{1,0:T(8,128)(2,1)}, u32[]{:S(2)}) copy-start(bf16[1024,256]{1,0:T(8,128)(2,1)} %param.23) | copy-start | bytes 1572868
  133.2 19.4 %all-to-all-start.2 = ((bf16[32,8,256]{2,1,0:T(8,128)(2,1)}), bf16[32,8,256]{2,1,0:T(8,128)(2,1)S(1)}, u32[]{:S(2)}, u32[]{:S(2)}) async-start(bf16[32,8,256]{2,1,0:T(8,128)(2,1)} %fusion.14), calls=%async_computation.2 | async-start | bytes 262144 | tf_op jit(solution)/shard_map/all_to_all | solution.py:61
  152.6 20.0 %all-to-all-start.4 = ((bf16[32,8,256]{2,1,0:T(8,128)(2,1)}), bf16[32,8,256]{2,1,0:T(8,128)(2,1)S(1)}, u32[]{:S(2)}, u32[]{:S(2)}) async-start(bf16[32,8,256]{2,1,0:T(8,128)(2,1)} %fusion.15), calls=%async_computation.4 | async-start | bytes 262144 | tf_op jit(solution)/shard_map/all_to_all | solution.py:62
  164.6 9.9 %copy-start.2 = (bf16[1024,128]{1,0:T(8,128)(2,1)}, bf16[1024,128]{1,0:T(8,128)(2,1)S(1)}, u32[]{:S(2)}) copy-start(bf16[1024,128]{1,0:T(8,128)(2,1)S(1)} %copy.24) | copy-start | bytes 786436
  172.6 1.9 copy-start.6
  174.5 35.3 %all-to-all-start.3 = ((bf16[16,8,128,64]{2,3,1,0:T(8,128)(2,1)}), bf16[16,8,128,64]{2,3,1,0:T(8,128)(2,1)S(1)}, u32[]{:S(2)}, u32[]{:S(2)}) async-start(bf16[16,8,128,64]{2,3,1,0:T(8,128)(2,1)} %broadcast_in_dim.46), calls=%async_computation.3 | async-start | bytes 4194304 | tf_op jit(solution)/shard_map/all_to_all | solution.py:17
  209.8 1.0 copy-start.5
  209.8 1.3 copy-start.3
  209.8 1.3 copy-start.4
Sparse Core Ops, SparseCore 0:
  9.4 59.8 all-gather.1
  92.1 71.3 reduce-scatter.3
where the time goes:
time: 220 us; the launch traced here: 219 us
  waiting for transfers between devices  132 us (60%)
  starting transfers between devices  34.5 us (16%)
  local copies, waits for them, and re-layouts  16.4 us (7%)
  matrix products  15.6 us (7%)
  between operations  14.2 us (6%)
  other arithmetic  6.5 us (3%)
    all_gather x1, waiting for transfers between devices, per_device(): full_rows = lax.all_gather(tokens, 'mp', axis=1, tiled=True)  61.3 us
    all_to_all x3, waiting for transfers between devices, from_everyone(): return lax.all_to_all(copies, axis, split_axis=0, concat_axis=0, tiled=True)  41.9 us
    all_to_all x3, starting transfers between devices, from_everyone(): return lax.all_to_all(copies, axis, split_axis=0, concat_axis=0, tiled=True)  25.4 us
    dot_general x5, matrix products, matmul(): return jnp.dot(left, right, preferred_element_type=jnp.float32)  15 us
    all_to_all x1, waiting for transfers between devices, per_device(): lax.all_to_all(made[0], 'dp', split_axis=0, concat_axis=1, tiled=True)  14.6 us
    unnamed x30, local copies, waits for them, and re-layouts  9.83 us
    all_to_all x1, waiting for transfers between devices, per_device(): lax.all_to_all(made[1], 'dp', split_axis=0, concat_axis=1, tiled=True)  7.75 us
    unnamed x3, waiting for transfers between devices  6.13 us
  transfers between devices with their start and end apart: 7, of which 7 were waited for; matrix products, arithmetic and copies ran while one was open for 5% of the time, Pallas kernels for 0%

commit v1 on v0

v1 whole, which is shorter than its diff:
```python
import jax
import jax.numpy as jnp
from jax import lax
from jax.experimental import pallas as pl
from jax.experimental.pallas import tpu as pltpu
from jax.sharding import PartitionSpec as P

R = 64
CORES = 2
CHIPS = 8
MP = CORES * CHIPS
DP = 32
VMEM = 56 * 1024 * 1024


def matmul(left, right):
    return jnp.dot(left, right, preferred_element_type=jnp.float32)


def matmul_nt(left, right):
    return lax.dot_general(
        left, right, (((1,), (1,)), ((), ())), preferred_element_type=jnp.float32
    )


def exchange(pieces, axis):
    return lax.all_to_all(pieces, axis, split_axis=0, concat_axis=0, tiled=True)


def doubling_gather(shard, axis, size):
    index = lax.axis_index(axis)
    held = shard
    bit = size // 2
    while bit:
        theirs = lax.ppermute(held, axis, [(i, i ^ bit) for i in range(size)])
        upper = (index & bit) != 0
        held = jnp.stack([jnp.where(upper, theirs, held), jnp.where(upper, held, theirs)])
        bit //= 2
    return held


def ffn_body(x_ref, gain_ref, wi_ref, wo_own_ref, wo_other_ref, out_ref):
    wide = jnp.concatenate([x_ref[i] for i in range(MP)], axis=1).astype(jnp.float32)
    scale = lax.rsqrt(jnp.mean(wide * wide, axis=-1, keepdims=True) + 1e-06)
    normed = (wide * scale * gain_ref[...].astype(jnp.float32)).astype(jnp.bfloat16)
    both = matmul_nt(normed, wi_ref[...])
    hid = both.shape[1] // 2
    act = (jax.nn.gelu(both[:, :hid], approximate=True) * both[:, hid:]).astype(jnp.bfloat16)
    own = hid // 2
    sums = matmul(act[:, :own], wo_own_ref[...]) + matmul(act[:, own:], wo_other_ref[...])
    sums = sums.astype(jnp.bfloat16)
    width = out_ref.shape[2]
    for i in range(MP):
        out_ref[i] = sums[:, i * width : (i + 1) * width]


def ffn(x, gain, wi, wo_own, wo_other):
    tile = 256
    rows, width = x.shape[1:]
    whole = lambda a: pl.BlockSpec(a.shape, lambda i: (0, 0))
    return pl.pallas_call(
        ffn_body,
        out_shape=jax.ShapeDtypeStruct((MP, rows, width), jnp.bfloat16),
        grid=(rows // tile,),
        in_specs=[
            pl.BlockSpec((MP, tile, width), lambda i: (0, i, 0)),
            whole(gain),
            whole(wi),
            whole(wo_own),
            whole(wo_other),
        ],
        out_specs=pl.BlockSpec((MP, tile, width), lambda i: (0, i, 0)),
        compiler_params=pltpu.CompilerParams(vmem_limit_bytes=VMEM),
        name="ffn",
    )(x, gain, wi, wo_own, wo_other)


def squeeze_body(ids_ref, parts_ref, down_ref, ffout_ref, squeezed_ref):
    s = pl.program_id(0)
    total = parts_ref[0, 0].astype(jnp.float32)
    for i in range(1, CHIPS):
        total = total + parts_ref[i, 0].astype(jnp.float32)
    ffout = total.astype(jnp.bfloat16)
    ffout_ref[...] = ffout
    sums = matmul(ffout, down_ref[ids_ref[s]]).astype(jnp.bfloat16)
    quarter = sums.shape[0] // 4
    for i in range(2):
        first = sums[2 * i * quarter : (2 * i + 1) * quarter]
        second = sums[(2 * i + 1) * quarter : (2 * i + 2) * quarter]
        squeezed_ref[i] = jnp.concatenate([first, second], axis=1)


def squeeze(task_ids, parts, down):
    rows, width = parts.shape[1:]
    seqs = task_ids.shape[0]
    seq = CORES * rows // seqs
    half = seqs // CORES
    return pl.pallas_call(
        squeeze_body,
        out_shape=(
            jax.ShapeDtypeStruct((CORES * rows, width), jnp.bfloat16),
            jax.ShapeDtypeStruct((2 * seqs, seq // 4, 2 * R), jnp.bfloat16),
        ),
        grid_spec=pltpu.PrefetchScalarGridSpec(
            num_scalar_prefetch=1,
            grid=(seqs,),
            in_specs=[
                pl.BlockSpec((CHIPS, 1, seq, width), lambda s, ids: (0, s // half, s % half, 0)),
                pl.BlockSpec(down.shape, lambda s, ids: (0, 0, 0)),
            ],
            out_specs=(
                pl.BlockSpec((seq, width), lambda s, ids: (s, 0)),
                pl.BlockSpec((2, seq // 4, 2 * R), lambda s, ids: (s, 0, 0)),
            ),
        ),
        compiler_params=pltpu.CompilerParams(vmem_limit_bytes=VMEM),
        name="squeeze",
    )(task_ids, parts.reshape(CHIPS, CORES, rows, width), down)


def relu_body(parts_ref, out_ref):
    total = parts_ref[0].astype(jnp.float32)
    for i in range(1, MP):
        total = total + parts_ref[i].astype(jnp.float32)
    squeezed = jnp.maximum(total, 0.0).astype(jnp.bfloat16)
    for i in range(MP):
        out_ref[i] = squeezed


def relu_for_everyone(parts):
    return pl.pallas_call(
        relu_body,
        out_shape=jax.ShapeDtypeStruct(parts.shape, parts.dtype),
        name="relu_for_everyone",
    )(parts)


def expand_body(ids_ref, tokens_ref, ffout_ref, squeezed_ref, up_ref, out_ref):
    s = pl.program_id(0)
    both = [squeezed_ref[i] for i in range(2)]
    squeezed = jnp.concatenate([both[i][:, j * R : (j + 1) * R] for i in range(2) for j in range(2)])
    expand = matmul_nt(squeezed, up_ref[ids_ref[s]])
    total = tokens_ref[...].astype(jnp.float32) + ffout_ref[...].astype(jnp.float32) + expand
    out_ref[...] = total.astype(jnp.bfloat16)


def expand(task_ids, tokens, ffout, squeezed, up):
    seqs = task_ids.shape[0]
    rows, width = tokens.shape
    seq = rows // seqs
    row_spec = pl.BlockSpec((seq, width), lambda s, ids: (s, 0))
    return pl.pallas_call(
        expand_body,
        out_shape=jax.ShapeDtypeStruct(tokens.shape, tokens.dtype),
        grid_spec=pltpu.PrefetchScalarGridSpec(
            num_scalar_prefetch=1,
            grid=(seqs,),
            in_specs=[
                row_spec,
                row_spec,
                pl.BlockSpec((2, *squeezed.shape[1:]), lambda s, ids: (s, 0, 0)),
                pl.BlockSpec(up.shape, lambda s, ids: (0, 0, 0)),
            ],
            out_specs=row_spec,
        ),
        compiler_params=pltpu.CompilerParams(vmem_limit_bytes=VMEM),
        name="expand",
    )(task_ids, tokens, ffout, squeezed, up)


def per_device(
    tokens,
    norm_gain,
    wi_gate,
    wi_linear,
    wo_out,
    task_table,
    layer_table,
    task_ids,
    layer_index,
    hyper_in,
    gen_down,
    gen_up,
):
    tok_dev, width = tokens.shape
    features = width * MP
    half = tok_dev // CORES

    sent = jnp.broadcast_to(tokens.reshape(1, CORES, half, width), (CHIPS, CORES, half, width))
    gathered = exchange(sent.reshape(MP, half, width), "mp")

    swap = lambda w: lax.ppermute(w, "mp", [(i, i ^ 1) for i in range(MP)])
    gate, linear = wi_gate.T, wi_linear.T
    gate_other, linear_other, wo_other = swap(gate), swap(linear), swap(wo_out)
    wi = jnp.concatenate([gate, gate_other, linear, linear_other], axis=0)

    task_count = task_table.shape[0]
    layer_row = jnp.take(layer_table, layer_index, axis=0)
    embed = jnp.concatenate(
        [task_table, jnp.broadcast_to(layer_row, (task_count, layer_row.shape[1]))], axis=1
    ).astype(jnp.bfloat16)
    hidden_part = jnp.maximum(matmul(embed, hyper_in), 0.0).astype(jnp.bfloat16)
    hidden = doubling_gather(hidden_part, "mp", MP)
    hidden = jnp.transpose(hidden, (4, 3, 2, 1, 0, 5)).reshape(task_count, -1)
    made = jnp.stack(
        [matmul(hidden, gen_down).astype(jnp.bfloat16), matmul(hidden, gen_up).astype(jnp.bfloat16)]
    )
    all_tasks = doubling_gather(made, "dp", DP)
    all_tasks = jnp.transpose(all_tasks, (5, 6, 4, 3, 2, 1, 0, 7))
    adapters = all_tasks.reshape(2, task_count, width, R)

    partial = ffn(gathered, norm_gain.reshape(1, features), wi, wo_out, wo_other)
    ffout, squeeze_part = squeeze(task_ids, exchange(partial, "mp"), adapters[0])
    squeezed = exchange(relu_for_everyone(exchange(squeeze_part, "mp")), "mp")
    return expand(task_ids, tokens, ffout, squeezed, adapters[1])


def solution(mesh):
    return jax.shard_map(
        per_device,
        mesh=mesh,
        in_specs=(
            P("dp", "mp"),
            P(),
            P(None, "mp"),
            P(None, "mp"),
            P("mp", None),
            P(),
            P(),
            P("dp"),
            P(),
            P(None, "mp"),
            P(None, ("mp", "dp")),
            P(None, ("mp", "dp")),
        ),
        out_specs=P("dp", "mp"),
        check_vma=False,
    )
```

time: 220 us -> 153 us (0.70)
  waiting for transfers between devices: 132 us -> 22.7 us
  starting transfers between devices: 34.5 us -> 67.6 us
  Pallas kernels: 0 us -> 27 us
  blocking collectives: 0 us -> 15.6 us
  matrix products: 15.6 us -> 1.2 us
  between operations: 14.2 us -> 0.97 us
  local copies, waits for them, and re-layouts: 16.4 us -> 9.09 us
    all_gather x1 -> x0, waiting for transfers between devices: 61.3 us -> none  [per_device(): full_rows = lax.all_gather(tokens, 'mp', axis=1, tiled=True)]
    all_to_all x5 -> x3, waiting for transfers between devices: 64.2 us -> 9.24 us  [exchange(): return lax.all_to_all(pieces, axis, split_axis=0, concat_axis=0, tiled=True)]
    ppermute x0 -> x12, starting transfers between devices: none -> 51.3 us  [the longest x9 40.9 us: doubling_gather(): theirs = lax.ppermute(held, axis, [(i, i ^ bit) for i in range(size)])]
    pallas_call x0 -> x4, Pallas kernels: none -> 27 us  [the longest x1 12.5 us: ffn(): pl.pallas_call(ffn_body, out_shape=jax.ShapeDtypeStruct((MP, rows, width)...]
    all_to_all x5 -> x3, starting transfers between devices: 34.4 us -> 16.2 us  [exchange(): return lax.all_to_all(pieces, axis, split_axis=0, concat_axis=0, tiled=True)]
    all_to_all x0 -> x1, blocking collectives: none -> 15.6 us  [exchange(): return lax.all_to_all(pieces, axis, split_axis=0, concat_axis=0, tiled=True)]
    dot_general x5 -> x3, matrix products: 15 us -> 1.2 us  [matmul(): return jnp.dot(left, right, preferred_element_type=jnp.float32)]
    ppermute x0 -> x12, waiting for transfers between devices: none -> 13.5 us  [the longest x9 13.4 us: doubling_gather(): theirs = lax.ppermute(held, axis, [(i, i ^ bit) for i in range(size)])]
  transfers between devices with their start and end apart: 7 -> 15, of which waited for: 7 -> 8; matrix products, arithmetic and copies ran while one was open for 5% -> 8% of each run, Pallas kernels for 0% -> 0%
where the time goes in v1:
time: 153 us; the launch traced here: 151 us
  starting transfers between devices  67.6 us (44%)
  Pallas kernels  27 us (18%)
  waiting for transfers between devices  22.7 us (15%)
  blocking collectives  15.6 us (10%)
  local copies, waits for them, and re-layouts  9.09 us (6%)
  other arithmetic  6.93 us (5%)
    ppermute x9, starting transfers between devices, doubling_gather(): theirs = lax.ppermute(held, axis, [(i, i ^ bit) for i in range(size)])  40.9 us
    all_to_all x3, starting transfers between devices, exchange(): return lax.all_to_all(pieces, axis, split_axis=0, concat_axis=0, tiled=True)  16.2 us
    all_to_all x1, blocking collectives, exchange(): return lax.all_to_all(pieces, axis, split_axis=0, concat_axis=0, tiled=True)  15.6 us
    ppermute x9, waiting for transfers between devices, doubling_gather(): theirs = lax.ppermute(held, axis, [(i, i ^ bit) for i in range(size)])  13.4 us
    pallas_call x1, Pallas kernels, ffn(): pl.pallas_call(ffn_body, out_shape=jax.ShapeDtypeStruct((MP, rows, width)...  12.5 us
    ppermute x3, starting transfers between devices, per_device(): swap = lambda w: lax.ppermute(w, 'mp', [(i, i ^ 1) for i in range(MP)])  10.4 us
    all_to_all x3, waiting for transfers between devices, exchange(): return lax.all_to_all(pieces, axis, split_axis=0, concat_axis=0, tiled=True)  9.24 us
    pallas_call x1, Pallas kernels, squeeze(): pl.pallas_call(squeeze_body, out_shape=(jax.ShapeDtypeStruct((CORES * row...  6.76 us
  transfers between devices with their start and end apart: 15, of which 8 were waited for; matrix products, arithmetic and copies ran while one was open for 8% of the time, Pallas kernels for 0%

profile of v1, /device:TPU:1, one launch (start us, length us, event | category | flops | bytes accessed | tf_op | source)
XLA Modules:
  0.0 151.0 jit_solution(12887072898484314178)
XLA Ops:
  0.0 0.7 convert.7
  1.4 0.7 fusion.7
  2.1 0.1 pad.23.clone
  2.2 0.8 fusion.2
  3.0 3.9 %collective-permute-start.3 = (bf16[8,64]{1,0:T(8,128)(2,1)S(1)}, bf16[8,64]{1,0:T(8,128)(2,1)S(1)}, u32[]{:S(2)}, u32[]{:S(2)}) collective-permute-start(bf16[8,64]{1,0:T(8,128)(2,1)S(1)} %fusion.2), channel_id=1, source_target_pairs={{0,8},{1,9},{2,10},{3,11},{4,12},{5,13},{6,14},{7,15},{8,0},{9,1},... | collective-permute-start | bytes 3080 | tf_op jit(solution)/shard_map/ppermute | solution.py:35
  7.0 1.0 collective-permute-done.3
  8.0 5.1 %collective-permute-start.4 = (bf16[2,8,64]{2,1,0:T(8,128)(2,1)S(1)}, bf16[2,8,64]{2,1,0:T(8,128)(2,1)S(1)}, u32[]{:S(2)}, u32[]{:S(2)}) collective-permute-start(bf16[2,8,64]{2,1,0:T(8,128)(2,1)S(1)} %pad_maximum_fusion.8), channel_id=1, source_target_pairs={{0,4},{1,5},{2,6},{3,7},{4,0},{5,1},{6,2},{7,3},{8,12},{9,13},{10,... | collective-permute-start | bytes 6152 | tf_op jit(solution)/shard_map/ppermute | solution.py:35
  13.0 6.2 %collective-permute-start.1 = (bf16[320,2048]{1,0:T(8,128)(2,1)}, bf16[320,2048]{1,0:T(8,128)(2,1)}, u32[]{:S(2)}, u32[]{:S(2)}) collective-permute-start(bf16[320,2048]{1,0:T(8,128)(2,1)} %bitcast.60), channel_id=1, source_target_pairs={{0,1},{1,0},{2,3},{3,2},{4,5},{5,4},{6,7},{7,6},{8,9},{9,8},{10,11... | collective-permute-start | bytes 3932168 | tf_op jit(solution)/shard_map/ppermute | solution.py:192
  19.2 1.9 %collective-permute-start = (bf16[320,2048]{1,0:T(8,128)(2,1)}, bf16[320,2048]{1,0:T(8,128)(2,1)}, u32[]{:S(2)}, u32[]{:S(2)}) collective-permute-start(bf16[320,2048]{1,0:T(8,128)(2,1)} %bitcast.62), channel_id=1, source_target_pairs={{0,1},{1,0},{2,3},{3,2},{4,5},{5,4},{6,7},{7,6},{8,9},{9,8},{10,11... | collective-permute-start | bytes 3932168 | tf_op jit(solution)/shard_map/ppermute | solution.py:192
  21.2 0.0 collective-permute-done.4
  21.2 1.9 %collective-permute-start.5 = (bf16[2,2,8,64]{3,2,1,0:T(8,128)(2,1)S(1)}, bf16[2,2,8,64]{3,2,1,0:T(8,128)(2,1)S(1)}, u32[]{:S(2)}, u32[]{:S(2)}) collective-permute-start(bf16[2,2,8,64]{3,2,1,0:T(8,128)(2,1)S(1)} %pad_maximum_fusion.6), channel_id=1, source_target_pairs={{0,2},{1,3},{2,0},{3,1},{4,6},{5,7},{6,4},{7,5},{8,10},{9,11},{10,... | collective-permute-start | bytes 12296 | tf_op jit(solution)/shard_map/ppermute | solution.py:35
  23.2 2.7 %broadcast_in_dim.25 = bf16[8,2,512,128]{3,2,1,0:T(8,128)(2,1)} broadcast(bf16[2,512,128]{2,1,0:T(8,128)(2,1)} %bitcast.64), dimensions={1,2,3} | broadcast | bytes 2359296 | tf_op jit(solution)/shard_map/broadcast_in_dim | solution.py:189
  25.9 6.0 %all-to-all-start = ((bf16[16,512,128]{2,1,0:T(8,128)(2,1)}), bf16[16,512,128]{2,1,0:T(8,128)(2,1)S(1)}, u32[]{:S(2)}, u32[]{:S(2)}) async-start(bf16[16,512,128]{2,1,0:T(8,128)(2,1)} %bitcast.59), calls=%async_computation | async-start | bytes 4194304 | tf_op jit(solution)/shard_map/all_to_all | solution.py:27
  31.9 0.0 collective-permute-done.5
  31.9 2.0 %collective-permute-start.6 = (bf16[2,2,2,8,64]{4,3,2,1,0:T(8,128)(2,1)S(1)}, bf16[2,2,2,8,64]{4,3,2,1,0:T(8,128)(2,1)S(1)}, u32[]{:S(2)}, u32[]{:S(2)}) collective-permute-start(bf16[2,2,2,8,64]{4,3,2,1,0:T(8,128)(2,1)S(1)} %pad_maximum_fusion.4), channel_id=1, source_target_pairs={{0,1},{1,0},{2,3},{3,2},{4,5},{5,4},{6,7},{7,6},{8,9},{9,8},{10,11... | collective-permute-start | bytes 24584 | tf_op jit(solution)/shard_map/ppermute | solution.py:35
  34.0 2.3 %collective-permute-start.2 = (bf16[320,2048]{1,0:T(8,128)(2,1)}, bf16[320,2048]{1,0:T(8,128)(2,1)}, u32[]{:S(2)}, u32[]{:S(2)}) collective-permute-start(bf16[320,2048]{1,0:T(8,128)(2,1)} %wo_own_ref.1), channel_id=1, source_target_pairs={{0,1},{1,0},{2,3},{3,2},{4,5},{5,4},{6,7},{7,6},{8,9},{9,8},{10,11... | collective-permute-start | bytes 3932168 | tf_op jit(solution)/shard_map/ppermute | solution.py:192
  36.3 0.0 collective-permute-done.6
  36.4 0.1 reshape.33
  36.5 0.2 fusion.1
  36.7 0.2 fusion
  36.8 12.6 %collective-permute-start.7 = (bf16[2,8,256]{2,1,0:T(8,128)(2,1)S(1)}, bf16[2,8,256]{2,1,0:T(8,128)(2,1)S(1)}, u32[]{:S(2)}, u32[]{:S(2)}) collective-permute-start(bf16[2,8,256]{2,1,0:T(8,128)(2,1)S(1)} %pad_maximum_fusion.7), channel_id=1, source_target_pairs={{0,256},{16,272},{32,288},{48,304},{64,320},{80,336},{96,352},{112... | collective-permute-start | bytes 24584 | tf_op jit(solution)/shard_map/ppermute | solution.py:35
  49.5 0.6 reshape.31.gain_ref
  50.1 0.4 collective-permute-done.7
  50.5 5.3 %pad_maximum_fusion.wi_ref = bf16[1280,2048]{1,0:T(8,128)(2,1)} fusion(bf16[320,2048]{1,0:T(8,128)(2,1)} %collective-permute-done.1, bf16[320,2048]{1,0:T(8,128)(2,1)} %bitcast.61, bf16[320,2048]{1,0:T(8,128)(2,1)} %collective-permute-done, bf16[320,2048]{1,0:T(8,128)(2,1)} %bitcast.63), kind=kLoop, calls=%fused_computation | loop fusion | flops 20971520 | bytes 10485760 | tf_op jit(solution)/shard_map/concatenate | solution.py:195
  55.8 4.1 %all-to-all-done.x_ref = bf16[16,512,128]{2,1,0:T(8,128)(2,1)S(1)} async-done(((bf16[16,512,128]{2,1,0:T(8,128)(2,1)}), bf16[16,512,128]{2,1,0:T(8,128)(2,1)S(1)}, u32[]{:S(2)}, u32[]{:S(2)}) %all-to-all-start) | async-done | bytes 2097184 | tf_op jit(solution)/shard_map/all_to_all | solution.py:27
  59.9 1.4 copy-done.1
  61.3 12.5 %ffn.1 = bf16[16,512,128]{2,1,0:T(8,128)(2,1)} custom-call(bf16[16,512,128]{2,1,0:T(8,128)(2,1)} %copy-done.1, bf16[1,2048]{1,0:T(2,128)(2,1)} %reshape.31.gain_ref, bf16[1280,2048]{1,0:T(8,128)(2,1)} %pad_maximum_fusion.wi_ref, bf16[320,2048]{1,0:T(8,128)(2,1)} %wo_own_ref.1, bf16[320,2048]{1,0:T(8,128)(2,1)} %collective-permute-done.2.wo_other_ref), custom_call_target="tpu_custom_call" | custom-call | tf_op jit(solution)/shard_map/ffn/pallas_call | solution.py:61
  73.8 6.3 %all-to-all-start.1 = ((bf16[16,512,128]{2,1,0:T(8,128)(2,1)}), bf16[16,512,128]{2,1,0:T(8,128)(2,1)S(1)}, u32[]{:S(2)}, u32[]{:S(2)}) async-start(bf16[16,512,128]{2,1,0:T(8,128)(2,1)} %ffn.1), calls=%async_computation.1 | async-start | bytes 4194304 | tf_op jit(solution)/shard_map/all_to_all | solution.py:27
  80.1 6.0 %collective-permute-start.8 = (bf16[2,2,8,256]{3,2,1,0:T(8,128)(2,1)S(1)}, bf16[2,2,8,256]{3,2,1,0:T(8,128)(2,1)S(1)}, u32[]{:S(2)}, u32[]{:S(2)}) collective-permute-start(bf16[2,2,8,256]{3,2,1,0:T(8,128)(2,1)S(1)} %pad_maximum_fusion.5), channel_id=1, source_target_pairs={{0,128},{16,144},{32,160},{48,176},{64,192},{80,208},{96,224},{112... | collective-permute-start | bytes 49160 | tf_op jit(solution)/shard_map/ppermute | solution.py:35
  86.1 2.7 %collective-permute-done.8 = bf16[2,2,8,256]{3,2,1,0:T(8,128)(2,1)S(1)} collective-permute-done((bf16[2,2,8,256]{3,2,1,0:T(8,128)(2,1)S(1)}, bf16[2,2,8,256]{3,2,1,0:T(8,128)(2,1)S(1)}, u32[]{:S(2)}, u32[]{:S(2)}) %collective-permute-start.8) | collective-permute-done | bytes 16416 | tf_op jit(solution)/shard_map/ppermute | solution.py:35
  88.9 3.2 %collective-permute-start.9 = (bf16[2,2,2,8,256]{4,3,2,1,0:T(8,128)(2,1)S(1)}, bf16[2,2,2,8,256]{4,3,2,1,0:T(8,128)(2,1)S(1)}, u32[]{:S(2)}, u32[]{:S(2)}) collective-permute-start(bf16[2,2,2,8,256]{4,3,2,1,0:T(8,128)(2,1)S(1)} %pad_maximum_fusion.3), channel_id=1, source_target_pairs={{0,64},{16,80},{32,96},{48,112},{64,0},{80,16},{96,32},{112,48},{1... | collective-permute-start | bytes 98312 | tf_op jit(solution)/shard_map/ppermute | solution.py:35
  92.1 2.6 %collective-permute-done.9 = bf16[2,2,2,8,256]{4,3,2,1,0:T(8,128)(2,1)S(1)} collective-permute-done((bf16[2,2,2,8,256]{4,3,2,1,0:T(8,128)(2,1)S(1)}, bf16[2,2,2,8,256]{4,3,2,1,0:T(8,128)(2,1)S(1)}, u32[]{:S(2)}, u32[]{:S(2)}) %collective-permute-start.9) | collective-permute-done | bytes 32800 | tf_op jit(solution)/shard_map/ppermute | solution.py:35
  94.8 2.5 %collective-permute-start.10 = (bf16[2,2,2,2,8,256]{5,4,3,2,1,0:T(8,128)(2,1)S(1)}, bf16[2,2,2,2,8,256]{5,4,3,2,1,0:T(8,128)(2,1)S(1)}, u32[]{:S(2)}, u32[]{:S(2)}) collective-permute-start(bf16[2,2,2,2,8,256]{5,4,3,2,1,0:T(8,128)(2,1)S(1)} %pad_maximum_fusion.2), channel_id=1, source_target_pairs={{0,32},{16,48},{32,0},{48,16},{64,96},{80,112},{96,64},{112,80},{1... | collective-permute-start | bytes 196616 | tf_op jit(solution)/shard_map/ppermute | solution.py:35
  97.3 2.8 %collective-permute-done.10 = bf16[2,2,2,2,8,256]{5,4,3,2,1,0:T(8,128)(2,1)S(1)} collective-permute-done((bf16[2,2,2,2,8,256]{5,4,3,2,1,0:T(8,128)(2,1)S(1)}, bf16[2,2,2,2,8,256]{5,4,3,2,1,0:T(8,128)(2,1)S(1)}, u32[]{:S(2)}, u32[]{:S(2)}) %collective-permute-start.10) | collective-permute-done | bytes 65568 | tf_op jit(solution)/shard_map/ppermute | solution.py:35
  100.1 3.5 %collective-permute-start.11 = (bf16[2,2,2,2,2,8,256]{6,5,4,3,2,1,0:T(8,128)(2,1)S(1)}, bf16[2,2,2,2,2,8,256]{6,5,4,3,2,1,0:T(8,128)(2,1)S(1)}, u32[]{:S(2)}, u32[]{:S(2)}) collective-permute-start(bf16[2,2,2,2,2,8,256]{6,5,4,3,2,1,0:T(8,128)(2,1)S(1)} %pad_maximum_fusion.1), channel_id=1, source_target_pairs={{0,16},{16,0},{32,48},{48,32},{64,80},{80,64},{96,112},{112,96},{1... | collective-permute-start | bytes 393224 | tf_op jit(solution)/shard_map/ppermute | solution.py:35
  103.7 4.0 %collective-permute-done.11 = bf16[2,2,2,2,2,8,256]{6,5,4,3,2,1,0:T(8,128)(2,1)S(1)} collective-permute-done((bf16[2,2,2,2,2,8,256]{6,5,4,3,2,1,0:T(8,128)(2,1)S(1)}, bf16[2,2,2,2,2,8,256]{6,5,4,3,2,1,0:T(8,128)(2,1)S(1)}, u32[]{:S(2)}, u32[]{:S(2)}) %collective-permute-start.11) | collective-permute-done | bytes 131104 | tf_op jit(solution)/shard_map/ppermute | solution.py:35
  107.7 0.1 copy.16
  107.9 0.9 squeeze.7.down_ref
  108.8 1.3 copy-done.2
  110.1 6.8 %squeeze.9 = (bf16[1024,128]{1,0:T(8,128)(2,1)}, bf16[16,32,128]{2,1,0:T(8,128)(2,1)}) custom-call(s32[8]{0:T(128)} %ids_ref.3, bf16[8,2,512,128]{3,2,1,0:T(8,128)(2,1)} %bitcast.58, bf16[8,128,64]{2,1,0:T(8,128)(2,1)} %squeeze.7.down_ref), custom_call_target="tpu_custom_call" | custom-call | tf_op jit(solution)/shard_map/squeeze/pallas_call | solution.py:98
  116.9 15.6 %all_to_all.20.parts_ref = bf16[16,32,128]{2,1,0:T(8,128)(2,1)} all-to-all(bf16[16,32,128]{2,1,0:T(8,128)(2,1)} %get-tuple-element.8), channel_id=1, replica_groups=mesh['dp'=32,'mp'=16] {'mp'}, dimensions={0} | all-to-all | bytes 262144 | tf_op jit(solution)/shard_map/all_to_all | solution.py:27
  132.5 1.6 %relu_for_everyone.1 = bf16[16,32,128]{2,1,0:T(8,128)(2,1)} custom-call(bf16[16,32,128]{2,1,0:T(8,128)(2,1)} %all_to_all.20.parts_ref), custom_call_target="tpu_custom_call" | custom-call | tf_op jit(solution)/shard_map/relu_for_everyone/pallas_call | solution.py:131
  134.1 4.0 %all-to-all-start.3 = ((bf16[16,32,128]{2,1,0:T(8,128)(2,1)}), bf16[16,32,128]{2,1,0:T(8,128)(2,1)S(1)}, u32[]{:S(2)}, u32[]{:S(2)}) async-start(bf16[16,32,128]{2,1,0:T(8,128)(2,1)} %relu_for_everyone.1), calls=%async_computation.3 | async-start | bytes 262144 | tf_op jit(solution)/shard_map/all_to_all | solution.py:27
  138.1 0.1 copy.17
  138.2 0.9 squeeze.8.up_ref
  139.2 5.2 %all-to-all-done.3.squeezed_ref = bf16[16,32,128]{2,1,0:T(8,128)(2,1)S(1)} async-done(((bf16[16,32,128]{2,1,0:T(8,128)(2,1)}), bf16[16,32,128]{2,1,0:T(8,128)(2,1)S(1)}, u32[]{:S(2)}, u32[]{:S(2)}) %all-to-all-start.3) | async-done | bytes 131104 | tf_op jit(solution)/shard_map/all_to_all | solution.py:27
  144.3 0.6 copy-done.3
  145.0 6.1 %expand.1 = bf16[1024,128]{1,0:T(8,128)(2,1)} custom-call(s32[8]{0:T(128)} %ids_ref.3, bf16[1024,128]{1,0:T(8,128)(2,1)} %tokens_ref.1, bf16[1024,128]{1,0:T(8,128)(2,1)} %get-tuple-element.7.ffout_ref, bf16[16,32,128]{2,1,0:T(8,128)(2,1)} %copy-done.3, bf16[8,128,64]{2,1,0:T(8,128)(2,1)} %squeeze.8.up_ref), custom_call_target="tpu_custom_call" | custom-call | tf_op jit(solution)/shard_map/expand/pallas_call | solution.py:152
  (34 shorter events, 0.3 us)
Async XLA Ops:
  0.0 36.5 %copy-start = (bf16[1024,256]{1,0:T(8,128)(2,1)S(1)}, bf16[1024,256]{1,0:T(8,128)(2,1)}, u32[]{:S(2)}) copy-start(bf16[1024,256]{1,0:T(8,128)(2,1)} %param.23) | copy-start | bytes 1572868
  3.0 4.9 %collective-permute-start.3 = (bf16[8,64]{1,0:T(8,128)(2,1)S(1)}, bf16[8,64]{1,0:T(8,128)(2,1)S(1)}, u32[]{:S(2)}, u32[]{:S(2)}) collective-permute-start(bf16[8,64]{1,0:T(8,128)(2,1)S(1)} %fusion.2), channel_id=1, source_target_pairs={{0,8},{1,9},{2,10},{3,11},{4,12},{5,13},{6,14},{7,15},{8,0},{9,1},... | collective-permute-start | bytes 3080 | tf_op jit(solution)/shard_map/ppermute | solution.py:35
  8.0 13.2 %collective-permute-start.4 = (bf16[2,8,64]{2,1,0:T(8,128)(2,1)S(1)}, bf16[2,8,64]{2,1,0:T(8,128)(2,1)S(1)}, u32[]{:S(2)}, u32[]{:S(2)}) collective-permute-start(bf16[2,8,64]{2,1,0:T(8,128)(2,1)S(1)} %pad_maximum_fusion.8), channel_id=1, source_target_pairs={{0,4},{1,5},{2,6},{3,7},{4,0},{5,1},{6,2},{7,3},{8,12},{9,13},{10,... | collective-permute-start | bytes 6152 | tf_op jit(solution)/shard_map/ppermute | solution.py:35
  13.0 37.5 %collective-permute-start.1 = (bf16[320,2048]{1,0:T(8,128)(2,1)}, bf16[320,2048]{1,0:T(8,128)(2,1)}, u32[]{:S(2)}, u32[]{:S(2)}) collective-permute-start(bf16[320,2048]{1,0:T(8,128)(2,1)} %bitcast.60), channel_id=1, source_target_pairs={{0,1},{1,0},{2,3},{3,2},{4,5},{5,4},{6,7},{7,6},{8,9},{9,8},{10,11... | collective-permute-start | bytes 3932168 | tf_op jit(solution)/shard_map/ppermute | solution.py:192
  19.2 31.3 %collective-permute-start = (bf16[320,2048]{1,0:T(8,128)(2,1)}, bf16[320,2048]{1,0:T(8,128)(2,1)}, u32[]{:S(2)}, u32[]{:S(2)}) collective-permute-start(bf16[320,2048]{1,0:T(8,128)(2,1)} %bitcast.62), channel_id=1, source_target_pairs={{0,1},{1,0},{2,3},{3,2},{4,5},{5,4},{6,7},{7,6},{8,9},{9,8},{10,11... | collective-permute-start | bytes 3932168 | tf_op jit(solution)/shard_map/ppermute | solution.py:192
  21.2 10.7 %collective-permute-start.5 = (bf16[2,2,8,64]{3,2,1,0:T(8,128)(2,1)S(1)}, bf16[2,2,8,64]{3,2,1,0:T(8,128)(2,1)S(1)}, u32[]{:S(2)}, u32[]{:S(2)}) collective-permute-start(bf16[2,2,8,64]{3,2,1,0:T(8,128)(2,1)S(1)} %pad_maximum_fusion.6), channel_id=1, source_target_pairs={{0,2},{1,3},{2,0},{3,1},{4,6},{5,7},{6,4},{7,5},{8,10},{9,11},{10,... | collective-permute-start | bytes 12296 | tf_op jit(solution)/shard_map/ppermute | solution.py:35
  25.9 10.8 %copy-start.4 = (bf16[1024,256]{1,0:T(8,128)(2,1)S(1)}, bf16[1024,256]{1,0:T(8,128)(2,1)}, u32[]{:S(2)}) copy-start(bf16[1024,256]{1,0:T(8,128)(2,1)} %param.22) | copy-start | bytes 1572868
  25.9 23.6 %copy-start.5 = (bf16[2048]{0:T(1024)(128)(2,1)S(1)}, bf16[2048]{0:T(1024)(128)(2,1)}, u32[]{:S(2)}) copy-start(bf16[2048]{0:T(1024)(128)(2,1)} %param.13) | copy-start | bytes 12292
  25.9 34.0 %all-to-all-start = ((bf16[16,512,128]{2,1,0:T(8,128)(2,1)}), bf16[16,512,128]{2,1,0:T(8,128)(2,1)S(1)}, u32[]{:S(2)}, u32[]{:S(2)}) async-start(bf16[16,512,128]{2,1,0:T(8,128)(2,1)} %bitcast.59), calls=%async_computation | async-start | bytes 4194304 | tf_op jit(solution)/shard_map/all_to_all | solution.py:27
  31.9 4.4 %collective-permute-start.6 = (bf16[2,2,2,8,64]{4,3,2,1,0:T(8,128)(2,1)S(1)}, bf16[2,2,2,8,64]{4,3,2,1,0:T(8,128)(2,1)S(1)}, u32[]{:S(2)}, u32[]{:S(2)}) collective-permute-start(bf16[2,2,2,8,64]{4,3,2,1,0:T(8,128)(2,1)S(1)} %pad_maximum_fusion.4), channel_id=1, source_target_pairs={{0,1},{1,0},{2,3},{3,2},{4,5},{5,4},{6,7},{7,6},{8,9},{9,8},{10,11... | collective-permute-start | bytes 24584 | tf_op jit(solution)/shard_map/ppermute | solution.py:35
  34.0 21.9 %collective-permute-start.2 = (bf16[320,2048]{1,0:T(8,128)(2,1)}, bf16[320,2048]{1,0:T(8,128)(2,1)}, u32[]{:S(2)}, u32[]{:S(2)}) collective-permute-start(bf16[320,2048]{1,0:T(8,128)(2,1)} %wo_own_ref.1), channel_id=1, source_target_pairs={{0,1},{1,0},{2,3},{3,2},{4,5},{5,4},{6,7},{7,6},{8,9},{9,8},{10,11... | collective-permute-start | bytes 3932168 | tf_op jit(solution)/shard_map/ppermute | solution.py:192
  36.8 13.6 %collective-permute-start.7 = (bf16[2,8,256]{2,1,0:T(8,128)(2,1)S(1)}, bf16[2,8,256]{2,1,0:T(8,128)(2,1)S(1)}, u32[]{:S(2)}, u32[]{:S(2)}) collective-permute-start(bf16[2,8,256]{2,1,0:T(8,128)(2,1)S(1)} %pad_maximum_fusion.7), channel_id=1, source_target_pairs={{0,256},{16,272},{32,288},{48,304},{64,320},{80,336},{96,352},{112... | collective-permute-start | bytes 24584 | tf_op jit(solution)/shard_map/ppermute | solution.py:35
  59.9 1.4 copy-start.1
  73.8 35.0 %all-to-all-start.1 = ((bf16[16,512,128]{2,1,0:T(8,128)(2,1)}), bf16[16,512,128]{2,1,0:T(8,128)(2,1)S(1)}, u32[]{:S(2)}, u32[]{:S(2)}) async-start(bf16[16,512,128]{2,1,0:T(8,128)(2,1)} %ffn.1), calls=%async_computation.1 | async-start | bytes 4194304 | tf_op jit(solution)/shard_map/all_to_all | solution.py:27
  80.1 8.8 %collective-permute-start.8 = (bf16[2,2,8,256]{3,2,1,0:T(8,128)(2,1)S(1)}, bf16[2,2,8,256]{3,2,1,0:T(8,128)(2,1)S(1)}, u32[]{:S(2)}, u32[]{:S(2)}) collective-permute-start(bf16[2,2,8,256]{3,2,1,0:T(8,128)(2,1)S(1)} %pad_maximum_fusion.5), channel_id=1, source_target_pairs={{0,128},{16,144},{32,160},{48,176},{64,192},{80,208},{96,224},{112... | collective-permute-start | bytes 49160 | tf_op jit(solution)/shard_map/ppermute | solution.py:35
  88.9 5.9 %collective-permute-start.9 = (bf16[2,2,2,8,256]{4,3,2,1,0:T(8,128)(2,1)S(1)}, bf16[2,2,2,8,256]{4,3,2,1,0:T(8,128)(2,1)S(1)}, u32[]{:S(2)}, u32[]{:S(2)}) collective-permute-start(bf16[2,2,2,8,256]{4,3,2,1,0:T(8,128)(2,1)S(1)} %pad_maximum_fusion.3), channel_id=1, source_target_pairs={{0,64},{16,80},{32,96},{48,112},{64,0},{80,16},{96,32},{112,48},{1... | collective-permute-start | bytes 98312 | tf_op jit(solution)/shard_map/ppermute | solution.py:35
  94.8 5.3 %collective-permute-start.10 = (bf16[2,2,2,2,8,256]{5,4,3,2,1,0:T(8,128)(2,1)S(1)}, bf16[2,2,2,2,8,256]{5,4,3,2,1,0:T(8,128)(2,1)S(1)}, u32[]{:S(2)}, u32[]{:S(2)}) collective-permute-start(bf16[2,2,2,2,8,256]{5,4,3,2,1,0:T(8,128)(2,1)S(1)} %pad_maximum_fusion.2), channel_id=1, source_target_pairs={{0,32},{16,48},{32,0},{48,16},{64,96},{80,112},{96,64},{112,80},{1... | collective-permute-start | bytes 196616 | tf_op jit(solution)/shard_map/ppermute | solution.py:35
  100.1 7.5 %collective-permute-start.11 = (bf16[2,2,2,2,2,8,256]{6,5,4,3,2,1,0:T(8,128)(2,1)S(1)}, bf16[2,2,2,2,2,8,256]{6,5,4,3,2,1,0:T(8,128)(2,1)S(1)}, u32[]{:S(2)}, u32[]{:S(2)}) collective-permute-start(bf16[2,2,2,2,2,8,256]{6,5,4,3,2,1,0:T(8,128)(2,1)S(1)} %pad_maximum_fusion.1), channel_id=1, source_target_pairs={{0,16},{16,0},{32,48},{48,32},{64,80},{80,64},{96,112},{112,96},{1... | collective-permute-start | bytes 393224 | tf_op jit(solution)/shard_map/ppermute | solution.py:35
  108.8 1.3 copy-start.2
  134.1 10.2 %all-to-all-start.3 = ((bf16[16,32,128]{2,1,0:T(8,128)(2,1)}), bf16[16,32,128]{2,1,0:T(8,128)(2,1)S(1)}, u32[]{:S(2)}, u32[]{:S(2)}) async-start(bf16[16,32,128]{2,1,0:T(8,128)(2,1)} %relu_for_everyone.1), calls=%async_computation.3 | async-start | bytes 262144 | tf_op jit(solution)/shard_map/all_to_all | solution.py:27
  144.3 0.7 copy-start.3

commit v2 on v0

v2 whole, which is shorter than its diff:
```python
import jax
import jax.numpy as jnp
from jax import lax
from jax.experimental import pallas as pl
from jax.experimental.pallas import tpu as pltpu
from jax.sharding import PartitionSpec as P

R = 64
CORES = 2
CHIPS = 8
MP = CORES * CHIPS
DP = 32
SAME_CORE = [[chip * CORES + core for chip in range(CHIPS)] for core in range(CORES)]
VMEM = 32 * 1024 * 1024
FFN_TILE = 256


def matmul(left, right):
    return jnp.dot(left, right, preferred_element_type=jnp.float32)


def matmul_nt(left, right):
    return lax.dot_general(
        left, right, (((1,), (1,)), ((), ())), preferred_element_type=jnp.float32
    )


def exchange(pieces, axis, groups=None):
    return lax.all_to_all(
        pieces, axis, split_axis=0, concat_axis=0, axis_index_groups=groups, tiled=True
    )


def swap_cores(array):
    return lax.ppermute(array, "mp", [(i, i ^ 1) for i in range(MP)])


def doubling_gather(shard, axis, size):
    index = lax.axis_index(axis)
    held = shard
    bit = size // 2
    while bit:
        theirs = lax.ppermute(held, axis, [(i, i ^ bit) for i in range(size)])
        upper = (index & bit) != 0
        held = jnp.stack([jnp.where(upper, theirs, held), jnp.where(upper, held, theirs)])
        bit //= 2
    return held


def in_vmem(array):
    return pltpu.with_memory_space_constraint(array, pltpu.VMEM)


def in_hbm(array):
    return pltpu.with_memory_space_constraint(array, pltpu.HBM)


def whole(array):
    return pl.BlockSpec(memory_space=pltpu.VMEM)


def call(name, body, outs, arrays, scalars=(), place=in_vmem):
    return pl.pallas_call(
        body,
        out_shape=outs,
        in_specs=[pl.BlockSpec(memory_space=pltpu.SMEM) for _ in scalars] + [whole(a) for a in arrays],
        out_specs=jax.tree.map(lambda a: whole(a), outs),
        compiler_params=pltpu.CompilerParams(vmem_limit_bytes=VMEM),
        name=name,
    )(*scalars, *[place(a) for a in arrays])


def spread_body(tokens_ref, given_ref, out_ref, sems):
    me = lax.axis_index("mp") % CORES
    copies = []
    for i in range(CHIPS):
        first, second = out_ref.at[CORES * i + me], out_ref.at[CORES * i + 1 - me]
        copies.append(pltpu.make_async_copy(tokens_ref.at[me], first, sems.at[CORES * i]))
        copies.append(pltpu.make_async_copy(given_ref, second, sems.at[CORES * i + 1]))
    for copy in copies:
        copy.start()
    for copy in copies:
        copy.wait()


def spread(halves, given):
    return pl.pallas_call(
        spread_body,
        out_shape=pltpu.HBM((MP, *given.shape), given.dtype),
        in_specs=[pl.BlockSpec(memory_space=pltpu.HBM), whole(given)],
        out_specs=pl.BlockSpec(memory_space=pltpu.HBM),
        scratch_shapes=[pltpu.SemaphoreType.DMA((MP,))],
        name="spread",
    )(in_hbm(halves), in_vmem(given))


def ffn_body(
    x_ref,
    gain_ref,
    gate_ref,
    gate_other_ref,
    linear_ref,
    linear_other_ref,
    wo_own_ref,
    wo_other_ref,
    out_ref,
    wi_ref,
    wo_ref,
    sums_ref,
    in_sems,
    out_sems,
):
    rows, width = x_ref.shape[1:]
    hid = wo_ref.shape[0]
    own = hid // 2
    placed = [
        (gate_ref, wi_ref.at[pl.ds(0, own)]),
        (gate_other_ref, wi_ref.at[pl.ds(own, own)]),
        (linear_ref, wi_ref.at[pl.ds(hid, own)]),
        (linear_other_ref, wi_ref.at[pl.ds(hid + own, own)]),
        (wo_own_ref, wo_ref.at[pl.ds(0, own)]),
        (wo_other_ref, wo_ref.at[pl.ds(own, own)]),
    ]
    loads = [pltpu.make_async_copy(a, b, in_sems.at[i]) for i, (a, b) in enumerate(placed)]
    for load in loads:
        load.start()
    gain = gain_ref[...].astype(jnp.float32)
    tiles = [pl.ds(k * FFN_TILE, FFN_TILE) for k in range(rows // FFN_TILE)]
    stores = []
    for k, tile in enumerate(tiles):
        wide = jnp.concatenate([x_ref[i, tile] for i in range(MP)], axis=1).astype(jnp.float32)
        scale = lax.rsqrt(jnp.mean(wide * wide, axis=-1, keepdims=True) + 1e-06)
        normed = (wide * scale * gain).astype(jnp.bfloat16)
        if k == 0:
            for load in loads[:4]:
                load.wait()
        both = matmul_nt(normed, wi_ref[...])
        act = (jax.nn.gelu(both[:, :hid], approximate=True) * both[:, hid:]).astype(jnp.bfloat16)
        if k == 0:
            for load in loads[4:]:
                load.wait()
        sums = matmul(act, wo_ref[...]).astype(jnp.bfloat16)
        for i in range(MP):
            sums_ref[k, i] = sums[:, i * width : (i + 1) * width]
        stores.append(pltpu.make_async_copy(sums_ref.at[k], out_ref.at[:, tile], out_sems.at[k]))
        stores[k].start()
    for store in stores:
        store.wait()


def ffn(x, gain, gates, linears, wos):
    rows, width = x.shape[1:]
    own, features = wos[0].shape
    tiles = rows // FFN_TILE
    weights = (*gates, *linears, *wos)
    hbm = pl.BlockSpec(memory_space=pltpu.HBM)
    return pl.pallas_call(
        ffn_body,
        out_shape=pltpu.HBM(x.shape, x.dtype),
        in_specs=[whole(x), whole(gain)] + [hbm] * len(weights),
        out_specs=hbm,
        scratch_shapes=[
            pltpu.VMEM((4 * own, features), x.dtype),
            pltpu.VMEM((2 * own, features), x.dtype),
            pltpu.VMEM((tiles, MP, FFN_TILE, width), x.dtype),
            pltpu.SemaphoreType.DMA((len(weights),)),
            pltpu.SemaphoreType.DMA((tiles,)),
        ],
        compiler_params=pltpu.CompilerParams(vmem_limit_bytes=VMEM),
        name="ffn",
    )(in_vmem(x), in_vmem(gain), *[in_hbm(w) for w in weights])


def squeeze_body(
    ids_ref,
    parts_ref,
    down_ref,
    other_ref,
    kept_out,
    given_out,
    squeezed_out,
    kept_ref,
    given_ref,
    squeezed_ref,
    sems,
):
    rows = parts_ref.shape[1]
    seqs = ids_ref.shape[0]
    seq = rows * CORES // seqs
    quarter = seq // 4
    me = lax.axis_index("mp") % CORES
    for s in range(rows // seq):
        tile = slice(s * seq, (s + 1) * seq)
        task = ids_ref[me * (rows // seq) + s]
        down, other = down_ref[task], other_ref[task]
        ffout = []
        for core in range(CORES):
            total = parts_ref[core, tile].astype(jnp.float32)
            for i in range(1, CHIPS):
                total = total + parts_ref[CORES * i + core, tile].astype(jnp.float32)
            ffout.append(total)
        kept = jnp.where(me == 0, ffout[0], ffout[1]).astype(jnp.bfloat16)
        given = jnp.where(me == 0, ffout[1], ffout[0]).astype(jnp.bfloat16)
        kept_ref[tile] = kept
        given_ref[tile] = given
        sums = (matmul(kept, down) + matmul(given, other)).astype(jnp.bfloat16)
        for i in range(2):
            first = sums[2 * i * quarter : (2 * i + 1) * quarter]
            second = sums[(2 * i + 1) * quarter : (2 * i + 2) * quarter]
            squeezed_ref[2 * s + i] = jnp.concatenate([first, second], axis=1)
    stores = [
        pltpu.make_async_copy(squeezed_ref, squeezed_out, sems.at[0]),
        pltpu.make_async_copy(given_ref, given_out, sems.at[1]),
        pltpu.make_async_copy(kept_ref, kept_out, sems.at[2]),
    ]
    for store in stores:
        store.start()
    for store in stores:
        store.wait()


def squeeze(task_ids, parts, down, other):
    rows, width = parts.shape[1:]
    share = (CHIPS, rows // CHIPS // 2, 2 * R)
    arrays = (parts, down, other)
    hbm = pl.BlockSpec(memory_space=pltpu.HBM)
    return pl.pallas_call(
        squeeze_body,
        out_shape=(
            pltpu.HBM((rows, width), parts.dtype),
            pltpu.HBM((rows, width), parts.dtype),
            pltpu.HBM(share, parts.dtype),
        ),
        in_specs=[pl.BlockSpec(memory_space=pltpu.SMEM)] + [whole(a) for a in arrays],
        out_specs=(hbm, hbm, hbm),
        scratch_shapes=[
            pltpu.VMEM((rows, width), parts.dtype),
            pltpu.VMEM((rows, width), parts.dtype),
            pltpu.VMEM(share, parts.dtype),
            pltpu.SemaphoreType.DMA((3,)),
        ],
        compiler_params=pltpu.CompilerParams(vmem_limit_bytes=VMEM),
        name="squeeze",
    )(task_ids, *[in_vmem(a) for a in arrays])


def relu_body(parts_ref, out_ref):
    total = parts_ref[0].astype(jnp.float32)
    for i in range(1, CHIPS):
        total = total + parts_ref[i].astype(jnp.float32)
    squeezed = jnp.maximum(total, 0.0).astype(jnp.bfloat16)
    for i in range(MP):
        out_ref[i] = squeezed


def relu_for_everyone(parts):
    return call("relu_for_everyone", relu_body, jax.ShapeDtypeStruct((MP, *parts.shape[1:]), parts.dtype), (parts,))


def expand_body(ids_ref, tokens_ref, mine_ref, theirs_ref, squeezed_ref, up_ref, out_ref):
    seqs = ids_ref.shape[0]
    seq = tokens_ref.shape[0] // seqs
    swapped = lax.axis_index("mp") % CORES
    for core in range(CORES):
        for j in range(seqs // CORES):
            s = core * (seqs // CORES) + j
            tile = slice(s * seq, (s + 1) * seq)
            part = slice(j * seq, (j + 1) * seq)
            both = [squeezed_ref[CORES * (2 * j + i) + core] for i in range(2)]
            squeezed = jnp.concatenate(
                [both[i][:, k * R : (k + 1) * R] for i in range(2) for k in range(2)]
            )
            expand = matmul_nt(squeezed, up_ref[ids_ref[s]])
            ffout = jnp.where(swapped == core, mine_ref[part], theirs_ref[part])
            total = tokens_ref[tile].astype(jnp.float32) + ffout.astype(jnp.float32) + expand
            out_ref[tile] = total.astype(jnp.bfloat16)


def expand(task_ids, tokens, mine, theirs, squeezed, up):
    out = jax.ShapeDtypeStruct(tokens.shape, tokens.dtype)
    return call("expand", expand_body, out, (tokens, mine, theirs, squeezed, up), (task_ids,))


def hidden_body(layer_ref, task_table_ref, layer_table_ref, hyper_in_ref, out_ref):
    task_table = task_table_ref[...]
    row = layer_table_ref[pl.ds(layer_ref[0], 1)]
    embed = jnp.concatenate([task_table, jnp.broadcast_to(row, task_table.shape)], axis=1)
    hidden = jnp.maximum(matmul_nt(embed.astype(jnp.bfloat16), hyper_in_ref[...]), 0.0)
    for i in range(MP):
        out_ref[i] = hidden.astype(jnp.bfloat16)


def per_device(
    tokens,
    norm_gain,
    wi_gate,
    wi_linear,
    wo_out,
    task_table,
    layer_table,
    task_ids,
    layer_index,
    hyper_in,
    gen_down,
    gen_up,
):
    tok_dev, width = tokens.shape
    features = width * MP
    half = tok_dev // CORES
    core = lax.axis_index("mp") % CORES
    task_count = task_table.shape[0]

    halves = tokens.reshape(CORES, half, width)
    given = swap_cores(lax.dynamic_index_in_dim(halves, 1 - core, 0, keepdims=False))

    share = hyper_in.shape[1]
    hidden = call(
        "hidden",
        hidden_body,
        jax.ShapeDtypeStruct((MP, task_count, share), jnp.bfloat16),
        (task_table, layer_table, hyper_in.T),
        (layer_index,),
        in_hbm,
    )
    hidden = exchange(hidden, "mp")

    sent, hidden = lax.optimization_barrier((spread(halves, given), hidden))
    gathered = exchange(sent, "mp", SAME_CORE)

    gate, linear = wi_gate.T, wi_linear.T
    gate_other, linear_other, wo_other = swap_cores(gate), swap_cores(linear), swap_cores(wo_out)

    hidden = jnp.moveaxis(hidden, 0, 1).reshape(task_count, -1)
    made = jnp.stack(
        [matmul(hidden, gen_down).astype(jnp.bfloat16), matmul(hidden, gen_up).astype(jnp.bfloat16)]
    )
    all_tasks = doubling_gather(made, "dp", DP)
    all_tasks = jnp.transpose(all_tasks, (5, 6, 4, 3, 2, 1, 0, 7))
    adapters = all_tasks.reshape(2, task_count, width, R)
    down, up = adapters[0], adapters[1]

    partial = ffn(
        gathered,
        norm_gain.reshape(1, features),
        (gate, gate_other),
        (linear, linear_other),
        (wo_out, wo_other),
    )
    parts = exchange(partial, "mp", SAME_CORE)
    mine, given, squeeze_part = squeeze(task_ids, parts, down, swap_cores(down))
    theirs = swap_cores(given)
    squeezed = exchange(relu_for_everyone(exchange(squeeze_part, "mp", SAME_CORE)), "mp")
    return expand(task_ids, tokens, mine, theirs, squeezed, up)


def solution(mesh):
    return jax.shard_map(
        per_device,
        mesh=mesh,
        in_specs=(
            P("dp", "mp"),
            P(),
            P(None, "mp"),
            P(None, "mp"),
            P("mp", None),
            P(),
            P(),
            P("dp"),
            P(),
            P(None, "mp"),
            P(None, ("mp", "dp")),
            P(None, ("mp", "dp")),
        ),
        out_specs=P("dp", "mp"),
        check_vma=False,
    )
```

time: 220 us -> 157 us (0.71)
  waiting for transfers between devices: 132 us -> 24.8 us
  Pallas kernels: 0 us -> 47.2 us
  starting transfers between devices: 34.5 us -> 72.8 us
  matrix products: 15.6 us -> 0.36 us
  local copies, waits for them, and re-layouts: 16.4 us -> 2.04 us
  between operations: 14.2 us -> 1.02 us
  blocking collectives: 0 us -> 8.26 us
  other arithmetic: 6.5 us -> 0.14 us
    all_gather x1 -> x0, waiting for transfers between devices: 61.3 us -> none  [per_device(): full_rows = lax.all_gather(tokens, 'mp', axis=1, tiled=True)]
    all_to_all x5 -> x4, waiting for transfers between devices: 64.2 us -> 8.5 us  [exchange(): lax.all_to_all(pieces, axis, split_axis=0, concat_axis=0, axis_index_grou...]
    ppermute x0 -> x11, starting transfers between devices: none -> 53.8 us  [the longest x5 31.1 us: doubling_gather(): theirs = lax.ppermute(held, axis, [(i, i ^ bit) for i in range(size)])]
    pallas_call x0 -> x6, Pallas kernels: none -> 47.2 us  [the longest x1 33 us: spread(): pl.pallas_call(spread_body, out_shape=pltpu.HBM((MP, *given.shape), given...]
    ppermute x0 -> x11, waiting for transfers between devices: none -> 16.3 us  [the longest x5 15.1 us: doubling_gather(): theirs = lax.ppermute(held, axis, [(i, i ^ bit) for i in range(size)])]
    all_to_all x5 -> x4, starting transfers between devices: 34.4 us -> 19 us  [exchange(): lax.all_to_all(pieces, axis, split_axis=0, concat_axis=0, axis_index_grou...]
    dot_general x5 -> x2, matrix products: 15 us -> 0.36 us  [matmul(): return jnp.dot(left, right, preferred_element_type=jnp.float32)]
    unnamed x30 -> x13, local copies, waits for them, and re-layouts: 9.83 us -> 0.14 us
  transfers between devices with their start and end apart: 7 -> 15, of which waited for: 7 -> 7; matrix products, arithmetic and copies ran while one was open for 5% -> 1% of each run, Pallas kernels for 0% -> 7%
where the time goes in v2:
time: 157 us
  starting transfers between devices  72.8 us (46%)
  Pallas kernels  47.2 us (30%)
  waiting for transfers between devices  24.8 us (16%)
  blocking collectives  8.26 us (5%)
  local copies, waits for them, and re-layouts  2.04 us (1%)
    pallas_call x1, Pallas kernels, spread(): pl.pallas_call(spread_body, out_shape=pltpu.HBM((MP, *given.shape), given...  33 us
    ppermute x5, starting transfers between devices, doubling_gather(): theirs = lax.ppermute(held, axis, [(i, i ^ bit) for i in range(size)])  31.1 us
    ppermute x6, starting transfers between devices, swap_cores(): return lax.ppermute(array, 'mp', [(i, i ^ 1) for i in range(MP)])  22.7 us
    all_to_all x4, starting transfers between devices, exchange(): lax.all_to_all(pieces, axis, split_axis=0, concat_axis=0, axis_index_grou...  19 us
    ppermute x5, waiting for transfers between devices, doubling_gather(): theirs = lax.ppermute(held, axis, [(i, i ^ bit) for i in range(size)])  15.1 us
    pallas_call x1, Pallas kernels, ffn(): pl.pallas_call(ffn_body, out_shape=pltpu.HBM(x.shape, x.dtype), in_specs=...  9.26 us
    all_to_all x4, waiting for transfers between devices, exchange(): lax.all_to_all(pieces, axis, split_axis=0, concat_axis=0, axis_index_grou...  8.5 us
    all_to_all x1, blocking collectives, exchange(): lax.all_to_all(pieces, axis, split_axis=0, concat_axis=0, axis_index_grou...  8.26 us
  transfers between devices with their start and end apart: 15, of which 7 were waited for; matrix products, arithmetic and copies ran while one was open for 1% of the time, Pallas kernels for 7%

profile of v2, /device:TPU:1, one launch (start us, length us, event | category | flops | bytes accessed | tf_op | source)
XLA Modules:
  0.0 156.6 jit_solution(6501328787512099125)
XLA Ops:
  0.0 1.0 dynamic-slice_bitcast_fusion
  1.0 8.8 %collective-permute-start = (bf16[512,128]{1,0:T(8,128)(2,1)S(1)}, bf16[512,128]{1,0:T(8,128)(2,1)S(1)}, u32[]{:S(2)}, u32[]{:S(2)}) collective-permute-start(bf16[512,128]{1,0:T(8,128)(2,1)S(1)} %dynamic-slice_bitcast_fusion), channel_id=1, source_target_pairs={{0,1},{1,0},{2,3},{3,2},{4,5},{5,4},{6,7},{7,6},{8,9},{9,8},{10,11... | collective-permute-start | bytes 393224 | tf_op jit(solution)/shard_map/ppermute | solution.py:35
  10.4 0.9 hidden.1
  11.4 0.1 reshape.17
  11.5 8.3 %all_to_all.25 = bf16[16,2,256]{2,1,0:T(2,128)(2,1)S(1)} all-to-all(bf16[16,2,256]{2,1,0:T(2,128)(2,1)S(1)} %reshape.17), channel_id=1, replica_groups=mesh['dp'=32,'mp'=16] {'mp'}, dimensions={0} | all-to-all | bytes 32768 | tf_op jit(solution)/shard_map/all_to_all | solution.py:29
  19.7 0.1 reshape.18
  19.8 33.0 %spread.1 = bf16[16,512,128]{2,1,0:T(8,128)(2,1)} custom-call(bf16[2,512,128]{2,1,0:T(8,128)(2,1)} %bitcast.38, bf16[512,128]{1,0:T(8,128)(2,1)S(1)} %collective-permute-done.given_ref), custom_call_target="tpu_custom_call" | custom-call | tf_op jit(solution)/shard_map/spread/pallas_call | solution.py:87
  52.9 0.0 copy-start.4
  52.9 3.7 %all-to-all-start.1 = ((bf16[16,512,128]{2,1,0:T(8,128)(2,1)}), bf16[16,512,128]{2,1,0:T(8,128)(2,1)S(1)}, u32[]{:S(2)}, u32[]{:S(2)}) async-start(bf16[16,512,128]{2,1,0:T(8,128)(2,1)} %spread.1), calls=%async_computation.1 | async-start | bytes 4194304 | tf_op jit(solution)/shard_map/all_to_all | solution.py:29
  56.6 0.0 copy-start.5
  56.6 2.3 %collective-permute-start.1 = (bf16[320,2048]{1,0:T(8,128)(2,1)}, bf16[320,2048]{1,0:T(8,128)(2,1)}, u32[]{:S(2)}, u32[]{:S(2)}) collective-permute-start(bf16[320,2048]{1,0:T(8,128)(2,1)} %bitcast.39), channel_id=1, source_target_pairs={{0,1},{1,0},{2,3},{3,2},{4,5},{5,4},{6,7},{7,6},{8,9},{9,8},{10,11... | collective-permute-start | bytes 3932168 | tf_op jit(solution)/shard_map/ppermute | solution.py:35
  58.9 2.0 %collective-permute-start.2 = (bf16[320,2048]{1,0:T(8,128)(2,1)}, bf16[320,2048]{1,0:T(8,128)(2,1)}, u32[]{:S(2)}, u32[]{:S(2)}) collective-permute-start(bf16[320,2048]{1,0:T(8,128)(2,1)} %bitcast.41), channel_id=1, source_target_pairs={{0,1},{1,0},{2,3},{3,2},{4,5},{5,4},{6,7},{7,6},{8,9},{9,8},{10,11... | collective-permute-start | bytes 3932168 | tf_op jit(solution)/shard_map/ppermute | solution.py:35
  61.0 2.3 %collective-permute-start.3 = (bf16[320,2048]{1,0:T(8,128)(2,1)}, bf16[320,2048]{1,0:T(8,128)(2,1)}, u32[]{:S(2)}, u32[]{:S(2)}) collective-permute-start(bf16[320,2048]{1,0:T(8,128)(2,1)} %wo_own_ref.1), channel_id=1, source_target_pairs={{0,1},{1,0},{2,3},{3,2},{4,5},{5,4},{6,7},{7,6},{8,9},{9,8},{10,11... | collective-permute-start | bytes 3932168 | tf_op jit(solution)/shard_map/ppermute | solution.py:35
  63.3 0.1 reshape.16
  63.4 0.2 fusion.1
  63.6 0.2 fusion
  63.8 12.9 %collective-permute-start.4 = (bf16[2,8,256]{2,1,0:T(8,128)(2,1)S(1)}, bf16[2,8,256]{2,1,0:T(8,128)(2,1)S(1)}, u32[]{:S(2)}, u32[]{:S(2)}) collective-permute-start(bf16[2,8,256]{2,1,0:T(8,128)(2,1)S(1)} %pad_maximum_fusion.4), channel_id=1, source_target_pairs={{0,256},{16,272},{32,288},{48,304},{64,320},{80,336},{96,352},{112... | collective-permute-start | bytes 24584 | tf_op jit(solution)/shard_map/ppermute | solution.py:43
  76.7 1.1 collective-permute-done.4
  77.8 5.4 %collective-permute-start.5 = (bf16[2,2,8,256]{3,2,1,0:T(8,128)(2,1)S(1)}, bf16[2,2,8,256]{3,2,1,0:T(8,128)(2,1)S(1)}, u32[]{:S(2)}, u32[]{:S(2)}) collective-permute-start(bf16[2,2,8,256]{3,2,1,0:T(8,128)(2,1)S(1)} %pad_maximum_fusion.3), channel_id=1, source_target_pairs={{0,128},{16,144},{32,160},{48,176},{64,192},{80,208},{96,224},{112... | collective-permute-start | bytes 49160 | tf_op jit(solution)/shard_map/ppermute | solution.py:43
  83.2 0.0 collective-permute-done.1.gate_other_ref
  83.3 0.0 collective-permute-done.3.wo_other_ref
  83.3 0.0 all-to-all-done.1.x_ref
  83.3 9.3 %ffn.1 = bf16[16,512,128]{2,1,0:T(8,128)(2,1)} custom-call(bf16[16,512,128]{2,1,0:T(8,128)(2,1)S(1)} %all-to-all-done.1.x_ref, bf16[1,2048]{1,0:T(2,128)(2,1)S(1)} %reshape.15.gain_ref, bf16[320,2048]{1,0:T(8,128)(2,1)} %bitcast.40, bf16[320,2048]{1,0:T(8,128)(2,1)} %collective-permute-done.1.gate_other_ref, bf16[320,2048]{1,0:T(8,128)(2,1)} %bitcast.42, ...), custom_call_target="tpu_custom_call" | custom-call | tf_op jit(solution)/shard_map/ffn/pallas_call | solution.py:157
  92.6 5.5 %all-to-all-start.2 = ((bf16[16,512,128]{2,1,0:T(8,128)(2,1)}), bf16[16,512,128]{2,1,0:T(8,128)(2,1)S(1)}, u32[]{:S(2)}, u32[]{:S(2)}) async-start(bf16[16,512,128]{2,1,0:T(8,128)(2,1)} %ffn.1), calls=%async_computation.2 | async-start | bytes 4194304 | tf_op jit(solution)/shard_map/all_to_all | solution.py:29
  98.0 0.0 collective-permute-done.5
  98.1 5.0 %collective-permute-start.6 = (bf16[2,2,2,8,256]{4,3,2,1,0:T(8,128)(2,1)S(1)}, bf16[2,2,2,8,256]{4,3,2,1,0:T(8,128)(2,1)S(1)}, u32[]{:S(2)}, u32[]{:S(2)}) collective-permute-start(bf16[2,2,2,8,256]{4,3,2,1,0:T(8,128)(2,1)S(1)} %pad_maximum_fusion.2), channel_id=1, source_target_pairs={{0,64},{16,80},{32,96},{48,112},{64,0},{80,16},{96,32},{112,48},{1... | collective-permute-start | bytes 98312 | tf_op jit(solution)/shard_map/ppermute | solution.py:43
  103.1 1.6 %collective-permute-done.6 = bf16[2,2,2,8,256]{4,3,2,1,0:T(8,128)(2,1)S(1)} collective-permute-done((bf16[2,2,2,8,256]{4,3,2,1,0:T(8,128)(2,1)S(1)}, bf16[2,2,2,8,256]{4,3,2,1,0:T(8,128)(2,1)S(1)}, u32[]{:S(2)}, u32[]{:S(2)}) %collective-permute-start.6) | collective-permute-done | bytes 32800 | tf_op jit(solution)/shard_map/ppermute | solution.py:43
  104.7 3.4 %collective-permute-start.7 = (bf16[2,2,2,2,8,256]{5,4,3,2,1,0:T(8,128)(2,1)S(1)}, bf16[2,2,2,2,8,256]{5,4,3,2,1,0:T(8,128)(2,1)S(1)}, u32[]{:S(2)}, u32[]{:S(2)}) collective-permute-start(bf16[2,2,2,2,8,256]{5,4,3,2,1,0:T(8,128)(2,1)S(1)} %pad_maximum_fusion.1), channel_id=1, source_target_pairs={{0,32},{16,48},{32,0},{48,16},{64,96},{80,112},{96,64},{112,80},{1... | collective-permute-start | bytes 196616 | tf_op jit(solution)/shard_map/ppermute | solution.py:43
  108.2 1.9 %collective-permute-done.7 = bf16[2,2,2,2,8,256]{5,4,3,2,1,0:T(8,128)(2,1)S(1)} collective-permute-done((bf16[2,2,2,2,8,256]{5,4,3,2,1,0:T(8,128)(2,1)S(1)}, bf16[2,2,2,2,8,256]{5,4,3,2,1,0:T(8,128)(2,1)S(1)}, u32[]{:S(2)}, u32[]{:S(2)}) %collective-permute-start.7) | collective-permute-done | bytes 65568 | tf_op jit(solution)/shard_map/ppermute | solution.py:43
  110.1 0.0 copy-start.3
  110.1 4.4 %collective-permute-start.8 = (bf16[2,2,2,2,2,8,256]{6,5,4,3,2,1,0:T(8,128)(2,1)S(1)}, bf16[2,2,2,2,2,8,256]{6,5,4,3,2,1,0:T(8,128)(2,1)S(1)}, u32[]{:S(2)}, u32[]{:S(2)}) collective-permute-start(bf16[2,2,2,2,2,8,256]{6,5,4,3,2,1,0:T(8,128)(2,1)S(1)} %pad_maximum_fusion), channel_id=1, source_target_pairs={{0,16},{16,0},{32,48},{48,32},{64,80},{80,64},{96,112},{112,96},{1... | collective-permute-start | bytes 393224 | tf_op jit(solution)/shard_map/ppermute | solution.py:43
  114.5 10.5 %collective-permute-done.8 = bf16[2,2,2,2,2,8,256]{6,5,4,3,2,1,0:T(8,128)(2,1)S(1)} collective-permute-done((bf16[2,2,2,2,2,8,256]{6,5,4,3,2,1,0:T(8,128)(2,1)S(1)}, bf16[2,2,2,2,2,8,256]{6,5,4,3,2,1,0:T(8,128)(2,1)S(1)}, u32[]{:S(2)}, u32[]{:S(2)}) %collective-permute-start.8) | collective-permute-done | bytes 131104 | tf_op jit(solution)/shard_map/ppermute | solution.py:43
  125.1 0.1 copy.16
  125.3 0.2 squeeze.12.down_ref
  125.5 0.0 copy-start.1
  125.5 4.7 %collective-permute-start.9 = (bf16[8,128,64]{2,1,0:T(8,128)(2,1)S(1)}, bf16[8,128,64]{2,1,0:T(8,128)(2,1)S(1)}, u32[]{:S(2)}, u32[]{:S(2)}) collective-permute-start(bf16[8,128,64]{2,1,0:T(8,128)(2,1)S(1)} %squeeze.12.down_ref), channel_id=1, source_target_pairs={{0,1},{1,0},{2,3},{3,2},{4,5},{5,4},{6,7},{7,6},{8,9},{9,8},{10,11... | collective-permute-start | bytes 393224 | tf_op jit(solution)/shard_map/ppermute | solution.py:35
  130.2 1.1 collective-permute-done.9.other_ref
  131.4 1.8 %squeeze.14 = (bf16[512,128]{1,0:T(8,128)(2,1)}, bf16[512,128]{1,0:T(8,128)(2,1)}, bf16[8,32,128]{2,1,0:T(8,128)(2,1)}) custom-call(s32[8]{0:T(128)S(1)} %copy-done.3, bf16[16,512,128]{2,1,0:T(8,128)(2,1)S(1)} %all-to-all-done.2.parts_ref, bf16[8,128,64]{2,1,0:T(8,128)(2,1)S(1)} %squeeze.12.down_ref, bf16[8,128,64]{2,1,0:T(8,128)(2,1)S(1)} %collective-permute-done.9.other_ref), custom_call_target="tpu_custom_call" | custom-call | tf_op jit(solution)/shard_map/squeeze/pallas_call | solution.py:227
  133.2 0.0 copy-start.2
  133.2 4.7 %all-to-all-start.3 = ((bf16[8,32,128]{2,1,0:T(8,128)(2,1)}), bf16[8,32,128]{2,1,0:T(8,128)(2,1)S(1)}, u32[]{:S(2)}, u32[]{:S(2)}) async-start(bf16[8,32,128]{2,1,0:T(8,128)(2,1)} %get-tuple-element.14), calls=%async_computation.3 | async-start | bytes 131072 | tf_op jit(solution)/shard_map/all_to_all | solution.py:29
  137.9 2.5 %collective-permute-start.10 = (bf16[512,128]{1,0:T(8,128)(2,1)}, bf16[512,128]{1,0:T(8,128)(2,1)S(1)}, u32[]{:S(2)}, u32[]{:S(2)}) collective-permute-start(bf16[512,128]{1,0:T(8,128)(2,1)} %get-tuple-element.13), channel_id=1, source_target_pairs={{0,1},{1,0},{2,3},{3,2},{4,5},{5,4},{6,7},{7,6},{8,9},{9,8},{10,11... | collective-permute-start | bytes 393224 | tf_op jit(solution)/shard_map/ppermute | solution.py:35
  140.4 2.6 %all-to-all-done.3.parts_ref = bf16[8,32,128]{2,1,0:T(8,128)(2,1)S(1)} async-done(((bf16[8,32,128]{2,1,0:T(8,128)(2,1)}), bf16[8,32,128]{2,1,0:T(8,128)(2,1)S(1)}, u32[]{:S(2)}, u32[]{:S(2)}) %all-to-all-start.3) | async-done | bytes 65568 | tf_op jit(solution)/shard_map/all_to_all | solution.py:29
  143.1 0.7 relu_for_everyone.1
  143.7 5.1 %all-to-all-start.4 = ((bf16[16,32,128]{2,1,0:T(8,128)(2,1)}), bf16[16,32,128]{2,1,0:T(8,128)(2,1)S(1)}, u32[]{:S(2)}, u32[]{:S(2)}) async-start(bf16[16,32,128]{2,1,0:T(8,128)(2,1)} %relu_for_everyone.1), calls=%async_computation.4 | async-start | bytes 262144 | tf_op jit(solution)/shard_map/all_to_all | solution.py:29
  148.8 0.1 copy.17
  149.0 0.2 squeeze.13.up_ref
  149.2 5.9 %all-to-all-done.4.squeezed_ref = bf16[16,32,128]{2,1,0:T(8,128)(2,1)S(1)} async-done(((bf16[16,32,128]{2,1,0:T(8,128)(2,1)}), bf16[16,32,128]{2,1,0:T(8,128)(2,1)S(1)}, u32[]{:S(2)}, u32[]{:S(2)}) %all-to-all-start.4) | async-done | bytes 131104 | tf_op jit(solution)/shard_map/all_to_all | solution.py:29
  155.0 1.6 expand.1
  (25 shorter events, 0.2 us)
Async XLA Ops:
  0.0 63.4 %copy-start = (bf16[1024,256]{1,0:T(8,128)(2,1)S(1)}, bf16[1024,256]{1,0:T(8,128)(2,1)}, u32[]{:S(2)}) copy-start(bf16[1024,256]{1,0:T(8,128)(2,1)} %param.23) | copy-start | bytes 1572868
  1.0 18.8 %collective-permute-start = (bf16[512,128]{1,0:T(8,128)(2,1)S(1)}, bf16[512,128]{1,0:T(8,128)(2,1)S(1)}, u32[]{:S(2)}, u32[]{:S(2)}) collective-permute-start(bf16[512,128]{1,0:T(8,128)(2,1)S(1)} %dynamic-slice_bitcast_fusion), channel_id=1, source_target_pairs={{0,1},{1,0},{2,3},{3,2},{4,5},{5,4},{6,7},{7,6},{8,9},{9,8},{10,11... | collective-permute-start | bytes 393224 | tf_op jit(solution)/shard_map/ppermute | solution.py:35
  52.9 10.7 %copy-start.4 = (bf16[1024,256]{1,0:T(8,128)(2,1)S(1)}, bf16[1024,256]{1,0:T(8,128)(2,1)}, u32[]{:S(2)}) copy-start(bf16[1024,256]{1,0:T(8,128)(2,1)} %param.22) | copy-start | bytes 1572868
  52.9 30.4 %all-to-all-start.1 = ((bf16[16,512,128]{2,1,0:T(8,128)(2,1)}), bf16[16,512,128]{2,1,0:T(8,128)(2,1)S(1)}, u32[]{:S(2)}, u32[]{:S(2)}) async-start(bf16[16,512,128]{2,1,0:T(8,128)(2,1)} %spread.1), calls=%async_computation.1 | async-start | bytes 4194304 | tf_op jit(solution)/shard_map/all_to_all | solution.py:29
  56.6 26.6 %copy-start.5 = (bf16[2048]{0:T(1024)(128)(2,1)S(1)}, bf16[2048]{0:T(1024)(128)(2,1)}, u32[]{:S(2)}) copy-start(bf16[2048]{0:T(1024)(128)(2,1)} %param.13) | copy-start | bytes 12292
  56.6 26.6 %collective-permute-start.1 = (bf16[320,2048]{1,0:T(8,128)(2,1)}, bf16[320,2048]{1,0:T(8,128)(2,1)}, u32[]{:S(2)}, u32[]{:S(2)}) collective-permute-start(bf16[320,2048]{1,0:T(8,128)(2,1)} %bitcast.39), channel_id=1, source_target_pairs={{0,1},{1,0},{2,3},{3,2},{4,5},{5,4},{6,7},{7,6},{8,9},{9,8},{10,11... | collective-permute-start | bytes 3932168 | tf_op jit(solution)/shard_map/ppermute | solution.py:35
  58.9 24.3 %collective-permute-start.2 = (bf16[320,2048]{1,0:T(8,128)(2,1)}, bf16[320,2048]{1,0:T(8,128)(2,1)}, u32[]{:S(2)}, u32[]{:S(2)}) collective-permute-start(bf16[320,2048]{1,0:T(8,128)(2,1)} %bitcast.41), channel_id=1, source_target_pairs={{0,1},{1,0},{2,3},{3,2},{4,5},{5,4},{6,7},{7,6},{8,9},{9,8},{10,11... | collective-permute-start | bytes 3932168 | tf_op jit(solution)/shard_map/ppermute | solution.py:35
  61.0 22.3 %collective-permute-start.3 = (bf16[320,2048]{1,0:T(8,128)(2,1)}, bf16[320,2048]{1,0:T(8,128)(2,1)}, u32[]{:S(2)}, u32[]{:S(2)}) collective-permute-start(bf16[320,2048]{1,0:T(8,128)(2,1)} %wo_own_ref.1), channel_id=1, source_target_pairs={{0,1},{1,0},{2,3},{3,2},{4,5},{5,4},{6,7},{7,6},{8,9},{9,8},{10,11... | collective-permute-start | bytes 3932168 | tf_op jit(solution)/shard_map/ppermute | solution.py:35
  63.8 14.0 %collective-permute-start.4 = (bf16[2,8,256]{2,1,0:T(8,128)(2,1)S(1)}, bf16[2,8,256]{2,1,0:T(8,128)(2,1)S(1)}, u32[]{:S(2)}, u32[]{:S(2)}) collective-permute-start(bf16[2,8,256]{2,1,0:T(8,128)(2,1)S(1)} %pad_maximum_fusion.4), channel_id=1, source_target_pairs={{0,256},{16,272},{32,288},{48,304},{64,320},{80,336},{96,352},{112... | collective-permute-start | bytes 24584 | tf_op jit(solution)/shard_map/ppermute | solution.py:43
  77.8 20.2 %collective-permute-start.5 = (bf16[2,2,8,256]{3,2,1,0:T(8,128)(2,1)S(1)}, bf16[2,2,8,256]{3,2,1,0:T(8,128)(2,1)S(1)}, u32[]{:S(2)}, u32[]{:S(2)}) collective-permute-start(bf16[2,2,8,256]{3,2,1,0:T(8,128)(2,1)S(1)} %pad_maximum_fusion.3), channel_id=1, source_target_pairs={{0,128},{16,144},{32,160},{48,176},{64,192},{80,208},{96,224},{112... | collective-permute-start | bytes 49160 | tf_op jit(solution)/shard_map/ppermute | solution.py:43
  92.6 38.8 %all-to-all-start.2 = ((bf16[16,512,128]{2,1,0:T(8,128)(2,1)}), bf16[16,512,128]{2,1,0:T(8,128)(2,1)S(1)}, u32[]{:S(2)}, u32[]{:S(2)}) async-start(bf16[16,512,128]{2,1,0:T(8,128)(2,1)} %ffn.1), calls=%async_computation.2 | async-start | bytes 4194304 | tf_op jit(solution)/shard_map/all_to_all | solution.py:29
  98.1 6.6 %collective-permute-start.6 = (bf16[2,2,2,8,256]{4,3,2,1,0:T(8,128)(2,1)S(1)}, bf16[2,2,2,8,256]{4,3,2,1,0:T(8,128)(2,1)S(1)}, u32[]{:S(2)}, u32[]{:S(2)}) collective-permute-start(bf16[2,2,2,8,256]{4,3,2,1,0:T(8,128)(2,1)S(1)} %pad_maximum_fusion.2), channel_id=1, source_target_pairs={{0,64},{16,80},{32,96},{48,112},{64,0},{80,16},{96,32},{112,48},{1... | collective-permute-start | bytes 98312 | tf_op jit(solution)/shard_map/ppermute | solution.py:43
  104.7 5.4 %collective-permute-start.7 = (bf16[2,2,2,2,8,256]{5,4,3,2,1,0:T(8,128)(2,1)S(1)}, bf16[2,2,2,2,8,256]{5,4,3,2,1,0:T(8,128)(2,1)S(1)}, u32[]{:S(2)}, u32[]{:S(2)}) collective-permute-start(bf16[2,2,2,2,8,256]{5,4,3,2,1,0:T(8,128)(2,1)S(1)} %pad_maximum_fusion.1), channel_id=1, source_target_pairs={{0,32},{16,48},{32,0},{48,16},{64,96},{80,112},{96,64},{112,80},{1... | collective-permute-start | bytes 196616 | tf_op jit(solution)/shard_map/ppermute | solution.py:43
  110.1 21.3 %copy-start.3 = (s32[8]{0:T(128)S(1)}, s32[8]{0:T(128)}, u32[]{:S(2)}) copy-start(s32[8]{0:T(128)} %ids_ref.3) | copy-start | bytes 100
  110.1 14.9 %collective-permute-start.8 = (bf16[2,2,2,2,2,8,256]{6,5,4,3,2,1,0:T(8,128)(2,1)S(1)}, bf16[2,2,2,2,2,8,256]{6,5,4,3,2,1,0:T(8,128)(2,1)S(1)}, u32[]{:S(2)}, u32[]{:S(2)}) collective-permute-start(bf16[2,2,2,2,2,8,256]{6,5,4,3,2,1,0:T(8,128)(2,1)S(1)} %pad_maximum_fusion), channel_id=1, source_target_pairs={{0,16},{16,0},{32,48},{48,32},{64,80},{80,64},{96,112},{112,96},{1... | collective-permute-start | bytes 393224 | tf_op jit(solution)/shard_map/ppermute | solution.py:43
  125.5 29.5 %copy-start.1 = (bf16[1024,128]{1,0:T(8,128)(2,1)S(1)}, bf16[1024,128]{1,0:T(8,128)(2,1)}, u32[]{:S(2)}) copy-start(bf16[1024,128]{1,0:T(8,128)(2,1)} %tokens_ref.1) | copy-start | bytes 786436
  125.5 5.8 %collective-permute-start.9 = (bf16[8,128,64]{2,1,0:T(8,128)(2,1)S(1)}, bf16[8,128,64]{2,1,0:T(8,128)(2,1)S(1)}, u32[]{:S(2)}, u32[]{:S(2)}) collective-permute-start(bf16[8,128,64]{2,1,0:T(8,128)(2,1)S(1)} %squeeze.12.down_ref), channel_id=1, source_target_pairs={{0,1},{1,0},{2,3},{3,2},{4,5},{5,4},{6,7},{7,6},{8,9},{9,8},{10,11... | collective-permute-start | bytes 393224 | tf_op jit(solution)/shard_map/ppermute | solution.py:35
  133.2 21.9 %copy-start.2 = (bf16[512,128]{1,0:T(8,128)(2,1)S(1)}, bf16[512,128]{1,0:T(8,128)(2,1)}, u32[]{:S(2)}) copy-start(bf16[512,128]{1,0:T(8,128)(2,1)} %get-tuple-element.12.mine_ref) | copy-start | bytes 393220
  133.2 9.9 %all-to-all-start.3 = ((bf16[8,32,128]{2,1,0:T(8,128)(2,1)}), bf16[8,32,128]{2,1,0:T(8,128)(2,1)S(1)}, u32[]{:S(2)}, u32[]{:S(2)}) async-start(bf16[8,32,128]{2,1,0:T(8,128)(2,1)} %get-tuple-element.14), calls=%async_computation.3 | async-start | bytes 131072 | tf_op jit(solution)/shard_map/all_to_all | solution.py:29
  137.9 11.3 %collective-permute-start.10 = (bf16[512,128]{1,0:T(8,128)(2,1)}, bf16[512,128]{1,0:T(8,128)(2,1)S(1)}, u32[]{:S(2)}, u32[]{:S(2)}) collective-permute-start(bf16[512,128]{1,0:T(8,128)(2,1)} %get-tuple-element.13), channel_id=1, source_target_pairs={{0,1},{1,0},{2,3},{3,2},{4,5},{5,4},{6,7},{7,6},{8,9},{9,8},{10,11... | collective-permute-start | bytes 393224 | tf_op jit(solution)/shard_map/ppermute | solution.py:35
  143.7 11.3 %all-to-all-start.4 = ((bf16[16,32,128]{2,1,0:T(8,128)(2,1)}), bf16[16,32,128]{2,1,0:T(8,128)(2,1)S(1)}, u32[]{:S(2)}, u32[]{:S(2)}) async-start(bf16[16,32,128]{2,1,0:T(8,128)(2,1)} %relu_for_everyone.1), calls=%async_computation.4 | async-start | bytes 262144 | tf_op jit(solution)/shard_map/all_to_all | solution.py:29

commit v3 on v2

--- a/solution.py
+++ b/solution.py
@@ -35,16 +35,18 @@
     return lax.ppermute(array, "mp", [(i, i ^ 1) for i in range(MP)])
 
 
-def doubling_gather(shard, axis, size):
+def doubling_gather(shard, axis, size, later):
     index = lax.axis_index(axis)
     held = shard
     bit = size // 2
     while bit:
         theirs = lax.ppermute(held, axis, [(i, i ^ bit) for i in range(size)])
+        if held is shard:
+            theirs, later = lax.optimization_barrier((theirs, later))
         upper = (index & bit) != 0
         held = jnp.stack([jnp.where(upper, theirs, held), jnp.where(upper, held, theirs)])
         bit //= 2
-    return held
+    return held, later
 
 
 def in_vmem(array):
@@ -70,15 +72,20 @@
     )(*scalars, *[place(a) for a in arrays])
 
 
-def spread_body(tokens_ref, given_ref, out_ref, sems):
+def spread_body(tokens_ref, given_ref, out_ref, kept_ref, load_sem, sems):
     me = lax.axis_index("mp") % CORES
+    load = pltpu.make_async_copy(tokens_ref.at[me], kept_ref, load_sem)
+    load.start()
     copies = []
     for i in range(CHIPS):
-        first, second = out_ref.at[CORES * i + me], out_ref.at[CORES * i + 1 - me]
-        copies.append(pltpu.make_async_copy(tokens_ref.at[me], first, sems.at[CORES * i]))
-        copies.append(pltpu.make_async_copy(given_ref, second, sems.at[CORES * i + 1]))
-    for copy in copies:
-        copy.start()
+        second = out_ref.at[CORES * i + 1 - me]
+        copies.append(pltpu.make_async_copy(given_ref, second, sems.at[CHIPS + i]))
+        copies[i].start()
+    load.wait()
+    for i in range(CHIPS):
+        first = out_ref.at[CORES * i + me]
+        copies.append(pltpu.make_async_copy(kept_ref, first, sems.at[i]))
+        copies[CHIPS + i].start()
     for copy in copies:
         copy.wait()
 
@@ -89,7 +96,11 @@
         out_shape=pltpu.HBM((MP, *given.shape), given.dtype),
         in_specs=[pl.BlockSpec(memory_space=pltpu.HBM), whole(given)],
         out_specs=pl.BlockSpec(memory_space=pltpu.HBM),
-        scratch_shapes=[pltpu.SemaphoreType.DMA((MP,))],
+        scratch_shapes=[
+            pltpu.VMEM(given.shape, given.dtype),
+            pltpu.SemaphoreType.DMA(()),
+            pltpu.SemaphoreType.DMA((MP,)),
+        ],
         name="spread",
     )(in_hbm(halves), in_vmem(given))
 
@@ -104,6 +115,7 @@
     wo_own_ref,
     wo_other_ref,
     out_ref,
+    normed_ref,
     wi_ref,
     wo_ref,
     sums_ref,
@@ -126,15 +138,15 @@
         load.start()
     gain = gain_ref[...].astype(jnp.float32)
     tiles = [pl.ds(k * FFN_TILE, FFN_TILE) for k in range(rows // FFN_TILE)]
+    for tile in tiles:
+        wide = jnp.concatenate([x_ref[i, tile] for i in range(MP)], axis=1).astype(jnp.float32)
+        scale = lax.rsqrt(jnp.mean(wide * wide, axis=-1, keepdims=True) + 1e-06)
+        normed_ref[tile] = (wide * scale * gain).astype(jnp.bfloat16)
+    for load in loads[:4]:
+        load.wait()
     stores = []
     for k, tile in enumerate(tiles):
-        wide = jnp.concatenate([x_ref[i, tile] for i in range(MP)], axis=1).astype(jnp.float32)
-        scale = lax.rsqrt(jnp.mean(wide * wide, axis=-1, keepdims=True) + 1e-06)
-        normed = (wide * scale * gain).astype(jnp.bfloat16)
-        if k == 0:
-            for load in loads[:4]:
-                load.wait()
-        both = matmul_nt(normed, wi_ref[...])
+        both = matmul_nt(normed_ref[tile], wi_ref[...])
         act = (jax.nn.gelu(both[:, :hid], approximate=True) * both[:, hid:]).astype(jnp.bfloat16)
         if k == 0:
             for load in loads[4:]:
@@ -160,6 +172,7 @@
         in_specs=[whole(x), whole(gain)] + [hbm] * len(weights),
         out_specs=hbm,
         scratch_shapes=[
+            pltpu.VMEM((rows, features), x.dtype),
             pltpu.VMEM((4 * own, features), x.dtype),
             pltpu.VMEM((2 * own, features), x.dtype),
             pltpu.VMEM((tiles, MP, FFN_TILE, width), x.dtype),
@@ -324,20 +337,22 @@
     )
     hidden = exchange(hidden, "mp")
 
-    sent, hidden = lax.optimization_barrier((spread(halves, given), hidden))
+    sent, hidden, gen_other = lax.optimization_barrier(
+        (spread(halves, given), hidden, swap_cores(gen_down))
+    )
     gathered = exchange(sent, "mp", SAME_CORE)
+
+    hidden = jnp.moveaxis(hidden, 0, 1).reshape(task_count, -1)
+    generators = (gen_down, gen_up, gen_other)
+    made = jnp.stack([matmul(hidden, generator).astype(jnp.bfloat16) for generator in generators])
+    all_tasks, (wi_gate, wi_linear, wo_out) = doubling_gather(
+        made, "dp", DP, (wi_gate, wi_linear, wo_out)
+    )
+    all_tasks = jnp.transpose(all_tasks, (5, 6, 4, 3, 2, 1, 0, 7))
+    down, up, down_other = all_tasks.reshape(len(generators), task_count, width, R)
 
     gate, linear = wi_gate.T, wi_linear.T
     gate_other, linear_other, wo_other = swap_cores(gate), swap_cores(linear), swap_cores(wo_out)
-
-    hidden = jnp.moveaxis(hidden, 0, 1).reshape(task_count, -1)
-    made = jnp.stack(
-        [matmul(hidden, gen_down).astype(jnp.bfloat16), matmul(hidden, gen_up).astype(jnp.bfloat16)]
-    )
-    all_tasks = doubling_gather(made, "dp", DP)
-    all_tasks = jnp.transpose(all_tasks, (5, 6, 4, 3, 2, 1, 0, 7))
-    adapters = all_tasks.reshape(2, task_count, width, R)
-    down, up = adapters[0], adapters[1]
 
     partial = ffn(
         gathered,
@@ -347,7 +362,7 @@
         (wo_out, wo_other),
     )
     parts = exchange(partial, "mp", SAME_CORE)
-    mine, given, squeeze_part = squeeze(task_ids, parts, down, swap_cores(down))
+    mine, given, squeeze_part = squeeze(task_ids, parts, down, down_other)
     theirs = swap_cores(given)
     squeezed = exchange(relu_for_everyone(exchange(squeeze_part, "mp", SAME_CORE)), "mp")
     return expand(task_ids, tokens, mine, theirs, squeezed, up)

time: 157 us -> 130 us (0.83)
  Pallas kernels: 47.2 us -> 16.4 us
    pallas_call x1, Pallas kernels: 33 us -> 2.27 us  [spread(): pl.pallas_call(spread_body, out_shape=pltpu.HBM((MP, *given.shape), given...]
    ppermute x5, waiting for transfers between devices: 15.1 us -> 18.1 us  [doubling_gather(): theirs = lax.ppermute(held, axis, [(i, i ^ bit) for i in range(size)])]
  transfers between devices with their start and end apart: 15 -> 15, of which waited for: 7 -> 6; matrix products, arithmetic and copies ran while one was open for 1% -> 3% of each run, Pallas kernels for 7% -> 10%
where the time goes in v3:
time: 130 us; the launch traced here: 129 us
  starting transfers between devices  72.7 us (56%)
  waiting for transfers between devices  25.5 us (20%)
  Pallas kernels  16.4 us (13%)
  blocking collectives  8.74 us (7%)
  local copies, waits for them, and re-layouts  3.15 us (2%)
  matrix products  1.59 us (1%)
    ppermute x5, starting transfers between devices, doubling_gather(): theirs = lax.ppermute(held, axis, [(i, i ^ bit) for i in range(size)])  31.3 us
    ppermute x6, starting transfers between devices, swap_cores(): return lax.ppermute(array, 'mp', [(i, i ^ 1) for i in range(MP)])  21.8 us
    all_to_all x4, starting transfers between devices, exchange(): lax.all_to_all(pieces, axis, split_axis=0, concat_axis=0, axis_index_grou...  19.5 us
    ppermute x5, waiting for transfers between devices, doubling_gather(): theirs = lax.ppermute(held, axis, [(i, i ^ bit) for i in range(size)])  18.1 us
    pallas_call x1, Pallas kernels, ffn(): pl.pallas_call(ffn_body, out_shape=pltpu.HBM(x.shape, x.dtype), in_specs=...  9.21 us
    all_to_all x1, blocking collectives, exchange(): lax.all_to_all(pieces, axis, split_axis=0, concat_axis=0, axis_index_grou...  8.74 us
    all_to_all x4, waiting for transfers between devices, exchange(): lax.all_to_all(pieces, axis, split_axis=0, concat_axis=0, axis_index_grou...  7.48 us
    pallas_call x3, Pallas kernels, call(): pl.pallas_call(body, out_shape=outs, in_specs=[pl.BlockSpec(memory_space=...  3.16 us
  transfers between devices with their start and end apart: 15, of which 6 were waited for; matrix products, arithmetic and copies ran while one was open for 3% of the time, Pallas kernels for 10%

profile of v3, /device:TPU:1, one launch (start us, length us, event | category | flops | bytes accessed | tf_op | source)
XLA Modules:
  0.0 129.4 jit_solution(8850439608495192510)
XLA Ops:
  0.0 8.9 %collective-permute-start.1 = (bf16[1024,256]{1,0:T(8,128)(2,1)}, bf16[1024,256]{1,0:T(8,128)(2,1)S(1)}, u32[]{:S(2)}, u32[]{:S(2)}) collective-permute-start(bf16[1024,256]{1,0:T(8,128)(2,1)} %param.22), channel_id=1, source_target_pairs={{0,1},{1,0},{2,3},{3,2},{4,5},{5,4},{6,7},{7,6},{8,9},{9,8},{10,11... | collective-permute-start | bytes 1572872 | tf_op jit(solution)/shard_map/ppermute | solution.py:35
  8.9 0.9 dynamic-slice_bitcast_fusion
  9.9 1.9 %collective-permute-start = (bf16[512,128]{1,0:T(8,128)(2,1)S(1)}, bf16[512,128]{1,0:T(8,128)(2,1)S(1)}, u32[]{:S(2)}, u32[]{:S(2)}) collective-permute-start(bf16[512,128]{1,0:T(8,128)(2,1)S(1)} %dynamic-slice_bitcast_fusion), channel_id=1, source_target_pairs={{0,1},{1,0},{2,3},{3,2},{4,5},{5,4},{6,7},{7,6},{8,9},{9,8},{10,11... | collective-permute-start | bytes 393224 | tf_op jit(solution)/shard_map/ppermute | solution.py:35
  12.4 0.9 hidden.1
  13.4 0.1 reshape.19
  13.5 8.7 %all_to_all.25 = bf16[16,2,256]{2,1,0:T(2,128)(2,1)S(1)} all-to-all(bf16[16,2,256]{2,1,0:T(2,128)(2,1)S(1)} %reshape.19), channel_id=1, replica_groups=mesh['dp'=32,'mp'=16] {'mp'}, dimensions={0} | all-to-all | bytes 32768 | tf_op jit(solution)/shard_map/all_to_all | solution.py:29
  22.2 0.1 reshape.20
  22.3 0.0 collective-permute-done.given_ref
  22.3 2.3 %spread.1 = bf16[16,512,128]{2,1,0:T(8,128)(2,1)} custom-call(bf16[2,512,128]{2,1,0:T(8,128)(2,1)} %bitcast.42, bf16[512,128]{1,0:T(8,128)(2,1)S(1)} %collective-permute-done.given_ref), custom_call_target="tpu_custom_call" | custom-call | tf_op jit(solution)/shard_map/spread/pallas_call | solution.py:94
  24.6 0.0 copy-start.4
  24.6 0.8 copy-done.5
  25.4 3.6 %all-to-all-start.1 = ((bf16[16,512,128]{2,1,0:T(8,128)(2,1)}), bf16[16,512,128]{2,1,0:T(8,128)(2,1)S(1)}, u32[]{:S(2)}, u32[]{:S(2)}) async-start(bf16[16,512,128]{2,1,0:T(8,128)(2,1)} %spread.1), calls=%async_computation.1 | async-start | bytes 4194304 | tf_op jit(solution)/shard_map/all_to_all | solution.py:29
  29.0 0.0 copy-start.6
  29.1 0.1 reshape.18
  29.2 0.2 fusion
  29.4 1.2 fusion.2
  30.6 0.2 fusion.1
  30.8 12.8 %collective-permute-start.2 = (bf16[3,8,256]{2,1,0:T(8,128)(2,1)S(1)}, bf16[3,8,256]{2,1,0:T(8,128)(2,1)S(1)}, u32[]{:S(2)}, u32[]{:S(2)}) collective-permute-start(bf16[3,8,256]{2,1,0:T(8,128)(2,1)S(1)} %pad_maximum_fusion.4), channel_id=1, source_target_pairs={{0,256},{16,272},{32,288},{48,304},{64,320},{80,336},{96,352},{112... | collective-permute-start | bytes 36872 | tf_op jit(solution)/shard_map/ppermute | solution.py:43
  43.6 1.1 collective-permute-done.2
  44.7 3.1 %collective-permute-start.3 = (bf16[320,2048]{1,0:T(8,128)(2,1)}, bf16[320,2048]{1,0:T(8,128)(2,1)}, u32[]{:S(2)}, u32[]{:S(2)}) collective-permute-start(bf16[320,2048]{1,0:T(8,128)(2,1)} %bitcast.7.gate_ref), channel_id=1, source_target_pairs={{0,1},{1,0},{2,3},{3,2},{4,5},{5,4},{6,7},{7,6},{8,9},{9,8},{10,11... | collective-permute-start | bytes 3932168 | tf_op jit(solution)/shard_map/ppermute | solution.py:35
  47.8 1.9 %collective-permute-start.4 = (bf16[320,2048]{1,0:T(8,128)(2,1)}, bf16[320,2048]{1,0:T(8,128)(2,1)}, u32[]{:S(2)}, u32[]{:S(2)}) collective-permute-start(bf16[320,2048]{1,0:T(8,128)(2,1)} %bitcast.8.linear_ref), channel_id=1, source_target_pairs={{0,1},{1,0},{2,3},{3,2},{4,5},{5,4},{6,7},{7,6},{8,9},{9,8},{10,11... | collective-permute-start | bytes 3932168 | tf_op jit(solution)/shard_map/ppermute | solution.py:35
  49.7 2.4 %collective-permute-start.5 = (bf16[320,2048]{1,0:T(8,128)(2,1)}, bf16[320,2048]{1,0:T(8,128)(2,1)}, u32[]{:S(2)}, u32[]{:S(2)}) collective-permute-start(bf16[320,2048]{1,0:T(8,128)(2,1)} %wo_own_ref), channel_id=1, source_target_pairs={{0,1},{1,0},{2,3},{3,2},{4,5},{5,4},{6,7},{7,6},{8,9},{9,8},{10,11... | collective-permute-start | bytes 3932168 | tf_op jit(solution)/shard_map/ppermute | solution.py:35
  52.1 5.8 %collective-permute-start.6 = (bf16[2,3,8,256]{3,2,1,0:T(8,128)(2,1)S(1)}, bf16[2,3,8,256]{3,2,1,0:T(8,128)(2,1)S(1)}, u32[]{:S(2)}, u32[]{:S(2)}) collective-permute-start(bf16[2,3,8,256]{3,2,1,0:T(8,128)(2,1)S(1)} %pad_maximum_fusion.3), channel_id=1, source_target_pairs={{0,128},{16,144},{32,160},{48,176},{64,192},{80,208},{96,224},{112... | collective-permute-start | bytes 73736 | tf_op jit(solution)/shard_map/ppermute | solution.py:43
  58.0 9.2 %ffn.1 = bf16[16,512,128]{2,1,0:T(8,128)(2,1)} custom-call(bf16[16,512,128]{2,1,0:T(8,128)(2,1)S(1)} %all-to-all-done.1.x_ref, bf16[1,2048]{1,0:T(2,128)(2,1)S(1)} %reshape.17.gain_ref, bf16[320,2048]{1,0:T(8,128)(2,1)} %bitcast.7.gate_ref, bf16[320,2048]{1,0:T(8,128)(2,1)} %collective-permute-done.3.gate_other_ref, bf16[320,2048]{1,0:T(8,128)(2,1)} %bitcast.8.linear_ref, ...), custom_call_target="tpu_custom_call" | custom-call | tf_op jit(solution)/shard_map/ffn/pallas_call | solution.py:169
  67.2 5.3 %all-to-all-start.2 = ((bf16[16,512,128]{2,1,0:T(8,128)(2,1)}), bf16[16,512,128]{2,1,0:T(8,128)(2,1)S(1)}, u32[]{:S(2)}, u32[]{:S(2)}) async-start(bf16[16,512,128]{2,1,0:T(8,128)(2,1)} %ffn.1), calls=%async_computation.2 | async-start | bytes 4194304 | tf_op jit(solution)/shard_map/all_to_all | solution.py:29
  72.6 4.9 %collective-permute-start.7 = (bf16[2,2,3,8,256]{4,3,2,1,0:T(8,128)(2,1)S(1)}, bf16[2,2,3,8,256]{4,3,2,1,0:T(8,128)(2,1)S(1)}, u32[]{:S(2)}, u32[]{:S(2)}) collective-permute-start(bf16[2,2,3,8,256]{4,3,2,1,0:T(8,128)(2,1)S(1)} %pad_maximum_fusion.2), channel_id=1, source_target_pairs={{0,64},{16,80},{32,96},{48,112},{64,0},{80,16},{96,32},{112,48},{1... | collective-permute-start | bytes 147464 | tf_op jit(solution)/shard_map/ppermute | solution.py:43
  77.5 1.8 %collective-permute-done.7 = bf16[2,2,3,8,256]{4,3,2,1,0:T(8,128)(2,1)S(1)} collective-permute-done((bf16[2,2,3,8,256]{4,3,2,1,0:T(8,128)(2,1)S(1)}, bf16[2,2,3,8,256]{4,3,2,1,0:T(8,128)(2,1)S(1)}, u32[]{:S(2)}, u32[]{:S(2)}) %collective-permute-start.7) | collective-permute-done | bytes 49184 | tf_op jit(solution)/shard_map/ppermute | solution.py:43
  79.3 3.5 %collective-permute-start.8 = (bf16[2,2,2,3,8,256]{5,4,3,2,1,0:T(8,128)(2,1)S(1)}, bf16[2,2,2,3,8,256]{5,4,3,2,1,0:T(8,128)(2,1)S(1)}, u32[]{:S(2)}, u32[]{:S(2)}) collective-permute-start(bf16[2,2,2,3,8,256]{5,4,3,2,1,0:T(8,128)(2,1)S(1)} %pad_maximum_fusion.1), channel_id=1, source_target_pairs={{0,32},{16,48},{32,0},{48,16},{64,96},{80,112},{96,64},{112,80},{1... | collective-permute-start | bytes 294920 | tf_op jit(solution)/shard_map/ppermute | solution.py:43
  82.8 2.3 %collective-permute-done.8 = bf16[2,2,2,3,8,256]{5,4,3,2,1,0:T(8,128)(2,1)S(1)} collective-permute-done((bf16[2,2,2,3,8,256]{5,4,3,2,1,0:T(8,128)(2,1)S(1)}, bf16[2,2,2,3,8,256]{5,4,3,2,1,0:T(8,128)(2,1)S(1)}, u32[]{:S(2)}, u32[]{:S(2)}) %collective-permute-start.8) | collective-permute-done | bytes 98336 | tf_op jit(solution)/shard_map/ppermute | solution.py:43
  85.2 4.4 %collective-permute-start.9 = (bf16[2,2,2,2,3,8,256]{6,5,4,3,2,1,0:T(8,128)(2,1)S(1)}, bf16[2,2,2,2,3,8,256]{6,5,4,3,2,1,0:T(8,128)(2,1)S(1)}, u32[]{:S(2)}, u32[]{:S(2)}) collective-permute-start(bf16[2,2,2,2,3,8,256]{6,5,4,3,2,1,0:T(8,128)(2,1)S(1)} %pad_maximum_fusion), channel_id=1, source_target_pairs={{0,16},{16,0},{32,48},{48,32},{64,80},{80,64},{96,112},{112,96},{1... | collective-permute-start | bytes 589832 | tf_op jit(solution)/shard_map/ppermute | solution.py:43
  89.5 12.9 %collective-permute-done.9 = bf16[2,2,2,2,3,8,256]{6,5,4,3,2,1,0:T(8,128)(2,1)S(1)} collective-permute-done((bf16[2,2,2,2,3,8,256]{6,5,4,3,2,1,0:T(8,128)(2,1)S(1)}, bf16[2,2,2,2,3,8,256]{6,5,4,3,2,1,0:T(8,128)(2,1)S(1)}, u32[]{:S(2)}, u32[]{:S(2)}) %collective-permute-start.9) | collective-permute-done | bytes 196640 | tf_op jit(solution)/shard_map/ppermute | solution.py:43
  102.5 0.0 copy-start.3
  102.6 0.1 copy.17
  102.8 0.2 unstack.19.down_ref
  103.0 0.1 copy.18
  103.1 0.2 unstack.21.other_ref
  103.3 0.0 copy-start.1
  103.4 1.8 %squeeze.6 = (bf16[512,128]{1,0:T(8,128)(2,1)}, bf16[512,128]{1,0:T(8,128)(2,1)}, bf16[8,32,128]{2,1,0:T(8,128)(2,1)}) custom-call(s32[8]{0:T(128)S(1)} %copy-done.3, bf16[16,512,128]{2,1,0:T(8,128)(2,1)S(1)} %all-to-all-done.2.parts_ref, bf16[8,128,64]{2,1,0:T(8,128)(2,1)S(1)} %unstack.19.down_ref, bf16[8,128,64]{2,1,0:T(8,128)(2,1)S(1)} %unstack.21.other_ref), custom_call_target="tpu_custom_call" | custom-call | tf_op jit(solution)/shard_map/squeeze/pallas_call | solution.py:240
  105.2 0.0 copy-start.2
  105.2 4.5 %all-to-all-start.3 = ((bf16[8,32,128]{2,1,0:T(8,128)(2,1)}), bf16[8,32,128]{2,1,0:T(8,128)(2,1)S(1)}, u32[]{:S(2)}, u32[]{:S(2)}) async-start(bf16[8,32,128]{2,1,0:T(8,128)(2,1)} %get-tuple-element.24), calls=%async_computation.3 | async-start | bytes 131072 | tf_op jit(solution)/shard_map/all_to_all | solution.py:29
  109.7 3.6 %collective-permute-start.10 = (bf16[512,128]{1,0:T(8,128)(2,1)}, bf16[512,128]{1,0:T(8,128)(2,1)S(1)}, u32[]{:S(2)}, u32[]{:S(2)}) collective-permute-start(bf16[512,128]{1,0:T(8,128)(2,1)} %get-tuple-element.23), channel_id=1, source_target_pairs={{0,1},{1,0},{2,3},{3,2},{4,5},{5,4},{6,7},{7,6},{8,9},{9,8},{10,11... | collective-permute-start | bytes 393224 | tf_op jit(solution)/shard_map/ppermute | solution.py:35
  113.2 1.6 %all-to-all-done.3.parts_ref = bf16[8,32,128]{2,1,0:T(8,128)(2,1)S(1)} async-done(((bf16[8,32,128]{2,1,0:T(8,128)(2,1)}), bf16[8,32,128]{2,1,0:T(8,128)(2,1)S(1)}, u32[]{:S(2)}, u32[]{:S(2)}) %all-to-all-start.3) | async-done | bytes 65568 | tf_op jit(solution)/shard_map/all_to_all | solution.py:29
  114.9 0.7 relu_for_everyone.1
  115.5 6.1 %all-to-all-start.4 = ((bf16[16,32,128]{2,1,0:T(8,128)(2,1)}), bf16[16,32,128]{2,1,0:T(8,128)(2,1)S(1)}, u32[]{:S(2)}, u32[]{:S(2)}) async-start(bf16[16,32,128]{2,1,0:T(8,128)(2,1)} %relu_for_everyone.1), calls=%async_computation.4 | async-start | bytes 262144 | tf_op jit(solution)/shard_map/all_to_all | solution.py:29
  121.7 0.1 copy.19
  121.8 0.2 unstack.23.up_ref
  122.0 5.9 %all-to-all-done.4.squeezed_ref = bf16[16,32,128]{2,1,0:T(8,128)(2,1)S(1)} async-done(((bf16[16,32,128]{2,1,0:T(8,128)(2,1)}), bf16[16,32,128]{2,1,0:T(8,128)(2,1)S(1)}, u32[]{:S(2)}, u32[]{:S(2)}) %all-to-all-start.4) | async-done | bytes 131104 | tf_op jit(solution)/shard_map/all_to_all | solution.py:29
  127.9 1.6 %expand.1 = bf16[1024,128]{1,0:T(8,128)(2,1)} custom-call(s32[8]{0:T(128)S(1)} %copy-done.3, bf16[1024,128]{1,0:T(8,128)(2,1)S(1)} %copy-done.1, bf16[512,128]{1,0:T(8,128)(2,1)S(1)} %copy-done.2, bf16[512,128]{1,0:T(8,128)(2,1)S(1)} %collective-permute-done.10.theirs_ref, bf16[16,32,128]{2,1,0:T(8,128)(2,1)S(1)} %all-to-all-done.4.squeezed_ref, ...), custom_call_target="tpu_custom_call" | custom-call | tf_op jit(solution)/shard_map/expand/pallas_call | solution.py:65
  (30 shorter events, 0.3 us)
Async XLA Ops:
  0.0 30.6 %copy-start = (bf16[1024,256]{1,0:T(8,128)(2,1)S(1)}, bf16[1024,256]{1,0:T(8,128)(2,1)}, u32[]{:S(2)}) copy-start(bf16[1024,256]{1,0:T(8,128)(2,1)} %param.23) | copy-start | bytes 1572868
  0.0 24.6 %collective-permute-start.1 = (bf16[1024,256]{1,0:T(8,128)(2,1)}, bf16[1024,256]{1,0:T(8,128)(2,1)S(1)}, u32[]{:S(2)}, u32[]{:S(2)}) collective-permute-start(bf16[1024,256]{1,0:T(8,128)(2,1)} %param.22), channel_id=1, source_target_pairs={{0,1},{1,0},{2,3},{3,2},{4,5},{5,4},{6,7},{7,6},{8,9},{9,8},{10,11... | collective-permute-start | bytes 1572872 | tf_op jit(solution)/shard_map/ppermute | solution.py:35
  9.9 12.5 %collective-permute-start = (bf16[512,128]{1,0:T(8,128)(2,1)S(1)}, bf16[512,128]{1,0:T(8,128)(2,1)S(1)}, u32[]{:S(2)}, u32[]{:S(2)}) collective-permute-start(bf16[512,128]{1,0:T(8,128)(2,1)S(1)} %dynamic-slice_bitcast_fusion), channel_id=1, source_target_pairs={{0,1},{1,0},{2,3},{3,2},{4,5},{5,4},{6,7},{7,6},{8,9},{9,8},{10,11... | collective-permute-start | bytes 393224 | tf_op jit(solution)/shard_map/ppermute | solution.py:35
  24.6 4.6 %copy-start.4 = (bf16[1024,256]{1,0:T(8,128)(2,1)S(1)}, bf16[1024,256]{1,0:T(8,128)(2,1)}, u32[]{:S(2)}) copy-start(bf16[1024,256]{1,0:T(8,128)(2,1)} %param.22) | copy-start | bytes 1572868
  24.6 0.8 copy-start.5
  25.4 32.5 %all-to-all-start.1 = ((bf16[16,512,128]{2,1,0:T(8,128)(2,1)}), bf16[16,512,128]{2,1,0:T(8,128)(2,1)S(1)}, u32[]{:S(2)}, u32[]{:S(2)}) async-start(bf16[16,512,128]{2,1,0:T(8,128)(2,1)} %spread.1), calls=%async_computation.1 | async-start | bytes 4194304 | tf_op jit(solution)/shard_map/all_to_all | solution.py:29
  29.0 28.9 %copy-start.6 = (bf16[2048]{0:T(1024)(128)(2,1)S(1)}, bf16[2048]{0:T(1024)(128)(2,1)}, u32[]{:S(2)}) copy-start(bf16[2048]{0:T(1024)(128)(2,1)} %param.13) | copy-start | bytes 12292
  30.8 13.9 %collective-permute-start.2 = (bf16[3,8,256]{2,1,0:T(8,128)(2,1)S(1)}, bf16[3,8,256]{2,1,0:T(8,128)(2,1)S(1)}, u32[]{:S(2)}, u32[]{:S(2)}) collective-permute-start(bf16[3,8,256]{2,1,0:T(8,128)(2,1)S(1)} %pad_maximum_fusion.4), channel_id=1, source_target_pairs={{0,256},{16,272},{32,288},{48,304},{64,320},{80,336},{96,352},{112... | collective-permute-start | bytes 36872 | tf_op jit(solution)/shard_map/ppermute | solution.py:43
  44.7 13.3 %collective-permute-start.3 = (bf16[320,2048]{1,0:T(8,128)(2,1)}, bf16[320,2048]{1,0:T(8,128)(2,1)}, u32[]{:S(2)}, u32[]{:S(2)}) collective-permute-start(bf16[320,2048]{1,0:T(8,128)(2,1)} %bitcast.7.gate_ref), channel_id=1, source_target_pairs={{0,1},{1,0},{2,3},{3,2},{4,5},{5,4},{6,7},{7,6},{8,9},{9,8},{10,11... | collective-permute-start | bytes 3932168 | tf_op jit(solution)/shard_map/ppermute | solution.py:35
  47.8 10.2 %collective-permute-start.4 = (bf16[320,2048]{1,0:T(8,128)(2,1)}, bf16[320,2048]{1,0:T(8,128)(2,1)}, u32[]{:S(2)}, u32[]{:S(2)}) collective-permute-start(bf16[320,2048]{1,0:T(8,128)(2,1)} %bitcast.8.linear_ref), channel_id=1, source_target_pairs={{0,1},{1,0},{2,3},{3,2},{4,5},{5,4},{6,7},{7,6},{8,9},{9,8},{10,11... | collective-permute-start | bytes 3932168 | tf_op jit(solution)/shard_map/ppermute | solution.py:35
  49.7 8.3 %collective-permute-start.5 = (bf16[320,2048]{1,0:T(8,128)(2,1)}, bf16[320,2048]{1,0:T(8,128)(2,1)}, u32[]{:S(2)}, u32[]{:S(2)}) collective-permute-start(bf16[320,2048]{1,0:T(8,128)(2,1)} %wo_own_ref), channel_id=1, source_target_pairs={{0,1},{1,0},{2,3},{3,2},{4,5},{5,4},{6,7},{7,6},{8,9},{9,8},{10,11... | collective-permute-start | bytes 3932168 | tf_op jit(solution)/shard_map/ppermute | solution.py:35
  52.1 20.4 %collective-permute-start.6 = (bf16[2,3,8,256]{3,2,1,0:T(8,128)(2,1)S(1)}, bf16[2,3,8,256]{3,2,1,0:T(8,128)(2,1)S(1)}, u32[]{:S(2)}, u32[]{:S(2)}) collective-permute-start(bf16[2,3,8,256]{3,2,1,0:T(8,128)(2,1)S(1)} %pad_maximum_fusion.3), channel_id=1, source_target_pairs={{0,128},{16,144},{32,160},{48,176},{64,192},{80,208},{96,224},{112... | collective-permute-start | bytes 73736 | tf_op jit(solution)/shard_map/ppermute | solution.py:43
  67.2 36.2 %all-to-all-start.2 = ((bf16[16,512,128]{2,1,0:T(8,128)(2,1)}), bf16[16,512,128]{2,1,0:T(8,128)(2,1)S(1)}, u32[]{:S(2)}, u32[]{:S(2)}) async-start(bf16[16,512,128]{2,1,0:T(8,128)(2,1)} %ffn.1), calls=%async_computation.2 | async-start | bytes 4194304 | tf_op jit(solution)/shard_map/all_to_all | solution.py:29
  72.6 6.7 %collective-permute-start.7 = (bf16[2,2,3,8,256]{4,3,2,1,0:T(8,128)(2,1)S(1)}, bf16[2,2,3,8,256]{4,3,2,1,0:T(8,128)(2,1)S(1)}, u32[]{:S(2)}, u32[]{:S(2)}) collective-permute-start(bf16[2,2,3,8,256]{4,3,2,1,0:T(8,128)(2,1)S(1)} %pad_maximum_fusion.2), channel_id=1, source_target_pairs={{0,64},{16,80},{32,96},{48,112},{64,0},{80,16},{96,32},{112,48},{1... | collective-permute-start | bytes 147464 | tf_op jit(solution)/shard_map/ppermute | solution.py:43
  79.3 5.8 %collective-permute-start.8 = (bf16[2,2,2,3,8,256]{5,4,3,2,1,0:T(8,128)(2,1)S(1)}, bf16[2,2,2,3,8,256]{5,4,3,2,1,0:T(8,128)(2,1)S(1)}, u32[]{:S(2)}, u32[]{:S(2)}) collective-permute-start(bf16[2,2,2,3,8,256]{5,4,3,2,1,0:T(8,128)(2,1)S(1)} %pad_maximum_fusion.1), channel_id=1, source_target_pairs={{0,32},{16,48},{32,0},{48,16},{64,96},{80,112},{96,64},{112,80},{1... | collective-permute-start | bytes 294920 | tf_op jit(solution)/shard_map/ppermute | solution.py:43
  85.2 17.3 %collective-permute-start.9 = (bf16[2,2,2,2,3,8,256]{6,5,4,3,2,1,0:T(8,128)(2,1)S(1)}, bf16[2,2,2,2,3,8,256]{6,5,4,3,2,1,0:T(8,128)(2,1)S(1)}, u32[]{:S(2)}, u32[]{:S(2)}) collective-permute-start(bf16[2,2,2,2,3,8,256]{6,5,4,3,2,1,0:T(8,128)(2,1)S(1)} %pad_maximum_fusion), channel_id=1, source_target_pairs={{0,16},{16,0},{32,48},{48,32},{64,80},{80,64},{96,112},{112,96},{1... | collective-permute-start | bytes 589832 | tf_op jit(solution)/shard_map/ppermute | solution.py:43
  102.5 0.9 copy-start.3
  103.3 24.5 %copy-start.1 = (bf16[1024,128]{1,0:T(8,128)(2,1)S(1)}, bf16[1024,128]{1,0:T(8,128)(2,1)}, u32[]{:S(2)}) copy-start(bf16[1024,128]{1,0:T(8,128)(2,1)} %tokens_ref.1) | copy-start | bytes 786436
  105.2 22.7 %copy-start.2 = (bf16[512,128]{1,0:T(8,128)(2,1)S(1)}, bf16[512,128]{1,0:T(8,128)(2,1)}, u32[]{:S(2)}) copy-start(bf16[512,128]{1,0:T(8,128)(2,1)} %get-tuple-element.22.mine_ref) | copy-start | bytes 393220
  105.2 9.7 %all-to-all-start.3 = ((bf16[8,32,128]{2,1,0:T(8,128)(2,1)}), bf16[8,32,128]{2,1,0:T(8,128)(2,1)S(1)}, u32[]{:S(2)}, u32[]{:S(2)}) async-start(bf16[8,32,128]{2,1,0:T(8,128)(2,1)} %get-tuple-element.24), calls=%async_computation.3 | async-start | bytes 131072 | tf_op jit(solution)/shard_map/all_to_all | solution.py:29
  109.7 12.4 %collective-permute-start.10 = (bf16[512,128]{1,0:T(8,128)(2,1)}, bf16[512,128]{1,0:T(8,128)(2,1)S(1)}, u32[]{:S(2)}, u32[]{:S(2)}) collective-permute-start(bf16[512,128]{1,0:T(8,128)(2,1)} %get-tuple-element.23), channel_id=1, source_target_pairs={{0,1},{1,0},{2,3},{3,2},{4,5},{5,4},{6,7},{7,6},{8,9},{9,8},{10,11... | collective-permute-start | bytes 393224 | tf_op jit(solution)/shard_map/ppermute | solution.py:35
  115.5 12.3 %all-to-all-start.4 = ((bf16[16,32,128]{2,1,0:T(8,128)(2,1)}), bf16[16,32,128]{2,1,0:T(8,128)(2,1)S(1)}, u32[]{:S(2)}, u32[]{:S(2)}) async-start(bf16[16,32,128]{2,1,0:T(8,128)(2,1)} %relu_for_everyone.1), calls=%async_computation.4 | async-start | bytes 262144 | tf_op jit(solution)/shard_map/all_to_all | solution.py:29

commit v4 on v3

--- a/solution.py
+++ b/solution.py
@@ -9,7 +9,6 @@
 CORES = 2
 CHIPS = 8
 MP = CORES * CHIPS
-DP = 32
 SAME_CORE = [[chip * CORES + core for chip in range(CHIPS)] for core in range(CORES)]
 VMEM = 32 * 1024 * 1024
 FFN_TILE = 256
@@ -35,18 +34,15 @@
     return lax.ppermute(array, "mp", [(i, i ^ 1) for i in range(MP)])
 
 
-def doubling_gather(shard, axis, size, later):
+def doubling_gather(shard, axis, bits):
     index = lax.axis_index(axis)
+    size = lax.axis_size(axis)
     held = shard
-    bit = size // 2
-    while bit:
+    for bit in bits:
         theirs = lax.ppermute(held, axis, [(i, i ^ bit) for i in range(size)])
-        if held is shard:
-            theirs, later = lax.optimization_barrier((theirs, later))
         upper = (index & bit) != 0
         held = jnp.stack([jnp.where(upper, theirs, held), jnp.where(upper, held, theirs)])
-        bit //= 2
-    return held, later
+    return held
 
 
 def in_vmem(array):
@@ -123,13 +119,15 @@
     out_sems,
 ):
     rows, width = x_ref.shape[1:]
-    hid = wo_ref.shape[0]
+    hid, features = wo_ref.shape
     own = hid // 2
+    sides = [slice(0, features // 2), slice(features // 2, features)]
     placed = [
-        (gate_ref, wi_ref.at[pl.ds(0, own)]),
-        (gate_other_ref, wi_ref.at[pl.ds(own, own)]),
-        (linear_ref, wi_ref.at[pl.ds(hid, own)]),
-        (linear_other_ref, wi_ref.at[pl.ds(hid + own, own)]),
+        (source.at[:, side], wi_ref.at[pl.ds(i * own, own), side])
+        for side in sides
+        for i, source in enumerate((gate_ref, gate_other_ref, linear_ref, linear_other_ref))
+    ]
+    placed += [
         (wo_own_ref, wo_ref.at[pl.ds(0, own)]),
         (wo_other_ref, wo_ref.at[pl.ds(own, own)]),
     ]
@@ -142,20 +140,31 @@
         wide = jnp.concatenate([x_ref[i, tile] for i in range(MP)], axis=1).astype(jnp.float32)
         scale = lax.rsqrt(jnp.mean(wide * wide, axis=-1, keepdims=True) + 1e-06)
         normed_ref[tile] = (wide * scale * gain).astype(jnp.bfloat16)
-    for load in loads[:4]:
-        load.wait()
     stores = []
     for k, tile in enumerate(tiles):
-        both = matmul_nt(normed_ref[tile], wi_ref[...])
+        if k == 0:
+            for load in loads[:4]:
+                load.wait()
+            both = matmul_nt(normed_ref[tile, sides[0]], wi_ref[:, sides[0]])
+            for load in loads[4:8]:
+                load.wait()
+            both = both + matmul_nt(normed_ref[tile, sides[1]], wi_ref[:, sides[1]])
+        else:
+            both = matmul_nt(normed_ref[tile], wi_ref[...])
         act = (jax.nn.gelu(both[:, :hid], approximate=True) * both[:, hid:]).astype(jnp.bfloat16)
         if k == 0:
-            for load in loads[4:]:
+            for load in loads[8:]:
                 load.wait()
-        sums = matmul(act, wo_ref[...]).astype(jnp.bfloat16)
-        for i in range(MP):
-            sums_ref[k, i] = sums[:, i * width : (i + 1) * width]
-        stores.append(pltpu.make_async_copy(sums_ref.at[k], out_ref.at[:, tile], out_sems.at[k]))
-        stores[k].start()
+        for j, side in enumerate(sides):
+            sums = matmul(act, wo_ref[:, side]).astype(jnp.bfloat16)
+            blocks = slice(j * MP // 2, (j + 1) * MP // 2)
+            for i in range(MP // 2):
+                sums_ref[k, j * MP // 2 + i] = sums[:, i * width : (i + 1) * width]
+            store = pltpu.make_async_copy(
+                sums_ref.at[k, blocks], out_ref.at[blocks, tile], out_sems.at[2 * k + j]
+            )
+            store.start()
+            stores.append(store)
     for store in stores:
         store.wait()
 
@@ -176,8 +185,8 @@
             pltpu.VMEM((4 * own, features), x.dtype),
             pltpu.VMEM((2 * own, features), x.dtype),
             pltpu.VMEM((tiles, MP, FFN_TILE, width), x.dtype),
-            pltpu.SemaphoreType.DMA((len(weights),)),
-            pltpu.SemaphoreType.DMA((tiles,)),
+            pltpu.SemaphoreType.DMA((10,)),
+            pltpu.SemaphoreType.DMA((2 * tiles,)),
         ],
         compiler_params=pltpu.CompilerParams(vmem_limit_bytes=VMEM),
         name="ffn",
@@ -200,12 +209,10 @@
     rows = parts_ref.shape[1]
     seqs = ids_ref.shape[0]
     seq = rows * CORES // seqs
-    quarter = seq // 4
     me = lax.axis_index("mp") % CORES
     for s in range(rows // seq):
         tile = slice(s * seq, (s + 1) * seq)
         task = ids_ref[me * (rows // seq) + s]
-        down, other = down_ref[task], other_ref[task]
         ffout = []
         for core in range(CORES):
             total = parts_ref[core, tile].astype(jnp.float32)
@@ -216,16 +223,12 @@
         given = jnp.where(me == 0, ffout[1], ffout[0]).astype(jnp.bfloat16)
         kept_ref[tile] = kept
         given_ref[tile] = given
-        sums = (matmul(kept, down) + matmul(given, other)).astype(jnp.bfloat16)
-        for i in range(2):
-            first = sums[2 * i * quarter : (2 * i + 1) * quarter]
-            second = sums[(2 * i + 1) * quarter : (2 * i + 2) * quarter]
-            squeezed_ref[2 * s + i] = jnp.concatenate([first, second], axis=1)
-    stores = [
-        pltpu.make_async_copy(squeezed_ref, squeezed_out, sems.at[0]),
-        pltpu.make_async_copy(given_ref, given_out, sems.at[1]),
-        pltpu.make_async_copy(kept_ref, kept_out, sems.at[2]),
-    ]
+        sums = (matmul(kept, down_ref[task]) + matmul(given, other_ref[task])).astype(jnp.bfloat16)
+        packed = slice(s // 2 * seq, (s // 2 + 1) * seq)
+        squeezed_ref[packed, s % 2 * R : (s % 2 + 1) * R] = sums
+    stores = [pltpu.make_async_copy(squeezed_ref, squeezed_out.at[i], sems.at[i]) for i in range(MP)]
+    stores.append(pltpu.make_async_copy(given_ref, given_out, sems.at[MP]))
+    stores.append(pltpu.make_async_copy(kept_ref, kept_out, sems.at[MP + 1]))
     for store in stores:
         store.start()
     for store in stores:
@@ -234,7 +237,7 @@
 
 def squeeze(task_ids, parts, down, other):
     rows, width = parts.shape[1:]
-    share = (CHIPS, rows // CHIPS // 2, 2 * R)
+    packed = (rows // 2, 2 * R)
     arrays = (parts, down, other)
     hbm = pl.BlockSpec(memory_space=pltpu.HBM)
     return pl.pallas_call(
@@ -242,56 +245,45 @@
         out_shape=(
             pltpu.HBM((rows, width), parts.dtype),
             pltpu.HBM((rows, width), parts.dtype),
-            pltpu.HBM(share, parts.dtype),
+            pltpu.HBM((MP, *packed), parts.dtype),
         ),
         in_specs=[pl.BlockSpec(memory_space=pltpu.SMEM)] + [whole(a) for a in arrays],
         out_specs=(hbm, hbm, hbm),
         scratch_shapes=[
             pltpu.VMEM((rows, width), parts.dtype),
             pltpu.VMEM((rows, width), parts.dtype),
-            pltpu.VMEM(share, parts.dtype),
-            pltpu.SemaphoreType.DMA((3,)),
+            pltpu.VMEM(packed, parts.dtype),
+            pltpu.SemaphoreType.DMA((MP + 2,)),
         ],
         compiler_params=pltpu.CompilerParams(vmem_limit_bytes=VMEM),
         name="squeeze",
     )(task_ids, *[in_vmem(a) for a in arrays])
 
 
-def relu_body(parts_ref, out_ref):
-    total = parts_ref[0].astype(jnp.float32)
-    for i in range(1, CHIPS):
-        total = total + parts_ref[i].astype(jnp.float32)
-    squeezed = jnp.maximum(total, 0.0).astype(jnp.bfloat16)
-    for i in range(MP):
-        out_ref[i] = squeezed
-
-
-def relu_for_everyone(parts):
-    return call("relu_for_everyone", relu_body, jax.ShapeDtypeStruct((MP, *parts.shape[1:]), parts.dtype), (parts,))
-
-
-def expand_body(ids_ref, tokens_ref, mine_ref, theirs_ref, squeezed_ref, up_ref, out_ref):
+def expand_body(ids_ref, tokens_ref, mine_ref, theirs_ref, parts_ref, up_ref, out_ref):
     seqs = ids_ref.shape[0]
     seq = tokens_ref.shape[0] // seqs
-    swapped = lax.axis_index("mp") % CORES
+    per_core = seqs // CORES
+    me = lax.axis_index("mp") % CORES
     for core in range(CORES):
-        for j in range(seqs // CORES):
-            s = core * (seqs // CORES) + j
+        total = parts_ref[core].astype(jnp.float32)
+        for i in range(1, CHIPS):
+            total = total + parts_ref[CORES * i + core].astype(jnp.float32)
+        squeezed = jnp.maximum(total, 0.0).astype(jnp.bfloat16)
+        for j in range(per_core):
+            s = core * per_core + j
             tile = slice(s * seq, (s + 1) * seq)
             part = slice(j * seq, (j + 1) * seq)
-            both = [squeezed_ref[CORES * (2 * j + i) + core] for i in range(2)]
-            squeezed = jnp.concatenate(
-                [both[i][:, k * R : (k + 1) * R] for i in range(2) for k in range(2)]
-            )
-            expand = matmul_nt(squeezed, up_ref[ids_ref[s]])
-            ffout = jnp.where(swapped == core, mine_ref[part], theirs_ref[part])
+            left = squeezed[j // 2 * seq : (j // 2 + 1) * seq, j % 2 * R : (j % 2 + 1) * R]
+            expand = matmul_nt(left, up_ref[ids_ref[s]])
+            ffout = jnp.where(me == core, mine_ref[part], theirs_ref[part])
             total = tokens_ref[tile].astype(jnp.float32) + ffout.astype(jnp.float32) + expand
             out_ref[tile] = total.astype(jnp.bfloat16)
 
 
-def expand(task_ids, tokens, mine, theirs, squeezed, up):
+def expand(task_ids, tokens, mine, theirs, parts, up):
     out = jax.ShapeDtypeStruct(tokens.shape, tokens.dtype)
-    return call("expand", expand_body, out, (tokens, mine, theirs, squeezed, up), (task_ids,))
+    return call("expand", expand_body, out, (tokens, mine, theirs, parts, up), (task_ids,))
 
 
 def hidden_body(layer_ref, task_table_ref, layer_table_ref, hyper_in_ref, out_ref):
@@ -326,46 +318,40 @@
     halves = tokens.reshape(CORES, half, width)
     given = swap_cores(lax.dynamic_index_in_dim(halves, 1 - core, 0, keepdims=False))
 
-    share = hyper_in.shape[1]
     hidden = call(
         "hidden",
         hidden_body,
-        jax.ShapeDtypeStruct((MP, task_count, share), jnp.bfloat16),
+        jax.ShapeDtypeStruct((MP, task_count, hyper_in.shape[1]), jnp.bfloat16),
         (task_table, layer_table, hyper_in.T),
         (layer_index,),
         in_hbm,
     )
     hidden = exchange(hidden, "mp")
-
-    sent, hidden, gen_other = lax.optimization_barrier(
-        (spread(halves, given), hidden, swap_cores(gen_down))
+    hidden, sent, gen_given, gate, linear, wo = lax.optimization_barrier(
+        (hidden, spread(halves, given), gen_down, wi_gate.T, wi_linear.T, wo_out)
     )
     gathered = exchange(sent, "mp", SAME_CORE)
 
+    gate_other, linear_other, wo_other = swap_cores(gate), swap_cores(linear), swap_cores(wo)
+
     hidden = jnp.moveaxis(hidden, 0, 1).reshape(task_count, -1)
-    generators = (gen_down, gen_up, gen_other)
+    generators = (gen_down, gen_up, swap_cores(gen_given))
     made = jnp.stack([matmul(hidden, generator).astype(jnp.bfloat16) for generator in generators])
-    all_tasks, (wi_gate, wi_linear, wo_out) = doubling_gather(
-        made, "dp", DP, (wi_gate, wi_linear, wo_out)
-    )
-    all_tasks = jnp.transpose(all_tasks, (5, 6, 4, 3, 2, 1, 0, 7))
+    all_tasks = doubling_gather(made, "dp", (16, 1, 8, 4, 2))
+    all_tasks = jnp.transpose(all_tasks, (5, 6, 4, 2, 1, 0, 3, 7))
     down, up, down_other = all_tasks.reshape(len(generators), task_count, width, R)
-
-    gate, linear = wi_gate.T, wi_linear.T
-    gate_other, linear_other, wo_other = swap_cores(gate), swap_cores(linear), swap_cores(wo_out)
 
     partial = ffn(
         gathered,
         norm_gain.reshape(1, features),
         (gate, gate_other),
         (linear, linear_other),
-        (wo_out, wo_other),
+        (wo, wo_other),
     )
     parts = exchange(partial, "mp", SAME_CORE)
     mine, given, squeeze_part = squeeze(task_ids, parts, down, down_other)
     theirs = swap_cores(given)
-    squeezed = exchange(relu_for_everyone(exchange(squeeze_part, "mp", SAME_CORE)), "mp")
-    return expand(task_ids, tokens, mine, theirs, squeezed, up)
+    return expand(task_ids, tokens, mine, theirs, exchange(squeeze_part, "mp"), up)
 
 
 def solution(mesh):

time: 130 us -> 125 us (0.962)
  starting transfers between devices: 72.7 us -> 64.6 us
  waiting for transfers between devices: 25.5 us -> 30.4 us
    all_to_all x4 -> x3, waiting for transfers between devices: 7.48 us -> 14.7 us  [exchange(): lax.all_to_all(pieces, axis, split_axis=0, concat_axis=0, axis_index_grou...]
    ppermute x5, waiting for transfers between devices: 18.1 us -> 13.5 us  [doubling_gather(): theirs = lax.ppermute(held, axis, [(i, i ^ bit) for i in range(size)])]
    ppermute x5, starting transfers between devices: 31.3 us -> 27.9 us  [doubling_gather(): theirs = lax.ppermute(held, axis, [(i, i ^ bit) for i in range(size)])]
    ppermute x6, starting transfers between devices: 21.8 us -> 19.5 us  [swap_cores(): return lax.ppermute(array, 'mp', [(i, i ^ 1) for i in range(MP)])]
    all_to_all x4 -> x3, starting transfers between devices: 19.5 us -> 17.2 us  [exchange(): lax.all_to_all(pieces, axis, split_axis=0, concat_axis=0, axis_index_grou...]
    ppermute x6, waiting for transfers between devices: 0.02 us -> 2.21 us  [swap_cores(): return lax.ppermute(array, 'mp', [(i, i ^ 1) for i in range(MP)])]
    pallas_call x3 -> x2, Pallas kernels: 3.16 us -> 2.54 us  [call(): pl.pallas_call(body, out_shape=outs, in_specs=[pl.BlockSpec(memory_space=...]
  transfers between devices with their start and end apart: 15 -> 14, of which waited for: 6 -> 8; matrix products, arithmetic and copies ran while one was open for 3% -> 2% of each run, Pallas kernels for 10% -> 8%
where the time goes in v4:
time: 125 us
  starting transfers between devices  64.6 us (52%)
  waiting for transfers between devices  30.4 us (24%)
  Pallas kernels  16.3 us (13%)
  blocking collectives  8.26 us (7%)
  local copies, waits for them, and re-layouts  2.31 us (2%)
  matrix products  1.58 us (1%)
    ppermute x5, starting transfers between devices, doubling_gather(): theirs = lax.ppermute(held, axis, [(i, i ^ bit) for i in range(size)])  27.9 us
    ppermute x6, starting transfers between devices, swap_cores(): return lax.ppermute(array, 'mp', [(i, i ^ 1) for i in range(MP)])  19.5 us
    all_to_all x3, starting transfers between devices, exchange(): lax.all_to_all(pieces, axis, split_axis=0, concat_axis=0, axis_index_grou...  17.2 us
    all_to_all x3, waiting for transfers between devices, exchange(): lax.all_to_all(pieces, axis, split_axis=0, concat_axis=0, axis_index_grou...  14.7 us
    ppermute x5, waiting for transfers between devices, doubling_gather(): theirs = lax.ppermute(held, axis, [(i, i ^ bit) for i in range(size)])  13.5 us
    pallas_call x1, Pallas kernels, ffn(): pl.pallas_call(ffn_body, out_shape=pltpu.HBM(x.shape, x.dtype), in_specs=...  9.27 us
    all_to_all x1, blocking collectives, exchange(): lax.all_to_all(pieces, axis, split_axis=0, concat_axis=0, axis_index_grou...  8.26 us
    pallas_call x2, Pallas kernels, call(): pl.pallas_call(body, out_shape=outs, in_specs=[pl.BlockSpec(memory_space=...  2.54 us
  transfers between devices with their start and end apart: 14, of which 8 were waited for; matrix products, arithmetic and copies ran while one was open for 2% of the time, Pallas kernels for 8%

profile of v4, /device:TPU:1, one launch (start us, length us, event | category | flops | bytes accessed | tf_op | source)
XLA Modules:
  0.0 124.7 jit_solution(5456203398900588400)
XLA Ops:
  0.0 1.0 dynamic-slice_bitcast_fusion
  1.0 8.8 %collective-permute-start = (bf16[512,128]{1,0:T(8,128)(2,1)S(1)}, bf16[512,128]{1,0:T(8,128)(2,1)S(1)}, u32[]{:S(2)}, u32[]{:S(2)}) collective-permute-start(bf16[512,128]{1,0:T(8,128)(2,1)S(1)} %dynamic-slice_bitcast_fusion), channel_id=1, source_target_pairs={{0,1},{1,0},{2,3},{3,2},{4,5},{5,4},{6,7},{7,6},{8,9},{9,8},{10,11... | collective-permute-start | bytes 393224 | tf_op jit(solution)/shard_map/ppermute | solution.py:34
  10.4 0.9 hidden.1
  11.4 0.1 reshape.19
  11.5 8.3 %all_to_all.20 = bf16[16,2,256]{2,1,0:T(2,128)(2,1)S(1)} all-to-all(bf16[16,2,256]{2,1,0:T(2,128)(2,1)S(1)} %reshape.19), channel_id=1, replica_groups=mesh['dp'=32,'mp'=16] {'mp'}, dimensions={0} | all-to-all | bytes 32768 | tf_op jit(solution)/shard_map/all_to_all | solution.py:28
  19.7 0.1 reshape.20
  19.8 2.3 %spread.1 = bf16[16,512,128]{2,1,0:T(8,128)(2,1)} custom-call(bf16[2,512,128]{2,1,0:T(8,128)(2,1)} %bitcast.42, bf16[512,128]{1,0:T(8,128)(2,1)S(1)} %collective-permute-done.given_ref), custom_call_target="tpu_custom_call" | custom-call | tf_op jit(solution)/shard_map/spread/pallas_call | solution.py:90
  22.2 0.0 copy-start.4
  22.2 3.7 %all-to-all-start.1 = ((bf16[16,512,128]{2,1,0:T(8,128)(2,1)}), bf16[16,512,128]{2,1,0:T(8,128)(2,1)S(1)}, u32[]{:S(2)}, u32[]{:S(2)}) async-start(bf16[16,512,128]{2,1,0:T(8,128)(2,1)} %spread.1), calls=%async_computation.1 | async-start | bytes 4194304 | tf_op jit(solution)/shard_map/all_to_all | solution.py:28
  25.9 0.0 copy-start.5
  25.9 2.2 %collective-permute-start.1 = (bf16[320,2048]{1,0:T(8,128)(2,1)}, bf16[320,2048]{1,0:T(8,128)(2,1)}, u32[]{:S(2)}, u32[]{:S(2)}) collective-permute-start(bf16[320,2048]{1,0:T(8,128)(2,1)} %bitcast.43), channel_id=1, source_target_pairs={{0,1},{1,0},{2,3},{3,2},{4,5},{5,4},{6,7},{7,6},{8,9},{9,8},{10,11... | collective-permute-start | bytes 3932168 | tf_op jit(solution)/shard_map/ppermute | solution.py:34
  28.1 2.1 %collective-permute-start.2 = (bf16[320,2048]{1,0:T(8,128)(2,1)}, bf16[320,2048]{1,0:T(8,128)(2,1)}, u32[]{:S(2)}, u32[]{:S(2)}) collective-permute-start(bf16[320,2048]{1,0:T(8,128)(2,1)} %bitcast.45), channel_id=1, source_target_pairs={{0,1},{1,0},{2,3},{3,2},{4,5},{5,4},{6,7},{7,6},{8,9},{9,8},{10,11... | collective-permute-start | bytes 3932168 | tf_op jit(solution)/shard_map/ppermute | solution.py:34
  30.3 2.2 %collective-permute-start.3 = (bf16[320,2048]{1,0:T(8,128)(2,1)}, bf16[320,2048]{1,0:T(8,128)(2,1)}, u32[]{:S(2)}, u32[]{:S(2)}) collective-permute-start(bf16[320,2048]{1,0:T(8,128)(2,1)} %wo_own_ref), channel_id=1, source_target_pairs={{0,1},{1,0},{2,3},{3,2},{4,5},{5,4},{6,7},{7,6},{8,9},{9,8},{10,11... | collective-permute-start | bytes 3932168 | tf_op jit(solution)/shard_map/ppermute | solution.py:34
  32.5 2.1 %collective-permute-start.4 = (bf16[1024,256]{1,0:T(8,128)(2,1)S(1)}, bf16[1024,256]{1,0:T(8,128)(2,1)}, u32[]{:S(2)}, u32[]{:S(2)}) collective-permute-start(bf16[1024,256]{1,0:T(8,128)(2,1)S(1)} %copy-done.4), channel_id=1, source_target_pairs={{0,1},{1,0},{2,3},{3,2},{4,5},{5,4},{6,7},{7,6},{8,9},{9,8},{10,11... | collective-permute-start | bytes 1572872 | tf_op jit(solution)/shard_map/ppermute | solution.py:34
  34.7 0.1 reshape.18
  34.8 0.2 fusion
  34.9 0.2 fusion.1
  35.1 1.3 %collective-permute-done.4 = bf16[1024,256]{1,0:T(8,128)(2,1)} collective-permute-done((bf16[1024,256]{1,0:T(8,128)(2,1)S(1)}, bf16[1024,256]{1,0:T(8,128)(2,1)}, u32[]{:S(2)}, u32[]{:S(2)}) %collective-permute-start.4) | collective-permute-done | bytes 524320 | tf_op jit(solution)/shard_map/ppermute | solution.py:34
  36.4 1.2 fusion.2
  37.7 12.9 %collective-permute-start.5 = (bf16[3,8,256]{2,1,0:T(8,128)(2,1)S(1)}, bf16[3,8,256]{2,1,0:T(8,128)(2,1)S(1)}, u32[]{:S(2)}, u32[]{:S(2)}) collective-permute-start(bf16[3,8,256]{2,1,0:T(8,128)(2,1)S(1)} %pad_maximum_fusion.4), channel_id=1, source_target_pairs={{0,256},{16,272},{32,288},{48,304},{64,320},{80,336},{96,352},{112... | collective-permute-start | bytes 36872 | tf_op jit(solution)/shard_map/ppermute | solution.py:42
  50.6 1.1 collective-permute-done.5
  51.7 4.4 %collective-permute-start.6 = (bf16[2,3,8,256]{3,2,1,0:T(8,128)(2,1)S(1)}, bf16[2,3,8,256]{3,2,1,0:T(8,128)(2,1)S(1)}, u32[]{:S(2)}, u32[]{:S(2)}) collective-permute-start(bf16[2,3,8,256]{3,2,1,0:T(8,128)(2,1)S(1)} %pad_maximum_fusion.3), channel_id=1, source_target_pairs={{0,16},{16,0},{32,48},{48,32},{64,80},{80,64},{96,112},{112,96},{1... | collective-permute-start | bytes 73736 | tf_op jit(solution)/shard_map/ppermute | solution.py:42
  56.1 0.0 collective-permute-done.1.gate_other_ref
  56.1 0.0 collective-permute-done.3.wo_other_ref
  56.1 9.3 %ffn.1 = bf16[16,512,128]{2,1,0:T(8,128)(2,1)} custom-call(bf16[16,512,128]{2,1,0:T(8,128)(2,1)S(1)} %all-to-all-done.1.x_ref, bf16[1,2048]{1,0:T(2,128)(2,1)S(1)} %reshape.17.gain_ref, bf16[320,2048]{1,0:T(8,128)(2,1)} %bitcast.44, bf16[320,2048]{1,0:T(8,128)(2,1)} %collective-permute-done.1.gate_other_ref, bf16[320,2048]{1,0:T(8,128)(2,1)} %bitcast.46, ...), custom_call_target="tpu_custom_call" | custom-call | tf_op jit(solution)/shard_map/ffn/pallas_call | solution.py:178
  65.4 4.9 %all-to-all-start.2 = ((bf16[16,512,128]{2,1,0:T(8,128)(2,1)}), bf16[16,512,128]{2,1,0:T(8,128)(2,1)S(1)}, u32[]{:S(2)}, u32[]{:S(2)}) async-start(bf16[16,512,128]{2,1,0:T(8,128)(2,1)} %ffn.1), calls=%async_computation.2 | async-start | bytes 4194304 | tf_op jit(solution)/shard_map/all_to_all | solution.py:28
  70.3 5.4 %collective-permute-start.7 = (bf16[2,2,3,8,256]{4,3,2,1,0:T(8,128)(2,1)S(1)}, bf16[2,2,3,8,256]{4,3,2,1,0:T(8,128)(2,1)S(1)}, u32[]{:S(2)}, u32[]{:S(2)}) collective-permute-start(bf16[2,2,3,8,256]{4,3,2,1,0:T(8,128)(2,1)S(1)} %pad_maximum_fusion.2), channel_id=1, source_target_pairs={{0,128},{16,144},{32,160},{48,176},{64,192},{80,208},{96,224},{112... | collective-permute-start | bytes 147464 | tf_op jit(solution)/shard_map/ppermute | solution.py:42
  75.7 3.3 %collective-permute-done.7 = bf16[2,2,3,8,256]{4,3,2,1,0:T(8,128)(2,1)S(1)} collective-permute-done((bf16[2,2,3,8,256]{4,3,2,1,0:T(8,128)(2,1)S(1)}, bf16[2,2,3,8,256]{4,3,2,1,0:T(8,128)(2,1)S(1)}, u32[]{:S(2)}, u32[]{:S(2)}) %collective-permute-start.7) | collective-permute-done | bytes 49184 | tf_op jit(solution)/shard_map/ppermute | solution.py:42
  79.1 3.2 %collective-permute-start.8 = (bf16[2,2,2,3,8,256]{5,4,3,2,1,0:T(8,128)(2,1)S(1)}, bf16[2,2,2,3,8,256]{5,4,3,2,1,0:T(8,128)(2,1)S(1)}, u32[]{:S(2)}, u32[]{:S(2)}) collective-permute-start(bf16[2,2,2,3,8,256]{5,4,3,2,1,0:T(8,128)(2,1)S(1)} %pad_maximum_fusion.1), channel_id=1, source_target_pairs={{0,64},{16,80},{32,96},{48,112},{64,0},{80,16},{96,32},{112,48},{1... | collective-permute-start | bytes 294920 | tf_op jit(solution)/shard_map/ppermute | solution.py:42
  82.3 4.4 %collective-permute-done.8 = bf16[2,2,2,3,8,256]{5,4,3,2,1,0:T(8,128)(2,1)S(1)} collective-permute-done((bf16[2,2,2,3,8,256]{5,4,3,2,1,0:T(8,128)(2,1)S(1)}, bf16[2,2,2,3,8,256]{5,4,3,2,1,0:T(8,128)(2,1)S(1)}, u32[]{:S(2)}, u32[]{:S(2)}) %collective-permute-start.8) | collective-permute-done | bytes 98336 | tf_op jit(solution)/shard_map/ppermute | solution.py:42
  86.7 1.9 %collective-permute-start.9 = (bf16[2,2,2,2,3,8,256]{6,5,4,3,2,1,0:T(8,128)(2,1)S(1)}, bf16[2,2,2,2,3,8,256]{6,5,4,3,2,1,0:T(8,128)(2,1)S(1)}, u32[]{:S(2)}, u32[]{:S(2)}) collective-permute-start(bf16[2,2,2,2,3,8,256]{6,5,4,3,2,1,0:T(8,128)(2,1)S(1)} %pad_maximum_fusion), channel_id=1, source_target_pairs={{0,32},{16,48},{32,0},{48,16},{64,96},{80,112},{96,64},{112,80},{1... | collective-permute-start | bytes 589832 | tf_op jit(solution)/shard_map/ppermute | solution.py:42
  88.7 4.8 %collective-permute-done.9 = bf16[2,2,2,2,3,8,256]{6,5,4,3,2,1,0:T(8,128)(2,1)S(1)} collective-permute-done((bf16[2,2,2,2,3,8,256]{6,5,4,3,2,1,0:T(8,128)(2,1)S(1)}, bf16[2,2,2,2,3,8,256]{6,5,4,3,2,1,0:T(8,128)(2,1)S(1)}, u32[]{:S(2)}, u32[]{:S(2)}) %collective-permute-start.9) | collective-permute-done | bytes 196640 | tf_op jit(solution)/shard_map/ppermute | solution.py:42
  93.5 0.0 copy-start.3
  93.6 0.1 copy.17
  93.7 0.2 unstack.19.down_ref
  93.9 0.1 copy.18
  94.0 0.2 unstack.21.other_ref
  94.3 2.1 %all-to-all-done.2.parts_ref = bf16[16,512,128]{2,1,0:T(8,128)(2,1)S(1)} async-done(((bf16[16,512,128]{2,1,0:T(8,128)(2,1)}), bf16[16,512,128]{2,1,0:T(8,128)(2,1)S(1)}, u32[]{:S(2)}, u32[]{:S(2)}) %all-to-all-start.2) | async-done | bytes 2097184 | tf_op jit(solution)/shard_map/all_to_all | solution.py:28
  96.4 2.2 %squeeze.6 = (bf16[512,128]{1,0:T(8,128)(2,1)}, bf16[512,128]{1,0:T(8,128)(2,1)}, bf16[16,256,128]{2,1,0:T(8,128)(2,1)}) custom-call(s32[8]{0:T(128)S(1)} %copy-done.3, bf16[16,512,128]{2,1,0:T(8,128)(2,1)S(1)} %all-to-all-done.2.parts_ref, bf16[8,128,64]{2,1,0:T(8,128)(2,1)S(1)} %unstack.19.down_ref, bf16[8,128,64]{2,1,0:T(8,128)(2,1)S(1)} %unstack.21.other_ref), custom_call_target="tpu_custom_call" | custom-call | tf_op jit(solution)/shard_map/squeeze/pallas_call | solution.py:243
  98.6 0.0 copy-start.1
  98.6 0.0 copy-start.2
  98.6 8.6 %all-to-all-start.3 = ((bf16[16,256,128]{2,1,0:T(8,128)(2,1)}), bf16[16,256,128]{2,1,0:T(8,128)(2,1)S(1)}, u32[]{:S(2)}, u32[]{:S(2)}) async-start(bf16[16,256,128]{2,1,0:T(8,128)(2,1)} %get-tuple-element.22), calls=%async_computation.3 | async-start | bytes 2097152 | tf_op jit(solution)/shard_map/all_to_all | solution.py:28
  107.2 2.0 %collective-permute-start.10 = (bf16[512,128]{1,0:T(8,128)(2,1)S(1)}, bf16[512,128]{1,0:T(8,128)(2,1)S(1)}, u32[]{:S(2)}, u32[]{:S(2)}) collective-permute-start(bf16[512,128]{1,0:T(8,128)(2,1)S(1)} %copy-done.6), channel_id=1, source_target_pairs={{0,1},{1,0},{2,3},{3,2},{4,5},{5,4},{6,7},{7,6},{8,9},{9,8},{10,11... | collective-permute-start | bytes 393224 | tf_op jit(solution)/shard_map/ppermute | solution.py:34
  109.2 0.1 copy.19
  109.4 0.2 unstack.23.up_ref
  109.6 0.9 collective-permute-done.10.theirs_ref
  110.5 12.6 %all-to-all-done.3.parts_ref = bf16[16,256,128]{2,1,0:T(8,128)(2,1)S(1)} async-done(((bf16[16,256,128]{2,1,0:T(8,128)(2,1)}), bf16[16,256,128]{2,1,0:T(8,128)(2,1)S(1)}, u32[]{:S(2)}, u32[]{:S(2)}) %all-to-all-start.3) | async-done | bytes 1048608 | tf_op jit(solution)/shard_map/all_to_all | solution.py:28
  123.1 1.6 %expand.1 = bf16[1024,128]{1,0:T(8,128)(2,1)} custom-call(s32[8]{0:T(128)S(1)} %copy-done.3, bf16[1024,128]{1,0:T(8,128)(2,1)S(1)} %copy-done.1, bf16[512,128]{1,0:T(8,128)(2,1)S(1)} %copy-done.2, bf16[512,128]{1,0:T(8,128)(2,1)S(1)} %collective-permute-done.10.theirs_ref, bf16[16,256,128]{2,1,0:T(8,128)(2,1)S(1)} %all-to-all-done.3.parts_ref, ...), custom_call_target="tpu_custom_call" | custom-call | tf_op jit(solution)/shard_map/expand/pallas_call | solution.py:61
  (27 shorter events, 0.3 us)
Async XLA Ops:
  0.0 34.9 %copy-start = (bf16[1024,256]{1,0:T(8,128)(2,1)S(1)}, bf16[1024,256]{1,0:T(8,128)(2,1)}, u32[]{:S(2)}) copy-start(bf16[1024,256]{1,0:T(8,128)(2,1)} %param.23) | copy-start | bytes 1572868
  1.0 18.8 %collective-permute-start = (bf16[512,128]{1,0:T(8,128)(2,1)S(1)}, bf16[512,128]{1,0:T(8,128)(2,1)S(1)}, u32[]{:S(2)}, u32[]{:S(2)}) collective-permute-start(bf16[512,128]{1,0:T(8,128)(2,1)S(1)} %dynamic-slice_bitcast_fusion), channel_id=1, source_target_pairs={{0,1},{1,0},{2,3},{3,2},{4,5},{5,4},{6,7},{7,6},{8,9},{9,8},{10,11... | collective-permute-start | bytes 393224 | tf_op jit(solution)/shard_map/ppermute | solution.py:34
  22.2 10.3 %copy-start.4 = (bf16[1024,256]{1,0:T(8,128)(2,1)S(1)}, bf16[1024,256]{1,0:T(8,128)(2,1)}, u32[]{:S(2)}) copy-start(bf16[1024,256]{1,0:T(8,128)(2,1)} %param.22) | copy-start | bytes 1572868
  22.2 33.9 %all-to-all-start.1 = ((bf16[16,512,128]{2,1,0:T(8,128)(2,1)}), bf16[16,512,128]{2,1,0:T(8,128)(2,1)S(1)}, u32[]{:S(2)}, u32[]{:S(2)}) async-start(bf16[16,512,128]{2,1,0:T(8,128)(2,1)} %spread.1), calls=%async_computation.1 | async-start | bytes 4194304 | tf_op jit(solution)/shard_map/all_to_all | solution.py:28
  25.9 30.1 %copy-start.5 = (bf16[2048]{0:T(1024)(128)(2,1)S(1)}, bf16[2048]{0:T(1024)(128)(2,1)}, u32[]{:S(2)}) copy-start(bf16[2048]{0:T(1024)(128)(2,1)} %param.13) | copy-start | bytes 12292
  25.9 30.1 %collective-permute-start.1 = (bf16[320,2048]{1,0:T(8,128)(2,1)}, bf16[320,2048]{1,0:T(8,128)(2,1)}, u32[]{:S(2)}, u32[]{:S(2)}) collective-permute-start(bf16[320,2048]{1,0:T(8,128)(2,1)} %bitcast.43), channel_id=1, source_target_pairs={{0,1},{1,0},{2,3},{3,2},{4,5},{5,4},{6,7},{7,6},{8,9},{9,8},{10,11... | collective-permute-start | bytes 3932168 | tf_op jit(solution)/shard_map/ppermute | solution.py:34
  28.1 27.9 %collective-permute-start.2 = (bf16[320,2048]{1,0:T(8,128)(2,1)}, bf16[320,2048]{1,0:T(8,128)(2,1)}, u32[]{:S(2)}, u32[]{:S(2)}) collective-permute-start(bf16[320,2048]{1,0:T(8,128)(2,1)} %bitcast.45), channel_id=1, source_target_pairs={{0,1},{1,0},{2,3},{3,2},{4,5},{5,4},{6,7},{7,6},{8,9},{9,8},{10,11... | collective-permute-start | bytes 3932168 | tf_op jit(solution)/shard_map/ppermute | solution.py:34
  30.3 25.8 %collective-permute-start.3 = (bf16[320,2048]{1,0:T(8,128)(2,1)}, bf16[320,2048]{1,0:T(8,128)(2,1)}, u32[]{:S(2)}, u32[]{:S(2)}) collective-permute-start(bf16[320,2048]{1,0:T(8,128)(2,1)} %wo_own_ref), channel_id=1, source_target_pairs={{0,1},{1,0},{2,3},{3,2},{4,5},{5,4},{6,7},{7,6},{8,9},{9,8},{10,11... | collective-permute-start | bytes 3932168 | tf_op jit(solution)/shard_map/ppermute | solution.py:34
  32.5 3.9 %collective-permute-start.4 = (bf16[1024,256]{1,0:T(8,128)(2,1)S(1)}, bf16[1024,256]{1,0:T(8,128)(2,1)}, u32[]{:S(2)}, u32[]{:S(2)}) collective-permute-start(bf16[1024,256]{1,0:T(8,128)(2,1)S(1)} %copy-done.4), channel_id=1, source_target_pairs={{0,1},{1,0},{2,3},{3,2},{4,5},{5,4},{6,7},{7,6},{8,9},{9,8},{10,11... | collective-permute-start | bytes 1572872 | tf_op jit(solution)/shard_map/ppermute | solution.py:34
  37.7 14.0 %collective-permute-start.5 = (bf16[3,8,256]{2,1,0:T(8,128)(2,1)S(1)}, bf16[3,8,256]{2,1,0:T(8,128)(2,1)S(1)}, u32[]{:S(2)}, u32[]{:S(2)}) collective-permute-start(bf16[3,8,256]{2,1,0:T(8,128)(2,1)S(1)} %pad_maximum_fusion.4), channel_id=1, source_target_pairs={{0,256},{16,272},{32,288},{48,304},{64,320},{80,336},{96,352},{112... | collective-permute-start | bytes 36872 | tf_op jit(solution)/shard_map/ppermute | solution.py:42
  51.7 18.6 %collective-permute-start.6 = (bf16[2,3,8,256]{3,2,1,0:T(8,128)(2,1)S(1)}, bf16[2,3,8,256]{3,2,1,0:T(8,128)(2,1)S(1)}, u32[]{:S(2)}, u32[]{:S(2)}) collective-permute-start(bf16[2,3,8,256]{3,2,1,0:T(8,128)(2,1)S(1)} %pad_maximum_fusion.3), channel_id=1, source_target_pairs={{0,16},{16,0},{32,48},{48,32},{64,80},{80,64},{96,112},{112,96},{1... | collective-permute-start | bytes 73736 | tf_op jit(solution)/shard_map/ppermute | solution.py:42
  65.4 31.0 %all-to-all-start.2 = ((bf16[16,512,128]{2,1,0:T(8,128)(2,1)}), bf16[16,512,128]{2,1,0:T(8,128)(2,1)S(1)}, u32[]{:S(2)}, u32[]{:S(2)}) async-start(bf16[16,512,128]{2,1,0:T(8,128)(2,1)} %ffn.1), calls=%async_computation.2 | async-start | bytes 4194304 | tf_op jit(solution)/shard_map/all_to_all | solution.py:28
  70.3 8.8 %collective-permute-start.7 = (bf16[2,2,3,8,256]{4,3,2,1,0:T(8,128)(2,1)S(1)}, bf16[2,2,3,8,256]{4,3,2,1,0:T(8,128)(2,1)S(1)}, u32[]{:S(2)}, u32[]{:S(2)}) collective-permute-start(bf16[2,2,3,8,256]{4,3,2,1,0:T(8,128)(2,1)S(1)} %pad_maximum_fusion.2), channel_id=1, source_target_pairs={{0,128},{16,144},{32,160},{48,176},{64,192},{80,208},{96,224},{112... | collective-permute-start | bytes 147464 | tf_op jit(solution)/shard_map/ppermute | solution.py:42
  79.1 7.6 %collective-permute-start.8 = (bf16[2,2,2,3,8,256]{5,4,3,2,1,0:T(8,128)(2,1)S(1)}, bf16[2,2,2,3,8,256]{5,4,3,2,1,0:T(8,128)(2,1)S(1)}, u32[]{:S(2)}, u32[]{:S(2)}) collective-permute-start(bf16[2,2,2,3,8,256]{5,4,3,2,1,0:T(8,128)(2,1)S(1)} %pad_maximum_fusion.1), channel_id=1, source_target_pairs={{0,64},{16,80},{32,96},{48,112},{64,0},{80,16},{96,32},{112,48},{1... | collective-permute-start | bytes 294920 | tf_op jit(solution)/shard_map/ppermute | solution.py:42
  86.7 6.7 %collective-permute-start.9 = (bf16[2,2,2,2,3,8,256]{6,5,4,3,2,1,0:T(8,128)(2,1)S(1)}, bf16[2,2,2,2,3,8,256]{6,5,4,3,2,1,0:T(8,128)(2,1)S(1)}, u32[]{:S(2)}, u32[]{:S(2)}) collective-permute-start(bf16[2,2,2,2,3,8,256]{6,5,4,3,2,1,0:T(8,128)(2,1)S(1)} %pad_maximum_fusion), channel_id=1, source_target_pairs={{0,32},{16,48},{32,0},{48,16},{64,96},{80,112},{96,64},{112,80},{1... | collective-permute-start | bytes 589832 | tf_op jit(solution)/shard_map/ppermute | solution.py:42
  93.5 2.9 %copy-start.3 = (s32[8]{0:T(128)S(1)}, s32[8]{0:T(128)}, u32[]{:S(2)}) copy-start(s32[8]{0:T(128)} %ids_ref.3) | copy-start | bytes 100
  98.6 8.7 %copy-start.6 = (bf16[512,128]{1,0:T(8,128)(2,1)S(1)}, bf16[512,128]{1,0:T(8,128)(2,1)}, u32[]{:S(2)}) copy-start(bf16[512,128]{1,0:T(8,128)(2,1)} %get-tuple-element.21) | copy-start | bytes 393220
  98.6 24.5 %copy-start.1 = (bf16[1024,128]{1,0:T(8,128)(2,1)S(1)}, bf16[1024,128]{1,0:T(8,128)(2,1)}, u32[]{:S(2)}) copy-start(bf16[1024,128]{1,0:T(8,128)(2,1)} %tokens_ref.1) | copy-start | bytes 786436
  98.6 24.5 %copy-start.2 = (bf16[512,128]{1,0:T(8,128)(2,1)S(1)}, bf16[512,128]{1,0:T(8,128)(2,1)}, u32[]{:S(2)}) copy-start(bf16[512,128]{1,0:T(8,128)(2,1)} %get-tuple-element.20.mine_ref) | copy-start | bytes 393220
  98.6 24.5 %all-to-all-start.3 = ((bf16[16,256,128]{2,1,0:T(8,128)(2,1)}), bf16[16,256,128]{2,1,0:T(8,128)(2,1)S(1)}, u32[]{:S(2)}, u32[]{:S(2)}) async-start(bf16[16,256,128]{2,1,0:T(8,128)(2,1)} %get-tuple-element.22), calls=%async_computation.3 | async-start | bytes 2097152 | tf_op jit(solution)/shard_map/all_to_all | solution.py:28
  107.2 3.2 %collective-permute-start.10 = (bf16[512,128]{1,0:T(8,128)(2,1)S(1)}, bf16[512,128]{1,0:T(8,128)(2,1)S(1)}, u32[]{:S(2)}, u32[]{:S(2)}) collective-permute-start(bf16[512,128]{1,0:T(8,128)(2,1)S(1)} %copy-done.6), channel_id=1, source_target_pairs={{0,1},{1,0},{2,3},{3,2},{4,5},{5,4},{6,7},{7,6},{8,9},{9,8},{10,11... | collective-permute-start | bytes 393224 | tf_op jit(solution)/shard_map/ppermute | solution.py:34

commit v5 on v4

--- a/solution.py
+++ b/solution.py
@@ -226,9 +226,9 @@
         sums = (matmul(kept, down_ref[task]) + matmul(given, other_ref[task])).astype(jnp.bfloat16)
         packed = slice(s // 2 * seq, (s // 2 + 1) * seq)
         squeezed_ref[packed, s % 2 * R : (s % 2 + 1) * R] = sums
-    stores = [pltpu.make_async_copy(squeezed_ref, squeezed_out.at[i], sems.at[i]) for i in range(MP)]
-    stores.append(pltpu.make_async_copy(given_ref, given_out, sems.at[MP]))
-    stores.append(pltpu.make_async_copy(kept_ref, kept_out, sems.at[MP + 1]))
+    stores = [pltpu.make_async_copy(squeezed_ref, squeezed_out.at[i], sems.at[i]) for i in range(CHIPS)]
+    stores.append(pltpu.make_async_copy(given_ref, given_out, sems.at[CHIPS]))
+    stores.append(pltpu.make_async_copy(kept_ref, kept_out, sems.at[CHIPS + 1]))
     for store in stores:
         store.start()
     for store in stores:
@@ -245,7 +245,7 @@
         out_shape=(
             pltpu.HBM((rows, width), parts.dtype),
             pltpu.HBM((rows, width), parts.dtype),
-            pltpu.HBM((MP, *packed), parts.dtype),
+            pltpu.HBM((CHIPS, *packed), parts.dtype),
         ),
         in_specs=[pl.BlockSpec(memory_space=pltpu.SMEM)] + [whole(a) for a in arrays],
         out_specs=(hbm, hbm, hbm),
@@ -253,23 +253,34 @@
             pltpu.VMEM((rows, width), parts.dtype),
             pltpu.VMEM((rows, width), parts.dtype),
             pltpu.VMEM(packed, parts.dtype),
-            pltpu.SemaphoreType.DMA((MP + 2,)),
+            pltpu.SemaphoreType.DMA((CHIPS + 2,)),
         ],
         compiler_params=pltpu.CompilerParams(vmem_limit_bytes=VMEM),
         name="squeeze",
     )(task_ids, *[in_vmem(a) for a in arrays])
 
 
-def expand_body(ids_ref, tokens_ref, mine_ref, theirs_ref, parts_ref, up_ref, out_ref):
+def relu_body(parts_ref, out_ref):
+    total = parts_ref[0].astype(jnp.float32)
+    for i in range(1, CHIPS):
+        total = total + parts_ref[i].astype(jnp.float32)
+    out_ref[...] = jnp.maximum(total, 0.0).astype(jnp.bfloat16)
+
+
+def relu_sum(parts):
+    out = jax.ShapeDtypeStruct(parts.shape[1:], parts.dtype)
+    return call("relu_sum", relu_body, out, (parts,))
+
+
+def expand_body(
+    ids_ref, tokens_ref, mine_ref, theirs_ref, squeezed_ref, their_squeezed_ref, up_ref, out_ref
+):
     seqs = ids_ref.shape[0]
     seq = tokens_ref.shape[0] // seqs
     per_core = seqs // CORES
     me = lax.axis_index("mp") % CORES
     for core in range(CORES):
-        total = parts_ref[core].astype(jnp.float32)
-        for i in range(1, CHIPS):
-            total = total + parts_ref[CORES * i + core].astype(jnp.float32)
-        squeezed = jnp.maximum(total, 0.0).astype(jnp.bfloat16)
+        squeezed = jnp.where(me == core, squeezed_ref[...], their_squeezed_ref[...])
         for j in range(per_core):
             s = core * per_core + j
             tile = slice(s * seq, (s + 1) * seq)
@@ -281,9 +292,10 @@
             out_ref[tile] = total.astype(jnp.bfloat16)
 
 
-def expand(task_ids, tokens, mine, theirs, parts, up):
+def expand(task_ids, tokens, mine, theirs, squeezed, their_squeezed, up):
     out = jax.ShapeDtypeStruct(tokens.shape, tokens.dtype)
-    return call("expand", expand_body, out, (tokens, mine, theirs, parts, up), (task_ids,))
+    arrays = (tokens, mine, theirs, squeezed, their_squeezed, up)
+    return call("expand", expand_body, out, arrays, (task_ids,))
 
 
 def hidden_body(layer_ref, task_table_ref, layer_table_ref, hyper_in_ref, out_ref):
@@ -326,16 +338,18 @@
         (layer_index,),
         in_hbm,
     )
+
+    hidden, gate, linear, wo, gen_down = lax.optimization_barrier(
+        (hidden, wi_gate.T, wi_linear.T, wo_out, gen_down)
+    )
     hidden = exchange(hidden, "mp")
-    hidden, sent, gen_given, gate, linear, wo = lax.optimization_barrier(
-        (hidden, spread(halves, given), gen_down, wi_gate.T, wi_linear.T, wo_out)
-    )
+    others = [swap_cores(w) for w in (gate, linear, wo, gen_down)]
+    hidden, sent, others = lax.optimization_barrier((hidden, spread(halves, given), others))
+    gate_other, linear_other, wo_other, gen_other = others
     gathered = exchange(sent, "mp", SAME_CORE)
 
-    gate_other, linear_other, wo_other = swap_cores(gate), swap_cores(linear), swap_cores(wo)
-
     hidden = jnp.moveaxis(hidden, 0, 1).reshape(task_count, -1)
-    generators = (gen_down, gen_up, swap_cores(gen_given))
+    generators = (gen_down, gen_up, gen_other)
     made = jnp.stack([matmul(hidden, generator).astype(jnp.bfloat16) for generator in generators])
     all_tasks = doubling_gather(made, "dp", (16, 1, 8, 4, 2))
     all_tasks = jnp.transpose(all_tasks, (5, 6, 4, 2, 1, 0, 3, 7))
@@ -351,7 +365,8 @@
     parts = exchange(partial, "mp", SAME_CORE)
     mine, given, squeeze_part = squeeze(task_ids, parts, down, down_other)
     theirs = swap_cores(given)
-    return expand(task_ids, tokens, mine, theirs, exchange(squeeze_part, "mp"), up)
+    squeezed = relu_sum(exchange(squeeze_part, "mp", SAME_CORE))
+    return expand(task_ids, tokens, mine, theirs, squeezed, swap_cores(squeezed), up)
 
 
 def solution(mesh):

time: 125 us -> 125 us (level)
  waiting for transfers between devices: 30.4 us -> 16.5 us
  starting transfers between devices: 64.6 us -> 75.8 us
  local copies, waits for them, and re-layouts: 2.31 us -> 3.7 us
    ppermute x6 -> x7, starting transfers between devices: 19.5 us -> 31.4 us  [swap_cores(): return lax.ppermute(array, 'mp', [(i, i ^ 1) for i in range(MP)])]
    all_to_all x3, waiting for transfers between devices: 14.7 us -> 6.25 us  [exchange(): lax.all_to_all(pieces, axis, split_axis=0, concat_axis=0, axis_index_grou...]
    all_to_all x3, starting transfers between devices: 17.2 us -> 11.1 us  [exchange(): lax.all_to_all(pieces, axis, split_axis=0, concat_axis=0, axis_index_grou...]
    ppermute x5, starting transfers between devices: 27.9 us -> 33.3 us  [doubling_gather(): theirs = lax.ppermute(held, axis, [(i, i ^ bit) for i in range(size)])]
    ppermute x5, waiting for transfers between devices: 13.5 us -> 9.72 us  [doubling_gather(): theirs = lax.ppermute(held, axis, [(i, i ^ bit) for i in range(size)])]
    ppermute x6 -> x7, waiting for transfers between devices: 2.21 us -> 0.55 us  [swap_cores(): return lax.ppermute(array, 'mp', [(i, i ^ 1) for i in range(MP)])]
    unnamed x15, local copies, waits for them, and re-layouts: 0.14 us -> 1.59 us
    pallas_call x2 -> x3, Pallas kernels: 2.54 us -> 2.58 us  [call(): pl.pallas_call(body, out_shape=outs, in_specs=[pl.BlockSpec(memory_space=...]
  transfers between devices with their start and end apart: 14 -> 15, of which waited for: 8 -> 8; matrix products, arithmetic and copies ran while one was open for 2% -> 4% of each run, Pallas kernels for 8% -> 9%
where the time goes in v5:
time: 125 us; the launch traced here: 124 us
  starting transfers between devices  75.8 us (61%)
  waiting for transfers between devices  16.5 us (13%)
  Pallas kernels  16 us (13%)
  blocking collectives  8.25 us (7%)
  local copies, waits for them, and re-layouts  3.7 us (3%)
  matrix products  2.63 us (2%)
    ppermute x5, starting transfers between devices, doubling_gather(): theirs = lax.ppermute(held, axis, [(i, i ^ bit) for i in range(size)])  33.3 us
    ppermute x7, starting transfers between devices, swap_cores(): return lax.ppermute(array, 'mp', [(i, i ^ 1) for i in range(MP)])  31.4 us
    all_to_all x3, starting transfers between devices, exchange(): lax.all_to_all(pieces, axis, split_axis=0, concat_axis=0, axis_index_grou...  11.1 us
    ppermute x5, waiting for transfers between devices, doubling_gather(): theirs = lax.ppermute(held, axis, [(i, i ^ bit) for i in range(size)])  9.72 us
    pallas_call x1, Pallas kernels, ffn(): pl.pallas_call(ffn_body, out_shape=pltpu.HBM(x.shape, x.dtype), in_specs=...  9.25 us
    all_to_all x1, blocking collectives, exchange(): lax.all_to_all(pieces, axis, split_axis=0, concat_axis=0, axis_index_grou...  8.25 us
    all_to_all x3, waiting for transfers between devices, exchange(): lax.all_to_all(pieces, axis, split_axis=0, concat_axis=0, axis_index_grou...  6.25 us
    dot_general x3, matrix products, matmul(): return jnp.dot(left, right, preferred_element_type=jnp.float32)  2.63 us
  transfers between devices with their start and end apart: 15, of which 8 were waited for; matrix products, arithmetic and copies ran while one was open for 4% of the time, Pallas kernels for 9%

profile of v5, /device:TPU:1, one launch (start us, length us, event | category | flops | bytes accessed | tf_op | source)
XLA Modules:
  0.0 124.2 jit_solution(17974919338518635883)
XLA Ops:
  0.7 0.9 hidden.1
  1.6 8.8 %collective-permute-start.1 = (bf16[320,2048]{1,0:T(8,128)(2,1)}, bf16[320,2048]{1,0:T(8,128)(2,1)S(1)}, u32[]{:S(2)}, u32[]{:S(2)}) collective-permute-start(bf16[320,2048]{1,0:T(8,128)(2,1)} %bitcast.43), channel_id=1, source_target_pairs={{0,1},{1,0},{2,3},{3,2},{4,5},{5,4},{6,7},{7,6},{8,9},{9,8},{10,11... | collective-permute-start | bytes 3932168 | tf_op jit(solution)/shard_map/ppermute | solution.py:34
  10.4 1.9 %collective-permute-start.2 = (bf16[320,2048]{1,0:T(8,128)(2,1)}, bf16[320,2048]{1,0:T(8,128)(2,1)S(1)}, u32[]{:S(2)}, u32[]{:S(2)}) collective-permute-start(bf16[320,2048]{1,0:T(8,128)(2,1)} %bitcast.45), channel_id=1, source_target_pairs={{0,1},{1,0},{2,3},{3,2},{4,5},{5,4},{6,7},{7,6},{8,9},{9,8},{10,11... | collective-permute-start | bytes 3932168 | tf_op jit(solution)/shard_map/ppermute | solution.py:34
  12.4 2.4 %collective-permute-start.3 = (bf16[320,2048]{1,0:T(8,128)(2,1)}, bf16[320,2048]{1,0:T(8,128)(2,1)}, u32[]{:S(2)}, u32[]{:S(2)}) collective-permute-start(bf16[320,2048]{1,0:T(8,128)(2,1)} %wo_own_ref), channel_id=1, source_target_pairs={{0,1},{1,0},{2,3},{3,2},{4,5},{5,4},{6,7},{7,6},{8,9},{9,8},{10,11... | collective-permute-start | bytes 3932168 | tf_op jit(solution)/shard_map/ppermute | solution.py:34
  14.8 1.9 %collective-permute-start.4 = (bf16[1024,256]{1,0:T(8,128)(2,1)}, bf16[1024,256]{1,0:T(8,128)(2,1)}, u32[]{:S(2)}, u32[]{:S(2)}) collective-permute-start(bf16[1024,256]{1,0:T(8,128)(2,1)} %param.22), channel_id=1, source_target_pairs={{0,1},{1,0},{2,3},{3,2},{4,5},{5,4},{6,7},{7,6},{8,9},{9,8},{10,11... | collective-permute-start | bytes 1572872 | tf_op jit(solution)/shard_map/ppermute | solution.py:34
  16.7 0.9 dynamic-slice_bitcast_fusion
  17.7 2.4 %collective-permute-start = (bf16[512,128]{1,0:T(8,128)(2,1)S(1)}, bf16[512,128]{1,0:T(8,128)(2,1)S(1)}, u32[]{:S(2)}, u32[]{:S(2)}) collective-permute-start(bf16[512,128]{1,0:T(8,128)(2,1)S(1)} %dynamic-slice_bitcast_fusion), channel_id=1, source_target_pairs={{0,1},{1,0},{2,3},{3,2},{4,5},{5,4},{6,7},{7,6},{8,9},{9,8},{10,11... | collective-permute-start | bytes 393224 | tf_op jit(solution)/shard_map/ppermute | solution.py:34
  20.1 0.1 reshape.19
  20.2 8.3 %all_to_all.20 = bf16[16,2,256]{2,1,0:T(2,128)(2,1)S(1)} all-to-all(bf16[16,2,256]{2,1,0:T(2,128)(2,1)S(1)} %reshape.19), channel_id=1, replica_groups=mesh['dp'=32,'mp'=16] {'mp'}, dimensions={0} | all-to-all | bytes 32768 | tf_op jit(solution)/shard_map/all_to_all | solution.py:28
  28.4 0.1 reshape.20
  28.5 2.3 %spread.1 = bf16[16,512,128]{2,1,0:T(8,128)(2,1)} custom-call(bf16[2,512,128]{2,1,0:T(8,128)(2,1)} %bitcast.42, bf16[512,128]{1,0:T(8,128)(2,1)S(1)} %collective-permute-done.given_ref), custom_call_target="tpu_custom_call" | custom-call | tf_op jit(solution)/shard_map/spread/pallas_call | solution.py:90
  30.9 1.0 copy-done.4
  31.9 0.4 copy-done.5
  32.4 3.6 %all-to-all-start.1 = ((bf16[16,512,128]{2,1,0:T(8,128)(2,1)}), bf16[16,512,128]{2,1,0:T(8,128)(2,1)S(1)}, u32[]{:S(2)}, u32[]{:S(2)}) async-start(bf16[16,512,128]{2,1,0:T(8,128)(2,1)} %spread.1), calls=%async_computation.1 | async-start | bytes 4194304 | tf_op jit(solution)/shard_map/all_to_all | solution.py:28
  36.0 0.0 copy-start.6
  36.0 0.1 reshape.18
  36.1 1.2 fusion
  37.3 1.2 fusion.2
  38.5 0.2 fusion.1
  38.7 12.9 %collective-permute-start.5 = (bf16[3,8,256]{2,1,0:T(8,128)(2,1)S(1)}, bf16[3,8,256]{2,1,0:T(8,128)(2,1)S(1)}, u32[]{:S(2)}, u32[]{:S(2)}) collective-permute-start(bf16[3,8,256]{2,1,0:T(8,128)(2,1)S(1)} %pad_maximum_fusion.4), channel_id=1, source_target_pairs={{0,256},{16,272},{32,288},{48,304},{64,320},{80,336},{96,352},{112... | collective-permute-start | bytes 36872 | tf_op jit(solution)/shard_map/ppermute | solution.py:42
  51.7 1.1 collective-permute-done.5
  52.7 4.4 %collective-permute-start.6 = (bf16[2,3,8,256]{3,2,1,0:T(8,128)(2,1)S(1)}, bf16[2,3,8,256]{3,2,1,0:T(8,128)(2,1)S(1)}, u32[]{:S(2)}, u32[]{:S(2)}) collective-permute-start(bf16[2,3,8,256]{3,2,1,0:T(8,128)(2,1)S(1)} %pad_maximum_fusion.3), channel_id=1, source_target_pairs={{0,16},{16,0},{32,48},{48,32},{64,80},{80,64},{96,112},{112,96},{1... | collective-permute-start | bytes 73736 | tf_op jit(solution)/shard_map/ppermute | solution.py:42
  57.1 5.0 %all-to-all-done.1.x_ref = bf16[16,512,128]{2,1,0:T(8,128)(2,1)S(1)} async-done(((bf16[16,512,128]{2,1,0:T(8,128)(2,1)}), bf16[16,512,128]{2,1,0:T(8,128)(2,1)S(1)}, u32[]{:S(2)}, u32[]{:S(2)}) %all-to-all-start.1) | async-done | bytes 2097184 | tf_op jit(solution)/shard_map/all_to_all | solution.py:28
  62.1 9.3 %ffn.1 = bf16[16,512,128]{2,1,0:T(8,128)(2,1)} custom-call(bf16[16,512,128]{2,1,0:T(8,128)(2,1)S(1)} %all-to-all-done.1.x_ref, bf16[1,2048]{1,0:T(2,128)(2,1)S(1)} %reshape.17.gain_ref, bf16[320,2048]{1,0:T(8,128)(2,1)} %bitcast.44, bf16[320,2048]{1,0:T(8,128)(2,1)} %copy-done.4, bf16[320,2048]{1,0:T(8,128)(2,1)} %bitcast.46, bf16[320,2048]{1,0:T(8,128)(2,1)} %copy-done.5, ...), custom_call_target="tpu_custom_call" | custom-call | tf_op jit(solution)/shard_map/ffn/pallas_call | solution.py:178
  71.4 3.6 %all-to-all-start.2 = ((bf16[16,512,128]{2,1,0:T(8,128)(2,1)}), bf16[16,512,128]{2,1,0:T(8,128)(2,1)S(1)}, u32[]{:S(2)}, u32[]{:S(2)}) async-start(bf16[16,512,128]{2,1,0:T(8,128)(2,1)} %ffn.1), calls=%async_computation.2 | async-start | bytes 4194304 | tf_op jit(solution)/shard_map/all_to_all | solution.py:28
  75.1 6.3 %collective-permute-start.7 = (bf16[2,2,3,8,256]{4,3,2,1,0:T(8,128)(2,1)S(1)}, bf16[2,2,3,8,256]{4,3,2,1,0:T(8,128)(2,1)S(1)}, u32[]{:S(2)}, u32[]{:S(2)}) collective-permute-start(bf16[2,2,3,8,256]{4,3,2,1,0:T(8,128)(2,1)S(1)} %pad_maximum_fusion.2), channel_id=1, source_target_pairs={{0,128},{16,144},{32,160},{48,176},{64,192},{80,208},{96,224},{112... | collective-permute-start | bytes 147464 | tf_op jit(solution)/shard_map/ppermute | solution.py:42
  81.4 3.0 %collective-permute-done.7 = bf16[2,2,3,8,256]{4,3,2,1,0:T(8,128)(2,1)S(1)} collective-permute-done((bf16[2,2,3,8,256]{4,3,2,1,0:T(8,128)(2,1)S(1)}, bf16[2,2,3,8,256]{4,3,2,1,0:T(8,128)(2,1)S(1)}, u32[]{:S(2)}, u32[]{:S(2)}) %collective-permute-start.7) | collective-permute-done | bytes 49184 | tf_op jit(solution)/shard_map/ppermute | solution.py:42
  84.4 4.4 %collective-permute-start.8 = (bf16[2,2,2,3,8,256]{5,4,3,2,1,0:T(8,128)(2,1)S(1)}, bf16[2,2,2,3,8,256]{5,4,3,2,1,0:T(8,128)(2,1)S(1)}, u32[]{:S(2)}, u32[]{:S(2)}) collective-permute-start(bf16[2,2,2,3,8,256]{5,4,3,2,1,0:T(8,128)(2,1)S(1)} %pad_maximum_fusion.1), channel_id=1, source_target_pairs={{0,64},{16,80},{32,96},{48,112},{64,0},{80,16},{96,32},{112,48},{1... | collective-permute-start | bytes 294920 | tf_op jit(solution)/shard_map/ppermute | solution.py:42
  88.7 2.3 %collective-permute-done.8 = bf16[2,2,2,3,8,256]{5,4,3,2,1,0:T(8,128)(2,1)S(1)} collective-permute-done((bf16[2,2,2,3,8,256]{5,4,3,2,1,0:T(8,128)(2,1)S(1)}, bf16[2,2,2,3,8,256]{5,4,3,2,1,0:T(8,128)(2,1)S(1)}, u32[]{:S(2)}, u32[]{:S(2)}) %collective-permute-start.8) | collective-permute-done | bytes 98336 | tf_op jit(solution)/shard_map/ppermute | solution.py:42
  91.1 5.4 %collective-permute-start.9 = (bf16[2,2,2,2,3,8,256]{6,5,4,3,2,1,0:T(8,128)(2,1)S(1)}, bf16[2,2,2,2,3,8,256]{6,5,4,3,2,1,0:T(8,128)(2,1)S(1)}, u32[]{:S(2)}, u32[]{:S(2)}) collective-permute-start(bf16[2,2,2,2,3,8,256]{6,5,4,3,2,1,0:T(8,128)(2,1)S(1)} %pad_maximum_fusion), channel_id=1, source_target_pairs={{0,32},{16,48},{32,0},{48,16},{64,96},{80,112},{96,64},{112,80},{1... | collective-permute-start | bytes 589832 | tf_op jit(solution)/shard_map/ppermute | solution.py:42
  96.4 3.4 %collective-permute-done.9 = bf16[2,2,2,2,3,8,256]{6,5,4,3,2,1,0:T(8,128)(2,1)S(1)} collective-permute-done((bf16[2,2,2,2,3,8,256]{6,5,4,3,2,1,0:T(8,128)(2,1)S(1)}, bf16[2,2,2,2,3,8,256]{6,5,4,3,2,1,0:T(8,128)(2,1)S(1)}, u32[]{:S(2)}, u32[]{:S(2)}) %collective-permute-start.9) | collective-permute-done | bytes 196640 | tf_op jit(solution)/shard_map/ppermute | solution.py:42
  99.9 0.0 copy-start.3
  100.0 0.1 copy.17
  100.1 0.2 unstack.19.down_ref
  100.3 0.1 copy.18
  100.4 0.2 unstack.21.other_ref
  100.6 0.5 all-to-all-done.2.parts_ref
  101.2 1.9 %squeeze.6 = (bf16[512,128]{1,0:T(8,128)(2,1)}, bf16[512,128]{1,0:T(8,128)(2,1)}, bf16[8,256,128]{2,1,0:T(8,128)(2,1)}) custom-call(s32[8]{0:T(128)S(1)} %copy-done.3, bf16[16,512,128]{2,1,0:T(8,128)(2,1)S(1)} %all-to-all-done.2.parts_ref, bf16[8,128,64]{2,1,0:T(8,128)(2,1)S(1)} %unstack.19.down_ref, bf16[8,128,64]{2,1,0:T(8,128)(2,1)S(1)} %unstack.21.other_ref), custom_call_target="tpu_custom_call" | custom-call | tf_op jit(solution)/shard_map/squeeze/pallas_call | solution.py:243
  103.1 0.0 copy-start.1
  103.1 3.8 %all-to-all-start.3 = ((bf16[8,256,128]{2,1,0:T(8,128)(2,1)}), bf16[8,256,128]{2,1,0:T(8,128)(2,1)S(1)}, u32[]{:S(2)}, u32[]{:S(2)}) async-start(bf16[8,256,128]{2,1,0:T(8,128)(2,1)} %get-tuple-element.32), calls=%async_computation.3 | async-start | bytes 1048576 | tf_op jit(solution)/shard_map/all_to_all | solution.py:28
  107.0 6.4 %collective-permute-start.10 = (bf16[512,128]{1,0:T(8,128)(2,1)}, bf16[512,128]{1,0:T(8,128)(2,1)S(1)}, u32[]{:S(2)}, u32[]{:S(2)}) collective-permute-start(bf16[512,128]{1,0:T(8,128)(2,1)} %get-tuple-element.31), channel_id=1, source_target_pairs={{0,1},{1,0},{2,3},{3,2},{4,5},{5,4},{6,7},{7,6},{8,9},{9,8},{10,11... | collective-permute-start | bytes 393224 | tf_op jit(solution)/shard_map/ppermute | solution.py:34
  113.4 0.7 all-to-all-done.3.parts_ref
  114.1 0.1 relu_sum.1.squeezed_ref
  114.2 7.6 %collective-permute-start.11 = (bf16[256,128]{1,0:T(8,128)(2,1)S(1)}, bf16[256,128]{1,0:T(8,128)(2,1)S(1)}, u32[]{:S(2)}, u32[]{:S(2)}) collective-permute-start(bf16[256,128]{1,0:T(8,128)(2,1)S(1)} %relu_sum.1.squeezed_ref), channel_id=1, source_target_pairs={{0,1},{1,0},{2,3},{3,2},{4,5},{5,4},{6,7},{7,6},{8,9},{9,8},{10,11... | collective-permute-start | bytes 196616 | tf_op jit(solution)/shard_map/ppermute | solution.py:34
  121.8 0.1 copy.19
  121.9 0.2 unstack.23.up_ref
  122.1 0.5 collective-permute-done.11.their_squeezed_ref
  122.6 1.6 %expand.1 = bf16[1024,128]{1,0:T(8,128)(2,1)} custom-call(s32[8]{0:T(128)S(1)} %copy-done.3, bf16[1024,128]{1,0:T(8,128)(2,1)S(1)} %copy-done.1, bf16[512,128]{1,0:T(8,128)(2,1)S(1)} %copy-done.2, bf16[512,128]{1,0:T(8,128)(2,1)S(1)} %collective-permute-done.10.theirs_ref, bf16[256,128]{1,0:T(8,128)(2,1)S(1)} %relu_sum.1.squeezed_ref, ...), custom_call_target="tpu_custom_call" | custom-call | tf_op jit(solution)/shard_map/expand/pallas_call | solution.py:61
  (30 shorter events, 0.3 us)
Async XLA Ops:
  0.0 38.5 %copy-start = (bf16[1024,256]{1,0:T(8,128)(2,1)S(1)}, bf16[1024,256]{1,0:T(8,128)(2,1)}, u32[]{:S(2)}) copy-start(bf16[1024,256]{1,0:T(8,128)(2,1)} %param.23) | copy-start | bytes 1572868
  1.6 29.2 %collective-permute-start.1 = (bf16[320,2048]{1,0:T(8,128)(2,1)}, bf16[320,2048]{1,0:T(8,128)(2,1)S(1)}, u32[]{:S(2)}, u32[]{:S(2)}) collective-permute-start(bf16[320,2048]{1,0:T(8,128)(2,1)} %bitcast.43), channel_id=1, source_target_pairs={{0,1},{1,0},{2,3},{3,2},{4,5},{5,4},{6,7},{7,6},{8,9},{9,8},{10,11... | collective-permute-start | bytes 3932168 | tf_op jit(solution)/shard_map/ppermute | solution.py:34
  10.4 20.4 %collective-permute-start.2 = (bf16[320,2048]{1,0:T(8,128)(2,1)}, bf16[320,2048]{1,0:T(8,128)(2,1)S(1)}, u32[]{:S(2)}, u32[]{:S(2)}) collective-permute-start(bf16[320,2048]{1,0:T(8,128)(2,1)} %bitcast.45), channel_id=1, source_target_pairs={{0,1},{1,0},{2,3},{3,2},{4,5},{5,4},{6,7},{7,6},{8,9},{9,8},{10,11... | collective-permute-start | bytes 3932168 | tf_op jit(solution)/shard_map/ppermute | solution.py:34
  12.4 18.5 %collective-permute-start.3 = (bf16[320,2048]{1,0:T(8,128)(2,1)}, bf16[320,2048]{1,0:T(8,128)(2,1)}, u32[]{:S(2)}, u32[]{:S(2)}) collective-permute-start(bf16[320,2048]{1,0:T(8,128)(2,1)} %wo_own_ref), channel_id=1, source_target_pairs={{0,1},{1,0},{2,3},{3,2},{4,5},{5,4},{6,7},{7,6},{8,9},{9,8},{10,11... | collective-permute-start | bytes 3932168 | tf_op jit(solution)/shard_map/ppermute | solution.py:34
  14.8 16.0 %collective-permute-start.4 = (bf16[1024,256]{1,0:T(8,128)(2,1)}, bf16[1024,256]{1,0:T(8,128)(2,1)}, u32[]{:S(2)}, u32[]{:S(2)}) collective-permute-start(bf16[1024,256]{1,0:T(8,128)(2,1)} %param.22), channel_id=1, source_target_pairs={{0,1},{1,0},{2,3},{3,2},{4,5},{5,4},{6,7},{7,6},{8,9},{9,8},{10,11... | collective-permute-start | bytes 1572872 | tf_op jit(solution)/shard_map/ppermute | solution.py:34
  17.7 10.9 %collective-permute-start = (bf16[512,128]{1,0:T(8,128)(2,1)S(1)}, bf16[512,128]{1,0:T(8,128)(2,1)S(1)}, u32[]{:S(2)}, u32[]{:S(2)}) collective-permute-start(bf16[512,128]{1,0:T(8,128)(2,1)S(1)} %dynamic-slice_bitcast_fusion), channel_id=1, source_target_pairs={{0,1},{1,0},{2,3},{3,2},{4,5},{5,4},{6,7},{7,6},{8,9},{9,8},{10,11... | collective-permute-start | bytes 393224 | tf_op jit(solution)/shard_map/ppermute | solution.py:34
  30.9 1.1 copy-start.4
  30.9 1.5 %copy-start.5 = (bf16[320,2048]{1,0:T(8,128)(2,1)}, bf16[320,2048]{1,0:T(8,128)(2,1)S(1)}, u32[]{:S(2)}) copy-start(bf16[320,2048]{1,0:T(8,128)(2,1)S(1)} %collective-permute-done.2.linear_other_ref) | copy-start | bytes 3932164
  32.4 29.8 %all-to-all-start.1 = ((bf16[16,512,128]{2,1,0:T(8,128)(2,1)}), bf16[16,512,128]{2,1,0:T(8,128)(2,1)S(1)}, u32[]{:S(2)}, u32[]{:S(2)}) async-start(bf16[16,512,128]{2,1,0:T(8,128)(2,1)} %spread.1), calls=%async_computation.1 | async-start | bytes 4194304 | tf_op jit(solution)/shard_map/all_to_all | solution.py:28
  36.0 21.1 %copy-start.6 = (bf16[2048]{0:T(1024)(128)(2,1)S(1)}, bf16[2048]{0:T(1024)(128)(2,1)}, u32[]{:S(2)}) copy-start(bf16[2048]{0:T(1024)(128)(2,1)} %param.13) | copy-start | bytes 12292
  38.7 14.0 %collective-permute-start.5 = (bf16[3,8,256]{2,1,0:T(8,128)(2,1)S(1)}, bf16[3,8,256]{2,1,0:T(8,128)(2,1)S(1)}, u32[]{:S(2)}, u32[]{:S(2)}) collective-permute-start(bf16[3,8,256]{2,1,0:T(8,128)(2,1)S(1)} %pad_maximum_fusion.4), channel_id=1, source_target_pairs={{0,256},{16,272},{32,288},{48,304},{64,320},{80,336},{96,352},{112... | collective-permute-start | bytes 36872 | tf_op jit(solution)/shard_map/ppermute | solution.py:42
  52.7 22.3 %collective-permute-start.6 = (bf16[2,3,8,256]{3,2,1,0:T(8,128)(2,1)S(1)}, bf16[2,3,8,256]{3,2,1,0:T(8,128)(2,1)S(1)}, u32[]{:S(2)}, u32[]{:S(2)}) collective-permute-start(bf16[2,3,8,256]{3,2,1,0:T(8,128)(2,1)S(1)} %pad_maximum_fusion.3), channel_id=1, source_target_pairs={{0,16},{16,0},{32,48},{48,32},{64,80},{80,64},{96,112},{112,96},{1... | collective-permute-start | bytes 73736 | tf_op jit(solution)/shard_map/ppermute | solution.py:42
  71.4 29.8 %all-to-all-start.2 = ((bf16[16,512,128]{2,1,0:T(8,128)(2,1)}), bf16[16,512,128]{2,1,0:T(8,128)(2,1)S(1)}, u32[]{:S(2)}, u32[]{:S(2)}) async-start(bf16[16,512,128]{2,1,0:T(8,128)(2,1)} %ffn.1), calls=%async_computation.2 | async-start | bytes 4194304 | tf_op jit(solution)/shard_map/all_to_all | solution.py:28
  75.1 9.3 %collective-permute-start.7 = (bf16[2,2,3,8,256]{4,3,2,1,0:T(8,128)(2,1)S(1)}, bf16[2,2,3,8,256]{4,3,2,1,0:T(8,128)(2,1)S(1)}, u32[]{:S(2)}, u32[]{:S(2)}) collective-permute-start(bf16[2,2,3,8,256]{4,3,2,1,0:T(8,128)(2,1)S(1)} %pad_maximum_fusion.2), channel_id=1, source_target_pairs={{0,128},{16,144},{32,160},{48,176},{64,192},{80,208},{96,224},{112... | collective-permute-start | bytes 147464 | tf_op jit(solution)/shard_map/ppermute | solution.py:42
  84.4 6.7 %collective-permute-start.8 = (bf16[2,2,2,3,8,256]{5,4,3,2,1,0:T(8,128)(2,1)S(1)}, bf16[2,2,2,3,8,256]{5,4,3,2,1,0:T(8,128)(2,1)S(1)}, u32[]{:S(2)}, u32[]{:S(2)}) collective-permute-start(bf16[2,2,2,3,8,256]{5,4,3,2,1,0:T(8,128)(2,1)S(1)} %pad_maximum_fusion.1), channel_id=1, source_target_pairs={{0,64},{16,80},{32,96},{48,112},{64,0},{80,16},{96,32},{112,48},{1... | collective-permute-start | bytes 294920 | tf_op jit(solution)/shard_map/ppermute | solution.py:42
  91.1 8.8 %collective-permute-start.9 = (bf16[2,2,2,2,3,8,256]{6,5,4,3,2,1,0:T(8,128)(2,1)S(1)}, bf16[2,2,2,2,3,8,256]{6,5,4,3,2,1,0:T(8,128)(2,1)S(1)}, u32[]{:S(2)}, u32[]{:S(2)}) collective-permute-start(bf16[2,2,2,2,3,8,256]{6,5,4,3,2,1,0:T(8,128)(2,1)S(1)} %pad_maximum_fusion), channel_id=1, source_target_pairs={{0,32},{16,48},{32,0},{48,16},{64,96},{80,112},{96,64},{112,80},{1... | collective-permute-start | bytes 589832 | tf_op jit(solution)/shard_map/ppermute | solution.py:42
  99.9 1.3 %copy-start.3 = (s32[8]{0:T(128)S(1)}, s32[8]{0:T(128)}, u32[]{:S(2)}) copy-start(s32[8]{0:T(128)} %ids_ref.3) | copy-start | bytes 100
  103.1 19.5 %copy-start.1 = (bf16[1024,128]{1,0:T(8,128)(2,1)S(1)}, bf16[1024,128]{1,0:T(8,128)(2,1)}, u32[]{:S(2)}) copy-start(bf16[1024,128]{1,0:T(8,128)(2,1)} %tokens_ref.1) | copy-start | bytes 786436
  103.1 19.5 %copy-start.2 = (bf16[512,128]{1,0:T(8,128)(2,1)S(1)}, bf16[512,128]{1,0:T(8,128)(2,1)}, u32[]{:S(2)}) copy-start(bf16[512,128]{1,0:T(8,128)(2,1)} %get-tuple-element.30.mine_ref) | copy-start | bytes 393220
  103.1 11.0 %all-to-all-start.3 = ((bf16[8,256,128]{2,1,0:T(8,128)(2,1)}), bf16[8,256,128]{2,1,0:T(8,128)(2,1)S(1)}, u32[]{:S(2)}, u32[]{:S(2)}) async-start(bf16[8,256,128]{2,1,0:T(8,128)(2,1)} %get-tuple-element.32), calls=%async_computation.3 | async-start | bytes 1048576 | tf_op jit(solution)/shard_map/all_to_all | solution.py:28
  107.0 15.1 %collective-permute-start.10 = (bf16[512,128]{1,0:T(8,128)(2,1)}, bf16[512,128]{1,0:T(8,128)(2,1)S(1)}, u32[]{:S(2)}, u32[]{:S(2)}) collective-permute-start(bf16[512,128]{1,0:T(8,128)(2,1)} %get-tuple-element.31), channel_id=1, source_target_pairs={{0,1},{1,0},{2,3},{3,2},{4,5},{5,4},{6,7},{7,6},{8,9},{9,8},{10,11... | collective-permute-start | bytes 393224 | tf_op jit(solution)/shard_map/ppermute | solution.py:34
  114.2 8.5 %collective-permute-start.11 = (bf16[256,128]{1,0:T(8,128)(2,1)S(1)}, bf16[256,128]{1,0:T(8,128)(2,1)S(1)}, u32[]{:S(2)}, u32[]{:S(2)}) collective-permute-start(bf16[256,128]{1,0:T(8,128)(2,1)S(1)} %relu_sum.1.squeezed_ref), channel_id=1, source_target_pairs={{0,1},{1,0},{2,3},{3,2},{4,5},{5,4},{6,7},{7,6},{8,9},{9,8},{10,11... | collective-permute-start | bytes 196616 | tf_op jit(solution)/shard_map/ppermute | solution.py:34

commit v6 on v5

--- a/solution.py
+++ b/solution.py
@@ -34,15 +34,18 @@
     return lax.ppermute(array, "mp", [(i, i ^ 1) for i in range(MP)])
 
 
-def doubling_gather(shard, axis, bits):
+def doubling_gather(shard, axis, bits, later):
     index = lax.axis_index(axis)
     size = lax.axis_size(axis)
     held = shard
-    for bit in bits:
+    released = []
+    for bit, array in zip(bits, later, strict=True):
+        held, array = lax.optimization_barrier((held, array))
+        released.append(array)
         theirs = lax.ppermute(held, axis, [(i, i ^ bit) for i in range(size)])
         upper = (index & bit) != 0
         held = jnp.stack([jnp.where(upper, theirs, held), jnp.where(upper, held, theirs)])
-    return held
+    return held, released
 
 
 def in_vmem(array):
@@ -338,22 +341,23 @@
         (layer_index,),
         in_hbm,
     )
-
-    hidden, gate, linear, wo, gen_down = lax.optimization_barrier(
-        (hidden, wi_gate.T, wi_linear.T, wo_out, gen_down)
-    )
     hidden = exchange(hidden, "mp")
-    others = [swap_cores(w) for w in (gate, linear, wo, gen_down)]
-    hidden, sent, others = lax.optimization_barrier((hidden, spread(halves, given), others))
-    gate_other, linear_other, wo_other, gen_other = others
+    hidden, sent = lax.optimization_barrier((hidden, spread(halves, given)))
     gathered = exchange(sent, "mp", SAME_CORE)
 
     hidden = jnp.moveaxis(hidden, 0, 1).reshape(task_count, -1)
-    generators = (gen_down, gen_up, gen_other)
-    made = jnp.stack([matmul(hidden, generator).astype(jnp.bfloat16) for generator in generators])
-    all_tasks = doubling_gather(made, "dp", (16, 1, 8, 4, 2))
-    all_tasks = jnp.transpose(all_tasks, (5, 6, 4, 2, 1, 0, 3, 7))
-    down, up, down_other = all_tasks.reshape(len(generators), task_count, width, R)
+    made = jnp.stack(
+        [matmul(hidden, gen_down).astype(jnp.bfloat16), matmul(hidden, gen_up).astype(jnp.bfloat16)]
+    )
+    near, (gate, linear, wo) = doubling_gather(
+        made, "dp", (1, 2, 4), (wi_gate.T, wi_linear.T, wo_out)
+    )
+    gate_other, linear_other, wo_other = swap_cores(gate), swap_cores(linear), swap_cores(wo)
+    gathered, near = lax.optimization_barrier((gathered, near))
+    far = lax.axis_size("dp") // 8
+    strided = [[8 * i + place for i in range(far)] for place in range(8)]
+    near = near.reshape(1, 8, *made.shape)
+    all_tasks = exchange(jnp.broadcast_to(near, (far, *near.shape[1:])), "dp", strided)
 
     partial = ffn(
         gathered,
@@ -362,8 +366,11 @@
         (linear, linear_other),
         (wo, wo_other),
     )
+    partial, all_tasks = lax.optimization_barrier((partial, all_tasks))
     parts = exchange(partial, "mp", SAME_CORE)
-    mine, given, squeeze_part = squeeze(task_ids, parts, down, down_other)
+    adapters = jnp.transpose(all_tasks, (2, 3, 0, 1, 4)).reshape(2, task_count, width, R)
+    down, up = adapters[0], adapters[1]
+    mine, given, squeeze_part = squeeze(task_ids, parts, down, swap_cores(down))
     theirs = swap_cores(given)
     squeezed = relu_sum(exchange(squeeze_part, "mp", SAME_CORE))
     return expand(task_ids, tokens, mine, theirs, squeezed, swap_cores(squeezed), up)

time: 125 us -> 151 us (1.21)
  the two profiles are of different devices: /device:TPU:1 before, /device:TPU:33 now
where the time goes in v6:
time: 151 us; the launch traced here: 150 us
  waiting for transfers between devices  60.4 us (40%)
  starting transfers between devices  58.6 us (39%)
  Pallas kernels  16 us (11%)
  blocking collectives  11.1 us (7%)
  local copies, waits for them, and re-layouts  2.41 us (2%)
    all_to_all x4, waiting for transfers between devices, exchange(): lax.all_to_all(pieces, axis, split_axis=0, concat_axis=0, axis_index_grou...  36 us
    all_to_all x4, starting transfers between devices, exchange(): lax.all_to_all(pieces, axis, split_axis=0, concat_axis=0, axis_index_grou...  25.9 us
    ppermute x3, waiting for transfers between devices, doubling_gather(): theirs = lax.ppermute(held, axis, [(i, i ^ bit) for i in range(size)])  22.6 us
    ppermute x7, starting transfers between devices, swap_cores(): return lax.ppermute(array, 'mp', [(i, i ^ 1) for i in range(MP)])  21.5 us
    ppermute x3, starting transfers between devices, doubling_gather(): theirs = lax.ppermute(held, axis, [(i, i ^ bit) for i in range(size)])  11.2 us
    all_to_all x1, blocking collectives, exchange(): lax.all_to_all(pieces, axis, split_axis=0, concat_axis=0, axis_index_grou...  11.1 us
    pallas_call x1, Pallas kernels, ffn(): pl.pallas_call(ffn_body, out_shape=pltpu.HBM(x.shape, x.dtype), in_specs=...  9.24 us
  transfers between devices with their start and end apart: 14, of which 7 were waited for; matrix products, arithmetic and copies ran while one was open for 1% of the time, Pallas kernels for 7%

profile of v6, /device:TPU:33, one launch (start us, length us, event | category | flops | bytes accessed | tf_op | source)
XLA Modules:
  0.0 149.9 jit_solution(6347096270406325600)
XLA Ops:
  0.0 1.0 dynamic-slice_bitcast_fusion
  1.0 2.6 %collective-permute-start = (bf16[512,128]{1,0:T(8,128)(2,1)S(1)}, bf16[512,128]{1,0:T(8,128)(2,1)S(1)}, u32[]{:S(2)}, u32[]{:S(2)}) collective-permute-start(bf16[512,128]{1,0:T(8,128)(2,1)S(1)} %dynamic-slice_bitcast_fusion), channel_id=1, source_target_pairs={{0,1},{1,0},{2,3},{3,2},{4,5},{5,4},{6,7},{7,6},{8,9},{9,8},{10,11... | collective-permute-start | bytes 393224 | tf_op jit(solution)/shard_map/ppermute | solution.py:34
  4.2 0.9 hidden.1
  5.2 0.1 reshape.19
  5.3 11.1 %all_to_all.25 = bf16[16,2,256]{2,1,0:T(2,128)(2,1)S(1)} all-to-all(bf16[16,2,256]{2,1,0:T(2,128)(2,1)S(1)} %reshape.19), channel_id=1, replica_groups=mesh['dp'=32,'mp'=16] {'mp'}, dimensions={0} | all-to-all | bytes 32768 | tf_op jit(solution)/shard_map/all_to_all | solution.py:28
  16.4 0.1 reshape.20
  16.5 0.0 collective-permute-done.given_ref
  16.5 2.2 %spread.1 = bf16[16,512,128]{2,1,0:T(8,128)(2,1)} custom-call(bf16[2,512,128]{2,1,0:T(8,128)(2,1)} %bitcast.34, bf16[512,128]{1,0:T(8,128)(2,1)S(1)} %collective-permute-done.given_ref), custom_call_target="tpu_custom_call" | custom-call | tf_op jit(solution)/shard_map/spread/pallas_call | solution.py:93
  18.7 0.0 copy-start.4
  18.7 3.7 %all-to-all-start.1 = ((bf16[16,512,128]{2,1,0:T(8,128)(2,1)}), bf16[16,512,128]{2,1,0:T(8,128)(2,1)S(1)}, u32[]{:S(2)}, u32[]{:S(2)}) async-start(bf16[16,512,128]{2,1,0:T(8,128)(2,1)} %spread.1), calls=%async_computation.1 | async-start | bytes 4194304 | tf_op jit(solution)/shard_map/all_to_all | solution.py:28
  22.5 0.0 copy-start.5
  22.5 0.1 reshape.17
  22.6 0.2 fusion.1
  22.8 0.2 fusion
  23.0 4.4 %collective-permute-start.1 = (bf16[2,8,256]{2,1,0:T(8,128)(2,1)S(1)}, bf16[2,8,256]{2,1,0:T(8,128)(2,1)S(1)}, u32[]{:S(2)}, u32[]{:S(2)}) collective-permute-start(bf16[2,8,256]{2,1,0:T(8,128)(2,1)S(1)} %pad_maximum_fusion.3), channel_id=1, source_target_pairs={{0,16},{16,0},{32,48},{48,32},{64,80},{80,64},{96,112},{112,96},{1... | collective-permute-start | bytes 24584 | tf_op jit(solution)/shard_map/ppermute | solution.py:45
  27.3 20.9 %collective-permute-done.1 = bf16[2,8,256]{2,1,0:T(8,128)(2,1)S(1)} collective-permute-done((bf16[2,8,256]{2,1,0:T(8,128)(2,1)S(1)}, bf16[2,8,256]{2,1,0:T(8,128)(2,1)S(1)}, u32[]{:S(2)}, u32[]{:S(2)}) %collective-permute-start.1) | collective-permute-done | bytes 8224 | tf_op jit(solution)/shard_map/ppermute | solution.py:45
  48.2 1.9 %collective-permute-start.2 = (bf16[2,2,8,256]{3,2,1,0:T(8,128)(2,1)S(1)}, bf16[2,2,8,256]{3,2,1,0:T(8,128)(2,1)S(1)}, u32[]{:S(2)}, u32[]{:S(2)}) collective-permute-start(bf16[2,2,8,256]{3,2,1,0:T(8,128)(2,1)S(1)} %pad_maximum_fusion.2), channel_id=1, source_target_pairs={{0,32},{16,48},{32,0},{48,16},{64,96},{80,112},{96,64},{112,80},{1... | collective-permute-start | bytes 49160 | tf_op jit(solution)/shard_map/ppermute | solution.py:45
  50.2 3.2 %collective-permute-start.4 = (bf16[320,2048]{1,0:T(8,128)(2,1)}, bf16[320,2048]{1,0:T(8,128)(2,1)}, u32[]{:S(2)}, u32[]{:S(2)}) collective-permute-start(bf16[320,2048]{1,0:T(8,128)(2,1)} %bitcast.35), channel_id=1, source_target_pairs={{0,1},{1,0},{2,3},{3,2},{4,5},{5,4},{6,7},{7,6},{8,9},{9,8},{10,11... | collective-permute-start | bytes 3932168 | tf_op jit(solution)/shard_map/ppermute | solution.py:34
  53.4 1.9 %collective-permute-start.5 = (bf16[320,2048]{1,0:T(8,128)(2,1)}, bf16[320,2048]{1,0:T(8,128)(2,1)}, u32[]{:S(2)}, u32[]{:S(2)}) collective-permute-start(bf16[320,2048]{1,0:T(8,128)(2,1)} %bitcast.37), channel_id=1, source_target_pairs={{0,1},{1,0},{2,3},{3,2},{4,5},{5,4},{6,7},{7,6},{8,9},{9,8},{10,11... | collective-permute-start | bytes 3932168 | tf_op jit(solution)/shard_map/ppermute | solution.py:34
  55.3 0.0 collective-permute-done.2
  55.4 2.4 %collective-permute-start.6 = (bf16[320,2048]{1,0:T(8,128)(2,1)}, bf16[320,2048]{1,0:T(8,128)(2,1)}, u32[]{:S(2)}, u32[]{:S(2)}) collective-permute-start(bf16[320,2048]{1,0:T(8,128)(2,1)} %wo_own_ref), channel_id=1, source_target_pairs={{0,1},{1,0},{2,3},{3,2},{4,5},{5,4},{6,7},{7,6},{8,9},{9,8},{10,11... | collective-permute-start | bytes 3932168 | tf_op jit(solution)/shard_map/ppermute | solution.py:34
  57.8 4.9 %collective-permute-start.3 = (bf16[2,2,2,8,256]{4,3,2,1,0:T(8,128)(2,1)S(1)}, bf16[2,2,2,8,256]{4,3,2,1,0:T(8,128)(2,1)S(1)}, u32[]{:S(2)}, u32[]{:S(2)}) collective-permute-start(bf16[2,2,2,8,256]{4,3,2,1,0:T(8,128)(2,1)S(1)} %pad_maximum_fusion.1), channel_id=1, source_target_pairs={{0,64},{16,80},{32,96},{48,112},{64,0},{80,16},{96,32},{112,48},{1... | collective-permute-start | bytes 98312 | tf_op jit(solution)/shard_map/ppermute | solution.py:45
  62.7 1.7 %collective-permute-done.3 = bf16[2,2,2,8,256]{4,3,2,1,0:T(8,128)(2,1)S(1)} collective-permute-done((bf16[2,2,2,8,256]{4,3,2,1,0:T(8,128)(2,1)S(1)}, bf16[2,2,2,8,256]{4,3,2,1,0:T(8,128)(2,1)S(1)}, u32[]{:S(2)}, u32[]{:S(2)}) %collective-permute-start.3) | collective-permute-done | bytes 32800 | tf_op jit(solution)/shard_map/ppermute | solution.py:45
  64.5 0.0 all-to-all-done.1.x_ref
  64.5 0.7 broadcast_in_dim.8
  65.2 13.7 %all-to-all-start.2 = ((bf16[4,8,2,8,256]{4,1,3,2,0:T(8,128)(2,1)}), bf16[4,8,2,8,256]{4,1,3,2,0:T(8,128)(2,1)S(1)}, u32[]{:S(2)}, u32[]{:S(2)}) async-start(bf16[4,8,2,8,256]{4,1,3,2,0:T(8,128)(2,1)} %broadcast_in_dim.8), calls=%async_computation.2 | async-start | bytes 524288 | tf_op jit(solution)/shard_map/all_to_all | solution.py:28
  79.0 0.0 collective-permute-done.4.gate_other_ref
  79.0 0.0 collective-permute-done.6.wo_other_ref
  79.0 9.2 %ffn.1 = bf16[16,512,128]{2,1,0:T(8,128)(2,1)} custom-call(bf16[16,512,128]{2,1,0:T(8,128)(2,1)S(1)} %all-to-all-done.1.x_ref, bf16[1,2048]{1,0:T(2,128)(2,1)S(1)} %reshape.18.gain_ref, bf16[320,2048]{1,0:T(8,128)(2,1)} %bitcast.36, bf16[320,2048]{1,0:T(8,128)(2,1)} %collective-permute-done.4.gate_other_ref, bf16[320,2048]{1,0:T(8,128)(2,1)} %bitcast.38, ...), custom_call_target="tpu_custom_call" | custom-call | tf_op jit(solution)/shard_map/ffn/pallas_call | solution.py:181
  88.3 0.0 copy-start.3
  88.3 10.3 %all-to-all-done.2 = bf16[4,8,2,8,256]{4,1,3,2,0:T(8,128)(2,1)S(1)} async-done(((bf16[4,8,2,8,256]{4,1,3,2,0:T(8,128)(2,1)}), bf16[4,8,2,8,256]{4,1,3,2,0:T(8,128)(2,1)S(1)}, u32[]{:S(2)}, u32[]{:S(2)}) %all-to-all-start.2) | async-done | bytes 262176 | tf_op jit(solution)/shard_map/all_to_all | solution.py:28
  98.6 4.6 %all-to-all-start.3 = ((bf16[16,512,128]{2,1,0:T(8,128)(2,1)}), bf16[16,512,128]{2,1,0:T(8,128)(2,1)S(1)}, u32[]{:S(2)}, u32[]{:S(2)}) async-start(bf16[16,512,128]{2,1,0:T(8,128)(2,1)} %ffn.1), calls=%async_computation.3 | async-start | bytes 4194304 | tf_op jit(solution)/shard_map/all_to_all | solution.py:28
  103.2 0.2 squeeze.12.down_ref
  103.3 4.5 %collective-permute-start.7 = (bf16[8,128,64]{2,1,0:T(8,128)(2,1)S(1)}, bf16[8,128,64]{2,1,0:T(8,128)(2,1)S(1)}, u32[]{:S(2)}, u32[]{:S(2)}) collective-permute-start(bf16[8,128,64]{2,1,0:T(8,128)(2,1)S(1)} %squeeze.12.down_ref), channel_id=1, source_target_pairs={{0,1},{1,0},{2,3},{3,2},{4,5},{5,4},{6,7},{7,6},{8,9},{9,8},{10,11... | collective-permute-start | bytes 393224 | tf_op jit(solution)/shard_map/ppermute | solution.py:34
  107.8 1.1 collective-permute-done.7.other_ref
  109.0 20.3 %all-to-all-done.3.parts_ref = bf16[16,512,128]{2,1,0:T(8,128)(2,1)S(1)} async-done(((bf16[16,512,128]{2,1,0:T(8,128)(2,1)}), bf16[16,512,128]{2,1,0:T(8,128)(2,1)S(1)}, u32[]{:S(2)}, u32[]{:S(2)}) %all-to-all-start.3) | async-done | bytes 2097184 | tf_op jit(solution)/shard_map/all_to_all | solution.py:28
  129.3 1.9 %squeeze.14 = (bf16[512,128]{1,0:T(8,128)(2,1)}, bf16[512,128]{1,0:T(8,128)(2,1)}, bf16[8,256,128]{2,1,0:T(8,128)(2,1)}) custom-call(s32[8]{0:T(128)S(1)} %copy-done.3, bf16[16,512,128]{2,1,0:T(8,128)(2,1)S(1)} %all-to-all-done.3.parts_ref, bf16[8,128,64]{2,1,0:T(8,128)(2,1)S(1)} %squeeze.12.down_ref, bf16[8,128,64]{2,1,0:T(8,128)(2,1)S(1)} %collective-permute-done.7.other_ref), custom_call_target="tpu_custom_call" | custom-call | tf_op jit(solution)/shard_map/squeeze/pallas_call | solution.py:246
  131.2 0.0 copy-start.1
  131.2 0.0 copy-start.2
  131.2 3.9 %all-to-all-start.4 = ((bf16[8,256,128]{2,1,0:T(8,128)(2,1)}), bf16[8,256,128]{2,1,0:T(8,128)(2,1)S(1)}, u32[]{:S(2)}, u32[]{:S(2)}) async-start(bf16[8,256,128]{2,1,0:T(8,128)(2,1)} %get-tuple-element.34), calls=%async_computation.4 | async-start | bytes 1048576 | tf_op jit(solution)/shard_map/all_to_all | solution.py:28
  135.1 2.7 %collective-permute-start.8 = (bf16[512,128]{1,0:T(8,128)(2,1)}, bf16[512,128]{1,0:T(8,128)(2,1)S(1)}, u32[]{:S(2)}, u32[]{:S(2)}) collective-permute-start(bf16[512,128]{1,0:T(8,128)(2,1)} %get-tuple-element.33), channel_id=1, source_target_pairs={{0,1},{1,0},{2,3},{3,2},{4,5},{5,4},{6,7},{7,6},{8,9},{9,8},{10,11... | collective-permute-start | bytes 393224 | tf_op jit(solution)/shard_map/ppermute | solution.py:34
  137.8 5.4 %all-to-all-done.4.parts_ref = bf16[8,256,128]{2,1,0:T(8,128)(2,1)S(1)} async-done(((bf16[8,256,128]{2,1,0:T(8,128)(2,1)}), bf16[8,256,128]{2,1,0:T(8,128)(2,1)S(1)}, u32[]{:S(2)}, u32[]{:S(2)}) %all-to-all-start.4) | async-done | bytes 524320 | tf_op jit(solution)/shard_map/all_to_all | solution.py:28
  143.1 0.1 relu_sum.1.squeezed_ref
  143.2 4.2 %collective-permute-start.9 = (bf16[256,128]{1,0:T(8,128)(2,1)S(1)}, bf16[256,128]{1,0:T(8,128)(2,1)S(1)}, u32[]{:S(2)}, u32[]{:S(2)}) collective-permute-start(bf16[256,128]{1,0:T(8,128)(2,1)S(1)} %relu_sum.1.squeezed_ref), channel_id=1, source_target_pairs={{0,1},{1,0},{2,3},{3,2},{4,5},{5,4},{6,7},{7,6},{8,9},{9,8},{10,11... | collective-permute-start | bytes 196616 | tf_op jit(solution)/shard_map/ppermute | solution.py:34
  147.5 0.2 squeeze.13.up_ref
  147.6 0.0 collective-permute-done.8.theirs_ref
  147.7 0.7 collective-permute-done.9.their_squeezed_ref
  148.3 1.6 %expand.1 = bf16[1024,128]{1,0:T(8,128)(2,1)} custom-call(s32[8]{0:T(128)S(1)} %copy-done.3, bf16[1024,128]{1,0:T(8,128)(2,1)S(1)} %copy-done.1, bf16[512,128]{1,0:T(8,128)(2,1)S(1)} %copy-done.2, bf16[512,128]{1,0:T(8,128)(2,1)S(1)} %collective-permute-done.8.theirs_ref, bf16[256,128]{1,0:T(8,128)(2,1)S(1)} %relu_sum.1.squeezed_ref, ...), custom_call_target="tpu_custom_call" | custom-call | tf_op jit(solution)/shard_map/expand/pallas_call | solution.py:64
  (21 shorter events, 0.1 us)
Async XLA Ops:
  0.0 22.6 %copy-start = (bf16[1024,256]{1,0:T(8,128)(2,1)S(1)}, bf16[1024,256]{1,0:T(8,128)(2,1)}, u32[]{:S(2)}) copy-start(bf16[1024,256]{1,0:T(8,128)(2,1)} %param.23) | copy-start | bytes 1572868
  1.0 15.5 %collective-permute-start = (bf16[512,128]{1,0:T(8,128)(2,1)S(1)}, bf16[512,128]{1,0:T(8,128)(2,1)S(1)}, u32[]{:S(2)}, u32[]{:S(2)}) collective-permute-start(bf16[512,128]{1,0:T(8,128)(2,1)S(1)} %dynamic-slice_bitcast_fusion), channel_id=1, source_target_pairs={{0,1},{1,0},{2,3},{3,2},{4,5},{5,4},{6,7},{7,6},{8,9},{9,8},{10,11... | collective-permute-start | bytes 393224 | tf_op jit(solution)/shard_map/ppermute | solution.py:34
  18.7 4.1 %copy-start.4 = (bf16[1024,256]{1,0:T(8,128)(2,1)S(1)}, bf16[1024,256]{1,0:T(8,128)(2,1)}, u32[]{:S(2)}) copy-start(bf16[1024,256]{1,0:T(8,128)(2,1)} %param.22) | copy-start | bytes 1572868
  18.7 45.8 %all-to-all-start.1 = ((bf16[16,512,128]{2,1,0:T(8,128)(2,1)}), bf16[16,512,128]{2,1,0:T(8,128)(2,1)S(1)}, u32[]{:S(2)}, u32[]{:S(2)}) async-start(bf16[16,512,128]{2,1,0:T(8,128)(2,1)} %spread.1), calls=%async_computation.1 | async-start | bytes 4194304 | tf_op jit(solution)/shard_map/all_to_all | solution.py:28
  22.5 56.5 %copy-start.5 = (bf16[2048]{0:T(1024)(128)(2,1)S(1)}, bf16[2048]{0:T(1024)(128)(2,1)}, u32[]{:S(2)}) copy-start(bf16[2048]{0:T(1024)(128)(2,1)} %param.13) | copy-start | bytes 12292
  23.0 25.3 %collective-permute-start.1 = (bf16[2,8,256]{2,1,0:T(8,128)(2,1)S(1)}, bf16[2,8,256]{2,1,0:T(8,128)(2,1)S(1)}, u32[]{:S(2)}, u32[]{:S(2)}) collective-permute-start(bf16[2,8,256]{2,1,0:T(8,128)(2,1)S(1)} %pad_maximum_fusion.3), channel_id=1, source_target_pairs={{0,16},{16,0},{32,48},{48,32},{64,80},{80,64},{96,112},{112,96},{1... | collective-permute-start | bytes 24584 | tf_op jit(solution)/shard_map/ppermute | solution.py:45
  48.2 7.1 %collective-permute-start.2 = (bf16[2,2,8,256]{3,2,1,0:T(8,128)(2,1)S(1)}, bf16[2,2,8,256]{3,2,1,0:T(8,128)(2,1)S(1)}, u32[]{:S(2)}, u32[]{:S(2)}) collective-permute-start(bf16[2,2,8,256]{3,2,1,0:T(8,128)(2,1)S(1)} %pad_maximum_fusion.2), channel_id=1, source_target_pairs={{0,32},{16,48},{32,0},{48,16},{64,96},{80,112},{96,64},{112,80},{1... | collective-permute-start | bytes 49160 | tf_op jit(solution)/shard_map/ppermute | solution.py:45
  50.2 28.8 %collective-permute-start.4 = (bf16[320,2048]{1,0:T(8,128)(2,1)}, bf16[320,2048]{1,0:T(8,128)(2,1)}, u32[]{:S(2)}, u32[]{:S(2)}) collective-permute-start(bf16[320,2048]{1,0:T(8,128)(2,1)} %bitcast.35), channel_id=1, source_target_pairs={{0,1},{1,0},{2,3},{3,2},{4,5},{5,4},{6,7},{7,6},{8,9},{9,8},{10,11... | collective-permute-start | bytes 3932168 | tf_op jit(solution)/shard_map/ppermute | solution.py:34
  53.4 25.6 %collective-permute-start.5 = (bf16[320,2048]{1,0:T(8,128)(2,1)}, bf16[320,2048]{1,0:T(8,128)(2,1)}, u32[]{:S(2)}, u32[]{:S(2)}) collective-permute-start(bf16[320,2048]{1,0:T(8,128)(2,1)} %bitcast.37), channel_id=1, source_target_pairs={{0,1},{1,0},{2,3},{3,2},{4,5},{5,4},{6,7},{7,6},{8,9},{9,8},{10,11... | collective-permute-start | bytes 3932168 | tf_op jit(solution)/shard_map/ppermute | solution.py:34
  55.4 23.6 %collective-permute-start.6 = (bf16[320,2048]{1,0:T(8,128)(2,1)}, bf16[320,2048]{1,0:T(8,128)(2,1)}, u32[]{:S(2)}, u32[]{:S(2)}) collective-permute-start(bf16[320,2048]{1,0:T(8,128)(2,1)} %wo_own_ref), channel_id=1, source_target_pairs={{0,1},{1,0},{2,3},{3,2},{4,5},{5,4},{6,7},{7,6},{8,9},{9,8},{10,11... | collective-permute-start | bytes 3932168 | tf_op jit(solution)/shard_map/ppermute | solution.py:34
  57.8 6.6 %collective-permute-start.3 = (bf16[2,2,2,8,256]{4,3,2,1,0:T(8,128)(2,1)S(1)}, bf16[2,2,2,8,256]{4,3,2,1,0:T(8,128)(2,1)S(1)}, u32[]{:S(2)}, u32[]{:S(2)}) collective-permute-start(bf16[2,2,2,8,256]{4,3,2,1,0:T(8,128)(2,1)S(1)} %pad_maximum_fusion.1), channel_id=1, source_target_pairs={{0,64},{16,80},{32,96},{48,112},{64,0},{80,16},{96,32},{112,48},{1... | collective-permute-start | bytes 98312 | tf_op jit(solution)/shard_map/ppermute | solution.py:45
  65.2 33.3 %all-to-all-start.2 = ((bf16[4,8,2,8,256]{4,1,3,2,0:T(8,128)(2,1)}), bf16[4,8,2,8,256]{4,1,3,2,0:T(8,128)(2,1)S(1)}, u32[]{:S(2)}, u32[]{:S(2)}) async-start(bf16[4,8,2,8,256]{4,1,3,2,0:T(8,128)(2,1)} %broadcast_in_dim.8), calls=%async_computation.2 | async-start | bytes 524288 | tf_op jit(solution)/shard_map/all_to_all | solution.py:28
  88.3 41.0 %copy-start.3 = (s32[8]{0:T(128)S(1)}, s32[8]{0:T(128)}, u32[]{:S(2)}) copy-start(s32[8]{0:T(128)} %ids_ref.3) | copy-start | bytes 100
  98.6 30.7 %all-to-all-start.3 = ((bf16[16,512,128]{2,1,0:T(8,128)(2,1)}), bf16[16,512,128]{2,1,0:T(8,128)(2,1)S(1)}, u32[]{:S(2)}, u32[]{:S(2)}) async-start(bf16[16,512,128]{2,1,0:T(8,128)(2,1)} %ffn.1), calls=%async_computation.3 | async-start | bytes 4194304 | tf_op jit(solution)/shard_map/all_to_all | solution.py:28
  103.3 5.6 %collective-permute-start.7 = (bf16[8,128,64]{2,1,0:T(8,128)(2,1)S(1)}, bf16[8,128,64]{2,1,0:T(8,128)(2,1)S(1)}, u32[]{:S(2)}, u32[]{:S(2)}) collective-permute-start(bf16[8,128,64]{2,1,0:T(8,128)(2,1)S(1)} %squeeze.12.down_ref), channel_id=1, source_target_pairs={{0,1},{1,0},{2,3},{3,2},{4,5},{5,4},{6,7},{7,6},{8,9},{9,8},{10,11... | collective-permute-start | bytes 393224 | tf_op jit(solution)/shard_map/ppermute | solution.py:34
  131.2 17.1 %copy-start.1 = (bf16[1024,128]{1,0:T(8,128)(2,1)S(1)}, bf16[1024,128]{1,0:T(8,128)(2,1)}, u32[]{:S(2)}) copy-start(bf16[1024,128]{1,0:T(8,128)(2,1)} %tokens_ref.1) | copy-start | bytes 786436
  131.2 17.1 %copy-start.2 = (bf16[512,128]{1,0:T(8,128)(2,1)S(1)}, bf16[512,128]{1,0:T(8,128)(2,1)}, u32[]{:S(2)}) copy-start(bf16[512,128]{1,0:T(8,128)(2,1)} %get-tuple-element.32.mine_ref) | copy-start | bytes 393220
  131.2 11.9 %all-to-all-start.4 = ((bf16[8,256,128]{2,1,0:T(8,128)(2,1)}), bf16[8,256,128]{2,1,0:T(8,128)(2,1)S(1)}, u32[]{:S(2)}, u32[]{:S(2)}) async-start(bf16[8,256,128]{2,1,0:T(8,128)(2,1)} %get-tuple-element.34), calls=%async_computation.4 | async-start | bytes 1048576 | tf_op jit(solution)/shard_map/all_to_all | solution.py:28
  135.1 12.6 %collective-permute-start.8 = (bf16[512,128]{1,0:T(8,128)(2,1)}, bf16[512,128]{1,0:T(8,128)(2,1)S(1)}, u32[]{:S(2)}, u32[]{:S(2)}) collective-permute-start(bf16[512,128]{1,0:T(8,128)(2,1)} %get-tuple-element.33), channel_id=1, source_target_pairs={{0,1},{1,0},{2,3},{3,2},{4,5},{5,4},{6,7},{7,6},{8,9},{9,8},{10,11... | collective-permute-start | bytes 393224 | tf_op jit(solution)/shard_map/ppermute | solution.py:34
  143.2 5.1 %collective-permute-start.9 = (bf16[256,128]{1,0:T(8,128)(2,1)S(1)}, bf16[256,128]{1,0:T(8,128)(2,1)S(1)}, u32[]{:S(2)}, u32[]{:S(2)}) collective-permute-start(bf16[256,128]{1,0:T(8,128)(2,1)S(1)} %relu_sum.1.squeezed_ref), channel_id=1, source_target_pairs={{0,1},{1,0},{2,3},{3,2},{4,5},{5,4},{6,7},{7,6},{8,9},{9,8},{10,11... | collective-permute-start | bytes 196616 | tf_op jit(solution)/shard_map/ppermute | solution.py:34

commit v7 on v5

--- a/solution.py
+++ b/solution.py
@@ -339,12 +339,11 @@
         in_hbm,
     )
 
-    hidden, gate, linear, wo, gen_down = lax.optimization_barrier(
-        (hidden, wi_gate.T, wi_linear.T, wo_out, gen_down)
-    )
     hidden = exchange(hidden, "mp")
+    hidden, sent, gate, linear, wo, gen_down = lax.optimization_barrier(
+        (hidden, spread(halves, given), wi_gate.T, wi_linear.T, wo_out, gen_down)
+    )
     others = [swap_cores(w) for w in (gate, linear, wo, gen_down)]
-    hidden, sent, others = lax.optimization_barrier((hidden, spread(halves, given), others))
     gate_other, linear_other, wo_other, gen_other = others
     gathered = exchange(sent, "mp", SAME_CORE)
 

time: 125 us -> 121 us (0.968)
  starting transfers between devices: 75.8 us -> 72.2 us
  waiting for transfers between devices: 16.5 us -> 18 us
  local copies, waits for them, and re-layouts: 3.7 us -> 2.3 us
    ppermute x5, starting transfers between devices: 33.3 us -> 27.9 us  [doubling_gather(): theirs = lax.ppermute(held, axis, [(i, i ^ bit) for i in range(size)])]
    ppermute x5, waiting for transfers between devices: 9.72 us -> 13.5 us  [doubling_gather(): theirs = lax.ppermute(held, axis, [(i, i ^ bit) for i in range(size)])]
    all_to_all x3, waiting for transfers between devices: 6.25 us -> 2.62 us  [exchange(): lax.all_to_all(pieces, axis, split_axis=0, concat_axis=0, axis_index_grou...]
    unnamed x15 -> x13, local copies, waits for them, and re-layouts: 1.59 us -> 0.14 us
    all_to_all x3, starting transfers between devices: 11.1 us -> 12.5 us  [exchange(): lax.all_to_all(pieces, axis, split_axis=0, concat_axis=0, axis_index_grou...]
    ppermute x7, waiting for transfers between devices: 0.55 us -> 1.86 us  [swap_cores(): return lax.ppermute(array, 'mp', [(i, i ^ 1) for i in range(MP)])]
  transfers between devices with their start and end apart: 15 -> 15, of which waited for: 8 -> 8; matrix products, arithmetic and copies ran while one was open for 4% -> 3% of each run, Pallas kernels for 9% -> 9%
where the time goes in v7:
time: 121 us; the launch traced here: 120 us
  starting transfers between devices  72.2 us (60%)
  waiting for transfers between devices  18 us (15%)
  Pallas kernels  16.1 us (13%)
  blocking collectives  8.26 us (7%)
  local copies, waits for them, and re-layouts  2.3 us (2%)
  matrix products  1.58 us (1%)
    ppermute x7, starting transfers between devices, swap_cores(): return lax.ppermute(array, 'mp', [(i, i ^ 1) for i in range(MP)])  31.9 us
    ppermute x5, starting transfers between devices, doubling_gather(): theirs = lax.ppermute(held, axis, [(i, i ^ bit) for i in range(size)])  27.9 us
    ppermute x5, waiting for transfers between devices, doubling_gather(): theirs = lax.ppermute(held, axis, [(i, i ^ bit) for i in range(size)])  13.5 us
    all_to_all x3, starting transfers between devices, exchange(): lax.all_to_all(pieces, axis, split_axis=0, concat_axis=0, axis_index_grou...  12.5 us
    pallas_call x1, Pallas kernels, ffn(): pl.pallas_call(ffn_body, out_shape=pltpu.HBM(x.shape, x.dtype), in_specs=...  9.27 us
    all_to_all x1, blocking collectives, exchange(): lax.all_to_all(pieces, axis, split_axis=0, concat_axis=0, axis_index_grou...  8.26 us
    all_to_all x3, waiting for transfers between devices, exchange(): lax.all_to_all(pieces, axis, split_axis=0, concat_axis=0, axis_index_grou...  2.62 us
    pallas_call x3, Pallas kernels, call(): pl.pallas_call(body, out_shape=outs, in_specs=[pl.BlockSpec(memory_space=...  2.58 us
  transfers between devices with their start and end apart: 15, of which 8 were waited for; matrix products, arithmetic and copies ran while one was open for 3% of the time, Pallas kernels for 9%

profile of v7, /device:TPU:1, one launch (start us, length us, event | category | flops | bytes accessed | tf_op | source)
XLA Modules:
  0.0 119.7 jit_solution(10542870212696874670)
XLA Ops:
  0.0 1.0 dynamic-slice_bitcast_fusion
  1.0 8.8 %collective-permute-start = (bf16[512,128]{1,0:T(8,128)(2,1)S(1)}, bf16[512,128]{1,0:T(8,128)(2,1)S(1)}, u32[]{:S(2)}, u32[]{:S(2)}) collective-permute-start(bf16[512,128]{1,0:T(8,128)(2,1)S(1)} %dynamic-slice_bitcast_fusion), channel_id=1, source_target_pairs={{0,1},{1,0},{2,3},{3,2},{4,5},{5,4},{6,7},{7,6},{8,9},{9,8},{10,11... | collective-permute-start | bytes 393224 | tf_op jit(solution)/shard_map/ppermute | solution.py:34
  10.4 0.9 hidden.1
  11.4 0.1 reshape.19
  11.5 8.3 %all_to_all.20 = bf16[16,2,256]{2,1,0:T(2,128)(2,1)S(1)} all-to-all(bf16[16,2,256]{2,1,0:T(2,128)(2,1)S(1)} %reshape.19), channel_id=1, replica_groups=mesh['dp'=32,'mp'=16] {'mp'}, dimensions={0} | all-to-all | bytes 32768 | tf_op jit(solution)/shard_map/all_to_all | solution.py:28
  19.7 0.1 reshape.20
  19.8 2.3 %spread.1 = bf16[16,512,128]{2,1,0:T(8,128)(2,1)} custom-call(bf16[2,512,128]{2,1,0:T(8,128)(2,1)} %bitcast.42, bf16[512,128]{1,0:T(8,128)(2,1)S(1)} %collective-permute-done.given_ref), custom_call_target="tpu_custom_call" | custom-call | tf_op jit(solution)/shard_map/spread/pallas_call | solution.py:90
  22.2 0.0 copy-start.4
  22.2 3.7 %all-to-all-start.1 = ((bf16[16,512,128]{2,1,0:T(8,128)(2,1)}), bf16[16,512,128]{2,1,0:T(8,128)(2,1)S(1)}, u32[]{:S(2)}, u32[]{:S(2)}) async-start(bf16[16,512,128]{2,1,0:T(8,128)(2,1)} %spread.1), calls=%async_computation.1 | async-start | bytes 4194304 | tf_op jit(solution)/shard_map/all_to_all | solution.py:28
  25.9 0.0 copy-start.5
  25.9 2.2 %collective-permute-start.1 = (bf16[320,2048]{1,0:T(8,128)(2,1)}, bf16[320,2048]{1,0:T(8,128)(2,1)}, u32[]{:S(2)}, u32[]{:S(2)}) collective-permute-start(bf16[320,2048]{1,0:T(8,128)(2,1)} %bitcast.43), channel_id=1, source_target_pairs={{0,1},{1,0},{2,3},{3,2},{4,5},{5,4},{6,7},{7,6},{8,9},{9,8},{10,11... | collective-permute-start | bytes 3932168 | tf_op jit(solution)/shard_map/ppermute | solution.py:34
  28.1 2.1 %collective-permute-start.2 = (bf16[320,2048]{1,0:T(8,128)(2,1)}, bf16[320,2048]{1,0:T(8,128)(2,1)}, u32[]{:S(2)}, u32[]{:S(2)}) collective-permute-start(bf16[320,2048]{1,0:T(8,128)(2,1)} %bitcast.45), channel_id=1, source_target_pairs={{0,1},{1,0},{2,3},{3,2},{4,5},{5,4},{6,7},{7,6},{8,9},{9,8},{10,11... | collective-permute-start | bytes 3932168 | tf_op jit(solution)/shard_map/ppermute | solution.py:34
  30.3 2.2 %collective-permute-start.3 = (bf16[320,2048]{1,0:T(8,128)(2,1)}, bf16[320,2048]{1,0:T(8,128)(2,1)}, u32[]{:S(2)}, u32[]{:S(2)}) collective-permute-start(bf16[320,2048]{1,0:T(8,128)(2,1)} %wo_own_ref), channel_id=1, source_target_pairs={{0,1},{1,0},{2,3},{3,2},{4,5},{5,4},{6,7},{7,6},{8,9},{9,8},{10,11... | collective-permute-start | bytes 3932168 | tf_op jit(solution)/shard_map/ppermute | solution.py:34
  32.5 2.1 %collective-permute-start.4 = (bf16[1024,256]{1,0:T(8,128)(2,1)S(1)}, bf16[1024,256]{1,0:T(8,128)(2,1)}, u32[]{:S(2)}, u32[]{:S(2)}) collective-permute-start(bf16[1024,256]{1,0:T(8,128)(2,1)S(1)} %copy-done.4), channel_id=1, source_target_pairs={{0,1},{1,0},{2,3},{3,2},{4,5},{5,4},{6,7},{7,6},{8,9},{9,8},{10,11... | collective-permute-start | bytes 1572872 | tf_op jit(solution)/shard_map/ppermute | solution.py:34
  34.7 0.1 reshape.18
  34.8 0.2 fusion
  34.9 0.2 fusion.1
  35.1 1.3 %collective-permute-done.4 = bf16[1024,256]{1,0:T(8,128)(2,1)} collective-permute-done((bf16[1024,256]{1,0:T(8,128)(2,1)S(1)}, bf16[1024,256]{1,0:T(8,128)(2,1)}, u32[]{:S(2)}, u32[]{:S(2)}) %collective-permute-start.4) | collective-permute-done | bytes 524320 | tf_op jit(solution)/shard_map/ppermute | solution.py:34
  36.4 1.2 %fusion.2 = bf16[1,8,256]{2,1,0:T(8,128)(2,1)S(1)} fusion(bf16[8,1024]{1,0:T(8,128)(2,1)S(1)} %reshape.18, bf16[1024,256]{1,0:T(8,128)(2,1)} %collective-permute-done.4), kind=kOutput, calls=%fused_computation.5 | convolution fusion | flops 4196352 | bytes 544768 | tf_op jit(solution)/shard_map/dot_general | solution.py:18
  37.7 12.9 %collective-permute-start.5 = (bf16[3,8,256]{2,1,0:T(8,128)(2,1)S(1)}, bf16[3,8,256]{2,1,0:T(8,128)(2,1)S(1)}, u32[]{:S(2)}, u32[]{:S(2)}) collective-permute-start(bf16[3,8,256]{2,1,0:T(8,128)(2,1)S(1)} %pad_maximum_fusion.4), channel_id=1, source_target_pairs={{0,256},{16,272},{32,288},{48,304},{64,320},{80,336},{96,352},{112... | collective-permute-start | bytes 36872 | tf_op jit(solution)/shard_map/ppermute | solution.py:42
  50.6 1.1 collective-permute-done.5
  51.7 4.4 %collective-permute-start.6 = (bf16[2,3,8,256]{3,2,1,0:T(8,128)(2,1)S(1)}, bf16[2,3,8,256]{3,2,1,0:T(8,128)(2,1)S(1)}, u32[]{:S(2)}, u32[]{:S(2)}) collective-permute-start(bf16[2,3,8,256]{3,2,1,0:T(8,128)(2,1)S(1)} %pad_maximum_fusion.3), channel_id=1, source_target_pairs={{0,16},{16,0},{32,48},{48,32},{64,80},{80,64},{96,112},{112,96},{1... | collective-permute-start | bytes 73736 | tf_op jit(solution)/shard_map/ppermute | solution.py:42
  56.1 9.3 %ffn.1 = bf16[16,512,128]{2,1,0:T(8,128)(2,1)} custom-call(bf16[16,512,128]{2,1,0:T(8,128)(2,1)S(1)} %all-to-all-done.1.x_ref, bf16[1,2048]{1,0:T(2,128)(2,1)S(1)} %reshape.17.gain_ref, bf16[320,2048]{1,0:T(8,128)(2,1)} %bitcast.44, bf16[320,2048]{1,0:T(8,128)(2,1)} %collective-permute-done.1.gate_other_ref, bf16[320,2048]{1,0:T(8,128)(2,1)} %bitcast.46, ...), custom_call_target="tpu_custom_call" | custom-call | tf_op jit(solution)/shard_map/ffn/pallas_call | solution.py:178
  65.4 4.9 %all-to-all-start.2 = ((bf16[16,512,128]{2,1,0:T(8,128)(2,1)}), bf16[16,512,128]{2,1,0:T(8,128)(2,1)S(1)}, u32[]{:S(2)}, u32[]{:S(2)}) async-start(bf16[16,512,128]{2,1,0:T(8,128)(2,1)} %ffn.1), calls=%async_computation.2 | async-start | bytes 4194304 | tf_op jit(solution)/shard_map/all_to_all | solution.py:28
  70.3 5.4 %collective-permute-start.7 = (bf16[2,2,3,8,256]{4,3,2,1,0:T(8,128)(2,1)S(1)}, bf16[2,2,3,8,256]{4,3,2,1,0:T(8,128)(2,1)S(1)}, u32[]{:S(2)}, u32[]{:S(2)}) collective-permute-start(bf16[2,2,3,8,256]{4,3,2,1,0:T(8,128)(2,1)S(1)} %pad_maximum_fusion.2), channel_id=1, source_target_pairs={{0,128},{16,144},{32,160},{48,176},{64,192},{80,208},{96,224},{112... | collective-permute-start | bytes 147464 | tf_op jit(solution)/shard_map/ppermute | solution.py:42
  75.7 3.3 %collective-permute-done.7 = bf16[2,2,3,8,256]{4,3,2,1,0:T(8,128)(2,1)S(1)} collective-permute-done((bf16[2,2,3,8,256]{4,3,2,1,0:T(8,128)(2,1)S(1)}, bf16[2,2,3,8,256]{4,3,2,1,0:T(8,128)(2,1)S(1)}, u32[]{:S(2)}, u32[]{:S(2)}) %collective-permute-start.7) | collective-permute-done | bytes 49184 | tf_op jit(solution)/shard_map/ppermute | solution.py:42
  79.1 3.2 %collective-permute-start.8 = (bf16[2,2,2,3,8,256]{5,4,3,2,1,0:T(8,128)(2,1)S(1)}, bf16[2,2,2,3,8,256]{5,4,3,2,1,0:T(8,128)(2,1)S(1)}, u32[]{:S(2)}, u32[]{:S(2)}) collective-permute-start(bf16[2,2,2,3,8,256]{5,4,3,2,1,0:T(8,128)(2,1)S(1)} %pad_maximum_fusion.1), channel_id=1, source_target_pairs={{0,64},{16,80},{32,96},{48,112},{64,0},{80,16},{96,32},{112,48},{1... | collective-permute-start | bytes 294920 | tf_op jit(solution)/shard_map/ppermute | solution.py:42
  82.3 4.4 %collective-permute-done.8 = bf16[2,2,2,3,8,256]{5,4,3,2,1,0:T(8,128)(2,1)S(1)} collective-permute-done((bf16[2,2,2,3,8,256]{5,4,3,2,1,0:T(8,128)(2,1)S(1)}, bf16[2,2,2,3,8,256]{5,4,3,2,1,0:T(8,128)(2,1)S(1)}, u32[]{:S(2)}, u32[]{:S(2)}) %collective-permute-start.8) | collective-permute-done | bytes 98336 | tf_op jit(solution)/shard_map/ppermute | solution.py:42
  86.7 1.9 %collective-permute-start.9 = (bf16[2,2,2,2,3,8,256]{6,5,4,3,2,1,0:T(8,128)(2,1)S(1)}, bf16[2,2,2,2,3,8,256]{6,5,4,3,2,1,0:T(8,128)(2,1)S(1)}, u32[]{:S(2)}, u32[]{:S(2)}) collective-permute-start(bf16[2,2,2,2,3,8,256]{6,5,4,3,2,1,0:T(8,128)(2,1)S(1)} %pad_maximum_fusion), channel_id=1, source_target_pairs={{0,32},{16,48},{32,0},{48,16},{64,96},{80,112},{96,64},{112,80},{1... | collective-permute-start | bytes 589832 | tf_op jit(solution)/shard_map/ppermute | solution.py:42
  88.7 4.8 %collective-permute-done.9 = bf16[2,2,2,2,3,8,256]{6,5,4,3,2,1,0:T(8,128)(2,1)S(1)} collective-permute-done((bf16[2,2,2,2,3,8,256]{6,5,4,3,2,1,0:T(8,128)(2,1)S(1)}, bf16[2,2,2,2,3,8,256]{6,5,4,3,2,1,0:T(8,128)(2,1)S(1)}, u32[]{:S(2)}, u32[]{:S(2)}) %collective-permute-start.9) | collective-permute-done | bytes 196640 | tf_op jit(solution)/shard_map/ppermute | solution.py:42
  93.5 0.0 copy-start.3
  93.6 0.1 copy.17
  93.7 0.2 unstack.19.down_ref
  93.9 0.1 copy.18
  94.0 0.2 unstack.21.other_ref
  94.3 2.1 %all-to-all-done.2.parts_ref = bf16[16,512,128]{2,1,0:T(8,128)(2,1)S(1)} async-done(((bf16[16,512,128]{2,1,0:T(8,128)(2,1)}), bf16[16,512,128]{2,1,0:T(8,128)(2,1)S(1)}, u32[]{:S(2)}, u32[]{:S(2)}) %all-to-all-start.2) | async-done | bytes 2097184 | tf_op jit(solution)/shard_map/all_to_all | solution.py:28
  96.4 1.9 %squeeze.6 = (bf16[512,128]{1,0:T(8,128)(2,1)}, bf16[512,128]{1,0:T(8,128)(2,1)}, bf16[8,256,128]{2,1,0:T(8,128)(2,1)}) custom-call(s32[8]{0:T(128)S(1)} %copy-done.3, bf16[16,512,128]{2,1,0:T(8,128)(2,1)S(1)} %all-to-all-done.2.parts_ref, bf16[8,128,64]{2,1,0:T(8,128)(2,1)S(1)} %unstack.19.down_ref, bf16[8,128,64]{2,1,0:T(8,128)(2,1)S(1)} %unstack.21.other_ref), custom_call_target="tpu_custom_call" | custom-call | tf_op jit(solution)/shard_map/squeeze/pallas_call | solution.py:243
  98.3 0.0 copy-start.1
  98.3 0.0 copy-start.2
  98.3 3.9 %all-to-all-start.3 = ((bf16[8,256,128]{2,1,0:T(8,128)(2,1)}), bf16[8,256,128]{2,1,0:T(8,128)(2,1)S(1)}, u32[]{:S(2)}, u32[]{:S(2)}) async-start(bf16[8,256,128]{2,1,0:T(8,128)(2,1)} %get-tuple-element.22), calls=%async_computation.3 | async-start | bytes 1048576 | tf_op jit(solution)/shard_map/all_to_all | solution.py:28
  102.2 6.6 %collective-permute-start.10 = (bf16[512,128]{1,0:T(8,128)(2,1)}, bf16[512,128]{1,0:T(8,128)(2,1)S(1)}, u32[]{:S(2)}, u32[]{:S(2)}) collective-permute-start(bf16[512,128]{1,0:T(8,128)(2,1)} %get-tuple-element.21), channel_id=1, source_target_pairs={{0,1},{1,0},{2,3},{3,2},{4,5},{5,4},{6,7},{7,6},{8,9},{9,8},{10,11... | collective-permute-start | bytes 393224 | tf_op jit(solution)/shard_map/ppermute | solution.py:34
  108.9 0.5 all-to-all-done.3.parts_ref
  109.3 0.1 relu_sum.1.squeezed_ref
  109.4 7.8 %collective-permute-start.11 = (bf16[256,128]{1,0:T(8,128)(2,1)S(1)}, bf16[256,128]{1,0:T(8,128)(2,1)S(1)}, u32[]{:S(2)}, u32[]{:S(2)}) collective-permute-start(bf16[256,128]{1,0:T(8,128)(2,1)S(1)} %relu_sum.1.squeezed_ref), channel_id=1, source_target_pairs={{0,1},{1,0},{2,3},{3,2},{4,5},{5,4},{6,7},{7,6},{8,9},{9,8},{10,11... | collective-permute-start | bytes 196616 | tf_op jit(solution)/shard_map/ppermute | solution.py:34
  117.2 0.1 copy.19
  117.3 0.2 unstack.23.up_ref
  117.6 0.5 collective-permute-done.11.their_squeezed_ref
  118.1 1.6 %expand.1 = bf16[1024,128]{1,0:T(8,128)(2,1)} custom-call(s32[8]{0:T(128)S(1)} %copy-done.3, bf16[1024,128]{1,0:T(8,128)(2,1)S(1)} %copy-done.1, bf16[512,128]{1,0:T(8,128)(2,1)S(1)} %copy-done.2, bf16[512,128]{1,0:T(8,128)(2,1)S(1)} %collective-permute-done.10.theirs_ref, bf16[256,128]{1,0:T(8,128)(2,1)S(1)} %relu_sum.1.squeezed_ref, ...), custom_call_target="tpu_custom_call" | custom-call | tf_op jit(solution)/shard_map/expand/pallas_call | solution.py:61
  (28 shorter events, 0.3 us)
Async XLA Ops:
  0.0 34.9 %copy-start = (bf16[1024,256]{1,0:T(8,128)(2,1)S(1)}, bf16[1024,256]{1,0:T(8,128)(2,1)}, u32[]{:S(2)}) copy-start(bf16[1024,256]{1,0:T(8,128)(2,1)} %param.23) | copy-start | bytes 1572868
  1.0 18.8 %collective-permute-start = (bf16[512,128]{1,0:T(8,128)(2,1)S(1)}, bf16[512,128]{1,0:T(8,128)(2,1)S(1)}, u32[]{:S(2)}, u32[]{:S(2)}) collective-permute-start(bf16[512,128]{1,0:T(8,128)(2,1)S(1)} %dynamic-slice_bitcast_fusion), channel_id=1, source_target_pairs={{0,1},{1,0},{2,3},{3,2},{4,5},{5,4},{6,7},{7,6},{8,9},{9,8},{10,11... | collective-permute-start | bytes 393224 | tf_op jit(solution)/shard_map/ppermute | solution.py:34
  22.2 10.3 %copy-start.4 = (bf16[1024,256]{1,0:T(8,128)(2,1)S(1)}, bf16[1024,256]{1,0:T(8,128)(2,1)}, u32[]{:S(2)}) copy-start(bf16[1024,256]{1,0:T(8,128)(2,1)} %param.22) | copy-start | bytes 1572868
  22.2 33.9 %all-to-all-start.1 = ((bf16[16,512,128]{2,1,0:T(8,128)(2,1)}), bf16[16,512,128]{2,1,0:T(8,128)(2,1)S(1)}, u32[]{:S(2)}, u32[]{:S(2)}) async-start(bf16[16,512,128]{2,1,0:T(8,128)(2,1)} %spread.1), calls=%async_computation.1 | async-start | bytes 4194304 | tf_op jit(solution)/shard_map/all_to_all | solution.py:28
  25.9 30.1 %copy-start.5 = (bf16[2048]{0:T(1024)(128)(2,1)S(1)}, bf16[2048]{0:T(1024)(128)(2,1)}, u32[]{:S(2)}) copy-start(bf16[2048]{0:T(1024)(128)(2,1)} %param.13) | copy-start | bytes 12292
  25.9 30.1 %collective-permute-start.1 = (bf16[320,2048]{1,0:T(8,128)(2,1)}, bf16[320,2048]{1,0:T(8,128)(2,1)}, u32[]{:S(2)}, u32[]{:S(2)}) collective-permute-start(bf16[320,2048]{1,0:T(8,128)(2,1)} %bitcast.43), channel_id=1, source_target_pairs={{0,1},{1,0},{2,3},{3,2},{4,5},{5,4},{6,7},{7,6},{8,9},{9,8},{10,11... | collective-permute-start | bytes 3932168 | tf_op jit(solution)/shard_map/ppermute | solution.py:34
  28.1 27.9 %collective-permute-start.2 = (bf16[320,2048]{1,0:T(8,128)(2,1)}, bf16[320,2048]{1,0:T(8,128)(2,1)}, u32[]{:S(2)}, u32[]{:S(2)}) collective-permute-start(bf16[320,2048]{1,0:T(8,128)(2,1)} %bitcast.45), channel_id=1, source_target_pairs={{0,1},{1,0},{2,3},{3,2},{4,5},{5,4},{6,7},{7,6},{8,9},{9,8},{10,11... | collective-permute-start | bytes 3932168 | tf_op jit(solution)/shard_map/ppermute | solution.py:34
  30.3 25.8 %collective-permute-start.3 = (bf16[320,2048]{1,0:T(8,128)(2,1)}, bf16[320,2048]{1,0:T(8,128)(2,1)}, u32[]{:S(2)}, u32[]{:S(2)}) collective-permute-start(bf16[320,2048]{1,0:T(8,128)(2,1)} %wo_own_ref), channel_id=1, source_target_pairs={{0,1},{1,0},{2,3},{3,2},{4,5},{5,4},{6,7},{7,6},{8,9},{9,8},{10,11... | collective-permute-start | bytes 3932168 | tf_op jit(solution)/shard_map/ppermute | solution.py:34
  32.5 3.9 %collective-permute-start.4 = (bf16[1024,256]{1,0:T(8,128)(2,1)S(1)}, bf16[1024,256]{1,0:T(8,128)(2,1)}, u32[]{:S(2)}, u32[]{:S(2)}) collective-permute-start(bf16[1024,256]{1,0:T(8,128)(2,1)S(1)} %copy-done.4), channel_id=1, source_target_pairs={{0,1},{1,0},{2,3},{3,2},{4,5},{5,4},{6,7},{7,6},{8,9},{9,8},{10,11... | collective-permute-start | bytes 1572872 | tf_op jit(solution)/shard_map/ppermute | solution.py:34
  37.7 14.0 %collective-permute-start.5 = (bf16[3,8,256]{2,1,0:T(8,128)(2,1)S(1)}, bf16[3,8,256]{2,1,0:T(8,128)(2,1)S(1)}, u32[]{:S(2)}, u32[]{:S(2)}) collective-permute-start(bf16[3,8,256]{2,1,0:T(8,128)(2,1)S(1)} %pad_maximum_fusion.4), channel_id=1, source_target_pairs={{0,256},{16,272},{32,288},{48,304},{64,320},{80,336},{96,352},{112... | collective-permute-start | bytes 36872 | tf_op jit(solution)/shard_map/ppermute | solution.py:42
  51.7 18.6 %collective-permute-start.6 = (bf16[2,3,8,256]{3,2,1,0:T(8,128)(2,1)S(1)}, bf16[2,3,8,256]{3,2,1,0:T(8,128)(2,1)S(1)}, u32[]{:S(2)}, u32[]{:S(2)}) collective-permute-start(bf16[2,3,8,256]{3,2,1,0:T(8,128)(2,1)S(1)} %pad_maximum_fusion.3), channel_id=1, source_target_pairs={{0,16},{16,0},{32,48},{48,32},{64,80},{80,64},{96,112},{112,96},{1... | collective-permute-start | bytes 73736 | tf_op jit(solution)/shard_map/ppermute | solution.py:42
  65.4 31.0 %all-to-all-start.2 = ((bf16[16,512,128]{2,1,0:T(8,128)(2,1)}), bf16[16,512,128]{2,1,0:T(8,128)(2,1)S(1)}, u32[]{:S(2)}, u32[]{:S(2)}) async-start(bf16[16,512,128]{2,1,0:T(8,128)(2,1)} %ffn.1), calls=%async_computation.2 | async-start | bytes 4194304 | tf_op jit(solution)/shard_map/all_to_all | solution.py:28
  70.3 8.8 %collective-permute-start.7 = (bf16[2,2,3,8,256]{4,3,2,1,0:T(8,128)(2,1)S(1)}, bf16[2,2,3,8,256]{4,3,2,1,0:T(8,128)(2,1)S(1)}, u32[]{:S(2)}, u32[]{:S(2)}) collective-permute-start(bf16[2,2,3,8,256]{4,3,2,1,0:T(8,128)(2,1)S(1)} %pad_maximum_fusion.2), channel_id=1, source_target_pairs={{0,128},{16,144},{32,160},{48,176},{64,192},{80,208},{96,224},{112... | collective-permute-start | bytes 147464 | tf_op jit(solution)/shard_map/ppermute | solution.py:42
  79.1 7.6 %collective-permute-start.8 = (bf16[2,2,2,3,8,256]{5,4,3,2,1,0:T(8,128)(2,1)S(1)}, bf16[2,2,2,3,8,256]{5,4,3,2,1,0:T(8,128)(2,1)S(1)}, u32[]{:S(2)}, u32[]{:S(2)}) collective-permute-start(bf16[2,2,2,3,8,256]{5,4,3,2,1,0:T(8,128)(2,1)S(1)} %pad_maximum_fusion.1), channel_id=1, source_target_pairs={{0,64},{16,80},{32,96},{48,112},{64,0},{80,16},{96,32},{112,48},{1... | collective-permute-start | bytes 294920 | tf_op jit(solution)/shard_map/ppermute | solution.py:42
  86.7 6.7 %collective-permute-start.9 = (bf16[2,2,2,2,3,8,256]{6,5,4,3,2,1,0:T(8,128)(2,1)S(1)}, bf16[2,2,2,2,3,8,256]{6,5,4,3,2,1,0:T(8,128)(2,1)S(1)}, u32[]{:S(2)}, u32[]{:S(2)}) collective-permute-start(bf16[2,2,2,2,3,8,256]{6,5,4,3,2,1,0:T(8,128)(2,1)S(1)} %pad_maximum_fusion), channel_id=1, source_target_pairs={{0,32},{16,48},{32,0},{48,16},{64,96},{80,112},{96,64},{112,80},{1... | collective-permute-start | bytes 589832 | tf_op jit(solution)/shard_map/ppermute | solution.py:42
  93.5 2.9 %copy-start.3 = (s32[8]{0:T(128)S(1)}, s32[8]{0:T(128)}, u32[]{:S(2)}) copy-start(s32[8]{0:T(128)} %ids_ref.3) | copy-start | bytes 100
  98.3 19.8 %copy-start.1 = (bf16[1024,128]{1,0:T(8,128)(2,1)S(1)}, bf16[1024,128]{1,0:T(8,128)(2,1)}, u32[]{:S(2)}) copy-start(bf16[1024,128]{1,0:T(8,128)(2,1)} %tokens_ref.1) | copy-start | bytes 786436
  98.3 19.8 %copy-start.2 = (bf16[512,128]{1,0:T(8,128)(2,1)S(1)}, bf16[512,128]{1,0:T(8,128)(2,1)}, u32[]{:S(2)}) copy-start(bf16[512,128]{1,0:T(8,128)(2,1)} %get-tuple-element.20.mine_ref) | copy-start | bytes 393220
  98.3 11.0 %all-to-all-start.3 = ((bf16[8,256,128]{2,1,0:T(8,128)(2,1)}), bf16[8,256,128]{2,1,0:T(8,128)(2,1)S(1)}, u32[]{:S(2)}, u32[]{:S(2)}) async-start(bf16[8,256,128]{2,1,0:T(8,128)(2,1)} %get-tuple-element.22), calls=%async_computation.3 | async-start | bytes 1048576 | tf_op jit(solution)/shard_map/all_to_all | solution.py:28
  102.2 15.4 %collective-permute-start.10 = (bf16[512,128]{1,0:T(8,128)(2,1)}, bf16[512,128]{1,0:T(8,128)(2,1)S(1)}, u32[]{:S(2)}, u32[]{:S(2)}) collective-permute-start(bf16[512,128]{1,0:T(8,128)(2,1)} %get-tuple-element.21), channel_id=1, source_target_pairs={{0,1},{1,0},{2,3},{3,2},{4,5},{5,4},{6,7},{7,6},{8,9},{9,8},{10,11... | collective-permute-start | bytes 393224 | tf_op jit(solution)/shard_map/ppermute | solution.py:34
  109.4 8.7 %collective-permute-start.11 = (bf16[256,128]{1,0:T(8,128)(2,1)S(1)}, bf16[256,128]{1,0:T(8,128)(2,1)S(1)}, u32[]{:S(2)}, u32[]{:S(2)}) collective-permute-start(bf16[256,128]{1,0:T(8,128)(2,1)S(1)} %relu_sum.1.squeezed_ref), channel_id=1, source_target_pairs={{0,1},{1,0},{2,3},{3,2},{4,5},{5,4},{6,7},{7,6},{8,9},{9,8},{10,11... | collective-permute-start | bytes 196616 | tf_op jit(solution)/shard_map/ppermute | solution.py:34

commit v8 on v7

--- a/solution.py
+++ b/solution.py
@@ -340,19 +340,23 @@
     )
 
     hidden = exchange(hidden, "mp")
-    hidden, sent, gate, linear, wo, gen_down = lax.optimization_barrier(
-        (hidden, spread(halves, given), wi_gate.T, wi_linear.T, wo_out, gen_down)
-    )
-    others = [swap_cores(w) for w in (gate, linear, wo, gen_down)]
-    gate_other, linear_other, wo_other, gen_other = others
+    hidden, sent, gate, linear, wo = lax.optimization_barrier(
+        (hidden, spread(halves, given), wi_gate.T, wi_linear.T, wo_out)
+    )
+    gate_other, linear_other, wo_other = [swap_cores(w) for w in (gate, linear, wo)]
     gathered = exchange(sent, "mp", SAME_CORE)
 
     hidden = jnp.moveaxis(hidden, 0, 1).reshape(task_count, -1)
-    generators = (gen_down, gen_up, gen_other)
-    made = jnp.stack([matmul(hidden, generator).astype(jnp.bfloat16) for generator in generators])
-    all_tasks = doubling_gather(made, "dp", (16, 1, 8, 4, 2))
-    all_tasks = jnp.transpose(all_tasks, (5, 6, 4, 2, 1, 0, 3, 7))
-    down, up, down_other = all_tasks.reshape(len(generators), task_count, width, R)
+    made_down, made_up = [
+        matmul(hidden, generator).astype(jnp.bfloat16) for generator in (gen_down, gen_up)
+    ]
+    made = jnp.stack([made_down, swap_cores(made_down), made_up])
+    most = doubling_gather(made, "dp", (16, 1, 8, 4))
+    downs = doubling_gather(most[:, :, :, :, :2], "dp", (2,))
+    downs = jnp.transpose(downs, (5, 6, 4, 2, 1, 0, 3, 7))
+    down, down_other = downs.reshape(2, task_count, width, R)
+    ups = doubling_gather(most[:, :, :, :, 2], "dp", (2,))
+    up = jnp.transpose(ups, (5, 4, 2, 1, 0, 3, 6)).reshape(task_count, width, R)
 
     partial = ffn(
         gathered,

time: 121 us -> 118 us (0.975)
  matrix products: 1.58 us -> 0.35 us
    ppermute x7, starting transfers between devices: 31.9 us -> 28.9 us  [swap_cores(): return lax.ppermute(array, 'mp', [(i, i ^ 1) for i in range(MP)])]
    ppermute x5 -> x6, starting transfers between devices: 27.9 us -> 30.5 us  [doubling_gather(): theirs = lax.ppermute(held, axis, [(i, i ^ bit) for i in range(size)])]
    dot_general x3 -> x2, matrix products: 1.58 us -> 0.35 us  [matmul(): return jnp.dot(left, right, preferred_element_type=jnp.float32)]
    ppermute x5 -> x6, waiting for transfers between devices: 13.5 us -> 12.8 us  [doubling_gather(): theirs = lax.ppermute(held, axis, [(i, i ^ bit) for i in range(size)])]
  transfers between devices with their start and end apart: 15 -> 16, of which waited for: 8 -> 7; matrix products, arithmetic and copies ran while one was open for 3% -> 2% of each run, Pallas kernels for 9% -> 9%
where the time goes in v8:
time: 118 us; the launch traced here: 117 us
  starting transfers between devices  71.9 us (61%)
  waiting for transfers between devices  17 us (14%)
  Pallas kernels  16 us (14%)
  blocking collectives  8.26 us (7%)
  local copies, waits for them, and re-layouts  2.29 us (2%)
    ppermute x6, starting transfers between devices, doubling_gather(): theirs = lax.ppermute(held, axis, [(i, i ^ bit) for i in range(size)])  30.5 us
    ppermute x7, starting transfers between devices, swap_cores(): return lax.ppermute(array, 'mp', [(i, i ^ 1) for i in range(MP)])  28.9 us
    ppermute x6, waiting for transfers between devices, doubling_gather(): theirs = lax.ppermute(held, axis, [(i, i ^ bit) for i in range(size)])  12.8 us
    all_to_all x3, starting transfers between devices, exchange(): lax.all_to_all(pieces, axis, split_axis=0, concat_axis=0, axis_index_grou...  12.5 us
    pallas_call x1, Pallas kernels, ffn(): pl.pallas_call(ffn_body, out_shape=pltpu.HBM(x.shape, x.dtype), in_specs=...  9.22 us
    all_to_all x1, blocking collectives, exchange(): lax.all_to_all(pieces, axis, split_axis=0, concat_axis=0, axis_index_grou...  8.26 us
    all_to_all x3, waiting for transfers between devices, exchange(): lax.all_to_all(pieces, axis, split_axis=0, concat_axis=0, axis_index_grou...  2.88 us
    pallas_call x3, Pallas kernels, call(): pl.pallas_call(body, out_shape=outs, in_specs=[pl.BlockSpec(memory_space=...  2.59 us
  transfers between devices with their start and end apart: 16, of which 7 were waited for; matrix products, arithmetic and copies ran while one was open for 2% of the time, Pallas kernels for 9%

profile of v8, /device:TPU:1, one launch (start us, length us, event | category | flops | bytes accessed | tf_op | source)
XLA Modules:
  0.0 117.1 jit_solution(6267056907292740221)
XLA Ops:
  0.0 1.0 dynamic-slice_bitcast_fusion
  1.0 8.8 %collective-permute-start = (bf16[512,128]{1,0:T(8,128)(2,1)S(1)}, bf16[512,128]{1,0:T(8,128)(2,1)S(1)}, u32[]{:S(2)}, u32[]{:S(2)}) collective-permute-start(bf16[512,128]{1,0:T(8,128)(2,1)S(1)} %dynamic-slice_bitcast_fusion), channel_id=1, source_target_pairs={{0,1},{1,0},{2,3},{3,2},{4,5},{5,4},{6,7},{7,6},{8,9},{9,8},{10,11... | collective-permute-start | bytes 393224 | tf_op jit(solution)/shard_map/ppermute | solution.py:34
  10.4 0.9 hidden.1
  11.4 0.1 reshape.21
  11.5 8.3 %all_to_all.20 = bf16[16,2,256]{2,1,0:T(2,128)(2,1)S(1)} all-to-all(bf16[16,2,256]{2,1,0:T(2,128)(2,1)S(1)} %reshape.21), channel_id=1, replica_groups=mesh['dp'=32,'mp'=16] {'mp'}, dimensions={0} | all-to-all | bytes 32768 | tf_op jit(solution)/shard_map/all_to_all | solution.py:28
  19.7 0.1 reshape.22
  19.8 2.2 %spread.1 = bf16[16,512,128]{2,1,0:T(8,128)(2,1)} custom-call(bf16[2,512,128]{2,1,0:T(8,128)(2,1)} %bitcast.46, bf16[512,128]{1,0:T(8,128)(2,1)S(1)} %collective-permute-done.given_ref), custom_call_target="tpu_custom_call" | custom-call | tf_op jit(solution)/shard_map/spread/pallas_call | solution.py:90
  22.1 0.0 copy-start.4
  22.1 3.7 %all-to-all-start.1 = ((bf16[16,512,128]{2,1,0:T(8,128)(2,1)}), bf16[16,512,128]{2,1,0:T(8,128)(2,1)S(1)}, u32[]{:S(2)}, u32[]{:S(2)}) async-start(bf16[16,512,128]{2,1,0:T(8,128)(2,1)} %spread.1), calls=%async_computation.1 | async-start | bytes 4194304 | tf_op jit(solution)/shard_map/all_to_all | solution.py:28
  25.8 0.0 copy-start.5
  25.8 2.3 %collective-permute-start.1 = (bf16[320,2048]{1,0:T(8,128)(2,1)}, bf16[320,2048]{1,0:T(8,128)(2,1)}, u32[]{:S(2)}, u32[]{:S(2)}) collective-permute-start(bf16[320,2048]{1,0:T(8,128)(2,1)} %bitcast.47), channel_id=1, source_target_pairs={{0,1},{1,0},{2,3},{3,2},{4,5},{5,4},{6,7},{7,6},{8,9},{9,8},{10,11... | collective-permute-start | bytes 3932168 | tf_op jit(solution)/shard_map/ppermute | solution.py:34
  28.1 2.1 %collective-permute-start.2 = (bf16[320,2048]{1,0:T(8,128)(2,1)}, bf16[320,2048]{1,0:T(8,128)(2,1)}, u32[]{:S(2)}, u32[]{:S(2)}) collective-permute-start(bf16[320,2048]{1,0:T(8,128)(2,1)} %bitcast.49), channel_id=1, source_target_pairs={{0,1},{1,0},{2,3},{3,2},{4,5},{5,4},{6,7},{7,6},{8,9},{9,8},{10,11... | collective-permute-start | bytes 3932168 | tf_op jit(solution)/shard_map/ppermute | solution.py:34
  30.2 2.3 %collective-permute-start.3 = (bf16[320,2048]{1,0:T(8,128)(2,1)}, bf16[320,2048]{1,0:T(8,128)(2,1)}, u32[]{:S(2)}, u32[]{:S(2)}) collective-permute-start(bf16[320,2048]{1,0:T(8,128)(2,1)} %wo_own_ref), channel_id=1, source_target_pairs={{0,1},{1,0},{2,3},{3,2},{4,5},{5,4},{6,7},{7,6},{8,9},{9,8},{10,11... | collective-permute-start | bytes 3932168 | tf_op jit(solution)/shard_map/ppermute | solution.py:34
  32.5 0.1 reshape.19
  32.6 0.2 convolution_convert_fusion.1
  32.8 2.1 %collective-permute-start.4 = (bf16[8,256]{1,0:T(8,128)(2,1)S(1)}, bf16[8,256]{1,0:T(8,128)(2,1)S(1)}, u32[]{:S(2)}, u32[]{:S(2)}) collective-permute-start(bf16[8,256]{1,0:T(8,128)(2,1)S(1)} %convolution_convert_fusion.1), channel_id=1, source_target_pairs={{0,1},{1,0},{2,3},{3,2},{4,5},{5,4},{6,7},{7,6},{8,9},{9,8},{10,11... | collective-permute-start | bytes 12296 | tf_op jit(solution)/shard_map/ppermute | solution.py:34
  34.8 0.2 fusion
  35.0 0.8 collective-permute-done.4
  35.8 12.9 %collective-permute-start.5 = (bf16[3,8,256]{2,1,0:T(8,128)(2,1)S(1)}, bf16[3,8,256]{2,1,0:T(8,128)(2,1)S(1)}, u32[]{:S(2)}, u32[]{:S(2)}) collective-permute-start(bf16[3,8,256]{2,1,0:T(8,128)(2,1)S(1)} %pad_maximum_fusion.4), channel_id=1, source_target_pairs={{0,256},{16,272},{32,288},{48,304},{64,320},{80,336},{96,352},{112... | collective-permute-start | bytes 36872 | tf_op jit(solution)/shard_map/ppermute | solution.py:42
  48.8 1.1 collective-permute-done.5
  49.9 4.4 %collective-permute-start.6 = (bf16[2,3,8,256]{3,2,1,0:T(8,128)(2,1)S(1)}, bf16[2,3,8,256]{3,2,1,0:T(8,128)(2,1)S(1)}, u32[]{:S(2)}, u32[]{:S(2)}) collective-permute-start(bf16[2,3,8,256]{3,2,1,0:T(8,128)(2,1)S(1)} %pad_maximum_fusion.3), channel_id=1, source_target_pairs={{0,16},{16,0},{32,48},{48,32},{64,80},{80,64},{96,112},{112,96},{1... | collective-permute-start | bytes 73736 | tf_op jit(solution)/shard_map/ppermute | solution.py:42
  54.3 0.0 collective-permute-done.3.wo_other_ref
  54.3 9.2 %ffn.1 = bf16[16,512,128]{2,1,0:T(8,128)(2,1)} custom-call(bf16[16,512,128]{2,1,0:T(8,128)(2,1)S(1)} %all-to-all-done.1.x_ref, bf16[1,2048]{1,0:T(2,128)(2,1)S(1)} %reshape.18.gain_ref, bf16[320,2048]{1,0:T(8,128)(2,1)} %bitcast.48, bf16[320,2048]{1,0:T(8,128)(2,1)} %collective-permute-done.1.gate_other_ref, bf16[320,2048]{1,0:T(8,128)(2,1)} %bitcast.50, ...), custom_call_target="tpu_custom_call" | custom-call | tf_op jit(solution)/shard_map/ffn/pallas_call | solution.py:178
  63.5 4.9 %all-to-all-start.2 = ((bf16[16,512,128]{2,1,0:T(8,128)(2,1)}), bf16[16,512,128]{2,1,0:T(8,128)(2,1)S(1)}, u32[]{:S(2)}, u32[]{:S(2)}) async-start(bf16[16,512,128]{2,1,0:T(8,128)(2,1)} %ffn.1), calls=%async_computation.2 | async-start | bytes 4194304 | tf_op jit(solution)/shard_map/all_to_all | solution.py:28
  68.4 5.4 %collective-permute-start.7 = (bf16[2,2,3,8,256]{4,3,2,1,0:T(8,128)(2,1)S(1)}, bf16[2,2,3,8,256]{4,3,2,1,0:T(8,128)(2,1)S(1)}, u32[]{:S(2)}, u32[]{:S(2)}) collective-permute-start(bf16[2,2,3,8,256]{4,3,2,1,0:T(8,128)(2,1)S(1)} %pad_maximum_fusion.2), channel_id=1, source_target_pairs={{0,128},{16,144},{32,160},{48,176},{64,192},{80,208},{96,224},{112... | collective-permute-start | bytes 147464 | tf_op jit(solution)/shard_map/ppermute | solution.py:42
  73.9 3.3 %collective-permute-done.7 = bf16[2,2,3,8,256]{4,3,2,1,0:T(8,128)(2,1)S(1)} collective-permute-done((bf16[2,2,3,8,256]{4,3,2,1,0:T(8,128)(2,1)S(1)}, bf16[2,2,3,8,256]{4,3,2,1,0:T(8,128)(2,1)S(1)}, u32[]{:S(2)}, u32[]{:S(2)}) %collective-permute-start.7) | collective-permute-done | bytes 49184 | tf_op jit(solution)/shard_map/ppermute | solution.py:42
  77.2 3.2 %collective-permute-start.8 = (bf16[2,2,2,3,8,256]{5,4,3,2,1,0:T(8,128)(2,1)S(1)}, bf16[2,2,2,3,8,256]{5,4,3,2,1,0:T(8,128)(2,1)S(1)}, u32[]{:S(2)}, u32[]{:S(2)}) collective-permute-start(bf16[2,2,2,3,8,256]{5,4,3,2,1,0:T(8,128)(2,1)S(1)} %pad_maximum_fusion), channel_id=1, source_target_pairs={{0,64},{16,80},{32,96},{48,112},{64,0},{80,16},{96,32},{112,48},{1... | collective-permute-start | bytes 294920 | tf_op jit(solution)/shard_map/ppermute | solution.py:42
  80.5 4.4 %collective-permute-done.8 = bf16[2,2,2,3,8,256]{5,4,3,2,1,0:T(8,128)(2,1)S(1)} collective-permute-done((bf16[2,2,2,3,8,256]{5,4,3,2,1,0:T(8,128)(2,1)S(1)}, bf16[2,2,2,3,8,256]{5,4,3,2,1,0:T(8,128)(2,1)S(1)}, u32[]{:S(2)}, u32[]{:S(2)}) %collective-permute-start.8) | collective-permute-done | bytes 98336 | tf_op jit(solution)/shard_map/ppermute | solution.py:42
  84.9 1.9 %collective-permute-start.9 = (bf16[2,2,2,2,2,8,256]{6,5,4,3,2,1,0:T(8,128)(2,1)S(1)}, bf16[2,2,2,2,2,8,256]{6,5,4,3,2,1,0:T(8,128)(2,1)S(1)}, u32[]{:S(2)}, u32[]{:S(2)}) collective-permute-start(bf16[2,2,2,2,2,8,256]{6,5,4,3,2,1,0:T(8,128)(2,1)S(1)} %fusion.1), channel_id=1, source_target_pairs={{0,32},{16,48},{32,0},{48,16},{64,96},{80,112},{96,64},{112,80},{1... | collective-permute-start | bytes 393224 | tf_op jit(solution)/shard_map/ppermute | solution.py:42
  86.8 4.1 %collective-permute-done.9 = bf16[2,2,2,2,2,8,256]{6,5,4,3,2,1,0:T(8,128)(2,1)S(1)} collective-permute-done((bf16[2,2,2,2,2,8,256]{6,5,4,3,2,1,0:T(8,128)(2,1)S(1)}, bf16[2,2,2,2,2,8,256]{6,5,4,3,2,1,0:T(8,128)(2,1)S(1)}, u32[]{:S(2)}, u32[]{:S(2)}) %collective-permute-start.9) | collective-permute-done | bytes 131104 | tf_op jit(solution)/shard_map/ppermute | solution.py:42
  90.9 0.0 copy-start.3
  91.0 0.1 copy.17
  91.1 0.2 unstack.13.down_ref
  91.3 0.1 copy.18
  91.4 0.2 unstack.15.other_ref
  91.6 2.9 %all-to-all-done.2.parts_ref = bf16[16,512,128]{2,1,0:T(8,128)(2,1)S(1)} async-done(((bf16[16,512,128]{2,1,0:T(8,128)(2,1)}), bf16[16,512,128]{2,1,0:T(8,128)(2,1)S(1)}, u32[]{:S(2)}, u32[]{:S(2)}) %all-to-all-start.2) | async-done | bytes 2097184 | tf_op jit(solution)/shard_map/all_to_all | solution.py:28
  94.5 1.9 %squeeze.10 = (bf16[512,128]{1,0:T(8,128)(2,1)}, bf16[512,128]{1,0:T(8,128)(2,1)}, bf16[8,256,128]{2,1,0:T(8,128)(2,1)}) custom-call(s32[8]{0:T(128)S(1)} %copy-done.3, bf16[16,512,128]{2,1,0:T(8,128)(2,1)S(1)} %all-to-all-done.2.parts_ref, bf16[8,128,64]{2,1,0:T(8,128)(2,1)S(1)} %unstack.13.down_ref, bf16[8,128,64]{2,1,0:T(8,128)(2,1)S(1)} %unstack.15.other_ref), custom_call_target="tpu_custom_call" | custom-call | tf_op jit(solution)/shard_map/squeeze/pallas_call | solution.py:243
  96.5 0.0 copy-start.1
  96.5 0.0 copy-start.2
  96.5 3.9 %all-to-all-start.3 = ((bf16[8,256,128]{2,1,0:T(8,128)(2,1)}), bf16[8,256,128]{2,1,0:T(8,128)(2,1)S(1)}, u32[]{:S(2)}, u32[]{:S(2)}) async-start(bf16[8,256,128]{2,1,0:T(8,128)(2,1)} %get-tuple-element.20), calls=%async_computation.3 | async-start | bytes 1048576 | tf_op jit(solution)/shard_map/all_to_all | solution.py:28
  100.4 2.6 %collective-permute-start.12 = (bf16[2,2,2,2,8,256]{5,4,3,2,1,0:T(8,128)(2,1)S(1)}, bf16[2,2,2,2,8,256]{5,4,3,2,1,0:T(8,128)(2,1)S(1)}, u32[]{:S(2)}, u32[]{:S(2)}) collective-permute-start(bf16[2,2,2,2,8,256]{5,4,3,2,1,0:T(8,128)(2,1)S(1)} %fusion.2), channel_id=1, source_target_pairs={{0,32},{16,48},{32,0},{48,16},{64,96},{80,112},{96,64},{112,80},{1... | collective-permute-start | bytes 196616 | tf_op jit(solution)/shard_map/ppermute | solution.py:42
  103.0 5.2 %collective-permute-start.10 = (bf16[512,128]{1,0:T(8,128)(2,1)S(1)}, bf16[512,128]{1,0:T(8,128)(2,1)S(1)}, u32[]{:S(2)}, u32[]{:S(2)}) collective-permute-start(bf16[512,128]{1,0:T(8,128)(2,1)S(1)} %copy-done.6), channel_id=1, source_target_pairs={{0,1},{1,0},{2,3},{3,2},{4,5},{5,4},{6,7},{7,6},{8,9},{9,8},{10,11... | collective-permute-start | bytes 393224 | tf_op jit(solution)/shard_map/ppermute | solution.py:34
  108.3 0.1 relu_sum.1.squeezed_ref
  108.3 6.3 %collective-permute-start.11 = (bf16[256,128]{1,0:T(8,128)(2,1)S(1)}, bf16[256,128]{1,0:T(8,128)(2,1)S(1)}, u32[]{:S(2)}, u32[]{:S(2)}) collective-permute-start(bf16[256,128]{1,0:T(8,128)(2,1)S(1)} %relu_sum.1.squeezed_ref), channel_id=1, source_target_pairs={{0,1},{1,0},{2,3},{3,2},{4,5},{5,4},{6,7},{7,6},{8,9},{9,8},{10,11... | collective-permute-start | bytes 196616 | tf_op jit(solution)/shard_map/ppermute | solution.py:34
  114.6 0.1 copy.19
  114.8 0.2 reshape.20.up_ref
  115.0 0.5 collective-permute-done.11.their_squeezed_ref
  115.5 1.6 %expand.1 = bf16[1024,128]{1,0:T(8,128)(2,1)} custom-call(s32[8]{0:T(128)S(1)} %copy-done.3, bf16[1024,128]{1,0:T(8,128)(2,1)S(1)} %copy-done.1, bf16[512,128]{1,0:T(8,128)(2,1)S(1)} %copy-done.2, bf16[512,128]{1,0:T(8,128)(2,1)S(1)} %collective-permute-done.10.theirs_ref, bf16[256,128]{1,0:T(8,128)(2,1)S(1)} %relu_sum.1.squeezed_ref, ...), custom_call_target="tpu_custom_call" | custom-call | tf_op jit(solution)/shard_map/expand/pallas_call | solution.py:61
  (34 shorter events, 0.3 us)
Async XLA Ops:
  0.0 32.6 %copy-start = (bf16[1024,256]{1,0:T(8,128)(2,1)S(1)}, bf16[1024,256]{1,0:T(8,128)(2,1)}, u32[]{:S(2)}) copy-start(bf16[1024,256]{1,0:T(8,128)(2,1)} %param.22) | copy-start | bytes 1572868
  1.0 18.8 %collective-permute-start = (bf16[512,128]{1,0:T(8,128)(2,1)S(1)}, bf16[512,128]{1,0:T(8,128)(2,1)S(1)}, u32[]{:S(2)}, u32[]{:S(2)}) collective-permute-start(bf16[512,128]{1,0:T(8,128)(2,1)S(1)} %dynamic-slice_bitcast_fusion), channel_id=1, source_target_pairs={{0,1},{1,0},{2,3},{3,2},{4,5},{5,4},{6,7},{7,6},{8,9},{9,8},{10,11... | collective-permute-start | bytes 393224 | tf_op jit(solution)/shard_map/ppermute | solution.py:34
  22.1 12.8 %copy-start.4 = (bf16[1024,256]{1,0:T(8,128)(2,1)S(1)}, bf16[1024,256]{1,0:T(8,128)(2,1)}, u32[]{:S(2)}) copy-start(bf16[1024,256]{1,0:T(8,128)(2,1)} %param.23) | copy-start | bytes 1572868
  22.1 32.2 %all-to-all-start.1 = ((bf16[16,512,128]{2,1,0:T(8,128)(2,1)}), bf16[16,512,128]{2,1,0:T(8,128)(2,1)S(1)}, u32[]{:S(2)}, u32[]{:S(2)}) async-start(bf16[16,512,128]{2,1,0:T(8,128)(2,1)} %spread.1), calls=%async_computation.1 | async-start | bytes 4194304 | tf_op jit(solution)/shard_map/all_to_all | solution.py:28
  25.8 28.4 %copy-start.5 = (bf16[2048]{0:T(1024)(128)(2,1)S(1)}, bf16[2048]{0:T(1024)(128)(2,1)}, u32[]{:S(2)}) copy-start(bf16[2048]{0:T(1024)(128)(2,1)} %param.13) | copy-start | bytes 12292
  25.8 28.4 %collective-permute-start.1 = (bf16[320,2048]{1,0:T(8,128)(2,1)}, bf16[320,2048]{1,0:T(8,128)(2,1)}, u32[]{:S(2)}, u32[]{:S(2)}) collective-permute-start(bf16[320,2048]{1,0:T(8,128)(2,1)} %bitcast.47), channel_id=1, source_target_pairs={{0,1},{1,0},{2,3},{3,2},{4,5},{5,4},{6,7},{7,6},{8,9},{9,8},{10,11... | collective-permute-start | bytes 3932168 | tf_op jit(solution)/shard_map/ppermute | solution.py:34
  28.1 26.1 %collective-permute-start.2 = (bf16[320,2048]{1,0:T(8,128)(2,1)}, bf16[320,2048]{1,0:T(8,128)(2,1)}, u32[]{:S(2)}, u32[]{:S(2)}) collective-permute-start(bf16[320,2048]{1,0:T(8,128)(2,1)} %bitcast.49), channel_id=1, source_target_pairs={{0,1},{1,0},{2,3},{3,2},{4,5},{5,4},{6,7},{7,6},{8,9},{9,8},{10,11... | collective-permute-start | bytes 3932168 | tf_op jit(solution)/shard_map/ppermute | solution.py:34
  30.2 24.1 %collective-permute-start.3 = (bf16[320,2048]{1,0:T(8,128)(2,1)}, bf16[320,2048]{1,0:T(8,128)(2,1)}, u32[]{:S(2)}, u32[]{:S(2)}) collective-permute-start(bf16[320,2048]{1,0:T(8,128)(2,1)} %wo_own_ref), channel_id=1, source_target_pairs={{0,1},{1,0},{2,3},{3,2},{4,5},{5,4},{6,7},{7,6},{8,9},{9,8},{10,11... | collective-permute-start | bytes 3932168 | tf_op jit(solution)/shard_map/ppermute | solution.py:34
  32.8 3.1 %collective-permute-start.4 = (bf16[8,256]{1,0:T(8,128)(2,1)S(1)}, bf16[8,256]{1,0:T(8,128)(2,1)S(1)}, u32[]{:S(2)}, u32[]{:S(2)}) collective-permute-start(bf16[8,256]{1,0:T(8,128)(2,1)S(1)} %convolution_convert_fusion.1), channel_id=1, source_target_pairs={{0,1},{1,0},{2,3},{3,2},{4,5},{5,4},{6,7},{7,6},{8,9},{9,8},{10,11... | collective-permute-start | bytes 12296 | tf_op jit(solution)/shard_map/ppermute | solution.py:34
  35.8 14.0 %collective-permute-start.5 = (bf16[3,8,256]{2,1,0:T(8,128)(2,1)S(1)}, bf16[3,8,256]{2,1,0:T(8,128)(2,1)S(1)}, u32[]{:S(2)}, u32[]{:S(2)}) collective-permute-start(bf16[3,8,256]{2,1,0:T(8,128)(2,1)S(1)} %pad_maximum_fusion.4), channel_id=1, source_target_pairs={{0,256},{16,272},{32,288},{48,304},{64,320},{80,336},{96,352},{112... | collective-permute-start | bytes 36872 | tf_op jit(solution)/shard_map/ppermute | solution.py:42
  49.9 18.5 %collective-permute-start.6 = (bf16[2,3,8,256]{3,2,1,0:T(8,128)(2,1)S(1)}, bf16[2,3,8,256]{3,2,1,0:T(8,128)(2,1)S(1)}, u32[]{:S(2)}, u32[]{:S(2)}) collective-permute-start(bf16[2,3,8,256]{3,2,1,0:T(8,128)(2,1)S(1)} %pad_maximum_fusion.3), channel_id=1, source_target_pairs={{0,16},{16,0},{32,48},{48,32},{64,80},{80,64},{96,112},{112,96},{1... | collective-permute-start | bytes 73736 | tf_op jit(solution)/shard_map/ppermute | solution.py:42
  63.5 31.0 %all-to-all-start.2 = ((bf16[16,512,128]{2,1,0:T(8,128)(2,1)}), bf16[16,512,128]{2,1,0:T(8,128)(2,1)S(1)}, u32[]{:S(2)}, u32[]{:S(2)}) async-start(bf16[16,512,128]{2,1,0:T(8,128)(2,1)} %ffn.1), calls=%async_computation.2 | async-start | bytes 4194304 | tf_op jit(solution)/shard_map/all_to_all | solution.py:28
  68.4 8.8 %collective-permute-start.7 = (bf16[2,2,3,8,256]{4,3,2,1,0:T(8,128)(2,1)S(1)}, bf16[2,2,3,8,256]{4,3,2,1,0:T(8,128)(2,1)S(1)}, u32[]{:S(2)}, u32[]{:S(2)}) collective-permute-start(bf16[2,2,3,8,256]{4,3,2,1,0:T(8,128)(2,1)S(1)} %pad_maximum_fusion.2), channel_id=1, source_target_pairs={{0,128},{16,144},{32,160},{48,176},{64,192},{80,208},{96,224},{112... | collective-permute-start | bytes 147464 | tf_op jit(solution)/shard_map/ppermute | solution.py:42
  77.2 7.6 %collective-permute-start.8 = (bf16[2,2,2,3,8,256]{5,4,3,2,1,0:T(8,128)(2,1)S(1)}, bf16[2,2,2,3,8,256]{5,4,3,2,1,0:T(8,128)(2,1)S(1)}, u32[]{:S(2)}, u32[]{:S(2)}) collective-permute-start(bf16[2,2,2,3,8,256]{5,4,3,2,1,0:T(8,128)(2,1)S(1)} %pad_maximum_fusion), channel_id=1, source_target_pairs={{0,64},{16,80},{32,96},{48,112},{64,0},{80,16},{96,32},{112,48},{1... | collective-permute-start | bytes 294920 | tf_op jit(solution)/shard_map/ppermute | solution.py:42
  84.9 6.0 %collective-permute-start.9 = (bf16[2,2,2,2,2,8,256]{6,5,4,3,2,1,0:T(8,128)(2,1)S(1)}, bf16[2,2,2,2,2,8,256]{6,5,4,3,2,1,0:T(8,128)(2,1)S(1)}, u32[]{:S(2)}, u32[]{:S(2)}) collective-permute-start(bf16[2,2,2,2,2,8,256]{6,5,4,3,2,1,0:T(8,128)(2,1)S(1)} %fusion.1), channel_id=1, source_target_pairs={{0,32},{16,48},{32,0},{48,16},{64,96},{80,112},{96,64},{112,80},{1... | collective-permute-start | bytes 393224 | tf_op jit(solution)/shard_map/ppermute | solution.py:42
  90.9 3.6 %copy-start.3 = (s32[8]{0:T(128)S(1)}, s32[8]{0:T(128)}, u32[]{:S(2)}) copy-start(s32[8]{0:T(128)} %ids_ref.3) | copy-start | bytes 100
  96.5 6.5 %copy-start.6 = (bf16[512,128]{1,0:T(8,128)(2,1)S(1)}, bf16[512,128]{1,0:T(8,128)(2,1)}, u32[]{:S(2)}) copy-start(bf16[512,128]{1,0:T(8,128)(2,1)} %get-tuple-element.19) | copy-start | bytes 393220
  96.5 19.0 %copy-start.1 = (bf16[1024,128]{1,0:T(8,128)(2,1)S(1)}, bf16[1024,128]{1,0:T(8,128)(2,1)}, u32[]{:S(2)}) copy-start(bf16[1024,128]{1,0:T(8,128)(2,1)} %tokens_ref.1) | copy-start | bytes 786436
  96.5 19.0 %copy-start.2 = (bf16[512,128]{1,0:T(8,128)(2,1)S(1)}, bf16[512,128]{1,0:T(8,128)(2,1)}, u32[]{:S(2)}) copy-start(bf16[512,128]{1,0:T(8,128)(2,1)} %get-tuple-element.18.mine_ref) | copy-start | bytes 393220
  96.5 11.8 %all-to-all-start.3 = ((bf16[8,256,128]{2,1,0:T(8,128)(2,1)}), bf16[8,256,128]{2,1,0:T(8,128)(2,1)S(1)}, u32[]{:S(2)}, u32[]{:S(2)}) async-start(bf16[8,256,128]{2,1,0:T(8,128)(2,1)} %get-tuple-element.20), calls=%async_computation.3 | async-start | bytes 1048576 | tf_op jit(solution)/shard_map/all_to_all | solution.py:28
  100.4 7.9 %collective-permute-start.12 = (bf16[2,2,2,2,8,256]{5,4,3,2,1,0:T(8,128)(2,1)S(1)}, bf16[2,2,2,2,8,256]{5,4,3,2,1,0:T(8,128)(2,1)S(1)}, u32[]{:S(2)}, u32[]{:S(2)}) collective-permute-start(bf16[2,2,2,2,8,256]{5,4,3,2,1,0:T(8,128)(2,1)S(1)} %fusion.2), channel_id=1, source_target_pairs={{0,32},{16,48},{32,0},{48,16},{64,96},{80,112},{96,64},{112,80},{1... | collective-permute-start | bytes 196616 | tf_op jit(solution)/shard_map/ppermute | solution.py:42
  103.0 12.0 %collective-permute-start.10 = (bf16[512,128]{1,0:T(8,128)(2,1)S(1)}, bf16[512,128]{1,0:T(8,128)(2,1)S(1)}, u32[]{:S(2)}, u32[]{:S(2)}) collective-permute-start(bf16[512,128]{1,0:T(8,128)(2,1)S(1)} %copy-done.6), channel_id=1, source_target_pairs={{0,1},{1,0},{2,3},{3,2},{4,5},{5,4},{6,7},{7,6},{8,9},{9,8},{10,11... | collective-permute-start | bytes 393224 | tf_op jit(solution)/shard_map/ppermute | solution.py:34
  108.3 7.2 %collective-permute-start.11 = (bf16[256,128]{1,0:T(8,128)(2,1)S(1)}, bf16[256,128]{1,0:T(8,128)(2,1)S(1)}, u32[]{:S(2)}, u32[]{:S(2)}) collective-permute-start(bf16[256,128]{1,0:T(8,128)(2,1)S(1)} %relu_sum.1.squeezed_ref), channel_id=1, source_target_pairs={{0,1},{1,0},{2,3},{3,2},{4,5},{5,4},{6,7},{7,6},{8,9},{9,8},{10,11... | collective-permute-start | bytes 196616 | tf_op jit(solution)/shard_map/ppermute | solution.py:34

commit v9 on v8

--- a/solution.py
+++ b/solution.py
@@ -340,17 +340,17 @@
     )
 
     hidden = exchange(hidden, "mp")
-    hidden, sent, gate, linear, wo = lax.optimization_barrier(
-        (hidden, spread(halves, given), wi_gate.T, wi_linear.T, wo_out)
-    )
-    gate_other, linear_other, wo_other = [swap_cores(w) for w in (gate, linear, wo)]
-    gathered = exchange(sent, "mp", SAME_CORE)
-
     hidden = jnp.moveaxis(hidden, 0, 1).reshape(task_count, -1)
     made_down, made_up = [
         matmul(hidden, generator).astype(jnp.bfloat16) for generator in (gen_down, gen_up)
     ]
     made = jnp.stack([made_down, swap_cores(made_down), made_up])
+    made, sent, gate, linear, wo = lax.optimization_barrier(
+        (made, spread(halves, given), wi_gate.T, wi_linear.T, wo_out)
+    )
+    gate_other, linear_other, wo_other = [swap_cores(w) for w in (gate, linear, wo)]
+    gathered = exchange(sent, "mp", SAME_CORE)
+
     most = doubling_gather(made, "dp", (16, 1, 8, 4))
     downs = doubling_gather(most[:, :, :, :, :2], "dp", (2,))
     downs = jnp.transpose(downs, (5, 6, 4, 2, 1, 0, 3, 7))

time: 118 us -> 117 us (level)
  blocking collectives: 8.26 us -> 0 us
  starting transfers between devices: 71.9 us -> 76 us
  waiting for transfers between devices: 17 us -> 18.2 us
    all_to_all x3 -> x4, starting transfers between devices: 12.5 us -> 21.2 us  [exchange(): lax.all_to_all(pieces, axis, split_axis=0, concat_axis=0, axis_index_grou...]
    all_to_all x1 -> x0, blocking collectives: 8.26 us -> none  [exchange(): lax.all_to_all(pieces, axis, split_axis=0, concat_axis=0, axis_index_grou...]
    ppermute x7, starting transfers between devices: 28.9 us -> 22.7 us  [swap_cores(): return lax.ppermute(array, 'mp', [(i, i ^ 1) for i in range(MP)])]
    all_to_all x3 -> x4, waiting for transfers between devices: 2.88 us -> 8.01 us  [exchange(): lax.all_to_all(pieces, axis, split_axis=0, concat_axis=0, axis_index_grou...]
    ppermute x6, waiting for transfers between devices: 12.8 us -> 9.61 us  [doubling_gather(): theirs = lax.ppermute(held, axis, [(i, i ^ bit) for i in range(size)])]
    ppermute x6, starting transfers between devices: 30.5 us -> 32 us  [doubling_gather(): theirs = lax.ppermute(held, axis, [(i, i ^ bit) for i in range(size)])]
  transfers between devices with their start and end apart: 16 -> 17, of which waited for: 7 -> 8; matrix products, arithmetic and copies ran while one was open for 2% -> 3% of each run, Pallas kernels for 9% -> 8%
where the time goes in v9:
time: 117 us; the launch traced here: 116 us
  starting transfers between devices  76 us (65%)
  waiting for transfers between devices  18.2 us (16%)
  Pallas kernels  16 us (14%)
  local copies, waits for them, and re-layouts  2.84 us (2%)
  matrix products  1.4 us (1%)
    ppermute x6, starting transfers between devices, doubling_gather(): theirs = lax.ppermute(held, axis, [(i, i ^ bit) for i in range(size)])  32 us
    ppermute x7, starting transfers between devices, swap_cores(): return lax.ppermute(array, 'mp', [(i, i ^ 1) for i in range(MP)])  22.7 us
    all_to_all x4, starting transfers between devices, exchange(): lax.all_to_all(pieces, axis, split_axis=0, concat_axis=0, axis_index_grou...  21.2 us
    ppermute x6, waiting for transfers between devices, doubling_gather(): theirs = lax.ppermute(held, axis, [(i, i ^ bit) for i in range(size)])  9.61 us
    pallas_call x1, Pallas kernels, ffn(): pl.pallas_call(ffn_body, out_shape=pltpu.HBM(x.shape, x.dtype), in_specs=...  9.23 us
    all_to_all x4, waiting for transfers between devices, exchange(): lax.all_to_all(pieces, axis, split_axis=0, concat_axis=0, axis_index_grou...  8.01 us
    pallas_call x3, Pallas kernels, call(): pl.pallas_call(body, out_shape=outs, in_specs=[pl.BlockSpec(memory_space=...  2.59 us
  transfers between devices with their start and end apart: 17, of which 8 were waited for; matrix products, arithmetic and copies ran while one was open for 3% of the time, Pallas kernels for 8%

profile of v9, /device:TPU:1, one launch (start us, length us, event | category | flops | bytes accessed | tf_op | source)
XLA Modules:
  0.0 115.7 jit_solution(9038525591381691390)
XLA Ops:
  0.7 0.9 hidden.1
  1.6 0.7 reshape.21
  2.4 10.2 %all-to-all-start = ((bf16[16,2,256]{2,1,0:T(2,128)(2,1)}), bf16[16,2,256]{2,1,0:T(2,128)(2,1)S(1)}, u32[]{:S(2)}, u32[]{:S(2)}) async-start(bf16[16,2,256]{2,1,0:T(2,128)(2,1)} %reshape.21), calls=%async_computation | async-start | bytes 32768 | tf_op jit(solution)/shard_map/all_to_all | solution.py:28
  12.5 0.9 dynamic-slice_bitcast_fusion
  13.4 2.1 %collective-permute-start.1 = (bf16[512,128]{1,0:T(8,128)(2,1)S(1)}, bf16[512,128]{1,0:T(8,128)(2,1)S(1)}, u32[]{:S(2)}, u32[]{:S(2)}) collective-permute-start(bf16[512,128]{1,0:T(8,128)(2,1)S(1)} %dynamic-slice_bitcast_fusion), channel_id=1, source_target_pairs={{0,1},{1,0},{2,3},{3,2},{4,5},{5,4},{6,7},{7,6},{8,9},{9,8},{10,11... | collective-permute-start | bytes 393224 | tf_op jit(solution)/shard_map/ppermute | solution.py:34
  15.6 2.8 %all-to-all-done = bf16[16,2,256]{2,1,0:T(2,128)(2,1)S(1)} async-done(((bf16[16,2,256]{2,1,0:T(2,128)(2,1)}), bf16[16,2,256]{2,1,0:T(2,128)(2,1)S(1)}, u32[]{:S(2)}, u32[]{:S(2)}) %all-to-all-start) | async-done | bytes 16416 | tf_op jit(solution)/shard_map/all_to_all | solution.py:28
  18.4 0.1 reshape.22
  18.5 0.1 reshape.17
  18.6 0.2 convolution_convert_fusion.1
  18.8 2.3 %collective-permute-start = (bf16[8,256]{1,0:T(8,128)(2,1)S(1)}, bf16[8,256]{1,0:T(8,128)(2,1)S(1)}, u32[]{:S(2)}, u32[]{:S(2)}) collective-permute-start(bf16[8,256]{1,0:T(8,128)(2,1)S(1)} %convolution_convert_fusion.1), channel_id=1, source_target_pairs={{0,1},{1,0},{2,3},{3,2},{4,5},{5,4},{6,7},{7,6},{8,9},{9,8},{10,11... | collective-permute-start | bytes 12296 | tf_op jit(solution)/shard_map/ppermute | solution.py:34
  21.1 1.2 %fusion = bf16[1,8,256]{2,1,0:T(8,128)(2,1)S(1)} fusion(bf16[8,1024]{1,0:T(8,128)(2,1)S(1)} %reshape.17, bf16[1024,256]{1,0:T(8,128)(2,1)} %param.23), kind=kOutput, calls=%fused_computation.2 | convolution fusion | flops 4196352 | bytes 544768 | tf_op jit(solution)/shard_map/dot_general | solution.py:18
  22.3 0.0 collective-permute-done.1.given_ref
  22.3 2.2 %spread.1 = bf16[16,512,128]{2,1,0:T(8,128)(2,1)} custom-call(bf16[2,512,128]{2,1,0:T(8,128)(2,1)} %bitcast.46, bf16[512,128]{1,0:T(8,128)(2,1)S(1)} %collective-permute-done.1.given_ref), custom_call_target="tpu_custom_call" | custom-call | tf_op jit(solution)/shard_map/spread/pallas_call | solution.py:90
  24.6 0.0 copy-start.4
  24.6 3.6 %all-to-all-start.1 = ((bf16[16,512,128]{2,1,0:T(8,128)(2,1)}), bf16[16,512,128]{2,1,0:T(8,128)(2,1)S(1)}, u32[]{:S(2)}, u32[]{:S(2)}) async-start(bf16[16,512,128]{2,1,0:T(8,128)(2,1)} %spread.1), calls=%async_computation.1 | async-start | bytes 4194304 | tf_op jit(solution)/shard_map/all_to_all | solution.py:28
  28.2 2.0 %collective-permute-start.2 = (bf16[320,2048]{1,0:T(8,128)(2,1)}, bf16[320,2048]{1,0:T(8,128)(2,1)}, u32[]{:S(2)}, u32[]{:S(2)}) collective-permute-start(bf16[320,2048]{1,0:T(8,128)(2,1)} %bitcast.47), channel_id=1, source_target_pairs={{0,1},{1,0},{2,3},{3,2},{4,5},{5,4},{6,7},{7,6},{8,9},{9,8},{10,11... | collective-permute-start | bytes 3932168 | tf_op jit(solution)/shard_map/ppermute | solution.py:34
  30.2 2.3 %collective-permute-start.3 = (bf16[320,2048]{1,0:T(8,128)(2,1)}, bf16[320,2048]{1,0:T(8,128)(2,1)}, u32[]{:S(2)}, u32[]{:S(2)}) collective-permute-start(bf16[320,2048]{1,0:T(8,128)(2,1)} %bitcast.49), channel_id=1, source_target_pairs={{0,1},{1,0},{2,3},{3,2},{4,5},{5,4},{6,7},{7,6},{8,9},{9,8},{10,11... | collective-permute-start | bytes 3932168 | tf_op jit(solution)/shard_map/ppermute | solution.py:34
  32.6 2.0 %collective-permute-start.4 = (bf16[320,2048]{1,0:T(8,128)(2,1)}, bf16[320,2048]{1,0:T(8,128)(2,1)}, u32[]{:S(2)}, u32[]{:S(2)}) collective-permute-start(bf16[320,2048]{1,0:T(8,128)(2,1)} %wo_own_ref), channel_id=1, source_target_pairs={{0,1},{1,0},{2,3},{3,2},{4,5},{5,4},{6,7},{7,6},{8,9},{9,8},{10,11... | collective-permute-start | bytes 3932168 | tf_op jit(solution)/shard_map/ppermute | solution.py:34
  34.6 12.1 %collective-permute-start.5 = (bf16[3,8,256]{2,1,0:T(8,128)(2,1)S(1)}, bf16[3,8,256]{2,1,0:T(8,128)(2,1)S(1)}, u32[]{:S(2)}, u32[]{:S(2)}) collective-permute-start(bf16[3,8,256]{2,1,0:T(8,128)(2,1)S(1)} %pad_maximum_fusion.4), channel_id=1, source_target_pairs={{0,256},{16,272},{32,288},{48,304},{64,320},{80,336},{96,352},{112... | collective-permute-start | bytes 36872 | tf_op jit(solution)/shard_map/ppermute | solution.py:42
  46.7 1.1 collective-permute-done.5
  47.8 4.4 %collective-permute-start.6 = (bf16[2,3,8,256]{3,2,1,0:T(8,128)(2,1)S(1)}, bf16[2,3,8,256]{3,2,1,0:T(8,128)(2,1)S(1)}, u32[]{:S(2)}, u32[]{:S(2)}) collective-permute-start(bf16[2,3,8,256]{3,2,1,0:T(8,128)(2,1)S(1)} %pad_maximum_fusion.3), channel_id=1, source_target_pairs={{0,16},{16,0},{32,48},{48,32},{64,80},{80,64},{96,112},{112,96},{1... | collective-permute-start | bytes 73736 | tf_op jit(solution)/shard_map/ppermute | solution.py:42
  52.2 2.1 %all-to-all-done.1.x_ref = bf16[16,512,128]{2,1,0:T(8,128)(2,1)S(1)} async-done(((bf16[16,512,128]{2,1,0:T(8,128)(2,1)}), bf16[16,512,128]{2,1,0:T(8,128)(2,1)S(1)}, u32[]{:S(2)}, u32[]{:S(2)}) %all-to-all-start.1) | async-done | bytes 2097184 | tf_op jit(solution)/shard_map/all_to_all | solution.py:28
  54.4 9.2 %ffn.1 = bf16[16,512,128]{2,1,0:T(8,128)(2,1)} custom-call(bf16[16,512,128]{2,1,0:T(8,128)(2,1)S(1)} %all-to-all-done.1.x_ref, bf16[1,2048]{1,0:T(2,128)(2,1)S(1)} %reshape.19.gain_ref, bf16[320,2048]{1,0:T(8,128)(2,1)} %bitcast.48, bf16[320,2048]{1,0:T(8,128)(2,1)} %collective-permute-done.2.gate_other_ref, bf16[320,2048]{1,0:T(8,128)(2,1)} %bitcast.50, ...), custom_call_target="tpu_custom_call" | custom-call | tf_op jit(solution)/shard_map/ffn/pallas_call | solution.py:178
  63.6 3.6 %all-to-all-start.2 = ((bf16[16,512,128]{2,1,0:T(8,128)(2,1)}), bf16[16,512,128]{2,1,0:T(8,128)(2,1)S(1)}, u32[]{:S(2)}, u32[]{:S(2)}) async-start(bf16[16,512,128]{2,1,0:T(8,128)(2,1)} %ffn.1), calls=%async_computation.2 | async-start | bytes 4194304 | tf_op jit(solution)/shard_map/all_to_all | solution.py:28
  67.3 5.5 %collective-permute-start.7 = (bf16[2,2,3,8,256]{4,3,2,1,0:T(8,128)(2,1)S(1)}, bf16[2,2,3,8,256]{4,3,2,1,0:T(8,128)(2,1)S(1)}, u32[]{:S(2)}, u32[]{:S(2)}) collective-permute-start(bf16[2,2,3,8,256]{4,3,2,1,0:T(8,128)(2,1)S(1)} %pad_maximum_fusion.2), channel_id=1, source_target_pairs={{0,128},{16,144},{32,160},{48,176},{64,192},{80,208},{96,224},{112... | collective-permute-start | bytes 147464 | tf_op jit(solution)/shard_map/ppermute | solution.py:42
  72.8 3.3 %collective-permute-done.7 = bf16[2,2,3,8,256]{4,3,2,1,0:T(8,128)(2,1)S(1)} collective-permute-done((bf16[2,2,3,8,256]{4,3,2,1,0:T(8,128)(2,1)S(1)}, bf16[2,2,3,8,256]{4,3,2,1,0:T(8,128)(2,1)S(1)}, u32[]{:S(2)}, u32[]{:S(2)}) %collective-permute-start.7) | collective-permute-done | bytes 49184 | tf_op jit(solution)/shard_map/ppermute | solution.py:42
  76.2 4.0 %collective-permute-start.8 = (bf16[2,2,2,3,8,256]{5,4,3,2,1,0:T(8,128)(2,1)S(1)}, bf16[2,2,2,3,8,256]{5,4,3,2,1,0:T(8,128)(2,1)S(1)}, u32[]{:S(2)}, u32[]{:S(2)}) collective-permute-start(bf16[2,2,2,3,8,256]{5,4,3,2,1,0:T(8,128)(2,1)S(1)} %pad_maximum_fusion), channel_id=1, source_target_pairs={{0,64},{16,80},{32,96},{48,112},{64,0},{80,16},{96,32},{112,48},{1... | collective-permute-start | bytes 294920 | tf_op jit(solution)/shard_map/ppermute | solution.py:42
  80.2 2.6 %collective-permute-done.8 = bf16[2,2,2,3,8,256]{5,4,3,2,1,0:T(8,128)(2,1)S(1)} collective-permute-done((bf16[2,2,2,3,8,256]{5,4,3,2,1,0:T(8,128)(2,1)S(1)}, bf16[2,2,2,3,8,256]{5,4,3,2,1,0:T(8,128)(2,1)S(1)}, u32[]{:S(2)}, u32[]{:S(2)}) %collective-permute-start.8) | collective-permute-done | bytes 98336 | tf_op jit(solution)/shard_map/ppermute | solution.py:42
  82.8 4.2 %collective-permute-start.9 = (bf16[2,2,2,2,2,8,256]{6,5,4,3,2,1,0:T(8,128)(2,1)S(1)}, bf16[2,2,2,2,2,8,256]{6,5,4,3,2,1,0:T(8,128)(2,1)S(1)}, u32[]{:S(2)}, u32[]{:S(2)}) collective-permute-start(bf16[2,2,2,2,2,8,256]{6,5,4,3,2,1,0:T(8,128)(2,1)S(1)} %fusion.1), channel_id=1, source_target_pairs={{0,32},{16,48},{32,0},{48,16},{64,96},{80,112},{96,64},{112,80},{1... | collective-permute-start | bytes 393224 | tf_op jit(solution)/shard_map/ppermute | solution.py:42
  87.0 2.6 %collective-permute-done.9 = bf16[2,2,2,2,2,8,256]{6,5,4,3,2,1,0:T(8,128)(2,1)S(1)} collective-permute-done((bf16[2,2,2,2,2,8,256]{6,5,4,3,2,1,0:T(8,128)(2,1)S(1)}, bf16[2,2,2,2,2,8,256]{6,5,4,3,2,1,0:T(8,128)(2,1)S(1)}, u32[]{:S(2)}, u32[]{:S(2)}) %collective-permute-start.9) | collective-permute-done | bytes 131104 | tf_op jit(solution)/shard_map/ppermute | solution.py:42
  89.6 0.0 copy-start.3
  89.7 0.1 copy.17
  89.8 0.2 unstack.13.down_ref
  90.0 0.1 copy.18
  90.1 0.2 unstack.15.other_ref
  90.3 3.1 %all-to-all-done.2.parts_ref = bf16[16,512,128]{2,1,0:T(8,128)(2,1)S(1)} async-done(((bf16[16,512,128]{2,1,0:T(8,128)(2,1)}), bf16[16,512,128]{2,1,0:T(8,128)(2,1)S(1)}, u32[]{:S(2)}, u32[]{:S(2)}) %all-to-all-start.2) | async-done | bytes 2097184 | tf_op jit(solution)/shard_map/all_to_all | solution.py:28
  93.4 1.9 %squeeze.10 = (bf16[512,128]{1,0:T(8,128)(2,1)}, bf16[512,128]{1,0:T(8,128)(2,1)}, bf16[8,256,128]{2,1,0:T(8,128)(2,1)}) custom-call(s32[8]{0:T(128)S(1)} %copy-done.3, bf16[16,512,128]{2,1,0:T(8,128)(2,1)S(1)} %all-to-all-done.2.parts_ref, bf16[8,128,64]{2,1,0:T(8,128)(2,1)S(1)} %unstack.13.down_ref, bf16[8,128,64]{2,1,0:T(8,128)(2,1)S(1)} %unstack.15.other_ref), custom_call_target="tpu_custom_call" | custom-call | tf_op jit(solution)/shard_map/squeeze/pallas_call | solution.py:243
  95.4 0.0 copy-start.1
  95.4 0.0 copy-start.2
  95.4 3.8 %all-to-all-start.3 = ((bf16[8,256,128]{2,1,0:T(8,128)(2,1)}), bf16[8,256,128]{2,1,0:T(8,128)(2,1)S(1)}, u32[]{:S(2)}, u32[]{:S(2)}) async-start(bf16[8,256,128]{2,1,0:T(8,128)(2,1)} %get-tuple-element.20), calls=%async_computation.3 | async-start | bytes 1048576 | tf_op jit(solution)/shard_map/all_to_all | solution.py:28
  99.2 1.9 %collective-permute-start.12 = (bf16[2,2,2,2,8,256]{5,4,3,2,1,0:T(8,128)(2,1)S(1)}, bf16[2,2,2,2,8,256]{5,4,3,2,1,0:T(8,128)(2,1)S(1)}, u32[]{:S(2)}, u32[]{:S(2)}) collective-permute-start(bf16[2,2,2,2,8,256]{5,4,3,2,1,0:T(8,128)(2,1)S(1)} %fusion.2), channel_id=1, source_target_pairs={{0,32},{16,48},{32,0},{48,16},{64,96},{80,112},{96,64},{112,80},{1... | collective-permute-start | bytes 196616 | tf_op jit(solution)/shard_map/ppermute | solution.py:42
  101.2 5.7 %collective-permute-start.10 = (bf16[512,128]{1,0:T(8,128)(2,1)S(1)}, bf16[512,128]{1,0:T(8,128)(2,1)S(1)}, u32[]{:S(2)}, u32[]{:S(2)}) collective-permute-start(bf16[512,128]{1,0:T(8,128)(2,1)S(1)} %copy-done.5), channel_id=1, source_target_pairs={{0,1},{1,0},{2,3},{3,2},{4,5},{5,4},{6,7},{7,6},{8,9},{9,8},{10,11... | collective-permute-start | bytes 393224 | tf_op jit(solution)/shard_map/ppermute | solution.py:34
  106.9 0.1 relu_sum.1.squeezed_ref
  107.0 6.3 %collective-permute-start.11 = (bf16[256,128]{1,0:T(8,128)(2,1)S(1)}, bf16[256,128]{1,0:T(8,128)(2,1)S(1)}, u32[]{:S(2)}, u32[]{:S(2)}) collective-permute-start(bf16[256,128]{1,0:T(8,128)(2,1)S(1)} %relu_sum.1.squeezed_ref), channel_id=1, source_target_pairs={{0,1},{1,0},{2,3},{3,2},{4,5},{5,4},{6,7},{7,6},{8,9},{9,8},{10,11... | collective-permute-start | bytes 196616 | tf_op jit(solution)/shard_map/ppermute | solution.py:34
  113.3 0.1 copy.19
  113.4 0.2 reshape.20.up_ref
  113.6 0.5 collective-permute-done.11.their_squeezed_ref
  114.1 1.6 %expand.1 = bf16[1024,128]{1,0:T(8,128)(2,1)} custom-call(s32[8]{0:T(128)S(1)} %copy-done.3, bf16[1024,128]{1,0:T(8,128)(2,1)S(1)} %copy-done.1, bf16[512,128]{1,0:T(8,128)(2,1)S(1)} %copy-done.2, bf16[512,128]{1,0:T(8,128)(2,1)S(1)} %collective-permute-done.10.theirs_ref, bf16[256,128]{1,0:T(8,128)(2,1)S(1)} %relu_sum.1.squeezed_ref, ...), custom_call_target="tpu_custom_call" | custom-call | tf_op jit(solution)/shard_map/expand/pallas_call | solution.py:61
  (33 shorter events, 0.3 us)
Async XLA Ops:
  0.0 18.6 %copy-start = (bf16[1024,256]{1,0:T(8,128)(2,1)S(1)}, bf16[1024,256]{1,0:T(8,128)(2,1)}, u32[]{:S(2)}) copy-start(bf16[1024,256]{1,0:T(8,128)(2,1)} %param.22) | copy-start | bytes 1572868
  2.4 16.0 %all-to-all-start = ((bf16[16,2,256]{2,1,0:T(2,128)(2,1)}), bf16[16,2,256]{2,1,0:T(2,128)(2,1)S(1)}, u32[]{:S(2)}, u32[]{:S(2)}) async-start(bf16[16,2,256]{2,1,0:T(2,128)(2,1)} %reshape.21), calls=%async_computation | async-start | bytes 32768 | tf_op jit(solution)/shard_map/all_to_all | solution.py:28
  13.4 8.9 %collective-permute-start.1 = (bf16[512,128]{1,0:T(8,128)(2,1)S(1)}, bf16[512,128]{1,0:T(8,128)(2,1)S(1)}, u32[]{:S(2)}, u32[]{:S(2)}) collective-permute-start(bf16[512,128]{1,0:T(8,128)(2,1)S(1)} %dynamic-slice_bitcast_fusion), channel_id=1, source_target_pairs={{0,1},{1,0},{2,3},{3,2},{4,5},{5,4},{6,7},{7,6},{8,9},{9,8},{10,11... | collective-permute-start | bytes 393224 | tf_op jit(solution)/shard_map/ppermute | solution.py:34
  18.8 3.5 %collective-permute-start = (bf16[8,256]{1,0:T(8,128)(2,1)S(1)}, bf16[8,256]{1,0:T(8,128)(2,1)S(1)}, u32[]{:S(2)}, u32[]{:S(2)}) collective-permute-start(bf16[8,256]{1,0:T(8,128)(2,1)S(1)} %convolution_convert_fusion.1), channel_id=1, source_target_pairs={{0,1},{1,0},{2,3},{3,2},{4,5},{5,4},{6,7},{7,6},{8,9},{9,8},{10,11... | collective-permute-start | bytes 12296 | tf_op jit(solution)/shard_map/ppermute | solution.py:34
  24.6 27.6 %copy-start.4 = (bf16[2048]{0:T(1024)(128)(2,1)S(1)}, bf16[2048]{0:T(1024)(128)(2,1)}, u32[]{:S(2)}) copy-start(bf16[2048]{0:T(1024)(128)(2,1)} %param.13) | copy-start | bytes 12292
  24.6 29.8 %all-to-all-start.1 = ((bf16[16,512,128]{2,1,0:T(8,128)(2,1)}), bf16[16,512,128]{2,1,0:T(8,128)(2,1)S(1)}, u32[]{:S(2)}, u32[]{:S(2)}) async-start(bf16[16,512,128]{2,1,0:T(8,128)(2,1)} %spread.1), calls=%async_computation.1 | async-start | bytes 4194304 | tf_op jit(solution)/shard_map/all_to_all | solution.py:28
  28.2 24.0 %collective-permute-start.2 = (bf16[320,2048]{1,0:T(8,128)(2,1)}, bf16[320,2048]{1,0:T(8,128)(2,1)}, u32[]{:S(2)}, u32[]{:S(2)}) collective-permute-start(bf16[320,2048]{1,0:T(8,128)(2,1)} %bitcast.47), channel_id=1, source_target_pairs={{0,1},{1,0},{2,3},{3,2},{4,5},{5,4},{6,7},{7,6},{8,9},{9,8},{10,11... | collective-permute-start | bytes 3932168 | tf_op jit(solution)/shard_map/ppermute | solution.py:34
  30.2 22.0 %collective-permute-start.3 = (bf16[320,2048]{1,0:T(8,128)(2,1)}, bf16[320,2048]{1,0:T(8,128)(2,1)}, u32[]{:S(2)}, u32[]{:S(2)}) collective-permute-start(bf16[320,2048]{1,0:T(8,128)(2,1)} %bitcast.49), channel_id=1, source_target_pairs={{0,1},{1,0},{2,3},{3,2},{4,5},{5,4},{6,7},{7,6},{8,9},{9,8},{10,11... | collective-permute-start | bytes 3932168 | tf_op jit(solution)/shard_map/ppermute | solution.py:34
  32.6 19.7 %collective-permute-start.4 = (bf16[320,2048]{1,0:T(8,128)(2,1)}, bf16[320,2048]{1,0:T(8,128)(2,1)}, u32[]{:S(2)}, u32[]{:S(2)}) collective-permute-start(bf16[320,2048]{1,0:T(8,128)(2,1)} %wo_own_ref), channel_id=1, source_target_pairs={{0,1},{1,0},{2,3},{3,2},{4,5},{5,4},{6,7},{7,6},{8,9},{9,8},{10,11... | collective-permute-start | bytes 3932168 | tf_op jit(solution)/shard_map/ppermute | solution.py:34
  34.6 13.2 %collective-permute-start.5 = (bf16[3,8,256]{2,1,0:T(8,128)(2,1)S(1)}, bf16[3,8,256]{2,1,0:T(8,128)(2,1)S(1)}, u32[]{:S(2)}, u32[]{:S(2)}) collective-permute-start(bf16[3,8,256]{2,1,0:T(8,128)(2,1)S(1)} %pad_maximum_fusion.4), channel_id=1, source_target_pairs={{0,256},{16,272},{32,288},{48,304},{64,320},{80,336},{96,352},{112... | collective-permute-start | bytes 36872 | tf_op jit(solution)/shard_map/ppermute | solution.py:42
  47.8 19.4 %collective-permute-start.6 = (bf16[2,3,8,256]{3,2,1,0:T(8,128)(2,1)S(1)}, bf16[2,3,8,256]{3,2,1,0:T(8,128)(2,1)S(1)}, u32[]{:S(2)}, u32[]{:S(2)}) collective-permute-start(bf16[2,3,8,256]{3,2,1,0:T(8,128)(2,1)S(1)} %pad_maximum_fusion.3), channel_id=1, source_target_pairs={{0,16},{16,0},{32,48},{48,32},{64,80},{80,64},{96,112},{112,96},{1... | collective-permute-start | bytes 73736 | tf_op jit(solution)/shard_map/ppermute | solution.py:42
  63.6 29.8 %all-to-all-start.2 = ((bf16[16,512,128]{2,1,0:T(8,128)(2,1)}), bf16[16,512,128]{2,1,0:T(8,128)(2,1)S(1)}, u32[]{:S(2)}, u32[]{:S(2)}) async-start(bf16[16,512,128]{2,1,0:T(8,128)(2,1)} %ffn.1), calls=%async_computation.2 | async-start | bytes 4194304 | tf_op jit(solution)/shard_map/all_to_all | solution.py:28
  67.3 8.9 %collective-permute-start.7 = (bf16[2,2,3,8,256]{4,3,2,1,0:T(8,128)(2,1)S(1)}, bf16[2,2,3,8,256]{4,3,2,1,0:T(8,128)(2,1)S(1)}, u32[]{:S(2)}, u32[]{:S(2)}) collective-permute-start(bf16[2,2,3,8,256]{4,3,2,1,0:T(8,128)(2,1)S(1)} %pad_maximum_fusion.2), channel_id=1, source_target_pairs={{0,128},{16,144},{32,160},{48,176},{64,192},{80,208},{96,224},{112... | collective-permute-start | bytes 147464 | tf_op jit(solution)/shard_map/ppermute | solution.py:42
  76.2 6.6 %collective-permute-start.8 = (bf16[2,2,2,3,8,256]{5,4,3,2,1,0:T(8,128)(2,1)S(1)}, bf16[2,2,2,3,8,256]{5,4,3,2,1,0:T(8,128)(2,1)S(1)}, u32[]{:S(2)}, u32[]{:S(2)}) collective-permute-start(bf16[2,2,2,3,8,256]{5,4,3,2,1,0:T(8,128)(2,1)S(1)} %pad_maximum_fusion), channel_id=1, source_target_pairs={{0,64},{16,80},{32,96},{48,112},{64,0},{80,16},{96,32},{112,48},{1... | collective-permute-start | bytes 294920 | tf_op jit(solution)/shard_map/ppermute | solution.py:42
  82.8 6.8 %collective-permute-start.9 = (bf16[2,2,2,2,2,8,256]{6,5,4,3,2,1,0:T(8,128)(2,1)S(1)}, bf16[2,2,2,2,2,8,256]{6,5,4,3,2,1,0:T(8,128)(2,1)S(1)}, u32[]{:S(2)}, u32[]{:S(2)}) collective-permute-start(bf16[2,2,2,2,2,8,256]{6,5,4,3,2,1,0:T(8,128)(2,1)S(1)} %fusion.1), channel_id=1, source_target_pairs={{0,32},{16,48},{32,0},{48,16},{64,96},{80,112},{96,64},{112,80},{1... | collective-permute-start | bytes 393224 | tf_op jit(solution)/shard_map/ppermute | solution.py:42
  89.6 3.8 %copy-start.3 = (s32[8]{0:T(128)S(1)}, s32[8]{0:T(128)}, u32[]{:S(2)}) copy-start(s32[8]{0:T(128)} %ids_ref.3) | copy-start | bytes 100
  95.4 5.8 %copy-start.5 = (bf16[512,128]{1,0:T(8,128)(2,1)S(1)}, bf16[512,128]{1,0:T(8,128)(2,1)}, u32[]{:S(2)}) copy-start(bf16[512,128]{1,0:T(8,128)(2,1)} %get-tuple-element.19) | copy-start | bytes 393220
  95.4 18.8 %copy-start.1 = (bf16[1024,128]{1,0:T(8,128)(2,1)S(1)}, bf16[1024,128]{1,0:T(8,128)(2,1)}, u32[]{:S(2)}) copy-start(bf16[1024,128]{1,0:T(8,128)(2,1)} %tokens_ref.1) | copy-start | bytes 786436
  95.4 18.7 %copy-start.2 = (bf16[512,128]{1,0:T(8,128)(2,1)S(1)}, bf16[512,128]{1,0:T(8,128)(2,1)}, u32[]{:S(2)}) copy-start(bf16[512,128]{1,0:T(8,128)(2,1)} %get-tuple-element.18.mine_ref) | copy-start | bytes 393220
  95.4 11.5 %all-to-all-start.3 = ((bf16[8,256,128]{2,1,0:T(8,128)(2,1)}), bf16[8,256,128]{2,1,0:T(8,128)(2,1)S(1)}, u32[]{:S(2)}, u32[]{:S(2)}) async-start(bf16[8,256,128]{2,1,0:T(8,128)(2,1)} %get-tuple-element.20), calls=%async_computation.3 | async-start | bytes 1048576 | tf_op jit(solution)/shard_map/all_to_all | solution.py:28
  99.2 7.6 %collective-permute-start.12 = (bf16[2,2,2,2,8,256]{5,4,3,2,1,0:T(8,128)(2,1)S(1)}, bf16[2,2,2,2,8,256]{5,4,3,2,1,0:T(8,128)(2,1)S(1)}, u32[]{:S(2)}, u32[]{:S(2)}) collective-permute-start(bf16[2,2,2,2,8,256]{5,4,3,2,1,0:T(8,128)(2,1)S(1)} %fusion.2), channel_id=1, source_target_pairs={{0,32},{16,48},{32,0},{48,16},{64,96},{80,112},{96,64},{112,80},{1... | collective-permute-start | bytes 196616 | tf_op jit(solution)/shard_map/ppermute | solution.py:42
  101.2 12.4 %collective-permute-start.10 = (bf16[512,128]{1,0:T(8,128)(2,1)S(1)}, bf16[512,128]{1,0:T(8,128)(2,1)S(1)}, u32[]{:S(2)}, u32[]{:S(2)}) collective-permute-start(bf16[512,128]{1,0:T(8,128)(2,1)S(1)} %copy-done.5), channel_id=1, source_target_pairs={{0,1},{1,0},{2,3},{3,2},{4,5},{5,4},{6,7},{7,6},{8,9},{9,8},{10,11... | collective-permute-start | bytes 393224 | tf_op jit(solution)/shard_map/ppermute | solution.py:34
  107.0 7.2 %collective-permute-start.11 = (bf16[256,128]{1,0:T(8,128)(2,1)S(1)}, bf16[256,128]{1,0:T(8,128)(2,1)S(1)}, u32[]{:S(2)}, u32[]{:S(2)}) collective-permute-start(bf16[256,128]{1,0:T(8,128)(2,1)S(1)} %relu_sum.1.squeezed_ref), channel_id=1, source_target_pairs={{0,1},{1,0},{2,3},{3,2},{4,5},{5,4},{6,7},{7,6},{8,9},{9,8},{10,11... | collective-permute-start | bytes 196616 | tf_op jit(solution)/shard_map/ppermute | solution.py:34

commit v10 on v9

--- a/solution.py
+++ b/solution.py
@@ -68,20 +68,15 @@
     )(*scalars, *[place(a) for a in arrays])
 
 
-def spread_body(tokens_ref, given_ref, out_ref, kept_ref, load_sem, sems):
+def spread_body(tokens_ref, given_ref, out_ref, sems):
     me = lax.axis_index("mp") % CORES
-    load = pltpu.make_async_copy(tokens_ref.at[me], kept_ref, load_sem)
-    load.start()
     copies = []
     for i in range(CHIPS):
-        second = out_ref.at[CORES * i + 1 - me]
-        copies.append(pltpu.make_async_copy(given_ref, second, sems.at[CHIPS + i]))
-        copies[i].start()
-    load.wait()
-    for i in range(CHIPS):
-        first = out_ref.at[CORES * i + me]
-        copies.append(pltpu.make_async_copy(kept_ref, first, sems.at[i]))
-        copies[CHIPS + i].start()
+        first, second = out_ref.at[CORES * i + me], out_ref.at[CORES * i + 1 - me]
+        copies.append(pltpu.make_async_copy(tokens_ref.at[me], first, sems.at[CORES * i]))
+        copies.append(pltpu.make_async_copy(given_ref, second, sems.at[CORES * i + 1]))
+    for copy in copies:
+        copy.start()
     for copy in copies:
         copy.wait()
 
@@ -90,15 +85,11 @@
     return pl.pallas_call(
         spread_body,
         out_shape=pltpu.HBM((MP, *given.shape), given.dtype),
-        in_specs=[pl.BlockSpec(memory_space=pltpu.HBM), whole(given)],
+        in_specs=[whole(halves), whole(given)],
         out_specs=pl.BlockSpec(memory_space=pltpu.HBM),
-        scratch_shapes=[
-            pltpu.VMEM(given.shape, given.dtype),
-            pltpu.SemaphoreType.DMA(()),
-            pltpu.SemaphoreType.DMA((MP,)),
-        ],
+        scratch_shapes=[pltpu.SemaphoreType.DMA((MP,))],
         name="spread",
-    )(in_hbm(halves), in_vmem(given))
+    )(in_vmem(halves), in_vmem(given))
 
 
 def ffn_body(
@@ -303,8 +294,10 @@
     row = layer_table_ref[pl.ds(layer_ref[0], 1)]
     embed = jnp.concatenate([task_table, jnp.broadcast_to(row, task_table.shape)], axis=1)
     hidden = jnp.maximum(matmul_nt(embed.astype(jnp.bfloat16), hyper_in_ref[...]), 0.0)
+    tasks = hidden.shape[0] // 2
+    packed = jnp.concatenate([hidden[:tasks], hidden[tasks:]], axis=1).astype(jnp.bfloat16)
     for i in range(MP):
-        out_ref[i] = hidden.astype(jnp.bfloat16)
+        out_ref[i] = packed
 
 
 def per_device(
@@ -330,16 +323,18 @@
     halves = tokens.reshape(CORES, half, width)
     given = swap_cores(lax.dynamic_index_in_dim(halves, 1 - core, 0, keepdims=False))
 
+    share = hyper_in.shape[1]
     hidden = call(
         "hidden",
         hidden_body,
-        jax.ShapeDtypeStruct((MP, task_count, hyper_in.shape[1]), jnp.bfloat16),
+        jax.ShapeDtypeStruct((MP, task_count // 2, 2 * share), jnp.bfloat16),
         (task_table, layer_table, hyper_in.T),
         (layer_index,),
         in_hbm,
     )
 
     hidden = exchange(hidden, "mp")
+    hidden = jnp.concatenate([hidden[:, :, :share], hidden[:, :, share:]], axis=1)
     hidden = jnp.moveaxis(hidden, 0, 1).reshape(task_count, -1)
     made_down, made_up = [
         matmul(hidden, generator).astype(jnp.bfloat16) for generator in (gen_down, gen_up)

time: 117 us -> 117 us (level)
  waiting for transfers between devices: 18.2 us -> 16.8 us
    another operation x5, local copies, waits for them, and re-layouts: 0.65 us -> 2.23 us  [per_device(): down, down_other = downs.reshape(2, task_count, width, R)]
    all_to_all x4, waiting for transfers between devices: 8.01 us -> 6.63 us  [exchange(): lax.all_to_all(pieces, axis, split_axis=0, concat_axis=0, axis_index_grou...]
  transfers between devices with their start and end apart: 17 -> 17, of which waited for: 8 -> 8; matrix products, arithmetic and copies ran while one was open for 3% -> 5% of each run, Pallas kernels for 8% -> 8%
where the time goes in v10:
time: 117 us
  starting transfers between devices  76.6 us (65%)
  waiting for transfers between devices  16.8 us (14%)
  Pallas kernels  15.9 us (14%)
  local copies, waits for them, and re-layouts  3.69 us (3%)
  matrix products  1.4 us (1%)
  between operations  1.18 us (1%)
    ppermute x6, starting transfers between devices, doubling_gather(): theirs = lax.ppermute(held, axis, [(i, i ^ bit) for i in range(size)])  33 us
    ppermute x7, starting transfers between devices, swap_cores(): return lax.ppermute(array, 'mp', [(i, i ^ 1) for i in range(MP)])  22.4 us
    all_to_all x4, starting transfers between devices, exchange(): lax.all_to_all(pieces, axis, split_axis=0, concat_axis=0, axis_index_grou...  21.2 us
    ppermute x6, waiting for transfers between devices, doubling_gather(): theirs = lax.ppermute(held, axis, [(i, i ^ bit) for i in range(size)])  9.61 us
    pallas_call x1, Pallas kernels, ffn(): pl.pallas_call(ffn_body, out_shape=pltpu.HBM(x.shape, x.dtype), in_specs=...  9.22 us
    all_to_all x4, waiting for transfers between devices, exchange(): lax.all_to_all(pieces, axis, split_axis=0, concat_axis=0, axis_index_grou...  6.63 us
    pallas_call x3, Pallas kernels, call(): pl.pallas_call(body, out_shape=outs, in_specs=[pl.BlockSpec(memory_space=...  3.27 us
  transfers between devices with their start and end apart: 17, of which 8 were waited for; matrix products, arithmetic and copies ran while one was open for 5% of the time, Pallas kernels for 8%

profile of v10, /device:TPU:1, one launch (start us, length us, event | category | flops | bytes accessed | tf_op | source)
XLA Modules:
  0.0 116.5 jit_solution(14330119015815327878)
XLA Ops:
  0.7 1.6 %hidden.1 = bf16[16,4,128]{2,1,0:T(4,128)(2,1)} custom-call(s32[1]{0:T(128)S(6)} %copy.20.layer_ref, f32[8,64]{1,0:T(8,128)} %task_table_ref.1, f32[24,64]{1,0:T(8,128)} %layer_table_ref.1, bf16[64,128]{1,0:T(8,128)(2,1)} %bitcast.53), custom_call_target="tpu_custom_call" | custom-call | tf_op jit(solution)/shard_map/hidden/pallas_call | solution.py:61
  2.3 10.2 %all-to-all-start = ((bf16[16,4,128]{2,1,0:T(4,128)(2,1)}), bf16[16,4,128]{2,1,0:T(4,128)(2,1)S(1)}, u32[]{:S(2)}, u32[]{:S(2)}) async-start(bf16[16,4,128]{2,1,0:T(4,128)(2,1)} %hidden.1), calls=%async_computation | async-start | bytes 32768 | tf_op jit(solution)/shard_map/all_to_all | solution.py:28
  12.5 0.9 dynamic-slice_bitcast_fusion
  13.4 2.1 %collective-permute-start.1 = (bf16[512,128]{1,0:T(8,128)(2,1)S(1)}, bf16[512,128]{1,0:T(8,128)(2,1)S(1)}, u32[]{:S(2)}, u32[]{:S(2)}) collective-permute-start(bf16[512,128]{1,0:T(8,128)(2,1)S(1)} %dynamic-slice_bitcast_fusion), channel_id=1, source_target_pairs={{0,1},{1,0},{2,3},{3,2},{4,5},{5,4},{6,7},{7,6},{8,9},{9,8},{10,11... | collective-permute-start | bytes 393224 | tf_op jit(solution)/shard_map/ppermute | solution.py:34
  15.6 2.8 %all-to-all-done = bf16[16,4,128]{2,1,0:T(4,128)(2,1)S(1)} async-done(((bf16[16,4,128]{2,1,0:T(4,128)(2,1)}), bf16[16,4,128]{2,1,0:T(4,128)(2,1)S(1)}, u32[]{:S(2)}, u32[]{:S(2)}) %all-to-all-start) | async-done | bytes 16416 | tf_op jit(solution)/shard_map/all_to_all | solution.py:28
  18.4 0.1 fusion.4
  18.5 0.1 reshape.17
  18.6 0.2 convolution_convert_fusion.1
  18.8 2.3 %collective-permute-start = (bf16[8,256]{1,0:T(8,128)(2,1)S(1)}, bf16[8,256]{1,0:T(8,128)(2,1)S(1)}, u32[]{:S(2)}, u32[]{:S(2)}) collective-permute-start(bf16[8,256]{1,0:T(8,128)(2,1)S(1)} %convolution_convert_fusion.1), channel_id=1, source_target_pairs={{0,1},{1,0},{2,3},{3,2},{4,5},{5,4},{6,7},{7,6},{8,9},{9,8},{10,11... | collective-permute-start | bytes 12296 | tf_op jit(solution)/shard_map/ppermute | solution.py:34
  21.1 1.2 %fusion = bf16[1,8,256]{2,1,0:T(8,128)(2,1)S(1)} fusion(bf16[8,1024]{1,0:T(8,128)(2,1)S(1)} %reshape.17, bf16[1024,256]{1,0:T(8,128)(2,1)} %param.23), kind=kOutput, calls=%fused_computation.2 | convolution fusion | flops 4196352 | bytes 544768 | tf_op jit(solution)/shard_map/dot_general | solution.py:18
  22.3 1.5 %spread.1 = bf16[16,512,128]{2,1,0:T(8,128)(2,1)} custom-call(bf16[2,512,128]{2,1,0:T(8,128)(2,1)S(1)} %bitcast.47, bf16[512,128]{1,0:T(8,128)(2,1)S(1)} %collective-permute-done.1.given_ref), custom_call_target="tpu_custom_call" | custom-call | tf_op jit(solution)/shard_map/spread/pallas_call | solution.py:85
  23.8 0.0 copy-start.5
  23.9 3.6 %all-to-all-start.1 = ((bf16[16,512,128]{2,1,0:T(8,128)(2,1)}), bf16[16,512,128]{2,1,0:T(8,128)(2,1)S(1)}, u32[]{:S(2)}, u32[]{:S(2)}) async-start(bf16[16,512,128]{2,1,0:T(8,128)(2,1)} %spread.1), calls=%async_computation.1 | async-start | bytes 4194304 | tf_op jit(solution)/shard_map/all_to_all | solution.py:28
  27.5 2.0 %collective-permute-start.2 = (bf16[320,2048]{1,0:T(8,128)(2,1)}, bf16[320,2048]{1,0:T(8,128)(2,1)}, u32[]{:S(2)}, u32[]{:S(2)}) collective-permute-start(bf16[320,2048]{1,0:T(8,128)(2,1)} %bitcast.48), channel_id=1, source_target_pairs={{0,1},{1,0},{2,3},{3,2},{4,5},{5,4},{6,7},{7,6},{8,9},{9,8},{10,11... | collective-permute-start | bytes 3932168 | tf_op jit(solution)/shard_map/ppermute | solution.py:34
  29.5 2.3 %collective-permute-start.3 = (bf16[320,2048]{1,0:T(8,128)(2,1)}, bf16[320,2048]{1,0:T(8,128)(2,1)}, u32[]{:S(2)}, u32[]{:S(2)}) collective-permute-start(bf16[320,2048]{1,0:T(8,128)(2,1)} %bitcast.50), channel_id=1, source_target_pairs={{0,1},{1,0},{2,3},{3,2},{4,5},{5,4},{6,7},{7,6},{8,9},{9,8},{10,11... | collective-permute-start | bytes 3932168 | tf_op jit(solution)/shard_map/ppermute | solution.py:34
  31.8 2.0 %collective-permute-start.4 = (bf16[320,2048]{1,0:T(8,128)(2,1)}, bf16[320,2048]{1,0:T(8,128)(2,1)}, u32[]{:S(2)}, u32[]{:S(2)}) collective-permute-start(bf16[320,2048]{1,0:T(8,128)(2,1)} %wo_own_ref), channel_id=1, source_target_pairs={{0,1},{1,0},{2,3},{3,2},{4,5},{5,4},{6,7},{7,6},{8,9},{9,8},{10,11... | collective-permute-start | bytes 3932168 | tf_op jit(solution)/shard_map/ppermute | solution.py:34
  33.9 12.1 %collective-permute-start.5 = (bf16[3,8,256]{2,1,0:T(8,128)(2,1)S(1)}, bf16[3,8,256]{2,1,0:T(8,128)(2,1)S(1)}, u32[]{:S(2)}, u32[]{:S(2)}) collective-permute-start(bf16[3,8,256]{2,1,0:T(8,128)(2,1)S(1)} %pad_maximum_fusion.4), channel_id=1, source_target_pairs={{0,256},{16,272},{32,288},{48,304},{64,320},{80,336},{96,352},{112... | collective-permute-start | bytes 36872 | tf_op jit(solution)/shard_map/ppermute | solution.py:42
  46.0 1.1 collective-permute-done.5
  47.1 4.4 %collective-permute-start.6 = (bf16[2,3,8,256]{3,2,1,0:T(8,128)(2,1)S(1)}, bf16[2,3,8,256]{3,2,1,0:T(8,128)(2,1)S(1)}, u32[]{:S(2)}, u32[]{:S(2)}) collective-permute-start(bf16[2,3,8,256]{3,2,1,0:T(8,128)(2,1)S(1)} %pad_maximum_fusion.3), channel_id=1, source_target_pairs={{0,16},{16,0},{32,48},{48,32},{64,80},{80,64},{96,112},{112,96},{1... | collective-permute-start | bytes 73736 | tf_op jit(solution)/shard_map/ppermute | solution.py:42
  51.5 0.0 collective-permute-done.3.linear_other_ref
  51.5 0.0 collective-permute-done.4.wo_other_ref
  51.5 2.1 %all-to-all-done.1.x_ref = bf16[16,512,128]{2,1,0:T(8,128)(2,1)S(1)} async-done(((bf16[16,512,128]{2,1,0:T(8,128)(2,1)}), bf16[16,512,128]{2,1,0:T(8,128)(2,1)S(1)}, u32[]{:S(2)}, u32[]{:S(2)}) %all-to-all-start.1) | async-done | bytes 2097184 | tf_op jit(solution)/shard_map/all_to_all | solution.py:28
  53.7 9.2 %ffn.1 = bf16[16,512,128]{2,1,0:T(8,128)(2,1)} custom-call(bf16[16,512,128]{2,1,0:T(8,128)(2,1)S(1)} %all-to-all-done.1.x_ref, bf16[1,2048]{1,0:T(2,128)(2,1)S(1)} %reshape.19.gain_ref, bf16[320,2048]{1,0:T(8,128)(2,1)} %bitcast.49, bf16[320,2048]{1,0:T(8,128)(2,1)} %collective-permute-done.2.gate_other_ref, bf16[320,2048]{1,0:T(8,128)(2,1)} %bitcast.51, ...), custom_call_target="tpu_custom_call" | custom-call | tf_op jit(solution)/shard_map/ffn/pallas_call | solution.py:169
  62.9 3.6 %all-to-all-start.2 = ((bf16[16,512,128]{2,1,0:T(8,128)(2,1)}), bf16[16,512,128]{2,1,0:T(8,128)(2,1)S(1)}, u32[]{:S(2)}, u32[]{:S(2)}) async-start(bf16[16,512,128]{2,1,0:T(8,128)(2,1)} %ffn.1), calls=%async_computation.2 | async-start | bytes 4194304 | tf_op jit(solution)/shard_map/all_to_all | solution.py:28
  66.6 5.5 %collective-permute-start.7 = (bf16[2,2,3,8,256]{4,3,2,1,0:T(8,128)(2,1)S(1)}, bf16[2,2,3,8,256]{4,3,2,1,0:T(8,128)(2,1)S(1)}, u32[]{:S(2)}, u32[]{:S(2)}) collective-permute-start(bf16[2,2,3,8,256]{4,3,2,1,0:T(8,128)(2,1)S(1)} %pad_maximum_fusion.2), channel_id=1, source_target_pairs={{0,128},{16,144},{32,160},{48,176},{64,192},{80,208},{96,224},{112... | collective-permute-start | bytes 147464 | tf_op jit(solution)/shard_map/ppermute | solution.py:42
  72.1 3.3 %collective-permute-done.7 = bf16[2,2,3,8,256]{4,3,2,1,0:T(8,128)(2,1)S(1)} collective-permute-done((bf16[2,2,3,8,256]{4,3,2,1,0:T(8,128)(2,1)S(1)}, bf16[2,2,3,8,256]{4,3,2,1,0:T(8,128)(2,1)S(1)}, u32[]{:S(2)}, u32[]{:S(2)}) %collective-permute-start.7) | collective-permute-done | bytes 49184 | tf_op jit(solution)/shard_map/ppermute | solution.py:42
  75.5 4.0 %collective-permute-start.8 = (bf16[2,2,2,3,8,256]{5,4,3,2,1,0:T(8,128)(2,1)S(1)}, bf16[2,2,2,3,8,256]{5,4,3,2,1,0:T(8,128)(2,1)S(1)}, u32[]{:S(2)}, u32[]{:S(2)}) collective-permute-start(bf16[2,2,2,3,8,256]{5,4,3,2,1,0:T(8,128)(2,1)S(1)} %pad_maximum_fusion), channel_id=1, source_target_pairs={{0,64},{16,80},{32,96},{48,112},{64,0},{80,16},{96,32},{112,48},{1... | collective-permute-start | bytes 294920 | tf_op jit(solution)/shard_map/ppermute | solution.py:42
  79.4 2.6 %collective-permute-done.8 = bf16[2,2,2,3,8,256]{5,4,3,2,1,0:T(8,128)(2,1)S(1)} collective-permute-done((bf16[2,2,2,3,8,256]{5,4,3,2,1,0:T(8,128)(2,1)S(1)}, bf16[2,2,2,3,8,256]{5,4,3,2,1,0:T(8,128)(2,1)S(1)}, u32[]{:S(2)}, u32[]{:S(2)}) %collective-permute-start.8) | collective-permute-done | bytes 98336 | tf_op jit(solution)/shard_map/ppermute | solution.py:42
  82.1 3.9 %collective-permute-start.9 = (bf16[2,2,2,2,2,8,256]{6,5,4,3,2,1,0:T(8,128)(2,1)S(1)}, bf16[2,2,2,2,2,8,256]{6,5,4,3,2,1,0:T(8,128)(2,1)S(1)}, u32[]{:S(2)}, u32[]{:S(2)}) collective-permute-start(bf16[2,2,2,2,2,8,256]{6,5,4,3,2,1,0:T(8,128)(2,1)S(1)} %fusion.1), channel_id=1, source_target_pairs={{0,32},{16,48},{32,0},{48,16},{64,96},{80,112},{96,64},{112,80},{1... | collective-permute-start | bytes 393224 | tf_op jit(solution)/shard_map/ppermute | solution.py:42
  86.0 2.6 %collective-permute-done.9 = bf16[2,2,2,2,2,8,256]{6,5,4,3,2,1,0:T(8,128)(2,1)S(1)} collective-permute-done((bf16[2,2,2,2,2,8,256]{6,5,4,3,2,1,0:T(8,128)(2,1)S(1)}, bf16[2,2,2,2,2,8,256]{6,5,4,3,2,1,0:T(8,128)(2,1)S(1)}, u32[]{:S(2)}, u32[]{:S(2)}) %collective-permute-start.9) | collective-permute-done | bytes 131104 | tf_op jit(solution)/shard_map/ppermute | solution.py:42
  88.7 0.0 copy-start.3
  88.8 0.1 copy.17
  88.9 0.2 unstack.13.down_ref
  89.1 0.8 copy.18
  89.8 1.1 unstack.15.other_ref
  91.0 1.7 %all-to-all-done.2.parts_ref = bf16[16,512,128]{2,1,0:T(8,128)(2,1)S(1)} async-done(((bf16[16,512,128]{2,1,0:T(8,128)(2,1)}), bf16[16,512,128]{2,1,0:T(8,128)(2,1)S(1)}, u32[]{:S(2)}, u32[]{:S(2)}) %all-to-all-start.2) | async-done | bytes 2097184 | tf_op jit(solution)/shard_map/all_to_all | solution.py:28
  92.7 1.9 %squeeze.10 = (bf16[512,128]{1,0:T(8,128)(2,1)}, bf16[512,128]{1,0:T(8,128)(2,1)}, bf16[8,256,128]{2,1,0:T(8,128)(2,1)}) custom-call(s32[8]{0:T(128)S(1)} %copy-done.3, bf16[16,512,128]{2,1,0:T(8,128)(2,1)S(1)} %all-to-all-done.2.parts_ref, bf16[8,128,64]{2,1,0:T(8,128)(2,1)S(1)} %unstack.13.down_ref, bf16[8,128,64]{2,1,0:T(8,128)(2,1)S(1)} %unstack.15.other_ref), custom_call_target="tpu_custom_call" | custom-call | tf_op jit(solution)/shard_map/squeeze/pallas_call | solution.py:234
  94.6 0.0 copy-start.2
  94.6 3.8 %all-to-all-start.3 = ((bf16[8,256,128]{2,1,0:T(8,128)(2,1)}), bf16[8,256,128]{2,1,0:T(8,128)(2,1)S(1)}, u32[]{:S(2)}, u32[]{:S(2)}) async-start(bf16[8,256,128]{2,1,0:T(8,128)(2,1)} %get-tuple-element.20), calls=%async_computation.3 | async-start | bytes 1048576 | tf_op jit(solution)/shard_map/all_to_all | solution.py:28
  98.5 0.8 fusion.2
  99.2 3.1 %collective-permute-start.12 = (bf16[2,2,2,2,8,256]{5,4,3,2,1,0:T(8,128)(2,1)S(1)}, bf16[2,2,2,2,8,256]{5,4,3,2,1,0:T(8,128)(2,1)S(1)}, u32[]{:S(2)}, u32[]{:S(2)}) collective-permute-start(bf16[2,2,2,2,8,256]{5,4,3,2,1,0:T(8,128)(2,1)S(1)} %fusion.2), channel_id=1, source_target_pairs={{0,32},{16,48},{32,0},{48,16},{64,96},{80,112},{96,64},{112,80},{1... | collective-permute-start | bytes 196616 | tf_op jit(solution)/shard_map/ppermute | solution.py:42
  102.4 6.0 %collective-permute-start.10 = (bf16[512,128]{1,0:T(8,128)(2,1)S(1)}, bf16[512,128]{1,0:T(8,128)(2,1)S(1)}, u32[]{:S(2)}, u32[]{:S(2)}) collective-permute-start(bf16[512,128]{1,0:T(8,128)(2,1)S(1)} %copy-done.6), channel_id=1, source_target_pairs={{0,1},{1,0},{2,3},{3,2},{4,5},{5,4},{6,7},{7,6},{8,9},{9,8},{10,11... | collective-permute-start | bytes 393224 | tf_op jit(solution)/shard_map/ppermute | solution.py:34
  108.5 0.1 relu_sum.1.squeezed_ref
  108.5 5.5 %collective-permute-start.11 = (bf16[256,128]{1,0:T(8,128)(2,1)S(1)}, bf16[256,128]{1,0:T(8,128)(2,1)S(1)}, u32[]{:S(2)}, u32[]{:S(2)}) collective-permute-start(bf16[256,128]{1,0:T(8,128)(2,1)S(1)} %relu_sum.1.squeezed_ref), channel_id=1, source_target_pairs={{0,1},{1,0},{2,3},{3,2},{4,5},{5,4},{6,7},{7,6},{8,9},{9,8},{10,11... | collective-permute-start | bytes 196616 | tf_op jit(solution)/shard_map/ppermute | solution.py:34
  114.1 0.1 copy.19
  114.2 0.2 reshape.20.up_ref
  114.5 0.5 collective-permute-done.11.their_squeezed_ref
  115.0 1.6 %expand.1 = bf16[1024,128]{1,0:T(8,128)(2,1)} custom-call(s32[8]{0:T(128)S(1)} %copy-done.3, bf16[1024,128]{1,0:T(8,128)(2,1)S(1)} %copy-done.1, bf16[512,128]{1,0:T(8,128)(2,1)S(1)} %copy-done.2, bf16[512,128]{1,0:T(8,128)(2,1)S(1)} %collective-permute-done.10.theirs_ref, bf16[256,128]{1,0:T(8,128)(2,1)S(1)} %relu_sum.1.squeezed_ref, ...), custom_call_target="tpu_custom_call" | custom-call | tf_op jit(solution)/shard_map/expand/pallas_call | solution.py:61
  (35 shorter events, 0.3 us)
Async XLA Ops:
  0.0 18.6 %copy-start = (bf16[1024,256]{1,0:T(8,128)(2,1)S(1)}, bf16[1024,256]{1,0:T(8,128)(2,1)}, u32[]{:S(2)}) copy-start(bf16[1024,256]{1,0:T(8,128)(2,1)} %param.22) | copy-start | bytes 1572868
  0.0 22.3 %copy-start.1 = (bf16[1024,128]{1,0:T(8,128)(2,1)S(1)}, bf16[1024,128]{1,0:T(8,128)(2,1)}, u32[]{:S(2)}) copy-start(bf16[1024,128]{1,0:T(8,128)(2,1)} %tokens_ref.1) | copy-start | bytes 786436
  2.3 16.0 %all-to-all-start = ((bf16[16,4,128]{2,1,0:T(4,128)(2,1)}), bf16[16,4,128]{2,1,0:T(4,128)(2,1)S(1)}, u32[]{:S(2)}, u32[]{:S(2)}) async-start(bf16[16,4,128]{2,1,0:T(4,128)(2,1)} %hidden.1), calls=%async_computation | async-start | bytes 32768 | tf_op jit(solution)/shard_map/all_to_all | solution.py:28
  13.4 8.9 %collective-permute-start.1 = (bf16[512,128]{1,0:T(8,128)(2,1)S(1)}, bf16[512,128]{1,0:T(8,128)(2,1)S(1)}, u32[]{:S(2)}, u32[]{:S(2)}) collective-permute-start(bf16[512,128]{1,0:T(8,128)(2,1)S(1)} %dynamic-slice_bitcast_fusion), channel_id=1, source_target_pairs={{0,1},{1,0},{2,3},{3,2},{4,5},{5,4},{6,7},{7,6},{8,9},{9,8},{10,11... | collective-permute-start | bytes 393224 | tf_op jit(solution)/shard_map/ppermute | solution.py:34
  18.8 3.5 %collective-permute-start = (bf16[8,256]{1,0:T(8,128)(2,1)S(1)}, bf16[8,256]{1,0:T(8,128)(2,1)S(1)}, u32[]{:S(2)}, u32[]{:S(2)}) collective-permute-start(bf16[8,256]{1,0:T(8,128)(2,1)S(1)} %convolution_convert_fusion.1), channel_id=1, source_target_pairs={{0,1},{1,0},{2,3},{3,2},{4,5},{5,4},{6,7},{7,6},{8,9},{9,8},{10,11... | collective-permute-start | bytes 12296 | tf_op jit(solution)/shard_map/ppermute | solution.py:34
  23.8 27.6 %copy-start.5 = (bf16[2048]{0:T(1024)(128)(2,1)S(1)}, bf16[2048]{0:T(1024)(128)(2,1)}, u32[]{:S(2)}) copy-start(bf16[2048]{0:T(1024)(128)(2,1)} %param.13) | copy-start | bytes 12292
  23.9 29.8 %all-to-all-start.1 = ((bf16[16,512,128]{2,1,0:T(8,128)(2,1)}), bf16[16,512,128]{2,1,0:T(8,128)(2,1)S(1)}, u32[]{:S(2)}, u32[]{:S(2)}) async-start(bf16[16,512,128]{2,1,0:T(8,128)(2,1)} %spread.1), calls=%async_computation.1 | async-start | bytes 4194304 | tf_op jit(solution)/shard_map/all_to_all | solution.py:28
  27.5 24.0 %collective-permute-start.2 = (bf16[320,2048]{1,0:T(8,128)(2,1)}, bf16[320,2048]{1,0:T(8,128)(2,1)}, u32[]{:S(2)}, u32[]{:S(2)}) collective-permute-start(bf16[320,2048]{1,0:T(8,128)(2,1)} %bitcast.48), channel_id=1, source_target_pairs={{0,1},{1,0},{2,3},{3,2},{4,5},{5,4},{6,7},{7,6},{8,9},{9,8},{10,11... | collective-permute-start | bytes 3932168 | tf_op jit(solution)/shard_map/ppermute | solution.py:34
  29.5 22.0 %collective-permute-start.3 = (bf16[320,2048]{1,0:T(8,128)(2,1)}, bf16[320,2048]{1,0:T(8,128)(2,1)}, u32[]{:S(2)}, u32[]{:S(2)}) collective-permute-start(bf16[320,2048]{1,0:T(8,128)(2,1)} %bitcast.50), channel_id=1, source_target_pairs={{0,1},{1,0},{2,3},{3,2},{4,5},{5,4},{6,7},{7,6},{8,9},{9,8},{10,11... | collective-permute-start | bytes 3932168 | tf_op jit(solution)/shard_map/ppermute | solution.py:34
  31.8 19.7 %collective-permute-start.4 = (bf16[320,2048]{1,0:T(8,128)(2,1)}, bf16[320,2048]{1,0:T(8,128)(2,1)}, u32[]{:S(2)}, u32[]{:S(2)}) collective-permute-start(bf16[320,2048]{1,0:T(8,128)(2,1)} %wo_own_ref), channel_id=1, source_target_pairs={{0,1},{1,0},{2,3},{3,2},{4,5},{5,4},{6,7},{7,6},{8,9},{9,8},{10,11... | collective-permute-start | bytes 3932168 | tf_op jit(solution)/shard_map/ppermute | solution.py:34
  33.9 13.2 %collective-permute-start.5 = (bf16[3,8,256]{2,1,0:T(8,128)(2,1)S(1)}, bf16[3,8,256]{2,1,0:T(8,128)(2,1)S(1)}, u32[]{:S(2)}, u32[]{:S(2)}) collective-permute-start(bf16[3,8,256]{2,1,0:T(8,128)(2,1)S(1)} %pad_maximum_fusion.4), channel_id=1, source_target_pairs={{0,256},{16,272},{32,288},{48,304},{64,320},{80,336},{96,352},{112... | collective-permute-start | bytes 36872 | tf_op jit(solution)/shard_map/ppermute | solution.py:42
  47.1 19.4 %collective-permute-start.6 = (bf16[2,3,8,256]{3,2,1,0:T(8,128)(2,1)S(1)}, bf16[2,3,8,256]{3,2,1,0:T(8,128)(2,1)S(1)}, u32[]{:S(2)}, u32[]{:S(2)}) collective-permute-start(bf16[2,3,8,256]{3,2,1,0:T(8,128)(2,1)S(1)} %pad_maximum_fusion.3), channel_id=1, source_target_pairs={{0,16},{16,0},{32,48},{48,32},{64,80},{80,64},{96,112},{112,96},{1... | collective-permute-start | bytes 73736 | tf_op jit(solution)/shard_map/ppermute | solution.py:42
  62.9 29.8 %all-to-all-start.2 = ((bf16[16,512,128]{2,1,0:T(8,128)(2,1)}), bf16[16,512,128]{2,1,0:T(8,128)(2,1)S(1)}, u32[]{:S(2)}, u32[]{:S(2)}) async-start(bf16[16,512,128]{2,1,0:T(8,128)(2,1)} %ffn.1), calls=%async_computation.2 | async-start | bytes 4194304 | tf_op jit(solution)/shard_map/all_to_all | solution.py:28
  66.6 8.9 %collective-permute-start.7 = (bf16[2,2,3,8,256]{4,3,2,1,0:T(8,128)(2,1)S(1)}, bf16[2,2,3,8,256]{4,3,2,1,0:T(8,128)(2,1)S(1)}, u32[]{:S(2)}, u32[]{:S(2)}) collective-permute-start(bf16[2,2,3,8,256]{4,3,2,1,0:T(8,128)(2,1)S(1)} %pad_maximum_fusion.2), channel_id=1, source_target_pairs={{0,128},{16,144},{32,160},{48,176},{64,192},{80,208},{96,224},{112... | collective-permute-start | bytes 147464 | tf_op jit(solution)/shard_map/ppermute | solution.py:42
  75.5 6.6 %collective-permute-start.8 = (bf16[2,2,2,3,8,256]{5,4,3,2,1,0:T(8,128)(2,1)S(1)}, bf16[2,2,2,3,8,256]{5,4,3,2,1,0:T(8,128)(2,1)S(1)}, u32[]{:S(2)}, u32[]{:S(2)}) collective-permute-start(bf16[2,2,2,3,8,256]{5,4,3,2,1,0:T(8,128)(2,1)S(1)} %pad_maximum_fusion), channel_id=1, source_target_pairs={{0,64},{16,80},{32,96},{48,112},{64,0},{80,16},{96,32},{112,48},{1... | collective-permute-start | bytes 294920 | tf_op jit(solution)/shard_map/ppermute | solution.py:42
  82.0 6.7 %copy-start.4 = (bf16[1,2,2,2,3,8,256]{6,5,4,3,2,1,0:T(8,128)(2,1)}, bf16[1,2,2,2,3,8,256]{6,5,4,3,2,1,0:T(8,128)(2,1)S(1)}, u32[]{:S(2)}) copy-start(bf16[1,2,2,2,3,8,256]{6,5,4,3,2,1,0:T(8,128)(2,1)S(1)} %get-tuple-element.26) | copy-start | bytes 294916
  82.1 6.6 %collective-permute-start.9 = (bf16[2,2,2,2,2,8,256]{6,5,4,3,2,1,0:T(8,128)(2,1)S(1)}, bf16[2,2,2,2,2,8,256]{6,5,4,3,2,1,0:T(8,128)(2,1)S(1)}, u32[]{:S(2)}, u32[]{:S(2)}) collective-permute-start(bf16[2,2,2,2,2,8,256]{6,5,4,3,2,1,0:T(8,128)(2,1)S(1)} %fusion.1), channel_id=1, source_target_pairs={{0,32},{16,48},{32,0},{48,16},{64,96},{80,112},{96,64},{112,80},{1... | collective-permute-start | bytes 393224 | tf_op jit(solution)/shard_map/ppermute | solution.py:42
  88.7 4.0 %copy-start.3 = (s32[8]{0:T(128)S(1)}, s32[8]{0:T(128)}, u32[]{:S(2)}) copy-start(s32[8]{0:T(128)} %ids_ref.3) | copy-start | bytes 100
  94.6 7.8 %copy-start.6 = (bf16[512,128]{1,0:T(8,128)(2,1)S(1)}, bf16[512,128]{1,0:T(8,128)(2,1)}, u32[]{:S(2)}) copy-start(bf16[512,128]{1,0:T(8,128)(2,1)} %get-tuple-element.19) | copy-start | bytes 393220
  94.6 20.3 %copy-start.2 = (bf16[512,128]{1,0:T(8,128)(2,1)S(1)}, bf16[512,128]{1,0:T(8,128)(2,1)}, u32[]{:S(2)}) copy-start(bf16[512,128]{1,0:T(8,128)(2,1)} %get-tuple-element.18.mine_ref) | copy-start | bytes 393220
  94.6 13.8 %all-to-all-start.3 = ((bf16[8,256,128]{2,1,0:T(8,128)(2,1)}), bf16[8,256,128]{2,1,0:T(8,128)(2,1)S(1)}, u32[]{:S(2)}, u32[]{:S(2)}) async-start(bf16[8,256,128]{2,1,0:T(8,128)(2,1)} %get-tuple-element.20), calls=%async_computation.3 | async-start | bytes 1048576 | tf_op jit(solution)/shard_map/all_to_all | solution.py:28
  99.2 9.2 %collective-permute-start.12 = (bf16[2,2,2,2,8,256]{5,4,3,2,1,0:T(8,128)(2,1)S(1)}, bf16[2,2,2,2,8,256]{5,4,3,2,1,0:T(8,128)(2,1)S(1)}, u32[]{:S(2)}, u32[]{:S(2)}) collective-permute-start(bf16[2,2,2,2,8,256]{5,4,3,2,1,0:T(8,128)(2,1)S(1)} %fusion.2), channel_id=1, source_target_pairs={{0,32},{16,48},{32,0},{48,16},{64,96},{80,112},{96,64},{112,80},{1... | collective-permute-start | bytes 196616 | tf_op jit(solution)/shard_map/ppermute | solution.py:42
  102.4 12.1 %collective-permute-start.10 = (bf16[512,128]{1,0:T(8,128)(2,1)S(1)}, bf16[512,128]{1,0:T(8,128)(2,1)S(1)}, u32[]{:S(2)}, u32[]{:S(2)}) collective-permute-start(bf16[512,128]{1,0:T(8,128)(2,1)S(1)} %copy-done.6), channel_id=1, source_target_pairs={{0,1},{1,0},{2,3},{3,2},{4,5},{5,4},{6,7},{7,6},{8,9},{9,8},{10,11... | collective-permute-start | bytes 393224 | tf_op jit(solution)/shard_map/ppermute | solution.py:34
  108.5 6.4 %collective-permute-start.11 = (bf16[256,128]{1,0:T(8,128)(2,1)S(1)}, bf16[256,128]{1,0:T(8,128)(2,1)S(1)}, u32[]{:S(2)}, u32[]{:S(2)}) collective-permute-start(bf16[256,128]{1,0:T(8,128)(2,1)S(1)} %relu_sum.1.squeezed_ref), channel_id=1, source_target_pairs={{0,1},{1,0},{2,3},{3,2},{4,5},{5,4},{6,7},{7,6},{8,9},{9,8},{10,11... | collective-permute-start | bytes 196616 | tf_op jit(solution)/shard_map/ppermute | solution.py:34

commit v11 on v10

--- a/solution.py
+++ b/solution.py
@@ -68,12 +68,12 @@
     )(*scalars, *[place(a) for a in arrays])
 
 
-def spread_body(tokens_ref, given_ref, out_ref, sems):
+def spread_body(kept_ref, given_ref, out_ref, sems):
     me = lax.axis_index("mp") % CORES
     copies = []
     for i in range(CHIPS):
         first, second = out_ref.at[CORES * i + me], out_ref.at[CORES * i + 1 - me]
-        copies.append(pltpu.make_async_copy(tokens_ref.at[me], first, sems.at[CORES * i]))
+        copies.append(pltpu.make_async_copy(kept_ref, first, sems.at[CORES * i]))
         copies.append(pltpu.make_async_copy(given_ref, second, sems.at[CORES * i + 1]))
     for copy in copies:
         copy.start()
@@ -81,15 +81,15 @@
         copy.wait()
 
 
-def spread(halves, given):
+def spread(kept, given):
     return pl.pallas_call(
         spread_body,
         out_shape=pltpu.HBM((MP, *given.shape), given.dtype),
-        in_specs=[whole(halves), whole(given)],
+        in_specs=[whole(kept), whole(given)],
         out_specs=pl.BlockSpec(memory_space=pltpu.HBM),
         scratch_shapes=[pltpu.SemaphoreType.DMA((MP,))],
         name="spread",
-    )(in_vmem(halves), in_vmem(given))
+    )(in_vmem(kept), in_vmem(given))
 
 
 def ffn_body(
@@ -294,10 +294,8 @@
     row = layer_table_ref[pl.ds(layer_ref[0], 1)]
     embed = jnp.concatenate([task_table, jnp.broadcast_to(row, task_table.shape)], axis=1)
     hidden = jnp.maximum(matmul_nt(embed.astype(jnp.bfloat16), hyper_in_ref[...]), 0.0)
-    tasks = hidden.shape[0] // 2
-    packed = jnp.concatenate([hidden[:tasks], hidden[tasks:]], axis=1).astype(jnp.bfloat16)
     for i in range(MP):
-        out_ref[i] = packed
+        out_ref[i] = hidden.astype(jnp.bfloat16)
 
 
 def per_device(
@@ -321,27 +319,26 @@
     task_count = task_table.shape[0]
 
     halves = tokens.reshape(CORES, half, width)
+    kept = lax.dynamic_index_in_dim(halves, core, 0, keepdims=False)
     given = swap_cores(lax.dynamic_index_in_dim(halves, 1 - core, 0, keepdims=False))
 
-    share = hyper_in.shape[1]
     hidden = call(
         "hidden",
         hidden_body,
-        jax.ShapeDtypeStruct((MP, task_count // 2, 2 * share), jnp.bfloat16),
+        jax.ShapeDtypeStruct((MP, task_count, hyper_in.shape[1]), jnp.bfloat16),
         (task_table, layer_table, hyper_in.T),
         (layer_index,),
         in_hbm,
     )
 
     hidden = exchange(hidden, "mp")
-    hidden = jnp.concatenate([hidden[:, :, :share], hidden[:, :, share:]], axis=1)
     hidden = jnp.moveaxis(hidden, 0, 1).reshape(task_count, -1)
     made_down, made_up = [
         matmul(hidden, generator).astype(jnp.bfloat16) for generator in (gen_down, gen_up)
     ]
     made = jnp.stack([made_down, swap_cores(made_down), made_up])
     made, sent, gate, linear, wo = lax.optimization_barrier(
-        (made, spread(halves, given), wi_gate.T, wi_linear.T, wo_out)
+        (made, spread(kept, given), wi_gate.T, wi_linear.T, wo_out)
     )
     gate_other, linear_other, wo_other = [swap_cores(w) for w in (gate, linear, wo)]
     gathered = exchange(sent, "mp", SAME_CORE)

time: 117 us -> 116 us (level)
  waiting for transfers between devices: 16.8 us -> 19.6 us
  starting transfers between devices: 76.6 us -> 75.4 us
    ppermute x6, starting transfers between devices: 33 us -> 30.8 us  [doubling_gather(): theirs = lax.ppermute(held, axis, [(i, i ^ bit) for i in range(size)])]
    another operation x5, local copies, waits for them, and re-layouts: 2.23 us -> 0.65 us  [per_device(): down, down_other = downs.reshape(2, task_count, width, R)]
    ppermute x6, waiting for transfers between devices: 9.61 us -> 10.8 us  [doubling_gather(): theirs = lax.ppermute(held, axis, [(i, i ^ bit) for i in range(size)])]
  transfers between devices with their start and end apart: 17 -> 17, of which waited for: 8 -> 9; matrix products, arithmetic and copies ran while one was open for 5% -> 2% of each run, Pallas kernels for 8% -> 8%
where the time goes in v11:
time: 116 us; the launch traced here: 115 us
  starting transfers between devices  75.4 us (65%)
  waiting for transfers between devices  19.6 us (17%)
  Pallas kernels  15.2 us (13%)
  local copies, waits for them, and re-layouts  2.91 us (3%)
  between operations  1.18 us (1%)
    ppermute x6, starting transfers between devices, doubling_gather(): theirs = lax.ppermute(held, axis, [(i, i ^ bit) for i in range(size)])  30.8 us
    ppermute x7, starting transfers between devices, swap_cores(): return lax.ppermute(array, 'mp', [(i, i ^ 1) for i in range(MP)])  23.4 us
    all_to_all x4, starting transfers between devices, exchange(): lax.all_to_all(pieces, axis, split_axis=0, concat_axis=0, axis_index_grou...  21.2 us
    ppermute x6, waiting for transfers between devices, doubling_gather(): theirs = lax.ppermute(held, axis, [(i, i ^ bit) for i in range(size)])  10.8 us
    pallas_call x1, Pallas kernels, ffn(): pl.pallas_call(ffn_body, out_shape=pltpu.HBM(x.shape, x.dtype), in_specs=...  9.23 us
    all_to_all x4, waiting for transfers between devices, exchange(): lax.all_to_all(pieces, axis, split_axis=0, concat_axis=0, axis_index_grou...  7.72 us
    pallas_call x3, Pallas kernels, call(): pl.pallas_call(body, out_shape=outs, in_specs=[pl.BlockSpec(memory_space=...  2.59 us
  transfers between devices with their start and end apart: 17, of which 9 were waited for; matrix products, arithmetic and copies ran while one was open for 2% of the time, Pallas kernels for 8%

profile of v11, /device:TPU:1, one launch (start us, length us, event | category | flops | bytes accessed | tf_op | source)
XLA Modules:
  0.0 114.9 jit_solution(3594775907271268576)
XLA Ops:
  0.7 0.9 hidden.1
  1.7 0.7 reshape.21
  2.4 10.2 %all-to-all-start = ((bf16[16,2,256]{2,1,0:T(2,128)(2,1)}), bf16[16,2,256]{2,1,0:T(2,128)(2,1)S(1)}, u32[]{:S(2)}, u32[]{:S(2)}) async-start(bf16[16,2,256]{2,1,0:T(2,128)(2,1)} %reshape.21), calls=%async_computation | async-start | bytes 32768 | tf_op jit(solution)/shard_map/all_to_all | solution.py:28
  12.6 1.0 dynamic-slice_bitcast_fusion
  13.5 2.2 %collective-permute-start.1 = (bf16[512,128]{1,0:T(8,128)(2,1)S(1)}, bf16[512,128]{1,0:T(8,128)(2,1)S(1)}, u32[]{:S(2)}, u32[]{:S(2)}) collective-permute-start(bf16[512,128]{1,0:T(8,128)(2,1)S(1)} %get-tuple-element.25), channel_id=1, source_target_pairs={{0,1},{1,0},{2,3},{3,2},{4,5},{5,4},{6,7},{7,6},{8,9},{9,8},{10,11... | collective-permute-start | bytes 393224 | tf_op jit(solution)/shard_map/ppermute | solution.py:34
  15.7 2.7 %all-to-all-done = bf16[16,2,256]{2,1,0:T(2,128)(2,1)S(1)} async-done(((bf16[16,2,256]{2,1,0:T(2,128)(2,1)}), bf16[16,2,256]{2,1,0:T(2,128)(2,1)S(1)}, u32[]{:S(2)}, u32[]{:S(2)}) %all-to-all-start) | async-done | bytes 16416 | tf_op jit(solution)/shard_map/all_to_all | solution.py:28
  18.4 0.1 reshape.22
  18.5 0.1 reshape.17
  18.6 0.2 convolution_convert_fusion.1
  18.8 2.3 %collective-permute-start = (bf16[8,256]{1,0:T(8,128)(2,1)S(1)}, bf16[8,256]{1,0:T(8,128)(2,1)S(1)}, u32[]{:S(2)}, u32[]{:S(2)}) collective-permute-start(bf16[8,256]{1,0:T(8,128)(2,1)S(1)} %convolution_convert_fusion.1), channel_id=1, source_target_pairs={{0,1},{1,0},{2,3},{3,2},{4,5},{5,4},{6,7},{7,6},{8,9},{9,8},{10,11... | collective-permute-start | bytes 12296 | tf_op jit(solution)/shard_map/ppermute | solution.py:34
  21.1 0.2 fusion
  21.3 0.6 collective-permute-done
  21.9 1.5 %spread.1 = bf16[16,512,128]{2,1,0:T(8,128)(2,1)} custom-call(bf16[512,128]{1,0:T(8,128)(2,1)S(1)} %get-tuple-element.26.kept_ref, bf16[512,128]{1,0:T(8,128)(2,1)S(1)} %collective-permute-done.1.given_ref), custom_call_target="tpu_custom_call" | custom-call | tf_op jit(solution)/shard_map/spread/pallas_call | solution.py:85
  23.4 0.0 copy-start.5
  23.4 3.6 %all-to-all-start.1 = ((bf16[16,512,128]{2,1,0:T(8,128)(2,1)}), bf16[16,512,128]{2,1,0:T(8,128)(2,1)S(1)}, u32[]{:S(2)}, u32[]{:S(2)}) async-start(bf16[16,512,128]{2,1,0:T(8,128)(2,1)} %spread.1), calls=%async_computation.1 | async-start | bytes 4194304 | tf_op jit(solution)/shard_map/all_to_all | solution.py:28
  27.1 2.3 %collective-permute-start.2 = (bf16[320,2048]{1,0:T(8,128)(2,1)}, bf16[320,2048]{1,0:T(8,128)(2,1)}, u32[]{:S(2)}, u32[]{:S(2)}) collective-permute-start(bf16[320,2048]{1,0:T(8,128)(2,1)} %bitcast.48), channel_id=1, source_target_pairs={{0,1},{1,0},{2,3},{3,2},{4,5},{5,4},{6,7},{7,6},{8,9},{9,8},{10,11... | collective-permute-start | bytes 3932168 | tf_op jit(solution)/shard_map/ppermute | solution.py:34
  29.3 2.1 %collective-permute-start.3 = (bf16[320,2048]{1,0:T(8,128)(2,1)}, bf16[320,2048]{1,0:T(8,128)(2,1)}, u32[]{:S(2)}, u32[]{:S(2)}) collective-permute-start(bf16[320,2048]{1,0:T(8,128)(2,1)} %bitcast.50), channel_id=1, source_target_pairs={{0,1},{1,0},{2,3},{3,2},{4,5},{5,4},{6,7},{7,6},{8,9},{9,8},{10,11... | collective-permute-start | bytes 3932168 | tf_op jit(solution)/shard_map/ppermute | solution.py:34
  31.4 2.3 %collective-permute-start.4 = (bf16[320,2048]{1,0:T(8,128)(2,1)}, bf16[320,2048]{1,0:T(8,128)(2,1)}, u32[]{:S(2)}, u32[]{:S(2)}) collective-permute-start(bf16[320,2048]{1,0:T(8,128)(2,1)} %wo_own_ref), channel_id=1, source_target_pairs={{0,1},{1,0},{2,3},{3,2},{4,5},{5,4},{6,7},{7,6},{8,9},{9,8},{10,11... | collective-permute-start | bytes 3932168 | tf_op jit(solution)/shard_map/ppermute | solution.py:34
  33.7 12.1 %collective-permute-start.5 = (bf16[3,8,256]{2,1,0:T(8,128)(2,1)S(1)}, bf16[3,8,256]{2,1,0:T(8,128)(2,1)S(1)}, u32[]{:S(2)}, u32[]{:S(2)}) collective-permute-start(bf16[3,8,256]{2,1,0:T(8,128)(2,1)S(1)} %pad_maximum_fusion.4), channel_id=1, source_target_pairs={{0,256},{16,272},{32,288},{48,304},{64,320},{80,336},{96,352},{112... | collective-permute-start | bytes 36872 | tf_op jit(solution)/shard_map/ppermute | solution.py:42
  45.8 1.1 collective-permute-done.5
  46.9 4.4 %collective-permute-start.6 = (bf16[2,3,8,256]{3,2,1,0:T(8,128)(2,1)S(1)}, bf16[2,3,8,256]{3,2,1,0:T(8,128)(2,1)S(1)}, u32[]{:S(2)}, u32[]{:S(2)}) collective-permute-start(bf16[2,3,8,256]{3,2,1,0:T(8,128)(2,1)S(1)} %pad_maximum_fusion.3), channel_id=1, source_target_pairs={{0,16},{16,0},{32,48},{48,32},{64,80},{80,64},{96,112},{112,96},{1... | collective-permute-start | bytes 73736 | tf_op jit(solution)/shard_map/ppermute | solution.py:42
  51.3 1.9 %all-to-all-done.1.x_ref = bf16[16,512,128]{2,1,0:T(8,128)(2,1)S(1)} async-done(((bf16[16,512,128]{2,1,0:T(8,128)(2,1)}), bf16[16,512,128]{2,1,0:T(8,128)(2,1)S(1)}, u32[]{:S(2)}, u32[]{:S(2)}) %all-to-all-start.1) | async-done | bytes 2097184 | tf_op jit(solution)/shard_map/all_to_all | solution.py:28
  53.2 9.2 %ffn.1 = bf16[16,512,128]{2,1,0:T(8,128)(2,1)} custom-call(bf16[16,512,128]{2,1,0:T(8,128)(2,1)S(1)} %all-to-all-done.1.x_ref, bf16[1,2048]{1,0:T(2,128)(2,1)S(1)} %reshape.19.gain_ref, bf16[320,2048]{1,0:T(8,128)(2,1)} %bitcast.49, bf16[320,2048]{1,0:T(8,128)(2,1)} %collective-permute-done.2.gate_other_ref, bf16[320,2048]{1,0:T(8,128)(2,1)} %bitcast.51, ...), custom_call_target="tpu_custom_call" | custom-call | tf_op jit(solution)/shard_map/ffn/pallas_call | solution.py:169
  62.4 3.6 %all-to-all-start.2 = ((bf16[16,512,128]{2,1,0:T(8,128)(2,1)}), bf16[16,512,128]{2,1,0:T(8,128)(2,1)S(1)}, u32[]{:S(2)}, u32[]{:S(2)}) async-start(bf16[16,512,128]{2,1,0:T(8,128)(2,1)} %ffn.1), calls=%async_computation.2 | async-start | bytes 4194304 | tf_op jit(solution)/shard_map/all_to_all | solution.py:28
  66.1 5.5 %collective-permute-start.7 = (bf16[2,2,3,8,256]{4,3,2,1,0:T(8,128)(2,1)S(1)}, bf16[2,2,3,8,256]{4,3,2,1,0:T(8,128)(2,1)S(1)}, u32[]{:S(2)}, u32[]{:S(2)}) collective-permute-start(bf16[2,2,3,8,256]{4,3,2,1,0:T(8,128)(2,1)S(1)} %pad_maximum_fusion.2), channel_id=1, source_target_pairs={{0,128},{16,144},{32,160},{48,176},{64,192},{80,208},{96,224},{112... | collective-permute-start | bytes 147464 | tf_op jit(solution)/shard_map/ppermute | solution.py:42
  71.6 3.4 %collective-permute-done.7 = bf16[2,2,3,8,256]{4,3,2,1,0:T(8,128)(2,1)S(1)} collective-permute-done((bf16[2,2,3,8,256]{4,3,2,1,0:T(8,128)(2,1)S(1)}, bf16[2,2,3,8,256]{4,3,2,1,0:T(8,128)(2,1)S(1)}, u32[]{:S(2)}, u32[]{:S(2)}) %collective-permute-start.7) | collective-permute-done | bytes 49184 | tf_op jit(solution)/shard_map/ppermute | solution.py:42
  75.1 2.9 %collective-permute-start.8 = (bf16[2,2,2,3,8,256]{5,4,3,2,1,0:T(8,128)(2,1)S(1)}, bf16[2,2,2,3,8,256]{5,4,3,2,1,0:T(8,128)(2,1)S(1)}, u32[]{:S(2)}, u32[]{:S(2)}) collective-permute-start(bf16[2,2,2,3,8,256]{5,4,3,2,1,0:T(8,128)(2,1)S(1)} %pad_maximum_fusion), channel_id=1, source_target_pairs={{0,64},{16,80},{32,96},{48,112},{64,0},{80,16},{96,32},{112,48},{1... | collective-permute-start | bytes 294920 | tf_op jit(solution)/shard_map/ppermute | solution.py:42
  78.0 3.6 %collective-permute-done.8 = bf16[2,2,2,3,8,256]{5,4,3,2,1,0:T(8,128)(2,1)S(1)} collective-permute-done((bf16[2,2,2,3,8,256]{5,4,3,2,1,0:T(8,128)(2,1)S(1)}, bf16[2,2,2,3,8,256]{5,4,3,2,1,0:T(8,128)(2,1)S(1)}, u32[]{:S(2)}, u32[]{:S(2)}) %collective-permute-start.8) | collective-permute-done | bytes 98336 | tf_op jit(solution)/shard_map/ppermute | solution.py:42
  81.7 4.0 %collective-permute-start.9 = (bf16[2,2,2,2,2,8,256]{6,5,4,3,2,1,0:T(8,128)(2,1)S(1)}, bf16[2,2,2,2,2,8,256]{6,5,4,3,2,1,0:T(8,128)(2,1)S(1)}, u32[]{:S(2)}, u32[]{:S(2)}) collective-permute-start(bf16[2,2,2,2,2,8,256]{6,5,4,3,2,1,0:T(8,128)(2,1)S(1)} %fusion.1), channel_id=1, source_target_pairs={{0,32},{16,48},{32,0},{48,16},{64,96},{80,112},{96,64},{112,80},{1... | collective-permute-start | bytes 393224 | tf_op jit(solution)/shard_map/ppermute | solution.py:42
  85.7 2.6 %collective-permute-done.9 = bf16[2,2,2,2,2,8,256]{6,5,4,3,2,1,0:T(8,128)(2,1)S(1)} collective-permute-done((bf16[2,2,2,2,2,8,256]{6,5,4,3,2,1,0:T(8,128)(2,1)S(1)}, bf16[2,2,2,2,2,8,256]{6,5,4,3,2,1,0:T(8,128)(2,1)S(1)}, u32[]{:S(2)}, u32[]{:S(2)}) %collective-permute-start.9) | collective-permute-done | bytes 131104 | tf_op jit(solution)/shard_map/ppermute | solution.py:42
  88.4 0.0 copy-start.3
  88.5 0.1 copy.17
  88.6 0.2 unstack.13.down_ref
  88.8 0.1 copy.18
  88.9 0.2 unstack.15.other_ref
  89.1 3.1 %all-to-all-done.2.parts_ref = bf16[16,512,128]{2,1,0:T(8,128)(2,1)S(1)} async-done(((bf16[16,512,128]{2,1,0:T(8,128)(2,1)}), bf16[16,512,128]{2,1,0:T(8,128)(2,1)S(1)}, u32[]{:S(2)}, u32[]{:S(2)}) %all-to-all-start.2) | async-done | bytes 2097184 | tf_op jit(solution)/shard_map/all_to_all | solution.py:28
  92.3 1.9 %squeeze.14 = (bf16[512,128]{1,0:T(8,128)(2,1)}, bf16[512,128]{1,0:T(8,128)(2,1)}, bf16[8,256,128]{2,1,0:T(8,128)(2,1)}) custom-call(s32[8]{0:T(128)S(1)} %copy-done.3, bf16[16,512,128]{2,1,0:T(8,128)(2,1)S(1)} %all-to-all-done.2.parts_ref, bf16[8,128,64]{2,1,0:T(8,128)(2,1)S(1)} %unstack.13.down_ref, bf16[8,128,64]{2,1,0:T(8,128)(2,1)S(1)} %unstack.15.other_ref), custom_call_target="tpu_custom_call" | custom-call | tf_op jit(solution)/shard_map/squeeze/pallas_call | solution.py:234
  94.2 0.0 copy-start.1
  94.2 0.0 copy-start.2
  94.2 3.8 %all-to-all-start.3 = ((bf16[8,256,128]{2,1,0:T(8,128)(2,1)}), bf16[8,256,128]{2,1,0:T(8,128)(2,1)S(1)}, u32[]{:S(2)}, u32[]{:S(2)}) async-start(bf16[8,256,128]{2,1,0:T(8,128)(2,1)} %get-tuple-element.20), calls=%async_computation.3 | async-start | bytes 1048576 | tf_op jit(solution)/shard_map/all_to_all | solution.py:28
  98.1 1.9 %collective-permute-start.12 = (bf16[2,2,2,2,8,256]{5,4,3,2,1,0:T(8,128)(2,1)S(1)}, bf16[2,2,2,2,8,256]{5,4,3,2,1,0:T(8,128)(2,1)S(1)}, u32[]{:S(2)}, u32[]{:S(2)}) collective-permute-start(bf16[2,2,2,2,8,256]{5,4,3,2,1,0:T(8,128)(2,1)S(1)} %fusion.2), channel_id=1, source_target_pairs={{0,32},{16,48},{32,0},{48,16},{64,96},{80,112},{96,64},{112,80},{1... | collective-permute-start | bytes 196616 | tf_op jit(solution)/shard_map/ppermute | solution.py:42
  100.0 6.1 %collective-permute-start.10 = (bf16[512,128]{1,0:T(8,128)(2,1)S(1)}, bf16[512,128]{1,0:T(8,128)(2,1)S(1)}, u32[]{:S(2)}, u32[]{:S(2)}) collective-permute-start(bf16[512,128]{1,0:T(8,128)(2,1)S(1)} %copy-done.6), channel_id=1, source_target_pairs={{0,1},{1,0},{2,3},{3,2},{4,5},{5,4},{6,7},{7,6},{8,9},{9,8},{10,11... | collective-permute-start | bytes 393224 | tf_op jit(solution)/shard_map/ppermute | solution.py:34
  106.1 0.1 relu_sum.1.squeezed_ref
  106.2 6.3 %collective-permute-start.11 = (bf16[256,128]{1,0:T(8,128)(2,1)S(1)}, bf16[256,128]{1,0:T(8,128)(2,1)S(1)}, u32[]{:S(2)}, u32[]{:S(2)}) collective-permute-start(bf16[256,128]{1,0:T(8,128)(2,1)S(1)} %relu_sum.1.squeezed_ref), channel_id=1, source_target_pairs={{0,1},{1,0},{2,3},{3,2},{4,5},{5,4},{6,7},{7,6},{8,9},{9,8},{10,11... | collective-permute-start | bytes 196616 | tf_op jit(solution)/shard_map/ppermute | solution.py:34
  112.5 0.1 copy.19
  112.6 0.2 reshape.20.up_ref
  112.8 0.5 collective-permute-done.11.their_squeezed_ref
  113.4 1.6 %expand.1 = bf16[1024,128]{1,0:T(8,128)(2,1)} custom-call(s32[8]{0:T(128)S(1)} %copy-done.3, bf16[1024,128]{1,0:T(8,128)(2,1)S(1)} %copy-done.1, bf16[512,128]{1,0:T(8,128)(2,1)S(1)} %copy-done.2, bf16[512,128]{1,0:T(8,128)(2,1)S(1)} %collective-permute-done.10.theirs_ref, bf16[256,128]{1,0:T(8,128)(2,1)S(1)} %relu_sum.1.squeezed_ref, ...), custom_call_target="tpu_custom_call" | custom-call | tf_op jit(solution)/shard_map/expand/pallas_call | solution.py:61
  (35 shorter events, 0.3 us)
Async XLA Ops:
  0.0 18.6 %copy-start = (bf16[1024,256]{1,0:T(8,128)(2,1)S(1)}, bf16[1024,256]{1,0:T(8,128)(2,1)}, u32[]{:S(2)}) copy-start(bf16[1024,256]{1,0:T(8,128)(2,1)} %param.22) | copy-start | bytes 1572868
  0.0 21.1 %copy-start.4 = (bf16[1024,256]{1,0:T(8,128)(2,1)S(1)}, bf16[1024,256]{1,0:T(8,128)(2,1)}, u32[]{:S(2)}) copy-start(bf16[1024,256]{1,0:T(8,128)(2,1)} %param.23) | copy-start | bytes 1572868
  2.4 16.0 %all-to-all-start = ((bf16[16,2,256]{2,1,0:T(2,128)(2,1)}), bf16[16,2,256]{2,1,0:T(2,128)(2,1)S(1)}, u32[]{:S(2)}, u32[]{:S(2)}) async-start(bf16[16,2,256]{2,1,0:T(2,128)(2,1)} %reshape.21), calls=%async_computation | async-start | bytes 32768 | tf_op jit(solution)/shard_map/all_to_all | solution.py:28
  13.5 8.4 %collective-permute-start.1 = (bf16[512,128]{1,0:T(8,128)(2,1)S(1)}, bf16[512,128]{1,0:T(8,128)(2,1)S(1)}, u32[]{:S(2)}, u32[]{:S(2)}) collective-permute-start(bf16[512,128]{1,0:T(8,128)(2,1)S(1)} %get-tuple-element.25), channel_id=1, source_target_pairs={{0,1},{1,0},{2,3},{3,2},{4,5},{5,4},{6,7},{7,6},{8,9},{9,8},{10,11... | collective-permute-start | bytes 393224 | tf_op jit(solution)/shard_map/ppermute | solution.py:34
  18.8 3.1 %collective-permute-start = (bf16[8,256]{1,0:T(8,128)(2,1)S(1)}, bf16[8,256]{1,0:T(8,128)(2,1)S(1)}, u32[]{:S(2)}, u32[]{:S(2)}) collective-permute-start(bf16[8,256]{1,0:T(8,128)(2,1)S(1)} %convolution_convert_fusion.1), channel_id=1, source_target_pairs={{0,1},{1,0},{2,3},{3,2},{4,5},{5,4},{6,7},{7,6},{8,9},{9,8},{10,11... | collective-permute-start | bytes 12296 | tf_op jit(solution)/shard_map/ppermute | solution.py:34
  23.4 27.9 %copy-start.5 = (bf16[2048]{0:T(1024)(128)(2,1)S(1)}, bf16[2048]{0:T(1024)(128)(2,1)}, u32[]{:S(2)}) copy-start(bf16[2048]{0:T(1024)(128)(2,1)} %param.13) | copy-start | bytes 12292
  23.4 29.8 %all-to-all-start.1 = ((bf16[16,512,128]{2,1,0:T(8,128)(2,1)}), bf16[16,512,128]{2,1,0:T(8,128)(2,1)S(1)}, u32[]{:S(2)}, u32[]{:S(2)}) async-start(bf16[16,512,128]{2,1,0:T(8,128)(2,1)} %spread.1), calls=%async_computation.1 | async-start | bytes 4194304 | tf_op jit(solution)/shard_map/all_to_all | solution.py:28
  27.1 24.2 %collective-permute-start.2 = (bf16[320,2048]{1,0:T(8,128)(2,1)}, bf16[320,2048]{1,0:T(8,128)(2,1)}, u32[]{:S(2)}, u32[]{:S(2)}) collective-permute-start(bf16[320,2048]{1,0:T(8,128)(2,1)} %bitcast.48), channel_id=1, source_target_pairs={{0,1},{1,0},{2,3},{3,2},{4,5},{5,4},{6,7},{7,6},{8,9},{9,8},{10,11... | collective-permute-start | bytes 3932168 | tf_op jit(solution)/shard_map/ppermute | solution.py:34
  29.3 22.0 %collective-permute-start.3 = (bf16[320,2048]{1,0:T(8,128)(2,1)}, bf16[320,2048]{1,0:T(8,128)(2,1)}, u32[]{:S(2)}, u32[]{:S(2)}) collective-permute-start(bf16[320,2048]{1,0:T(8,128)(2,1)} %bitcast.50), channel_id=1, source_target_pairs={{0,1},{1,0},{2,3},{3,2},{4,5},{5,4},{6,7},{7,6},{8,9},{9,8},{10,11... | collective-permute-start | bytes 3932168 | tf_op jit(solution)/shard_map/ppermute | solution.py:34
  31.4 19.9 %collective-permute-start.4 = (bf16[320,2048]{1,0:T(8,128)(2,1)}, bf16[320,2048]{1,0:T(8,128)(2,1)}, u32[]{:S(2)}, u32[]{:S(2)}) collective-permute-start(bf16[320,2048]{1,0:T(8,128)(2,1)} %wo_own_ref), channel_id=1, source_target_pairs={{0,1},{1,0},{2,3},{3,2},{4,5},{5,4},{6,7},{7,6},{8,9},{9,8},{10,11... | collective-permute-start | bytes 3932168 | tf_op jit(solution)/shard_map/ppermute | solution.py:34
  33.7 13.2 %collective-permute-start.5 = (bf16[3,8,256]{2,1,0:T(8,128)(2,1)S(1)}, bf16[3,8,256]{2,1,0:T(8,128)(2,1)S(1)}, u32[]{:S(2)}, u32[]{:S(2)}) collective-permute-start(bf16[3,8,256]{2,1,0:T(8,128)(2,1)S(1)} %pad_maximum_fusion.4), channel_id=1, source_target_pairs={{0,256},{16,272},{32,288},{48,304},{64,320},{80,336},{96,352},{112... | collective-permute-start | bytes 36872 | tf_op jit(solution)/shard_map/ppermute | solution.py:42
  46.9 19.2 %collective-permute-start.6 = (bf16[2,3,8,256]{3,2,1,0:T(8,128)(2,1)S(1)}, bf16[2,3,8,256]{3,2,1,0:T(8,128)(2,1)S(1)}, u32[]{:S(2)}, u32[]{:S(2)}) collective-permute-start(bf16[2,3,8,256]{3,2,1,0:T(8,128)(2,1)S(1)} %pad_maximum_fusion.3), channel_id=1, source_target_pairs={{0,16},{16,0},{32,48},{48,32},{64,80},{80,64},{96,112},{112,96},{1... | collective-permute-start | bytes 73736 | tf_op jit(solution)/shard_map/ppermute | solution.py:42
  62.4 29.8 %all-to-all-start.2 = ((bf16[16,512,128]{2,1,0:T(8,128)(2,1)}), bf16[16,512,128]{2,1,0:T(8,128)(2,1)S(1)}, u32[]{:S(2)}, u32[]{:S(2)}) async-start(bf16[16,512,128]{2,1,0:T(8,128)(2,1)} %ffn.1), calls=%async_computation.2 | async-start | bytes 4194304 | tf_op jit(solution)/shard_map/all_to_all | solution.py:28
  66.1 9.0 %collective-permute-start.7 = (bf16[2,2,3,8,256]{4,3,2,1,0:T(8,128)(2,1)S(1)}, bf16[2,2,3,8,256]{4,3,2,1,0:T(8,128)(2,1)S(1)}, u32[]{:S(2)}, u32[]{:S(2)}) collective-permute-start(bf16[2,2,3,8,256]{4,3,2,1,0:T(8,128)(2,1)S(1)} %pad_maximum_fusion.2), channel_id=1, source_target_pairs={{0,128},{16,144},{32,160},{48,176},{64,192},{80,208},{96,224},{112... | collective-permute-start | bytes 147464 | tf_op jit(solution)/shard_map/ppermute | solution.py:42
  75.1 6.6 %collective-permute-start.8 = (bf16[2,2,2,3,8,256]{5,4,3,2,1,0:T(8,128)(2,1)S(1)}, bf16[2,2,2,3,8,256]{5,4,3,2,1,0:T(8,128)(2,1)S(1)}, u32[]{:S(2)}, u32[]{:S(2)}) collective-permute-start(bf16[2,2,2,3,8,256]{5,4,3,2,1,0:T(8,128)(2,1)S(1)} %pad_maximum_fusion), channel_id=1, source_target_pairs={{0,64},{16,80},{32,96},{48,112},{64,0},{80,16},{96,32},{112,48},{1... | collective-permute-start | bytes 294920 | tf_op jit(solution)/shard_map/ppermute | solution.py:42
  81.7 6.6 %collective-permute-start.9 = (bf16[2,2,2,2,2,8,256]{6,5,4,3,2,1,0:T(8,128)(2,1)S(1)}, bf16[2,2,2,2,2,8,256]{6,5,4,3,2,1,0:T(8,128)(2,1)S(1)}, u32[]{:S(2)}, u32[]{:S(2)}) collective-permute-start(bf16[2,2,2,2,2,8,256]{6,5,4,3,2,1,0:T(8,128)(2,1)S(1)} %fusion.1), channel_id=1, source_target_pairs={{0,32},{16,48},{32,0},{48,16},{64,96},{80,112},{96,64},{112,80},{1... | collective-permute-start | bytes 393224 | tf_op jit(solution)/shard_map/ppermute | solution.py:42
  88.4 3.9 %copy-start.3 = (s32[8]{0:T(128)S(1)}, s32[8]{0:T(128)}, u32[]{:S(2)}) copy-start(s32[8]{0:T(128)} %ids_ref.3) | copy-start | bytes 100
  94.2 5.8 %copy-start.6 = (bf16[512,128]{1,0:T(8,128)(2,1)S(1)}, bf16[512,128]{1,0:T(8,128)(2,1)}, u32[]{:S(2)}) copy-start(bf16[512,128]{1,0:T(8,128)(2,1)} %get-tuple-element.19) | copy-start | bytes 393220
  94.2 19.2 %copy-start.1 = (bf16[1024,128]{1,0:T(8,128)(2,1)S(1)}, bf16[1024,128]{1,0:T(8,128)(2,1)}, u32[]{:S(2)}) copy-start(bf16[1024,128]{1,0:T(8,128)(2,1)} %tokens_ref.1) | copy-start | bytes 786436
  94.2 19.1 %copy-start.2 = (bf16[512,128]{1,0:T(8,128)(2,1)S(1)}, bf16[512,128]{1,0:T(8,128)(2,1)}, u32[]{:S(2)}) copy-start(bf16[512,128]{1,0:T(8,128)(2,1)} %get-tuple-element.18.mine_ref) | copy-start | bytes 393220
  94.2 11.9 %all-to-all-start.3 = ((bf16[8,256,128]{2,1,0:T(8,128)(2,1)}), bf16[8,256,128]{2,1,0:T(8,128)(2,1)S(1)}, u32[]{:S(2)}, u32[]{:S(2)}) async-start(bf16[8,256,128]{2,1,0:T(8,128)(2,1)} %get-tuple-element.20), calls=%async_computation.3 | async-start | bytes 1048576 | tf_op jit(solution)/shard_map/all_to_all | solution.py:28
  98.1 8.0 %collective-permute-start.12 = (bf16[2,2,2,2,8,256]{5,4,3,2,1,0:T(8,128)(2,1)S(1)}, bf16[2,2,2,2,8,256]{5,4,3,2,1,0:T(8,128)(2,1)S(1)}, u32[]{:S(2)}, u32[]{:S(2)}) collective-permute-start(bf16[2,2,2,2,8,256]{5,4,3,2,1,0:T(8,128)(2,1)S(1)} %fusion.2), channel_id=1, source_target_pairs={{0,32},{16,48},{32,0},{48,16},{64,96},{80,112},{96,64},{112,80},{1... | collective-permute-start | bytes 196616 | tf_op jit(solution)/shard_map/ppermute | solution.py:42
  100.0 12.8 %collective-permute-start.10 = (bf16[512,128]{1,0:T(8,128)(2,1)S(1)}, bf16[512,128]{1,0:T(8,128)(2,1)S(1)}, u32[]{:S(2)}, u32[]{:S(2)}) collective-permute-start(bf16[512,128]{1,0:T(8,128)(2,1)S(1)} %copy-done.6), channel_id=1, source_target_pairs={{0,1},{1,0},{2,3},{3,2},{4,5},{5,4},{6,7},{7,6},{8,9},{9,8},{10,11... | collective-permute-start | bytes 393224 | tf_op jit(solution)/shard_map/ppermute | solution.py:34
  106.2 7.2 %collective-permute-start.11 = (bf16[256,128]{1,0:T(8,128)(2,1)S(1)}, bf16[256,128]{1,0:T(8,128)(2,1)S(1)}, u32[]{:S(2)}, u32[]{:S(2)}) collective-permute-start(bf16[256,128]{1,0:T(8,128)(2,1)S(1)} %relu_sum.1.squeezed_ref), channel_id=1, source_target_pairs={{0,1},{1,0},{2,3},{3,2},{4,5},{5,4},{6,7},{7,6},{8,9},{9,8},{10,11... | collective-permute-start | bytes 196616 | tf_op jit(solution)/shard_map/ppermute | solution.py:34

commit v12 on v11

--- a/solution.py
+++ b/solution.py
@@ -201,6 +201,7 @@
     seqs = ids_ref.shape[0]
     seq = rows * CORES // seqs
     me = lax.axis_index("mp") % CORES
+    early = []
     for s in range(rows // seq):
         tile = slice(s * seq, (s + 1) * seq)
         task = ids_ref[me * (rows // seq) + s]
@@ -214,15 +215,18 @@
         given = jnp.where(me == 0, ffout[1], ffout[0]).astype(jnp.bfloat16)
         kept_ref[tile] = kept
         given_ref[tile] = given
+        here = pl.ds(s * seq, seq)
+        for i, pair in enumerate(((given_ref, given_out), (kept_ref, kept_out))):
+            sem = sems.at[CHIPS + 2 * s + i]
+            early.append(pltpu.make_async_copy(pair[0].at[here], pair[1].at[here], sem))
+            early[-1].start()
         sums = (matmul(kept, down_ref[task]) + matmul(given, other_ref[task])).astype(jnp.bfloat16)
         packed = slice(s // 2 * seq, (s // 2 + 1) * seq)
         squeezed_ref[packed, s % 2 * R : (s % 2 + 1) * R] = sums
     stores = [pltpu.make_async_copy(squeezed_ref, squeezed_out.at[i], sems.at[i]) for i in range(CHIPS)]
-    stores.append(pltpu.make_async_copy(given_ref, given_out, sems.at[CHIPS]))
-    stores.append(pltpu.make_async_copy(kept_ref, kept_out, sems.at[CHIPS + 1]))
     for store in stores:
         store.start()
-    for store in stores:
+    for store in early + stores:
         store.wait()
 
 
@@ -244,7 +248,7 @@
             pltpu.VMEM((rows, width), parts.dtype),
             pltpu.VMEM((rows, width), parts.dtype),
             pltpu.VMEM(packed, parts.dtype),
-            pltpu.SemaphoreType.DMA((CHIPS + 2,)),
+            pltpu.SemaphoreType.DMA((2 * CHIPS,)),
         ],
         compiler_params=pltpu.CompilerParams(vmem_limit_bytes=VMEM),
         name="squeeze",

time: 116 us -> 116 us (level)
  no operation moved by 1% of the time
where the time goes in v12:
time: 116 us; the launch traced here: 115 us
  starting transfers between devices  75.4 us (65%)
  waiting for transfers between devices  19.6 us (17%)
  Pallas kernels  15.2 us (13%)
  local copies, waits for them, and re-layouts  2.91 us (3%)
  between operations  1.18 us (1%)
    ppermute x6, starting transfers between devices, doubling_gather(): theirs = lax.ppermute(held, axis, [(i, i ^ bit) for i in range(size)])  30.8 us
    ppermute x7, starting transfers between devices, swap_cores(): return lax.ppermute(array, 'mp', [(i, i ^ 1) for i in range(MP)])  23.4 us
    all_to_all x4, starting transfers between devices, exchange(): lax.all_to_all(pieces, axis, split_axis=0, concat_axis=0, axis_index_grou...  21.2 us
    ppermute x6, waiting for transfers between devices, doubling_gather(): theirs = lax.ppermute(held, axis, [(i, i ^ bit) for i in range(size)])  10.8 us
    pallas_call x1, Pallas kernels, ffn(): pl.pallas_call(ffn_body, out_shape=pltpu.HBM(x.shape, x.dtype), in_specs=...  9.23 us
    all_to_all x4, waiting for transfers between devices, exchange(): lax.all_to_all(pieces, axis, split_axis=0, concat_axis=0, axis_index_grou...  7.71 us
    pallas_call x3, Pallas kernels, call(): pl.pallas_call(body, out_shape=outs, in_specs=[pl.BlockSpec(memory_space=...  2.59 us
  transfers between devices with their start and end apart: 17, of which 9 were waited for; matrix products, arithmetic and copies ran while one was open for 2% of the time, Pallas kernels for 8%

profile of v12, /device:TPU:1, one launch (start us, length us, event | category | flops | bytes accessed | tf_op | source)
XLA Modules:
  0.0 114.9 jit_solution(12253191311377150405)
XLA Ops:
  0.7 0.9 hidden.1
  1.7 0.7 reshape.21
  2.4 10.2 %all-to-all-start = ((bf16[16,2,256]{2,1,0:T(2,128)(2,1)}), bf16[16,2,256]{2,1,0:T(2,128)(2,1)S(1)}, u32[]{:S(2)}, u32[]{:S(2)}) async-start(bf16[16,2,256]{2,1,0:T(2,128)(2,1)} %reshape.21), calls=%async_computation | async-start | bytes 32768 | tf_op jit(solution)/shard_map/all_to_all | solution.py:28
  12.6 1.0 dynamic-slice_bitcast_fusion
  13.5 2.2 %collective-permute-start.1 = (bf16[512,128]{1,0:T(8,128)(2,1)S(1)}, bf16[512,128]{1,0:T(8,128)(2,1)S(1)}, u32[]{:S(2)}, u32[]{:S(2)}) collective-permute-start(bf16[512,128]{1,0:T(8,128)(2,1)S(1)} %get-tuple-element.25), channel_id=1, source_target_pairs={{0,1},{1,0},{2,3},{3,2},{4,5},{5,4},{6,7},{7,6},{8,9},{9,8},{10,11... | collective-permute-start | bytes 393224 | tf_op jit(solution)/shard_map/ppermute | solution.py:34
  15.7 2.7 %all-to-all-done = bf16[16,2,256]{2,1,0:T(2,128)(2,1)S(1)} async-done(((bf16[16,2,256]{2,1,0:T(2,128)(2,1)}), bf16[16,2,256]{2,1,0:T(2,128)(2,1)S(1)}, u32[]{:S(2)}, u32[]{:S(2)}) %all-to-all-start) | async-done | bytes 16416 | tf_op jit(solution)/shard_map/all_to_all | solution.py:28
  18.4 0.1 reshape.22
  18.5 0.1 reshape.17
  18.6 0.2 convolution_convert_fusion.1
  18.8 2.3 %collective-permute-start = (bf16[8,256]{1,0:T(8,128)(2,1)S(1)}, bf16[8,256]{1,0:T(8,128)(2,1)S(1)}, u32[]{:S(2)}, u32[]{:S(2)}) collective-permute-start(bf16[8,256]{1,0:T(8,128)(2,1)S(1)} %convolution_convert_fusion.1), channel_id=1, source_target_pairs={{0,1},{1,0},{2,3},{3,2},{4,5},{5,4},{6,7},{7,6},{8,9},{9,8},{10,11... | collective-permute-start | bytes 12296 | tf_op jit(solution)/shard_map/ppermute | solution.py:34
  21.1 0.2 fusion
  21.3 0.6 collective-permute-done
  21.9 1.5 %spread.1 = bf16[16,512,128]{2,1,0:T(8,128)(2,1)} custom-call(bf16[512,128]{1,0:T(8,128)(2,1)S(1)} %get-tuple-element.26.kept_ref, bf16[512,128]{1,0:T(8,128)(2,1)S(1)} %collective-permute-done.1.given_ref), custom_call_target="tpu_custom_call" | custom-call | tf_op jit(solution)/shard_map/spread/pallas_call | solution.py:85
  23.4 0.0 copy-start.5
  23.4 3.6 %all-to-all-start.1 = ((bf16[16,512,128]{2,1,0:T(8,128)(2,1)}), bf16[16,512,128]{2,1,0:T(8,128)(2,1)S(1)}, u32[]{:S(2)}, u32[]{:S(2)}) async-start(bf16[16,512,128]{2,1,0:T(8,128)(2,1)} %spread.1), calls=%async_computation.1 | async-start | bytes 4194304 | tf_op jit(solution)/shard_map/all_to_all | solution.py:28
  27.1 2.3 %collective-permute-start.2 = (bf16[320,2048]{1,0:T(8,128)(2,1)}, bf16[320,2048]{1,0:T(8,128)(2,1)}, u32[]{:S(2)}, u32[]{:S(2)}) collective-permute-start(bf16[320,2048]{1,0:T(8,128)(2,1)} %bitcast.48), channel_id=1, source_target_pairs={{0,1},{1,0},{2,3},{3,2},{4,5},{5,4},{6,7},{7,6},{8,9},{9,8},{10,11... | collective-permute-start | bytes 3932168 | tf_op jit(solution)/shard_map/ppermute | solution.py:34
  29.3 2.1 %collective-permute-start.3 = (bf16[320,2048]{1,0:T(8,128)(2,1)}, bf16[320,2048]{1,0:T(8,128)(2,1)}, u32[]{:S(2)}, u32[]{:S(2)}) collective-permute-start(bf16[320,2048]{1,0:T(8,128)(2,1)} %bitcast.50), channel_id=1, source_target_pairs={{0,1},{1,0},{2,3},{3,2},{4,5},{5,4},{6,7},{7,6},{8,9},{9,8},{10,11... | collective-permute-start | bytes 3932168 | tf_op jit(solution)/shard_map/ppermute | solution.py:34
  31.4 2.3 %collective-permute-start.4 = (bf16[320,2048]{1,0:T(8,128)(2,1)}, bf16[320,2048]{1,0:T(8,128)(2,1)}, u32[]{:S(2)}, u32[]{:S(2)}) collective-permute-start(bf16[320,2048]{1,0:T(8,128)(2,1)} %wo_own_ref), channel_id=1, source_target_pairs={{0,1},{1,0},{2,3},{3,2},{4,5},{5,4},{6,7},{7,6},{8,9},{9,8},{10,11... | collective-permute-start | bytes 3932168 | tf_op jit(solution)/shard_map/ppermute | solution.py:34
  33.7 12.1 %collective-permute-start.5 = (bf16[3,8,256]{2,1,0:T(8,128)(2,1)S(1)}, bf16[3,8,256]{2,1,0:T(8,128)(2,1)S(1)}, u32[]{:S(2)}, u32[]{:S(2)}) collective-permute-start(bf16[3,8,256]{2,1,0:T(8,128)(2,1)S(1)} %pad_maximum_fusion.4), channel_id=1, source_target_pairs={{0,256},{16,272},{32,288},{48,304},{64,320},{80,336},{96,352},{112... | collective-permute-start | bytes 36872 | tf_op jit(solution)/shard_map/ppermute | solution.py:42
  45.8 1.1 collective-permute-done.5
  46.9 4.4 %collective-permute-start.6 = (bf16[2,3,8,256]{3,2,1,0:T(8,128)(2,1)S(1)}, bf16[2,3,8,256]{3,2,1,0:T(8,128)(2,1)S(1)}, u32[]{:S(2)}, u32[]{:S(2)}) collective-permute-start(bf16[2,3,8,256]{3,2,1,0:T(8,128)(2,1)S(1)} %pad_maximum_fusion.3), channel_id=1, source_target_pairs={{0,16},{16,0},{32,48},{48,32},{64,80},{80,64},{96,112},{112,96},{1... | collective-permute-start | bytes 73736 | tf_op jit(solution)/shard_map/ppermute | solution.py:42
  51.3 1.9 %all-to-all-done.1.x_ref = bf16[16,512,128]{2,1,0:T(8,128)(2,1)S(1)} async-done(((bf16[16,512,128]{2,1,0:T(8,128)(2,1)}), bf16[16,512,128]{2,1,0:T(8,128)(2,1)S(1)}, u32[]{:S(2)}, u32[]{:S(2)}) %all-to-all-start.1) | async-done | bytes 2097184 | tf_op jit(solution)/shard_map/all_to_all | solution.py:28
  53.2 9.2 %ffn.1 = bf16[16,512,128]{2,1,0:T(8,128)(2,1)} custom-call(bf16[16,512,128]{2,1,0:T(8,128)(2,1)S(1)} %all-to-all-done.1.x_ref, bf16[1,2048]{1,0:T(2,128)(2,1)S(1)} %reshape.19.gain_ref, bf16[320,2048]{1,0:T(8,128)(2,1)} %bitcast.49, bf16[320,2048]{1,0:T(8,128)(2,1)} %collective-permute-done.2.gate_other_ref, bf16[320,2048]{1,0:T(8,128)(2,1)} %bitcast.51, ...), custom_call_target="tpu_custom_call" | custom-call | tf_op jit(solution)/shard_map/ffn/pallas_call | solution.py:169
  62.4 3.6 %all-to-all-start.2 = ((bf16[16,512,128]{2,1,0:T(8,128)(2,1)}), bf16[16,512,128]{2,1,0:T(8,128)(2,1)S(1)}, u32[]{:S(2)}, u32[]{:S(2)}) async-start(bf16[16,512,128]{2,1,0:T(8,128)(2,1)} %ffn.1), calls=%async_computation.2 | async-start | bytes 4194304 | tf_op jit(solution)/shard_map/all_to_all | solution.py:28
  66.1 5.5 %collective-permute-start.7 = (bf16[2,2,3,8,256]{4,3,2,1,0:T(8,128)(2,1)S(1)}, bf16[2,2,3,8,256]{4,3,2,1,0:T(8,128)(2,1)S(1)}, u32[]{:S(2)}, u32[]{:S(2)}) collective-permute-start(bf16[2,2,3,8,256]{4,3,2,1,0:T(8,128)(2,1)S(1)} %pad_maximum_fusion.2), channel_id=1, source_target_pairs={{0,128},{16,144},{32,160},{48,176},{64,192},{80,208},{96,224},{112... | collective-permute-start | bytes 147464 | tf_op jit(solution)/shard_map/ppermute | solution.py:42
  71.6 3.4 %collective-permute-done.7 = bf16[2,2,3,8,256]{4,3,2,1,0:T(8,128)(2,1)S(1)} collective-permute-done((bf16[2,2,3,8,256]{4,3,2,1,0:T(8,128)(2,1)S(1)}, bf16[2,2,3,8,256]{4,3,2,1,0:T(8,128)(2,1)S(1)}, u32[]{:S(2)}, u32[]{:S(2)}) %collective-permute-start.7) | collective-permute-done | bytes 49184 | tf_op jit(solution)/shard_map/ppermute | solution.py:42
  75.1 2.9 %collective-permute-start.8 = (bf16[2,2,2,3,8,256]{5,4,3,2,1,0:T(8,128)(2,1)S(1)}, bf16[2,2,2,3,8,256]{5,4,3,2,1,0:T(8,128)(2,1)S(1)}, u32[]{:S(2)}, u32[]{:S(2)}) collective-permute-start(bf16[2,2,2,3,8,256]{5,4,3,2,1,0:T(8,128)(2,1)S(1)} %pad_maximum_fusion), channel_id=1, source_target_pairs={{0,64},{16,80},{32,96},{48,112},{64,0},{80,16},{96,32},{112,48},{1... | collective-permute-start | bytes 294920 | tf_op jit(solution)/shard_map/ppermute | solution.py:42
  78.0 3.6 %collective-permute-done.8 = bf16[2,2,2,3,8,256]{5,4,3,2,1,0:T(8,128)(2,1)S(1)} collective-permute-done((bf16[2,2,2,3,8,256]{5,4,3,2,1,0:T(8,128)(2,1)S(1)}, bf16[2,2,2,3,8,256]{5,4,3,2,1,0:T(8,128)(2,1)S(1)}, u32[]{:S(2)}, u32[]{:S(2)}) %collective-permute-start.8) | collective-permute-done | bytes 98336 | tf_op jit(solution)/shard_map/ppermute | solution.py:42
  81.7 4.0 %collective-permute-start.9 = (bf16[2,2,2,2,2,8,256]{6,5,4,3,2,1,0:T(8,128)(2,1)S(1)}, bf16[2,2,2,2,2,8,256]{6,5,4,3,2,1,0:T(8,128)(2,1)S(1)}, u32[]{:S(2)}, u32[]{:S(2)}) collective-permute-start(bf16[2,2,2,2,2,8,256]{6,5,4,3,2,1,0:T(8,128)(2,1)S(1)} %fusion.1), channel_id=1, source_target_pairs={{0,32},{16,48},{32,0},{48,16},{64,96},{80,112},{96,64},{112,80},{1... | collective-permute-start | bytes 393224 | tf_op jit(solution)/shard_map/ppermute | solution.py:42
  85.7 2.6 %collective-permute-done.9 = bf16[2,2,2,2,2,8,256]{6,5,4,3,2,1,0:T(8,128)(2,1)S(1)} collective-permute-done((bf16[2,2,2,2,2,8,256]{6,5,4,3,2,1,0:T(8,128)(2,1)S(1)}, bf16[2,2,2,2,2,8,256]{6,5,4,3,2,1,0:T(8,128)(2,1)S(1)}, u32[]{:S(2)}, u32[]{:S(2)}) %collective-permute-start.9) | collective-permute-done | bytes 131104 | tf_op jit(solution)/shard_map/ppermute | solution.py:42
  88.4 0.0 copy-start.3
  88.5 0.1 copy.17
  88.6 0.2 unstack.13.down_ref
  88.8 0.1 copy.18
  88.9 0.2 unstack.15.other_ref
  89.1 3.1 %all-to-all-done.2.parts_ref = bf16[16,512,128]{2,1,0:T(8,128)(2,1)S(1)} async-done(((bf16[16,512,128]{2,1,0:T(8,128)(2,1)}), bf16[16,512,128]{2,1,0:T(8,128)(2,1)S(1)}, u32[]{:S(2)}, u32[]{:S(2)}) %all-to-all-start.2) | async-done | bytes 2097184 | tf_op jit(solution)/shard_map/all_to_all | solution.py:28
  92.3 1.9 %squeeze.14 = (bf16[512,128]{1,0:T(8,128)(2,1)}, bf16[512,128]{1,0:T(8,128)(2,1)}, bf16[8,256,128]{2,1,0:T(8,128)(2,1)}) custom-call(s32[8]{0:T(128)S(1)} %copy-done.3, bf16[16,512,128]{2,1,0:T(8,128)(2,1)S(1)} %all-to-all-done.2.parts_ref, bf16[8,128,64]{2,1,0:T(8,128)(2,1)S(1)} %unstack.13.down_ref, bf16[8,128,64]{2,1,0:T(8,128)(2,1)S(1)} %unstack.15.other_ref), custom_call_target="tpu_custom_call" | custom-call | tf_op jit(solution)/shard_map/squeeze/pallas_call | solution.py:238
  94.2 0.0 copy-start.1
  94.2 0.0 copy-start.2
  94.2 3.8 %all-to-all-start.3 = ((bf16[8,256,128]{2,1,0:T(8,128)(2,1)}), bf16[8,256,128]{2,1,0:T(8,128)(2,1)S(1)}, u32[]{:S(2)}, u32[]{:S(2)}) async-start(bf16[8,256,128]{2,1,0:T(8,128)(2,1)} %get-tuple-element.20), calls=%async_computation.3 | async-start | bytes 1048576 | tf_op jit(solution)/shard_map/all_to_all | solution.py:28
  98.0 1.9 %collective-permute-start.12 = (bf16[2,2,2,2,8,256]{5,4,3,2,1,0:T(8,128)(2,1)S(1)}, bf16[2,2,2,2,8,256]{5,4,3,2,1,0:T(8,128)(2,1)S(1)}, u32[]{:S(2)}, u32[]{:S(2)}) collective-permute-start(bf16[2,2,2,2,8,256]{5,4,3,2,1,0:T(8,128)(2,1)S(1)} %fusion.2), channel_id=1, source_target_pairs={{0,32},{16,48},{32,0},{48,16},{64,96},{80,112},{96,64},{112,80},{1... | collective-permute-start | bytes 196616 | tf_op jit(solution)/shard_map/ppermute | solution.py:42
  100.0 6.1 %collective-permute-start.10 = (bf16[512,128]{1,0:T(8,128)(2,1)S(1)}, bf16[512,128]{1,0:T(8,128)(2,1)S(1)}, u32[]{:S(2)}, u32[]{:S(2)}) collective-permute-start(bf16[512,128]{1,0:T(8,128)(2,1)S(1)} %copy-done.6), channel_id=1, source_target_pairs={{0,1},{1,0},{2,3},{3,2},{4,5},{5,4},{6,7},{7,6},{8,9},{9,8},{10,11... | collective-permute-start | bytes 393224 | tf_op jit(solution)/shard_map/ppermute | solution.py:34
  106.1 0.1 relu_sum.1.squeezed_ref
  106.2 6.3 %collective-permute-start.11 = (bf16[256,128]{1,0:T(8,128)(2,1)S(1)}, bf16[256,128]{1,0:T(8,128)(2,1)S(1)}, u32[]{:S(2)}, u32[]{:S(2)}) collective-permute-start(bf16[256,128]{1,0:T(8,128)(2,1)S(1)} %relu_sum.1.squeezed_ref), channel_id=1, source_target_pairs={{0,1},{1,0},{2,3},{3,2},{4,5},{5,4},{6,7},{7,6},{8,9},{9,8},{10,11... | collective-permute-start | bytes 196616 | tf_op jit(solution)/shard_map/ppermute | solution.py:34
  112.5 0.1 copy.19
  112.6 0.2 reshape.20.up_ref
  112.8 0.5 collective-permute-done.11.their_squeezed_ref
  113.3 1.6 %expand.1 = bf16[1024,128]{1,0:T(8,128)(2,1)} custom-call(s32[8]{0:T(128)S(1)} %copy-done.3, bf16[1024,128]{1,0:T(8,128)(2,1)S(1)} %copy-done.1, bf16[512,128]{1,0:T(8,128)(2,1)S(1)} %copy-done.2, bf16[512,128]{1,0:T(8,128)(2,1)S(1)} %collective-permute-done.10.theirs_ref, bf16[256,128]{1,0:T(8,128)(2,1)S(1)} %relu_sum.1.squeezed_ref, ...), custom_call_target="tpu_custom_call" | custom-call | tf_op jit(solution)/shard_map/expand/pallas_call | solution.py:61
  (35 shorter events, 0.3 us)
Async XLA Ops:
  0.0 18.6 %copy-start = (bf16[1024,256]{1,0:T(8,128)(2,1)S(1)}, bf16[1024,256]{1,0:T(8,128)(2,1)}, u32[]{:S(2)}) copy-start(bf16[1024,256]{1,0:T(8,128)(2,1)} %param.22) | copy-start | bytes 1572868
  0.0 21.1 %copy-start.4 = (bf16[1024,256]{1,0:T(8,128)(2,1)S(1)}, bf16[1024,256]{1,0:T(8,128)(2,1)}, u32[]{:S(2)}) copy-start(bf16[1024,256]{1,0:T(8,128)(2,1)} %param.23) | copy-start | bytes 1572868
  2.4 16.0 %all-to-all-start = ((bf16[16,2,256]{2,1,0:T(2,128)(2,1)}), bf16[16,2,256]{2,1,0:T(2,128)(2,1)S(1)}, u32[]{:S(2)}, u32[]{:S(2)}) async-start(bf16[16,2,256]{2,1,0:T(2,128)(2,1)} %reshape.21), calls=%async_computation | async-start | bytes 32768 | tf_op jit(solution)/shard_map/all_to_all | solution.py:28
  13.5 8.4 %collective-permute-start.1 = (bf16[512,128]{1,0:T(8,128)(2,1)S(1)}, bf16[512,128]{1,0:T(8,128)(2,1)S(1)}, u32[]{:S(2)}, u32[]{:S(2)}) collective-permute-start(bf16[512,128]{1,0:T(8,128)(2,1)S(1)} %get-tuple-element.25), channel_id=1, source_target_pairs={{0,1},{1,0},{2,3},{3,2},{4,5},{5,4},{6,7},{7,6},{8,9},{9,8},{10,11... | collective-permute-start | bytes 393224 | tf_op jit(solution)/shard_map/ppermute | solution.py:34
  18.8 3.1 %collective-permute-start = (bf16[8,256]{1,0:T(8,128)(2,1)S(1)}, bf16[8,256]{1,0:T(8,128)(2,1)S(1)}, u32[]{:S(2)}, u32[]{:S(2)}) collective-permute-start(bf16[8,256]{1,0:T(8,128)(2,1)S(1)} %convolution_convert_fusion.1), channel_id=1, source_target_pairs={{0,1},{1,0},{2,3},{3,2},{4,5},{5,4},{6,7},{7,6},{8,9},{9,8},{10,11... | collective-permute-start | bytes 12296 | tf_op jit(solution)/shard_map/ppermute | solution.py:34
  23.4 27.9 %copy-start.5 = (bf16[2048]{0:T(1024)(128)(2,1)S(1)}, bf16[2048]{0:T(1024)(128)(2,1)}, u32[]{:S(2)}) copy-start(bf16[2048]{0:T(1024)(128)(2,1)} %param.13) | copy-start | bytes 12292
  23.4 29.8 %all-to-all-start.1 = ((bf16[16,512,128]{2,1,0:T(8,128)(2,1)}), bf16[16,512,128]{2,1,0:T(8,128)(2,1)S(1)}, u32[]{:S(2)}, u32[]{:S(2)}) async-start(bf16[16,512,128]{2,1,0:T(8,128)(2,1)} %spread.1), calls=%async_computation.1 | async-start | bytes 4194304 | tf_op jit(solution)/shard_map/all_to_all | solution.py:28
  27.1 24.2 %collective-permute-start.2 = (bf16[320,2048]{1,0:T(8,128)(2,1)}, bf16[320,2048]{1,0:T(8,128)(2,1)}, u32[]{:S(2)}, u32[]{:S(2)}) collective-permute-start(bf16[320,2048]{1,0:T(8,128)(2,1)} %bitcast.48), channel_id=1, source_target_pairs={{0,1},{1,0},{2,3},{3,2},{4,5},{5,4},{6,7},{7,6},{8,9},{9,8},{10,11... | collective-permute-start | bytes 3932168 | tf_op jit(solution)/shard_map/ppermute | solution.py:34
  29.3 22.0 %collective-permute-start.3 = (bf16[320,2048]{1,0:T(8,128)(2,1)}, bf16[320,2048]{1,0:T(8,128)(2,1)}, u32[]{:S(2)}, u32[]{:S(2)}) collective-permute-start(bf16[320,2048]{1,0:T(8,128)(2,1)} %bitcast.50), channel_id=1, source_target_pairs={{0,1},{1,0},{2,3},{3,2},{4,5},{5,4},{6,7},{7,6},{8,9},{9,8},{10,11... | collective-permute-start | bytes 3932168 | tf_op jit(solution)/shard_map/ppermute | solution.py:34
  31.4 19.9 %collective-permute-start.4 = (bf16[320,2048]{1,0:T(8,128)(2,1)}, bf16[320,2048]{1,0:T(8,128)(2,1)}, u32[]{:S(2)}, u32[]{:S(2)}) collective-permute-start(bf16[320,2048]{1,0:T(8,128)(2,1)} %wo_own_ref), channel_id=1, source_target_pairs={{0,1},{1,0},{2,3},{3,2},{4,5},{5,4},{6,7},{7,6},{8,9},{9,8},{10,11... | collective-permute-start | bytes 3932168 | tf_op jit(solution)/shard_map/ppermute | solution.py:34
  33.7 13.2 %collective-permute-start.5 = (bf16[3,8,256]{2,1,0:T(8,128)(2,1)S(1)}, bf16[3,8,256]{2,1,0:T(8,128)(2,1)S(1)}, u32[]{:S(2)}, u32[]{:S(2)}) collective-permute-start(bf16[3,8,256]{2,1,0:T(8,128)(2,1)S(1)} %pad_maximum_fusion.4), channel_id=1, source_target_pairs={{0,256},{16,272},{32,288},{48,304},{64,320},{80,336},{96,352},{112... | collective-permute-start | bytes 36872 | tf_op jit(solution)/shard_map/ppermute | solution.py:42
  46.9 19.2 %collective-permute-start.6 = (bf16[2,3,8,256]{3,2,1,0:T(8,128)(2,1)S(1)}, bf16[2,3,8,256]{3,2,1,0:T(8,128)(2,1)S(1)}, u32[]{:S(2)}, u32[]{:S(2)}) collective-permute-start(bf16[2,3,8,256]{3,2,1,0:T(8,128)(2,1)S(1)} %pad_maximum_fusion.3), channel_id=1, source_target_pairs={{0,16},{16,0},{32,48},{48,32},{64,80},{80,64},{96,112},{112,96},{1... | collective-permute-start | bytes 73736 | tf_op jit(solution)/shard_map/ppermute | solution.py:42
  62.4 29.8 %all-to-all-start.2 = ((bf16[16,512,128]{2,1,0:T(8,128)(2,1)}), bf16[16,512,128]{2,1,0:T(8,128)(2,1)S(1)}, u32[]{:S(2)}, u32[]{:S(2)}) async-start(bf16[16,512,128]{2,1,0:T(8,128)(2,1)} %ffn.1), calls=%async_computation.2 | async-start | bytes 4194304 | tf_op jit(solution)/shard_map/all_to_all | solution.py:28
  66.1 9.0 %collective-permute-start.7 = (bf16[2,2,3,8,256]{4,3,2,1,0:T(8,128)(2,1)S(1)}, bf16[2,2,3,8,256]{4,3,2,1,0:T(8,128)(2,1)S(1)}, u32[]{:S(2)}, u32[]{:S(2)}) collective-permute-start(bf16[2,2,3,8,256]{4,3,2,1,0:T(8,128)(2,1)S(1)} %pad_maximum_fusion.2), channel_id=1, source_target_pairs={{0,128},{16,144},{32,160},{48,176},{64,192},{80,208},{96,224},{112... | collective-permute-start | bytes 147464 | tf_op jit(solution)/shard_map/ppermute | solution.py:42
  75.1 6.6 %collective-permute-start.8 = (bf16[2,2,2,3,8,256]{5,4,3,2,1,0:T(8,128)(2,1)S(1)}, bf16[2,2,2,3,8,256]{5,4,3,2,1,0:T(8,128)(2,1)S(1)}, u32[]{:S(2)}, u32[]{:S(2)}) collective-permute-start(bf16[2,2,2,3,8,256]{5,4,3,2,1,0:T(8,128)(2,1)S(1)} %pad_maximum_fusion), channel_id=1, source_target_pairs={{0,64},{16,80},{32,96},{48,112},{64,0},{80,16},{96,32},{112,48},{1... | collective-permute-start | bytes 294920 | tf_op jit(solution)/shard_map/ppermute | solution.py:42
  81.7 6.6 %collective-permute-start.9 = (bf16[2,2,2,2,2,8,256]{6,5,4,3,2,1,0:T(8,128)(2,1)S(1)}, bf16[2,2,2,2,2,8,256]{6,5,4,3,2,1,0:T(8,128)(2,1)S(1)}, u32[]{:S(2)}, u32[]{:S(2)}) collective-permute-start(bf16[2,2,2,2,2,8,256]{6,5,4,3,2,1,0:T(8,128)(2,1)S(1)} %fusion.1), channel_id=1, source_target_pairs={{0,32},{16,48},{32,0},{48,16},{64,96},{80,112},{96,64},{112,80},{1... | collective-permute-start | bytes 393224 | tf_op jit(solution)/shard_map/ppermute | solution.py:42
  88.4 3.9 %copy-start.3 = (s32[8]{0:T(128)S(1)}, s32[8]{0:T(128)}, u32[]{:S(2)}) copy-start(s32[8]{0:T(128)} %ids_ref.3) | copy-start | bytes 100
  94.2 5.8 %copy-start.6 = (bf16[512,128]{1,0:T(8,128)(2,1)S(1)}, bf16[512,128]{1,0:T(8,128)(2,1)}, u32[]{:S(2)}) copy-start(bf16[512,128]{1,0:T(8,128)(2,1)} %get-tuple-element.19) | copy-start | bytes 393220
  94.2 19.2 %copy-start.1 = (bf16[1024,128]{1,0:T(8,128)(2,1)S(1)}, bf16[1024,128]{1,0:T(8,128)(2,1)}, u32[]{:S(2)}) copy-start(bf16[1024,128]{1,0:T(8,128)(2,1)} %tokens_ref.1) | copy-start | bytes 786436
  94.2 19.1 %copy-start.2 = (bf16[512,128]{1,0:T(8,128)(2,1)S(1)}, bf16[512,128]{1,0:T(8,128)(2,1)}, u32[]{:S(2)}) copy-start(bf16[512,128]{1,0:T(8,128)(2,1)} %get-tuple-element.18.mine_ref) | copy-start | bytes 393220
  94.2 11.9 %all-to-all-start.3 = ((bf16[8,256,128]{2,1,0:T(8,128)(2,1)}), bf16[8,256,128]{2,1,0:T(8,128)(2,1)S(1)}, u32[]{:S(2)}, u32[]{:S(2)}) async-start(bf16[8,256,128]{2,1,0:T(8,128)(2,1)} %get-tuple-element.20), calls=%async_computation.3 | async-start | bytes 1048576 | tf_op jit(solution)/shard_map/all_to_all | solution.py:28
  98.0 8.0 %collective-permute-start.12 = (bf16[2,2,2,2,8,256]{5,4,3,2,1,0:T(8,128)(2,1)S(1)}, bf16[2,2,2,2,8,256]{5,4,3,2,1,0:T(8,128)(2,1)S(1)}, u32[]{:S(2)}, u32[]{:S(2)}) collective-permute-start(bf16[2,2,2,2,8,256]{5,4,3,2,1,0:T(8,128)(2,1)S(1)} %fusion.2), channel_id=1, source_target_pairs={{0,32},{16,48},{32,0},{48,16},{64,96},{80,112},{96,64},{112,80},{1... | collective-permute-start | bytes 196616 | tf_op jit(solution)/shard_map/ppermute | solution.py:42
  100.0 12.8 %collective-permute-start.10 = (bf16[512,128]{1,0:T(8,128)(2,1)S(1)}, bf16[512,128]{1,0:T(8,128)(2,1)S(1)}, u32[]{:S(2)}, u32[]{:S(2)}) collective-permute-start(bf16[512,128]{1,0:T(8,128)(2,1)S(1)} %copy-done.6), channel_id=1, source_target_pairs={{0,1},{1,0},{2,3},{3,2},{4,5},{5,4},{6,7},{7,6},{8,9},{9,8},{10,11... | collective-permute-start | bytes 393224 | tf_op jit(solution)/shard_map/ppermute | solution.py:34
  106.2 7.2 %collective-permute-start.11 = (bf16[256,128]{1,0:T(8,128)(2,1)S(1)}, bf16[256,128]{1,0:T(8,128)(2,1)S(1)}, u32[]{:S(2)}, u32[]{:S(2)}) collective-permute-start(bf16[256,128]{1,0:T(8,128)(2,1)S(1)} %relu_sum.1.squeezed_ref), channel_id=1, source_target_pairs={{0,1},{1,0},{2,3},{3,2},{4,5},{5,4},{6,7},{7,6},{8,9},{9,8},{10,11... | collective-permute-start | bytes 196616 | tf_op jit(solution)/shard_map/ppermute | solution.py:34
